TPU v7x, 128 devices: a whole 4x4x4 slice. The times are simulated.
128 devices in a mesh: chan: 8 (over y_hi, z), frame: 16 (over x, y_lo, core).
Axes of the slice: x: 4, y: 4 (y_hi: 2, y_lo: 2; y = y_hi * 2 + y_lo), z: 4, core: 2. Of those that a mesh axis runs over, the one named last changes fastest.
Arguments:
- rf_data: bfloat16 [2, 8, 256, 1024], P(None, None, 'frame', 'chan'), may hold values from -6 to 6
- elem_pos: int32 [3, 1024], replicated, may hold values from -16 to 15, as said below
- vox_pos: int32 [3, 16384], P(None, 'chan'), may hold values from -32 to 62, as said below
- subbands: int32 [8], replicated, may hold values from 0 to 63, as said below
Outputs:
- filtered: bfloat16 [256, 2, 8, 16384], P('frame', None, None, 'chan')
Inputs may be any that keep to these rules, and one draw needn't show every extreme that they name: `elem_pos`: the element positions are the 32 x 32 grid with x and y from -16, each point once in a drawn order; z is 0, 1 or 2. `vox_pos`: distinct voxels of a box: x and y from -32 to 31, z from 48 to 62 in steps of 2. `subbands`: 8 distinct bin numbers.
All inputs are finite; a program needn't handle non-finite values.
Results may differ from a plain program's by a relative error of at most 0.0075.
Values may be sent and summed in bfloat16 or wider, within the bound.
No kernel may reach another device: no remote copies, remote signals or barrier semaphores. Data moves between devices by JAX's collectives and lax.ppermute only.
A program may use at most 128 MiB of HBM per device.

v0:
```python
import math

import jax
import jax.numpy as jnp
from jax import lax
from jax.sharding import PartitionSpec as P

TWO_PI = 2.0 * math.pi
EPSILON = 1e-06


def geometry(elem_pos, coords):
    elem = elem_pos.astype(jnp.float32)
    voxel = coords.astype(jnp.float32)
    delta_x = voxel[0][:, None] - elem[0][None, :]
    delta_y = voxel[1][:, None] - elem[1][None, :]
    delta_z = voxel[2][:, None] - elem[2][None, :]
    distance = jnp.sqrt(delta_x * delta_x + delta_y * delta_y + delta_z * delta_z)
    inverse = 1.0 / math.sqrt(elem_pos.shape[1])
    weight = delta_z / distance * inverse
    travel = voxel[2][:, None] + distance
    return (weight, travel)


def data_matrix(gathered):
    data_re = jnp.swapaxes(gathered[0], 1, 2)
    data_im = jnp.swapaxes(gathered[1], 1, 2)
    upper_rows = jnp.concatenate([data_re, data_im], axis=2)
    lower_rows = jnp.concatenate([-data_im, data_re], axis=2)
    return jnp.concatenate([upper_rows, lower_rows], axis=1)


def beamform(gathered, elem_pos, coords, subbands):
    weight, travel = geometry(elem_pos, coords)
    wavenum = (32.0 + subbands.astype(jnp.float32)) / 64.0
    matrix = data_matrix(gathered)
    nbins = gathered.shape[1]
    frames = gathered.shape[2]
    results = []
    for index in range(nbins):
        phase_angle = TWO_PI * wavenum[index] * travel
        operator = jnp.concatenate(
            [weight * jnp.cos(phase_angle), -(weight * jnp.sin(phase_angle))], axis=1
        ).astype(jnp.bfloat16)
        results.append(
            jnp.dot(operator, matrix[index], preferred_element_type=jnp.float32).astype(
                jnp.bfloat16
            )
        )
    volumes = jnp.stack(results, axis=1)
    return volumes.reshape(volumes.shape[0], nbins, 2, frames)


def complex_product(left_pair, right_pair):
    first_re, first_im = left_pair
    second_re, second_im = right_pair
    high = lax.Precision.HIGHEST
    real_part = jnp.einsum("bij,bjk->bik", first_re, second_re, precision=high) - jnp.einsum(
        "bij,bjk->bik", first_im, second_im, precision=high
    )
    imag_part = jnp.einsum("bij,bjk->bik", first_re, second_im, precision=high) + jnp.einsum(
        "bij,bjk->bik", first_im, second_re, precision=high
    )
    return (real_part, imag_part)


def filter_matrix(gram):
    gram_re = gram[:, 0]
    gram_im = gram[:, 1]
    frames = gram.shape[2]
    squares = jnp.sum(gram_re * gram_re + gram_im * gram_im, axis=(1, 2))
    factor = 4.0 / jnp.sqrt(squares + EPSILON)
    mat_re = gram_re * factor[:, None, None]
    mat_im = gram_im * factor[:, None, None]
    second = complex_product((mat_re, mat_im), (mat_re, mat_im))
    third = complex_product(second, (mat_re, mat_im))
    identity = jnp.eye(frames, dtype=jnp.float32)[None]
    filter_re = identity - mat_re + 0.3 * second[0] - 0.03 * third[0]
    filter_im = -mat_im + 0.3 * second[1] - 0.03 * third[1]
    return jnp.stack([filter_re, filter_im], axis=1).astype(jnp.bfloat16)


def block_filter(filter_bf):
    filter_re = filter_bf[:, 0]
    filter_im = filter_bf[:, 1]
    upper_rows = jnp.concatenate([filter_re, filter_im], axis=2)
    lower_rows = jnp.concatenate([-filter_im, filter_re], axis=2)
    return jnp.concatenate([upper_rows, lower_rows], axis=1)


def shards(rf_data, elem_pos, vox_pos, subbands):
    gathered = lax.all_gather(rf_data, "chan", axis=3, tiled=True)
    beamed = beamform(gathered, elem_pos, vox_pos, subbands)
    voxel_major = lax.all_to_all(beamed, "frame", split_axis=0, concat_axis=3, tiled=True)
    rows = voxel_major.shape[0]
    nbins = voxel_major.shape[1]
    frames = voxel_major.shape[3]
    stacked = voxel_major.reshape(rows, nbins, 2 * frames)
    products = jnp.einsum("vbi,vbj->bij", stacked, stacked, preferred_element_type=jnp.float32)
    gram_re = products[:, :frames, :frames] + products[:, frames:, frames:]
    gram_im = products[:, :frames, frames:] - products[:, frames:, :frames]
    gram = jnp.stack([gram_re, gram_im], axis=1)
    summed = lax.psum(gram, ("chan", "frame"))
    filter_bf = filter_matrix(summed)
    blocks = block_filter(filter_bf)
    applied = jnp.einsum(
        "vbi,bij->vbj", stacked, blocks, preferred_element_type=jnp.float32
    ).astype(jnp.bfloat16)
    applied = applied.reshape(rows, nbins, 2, frames)
    returned = lax.all_to_all(applied, "frame", split_axis=3, concat_axis=0, tiled=True)
    return jnp.transpose(returned, (3, 2, 1, 0))


def solution(mesh):
    return jax.shard_map(
        shards,
        mesh=mesh,
        in_specs=(P(None, None, "frame", "chan"), P(), P(None, "chan"), P()),
        out_specs=P("frame", None, None, "chan"),
        check_vma=False,
    )
```

profile of v0, /device:TPU:0, one launch (start us, length us, event | category | flops | bytes accessed | tf_op | source)
XLA Modules:
  0.0 637.7 jit_solution(4213955499166881249)
XLA Ops:
  6.5 32.4 %all_gather.3 = bf16[2,8,16,1024]{3,2,1,0:T(8,128)(2,1)S(1)} all-gather(bf16[2,8,16,128]{3,2,1,0:T(8,128)(2,1)} %param.4), channel_id=1, replica_groups=mesh['chan'=8,'frame'=16] {'chan'}, dimensions={3}, use_global_device_ids=true | all-gather | bytes 589824 | tf_op jit(solution)/shard_map/all_gather | solution.py:92
  46.1 0.8 convert_element_type.56
  47.0 270.8 %multiply_convert_fusion = (bf16[2048,1024]{1,0:T(8,128)(2,1)}, bf16[2048,1024]{1,0:T(8,128)(2,1)}, bf16[2048,1024]{1,0:T(8,128)(2,1)}, bf16[2048,1024]{1,0:T(8,...) fusion(f32[]{:T(128)} %bitcast.33, ...), kind=kLoop, calls=%fused_computation.38 | loop fusion | flops 123731968 | bytes 67145760 | tf_op jit(solution)/shard_map/convert.4
  317.9 4.8 fusion.73
  322.7 6.0 fusion.52
  328.7 6.1 fusion.67
  334.8 6.1 fusion.64
  340.8 4.1 fusion.61
  344.9 2.7 fusion.58
  347.6 2.7 fusion.55
  350.3 2.7 fusion.70
  353.2 14.7 %copy.97 = bf16[2048,8,2,16]{3,2,1,0:T(2,128)(2,1)} copy(bf16[2048,8,2,16]{0,3,2,1:T(8,128)(2,1)S(1)} %constant_dynamic-update-slice_fusion) | data formatting | bytes 2097152 | tf_op jit(solution)/shard_map/stack | solution.py:50
  367.9 10.4 %reshape.60 = bf16[16,2,16384]{2,1,0:T(2,128)(2,1)S(1)} reshape(bf16[2048,8,2,16]{3,2,1,0:T(2,128)(2,1)} %copy.97) | data formatting | bytes 2097152
  378.3 20.8 %all_to_all.33 = bf16[16,2,16384]{2,1,0:T(2,128)(2,1)S(1)} all-to-all(bf16[16,2,16384]{2,1,0:T(2,128)(2,1)S(1)} %reshape.60), channel_id=1, replica_groups=mesh['chan'=8,'frame'=16] {'frame'}, dimensions={0} | all-to-all | bytes 2097152 | tf_op jit(solution)/shard_map/all_to_all | solution.py:94
  399.1 7.5 %reshape.61 = bf16[2048,8,2,16]{3,2,1,0:T(2,128)(2,1)} reshape(bf16[16,2,16384]{2,1,0:T(2,128)(2,1)S(1)} %all_to_all.33) | data formatting | bytes 2097152
  406.6 18.2 %copy.141 = bf16[16,128,8,2,16]{1,4,0,3,2:T(8,128)(2,1)S(1)} copy(bf16[16,128,8,2,16]{4,3,2,1,0:T(2,128)(2,1)} %bitcast.109) | data formatting | bytes 2097152 | tf_op jit(solution)/shard_map/all_to_all | solution.py:94
  424.8 1.3 fusion.130
  426.7 2.4 pad_maximum_fusion
  429.2 152.6 %all-reduce.2.cloned.1.call-done = f32[8,2,256,256]{3,2,0,1:T(8,128)} async-done(((f32[8,2,256,256]{3,2,0,1:T(8,128)}), f32[8,2,256,256]{3,2,0,1:T(8,128)}) %all-reduce.2.cloned.1.call-update) | async-done | bytes 4194320 | tf_op jit(solution)/shard_map/psum | solution.py:103
  581.7 2.8 add_reduce_fusion
  585.2 2.3 fusion.95
  587.5 2.4 fusion.97
  589.9 2.4 fusion.99
  592.2 2.4 fusion.104
  594.6 2.6 fusion.44
  597.2 2.4 fusion.46
  599.6 3.1 fusion.129
  602.7 3.1 fusion.78
  605.8 1.9 fusion.90
  607.7 1.1 copy.119
  608.8 20.7 %all_to_all.34 = bf16[128,8,2,256]{0,2,1,3:T(2,128)(2,1)S(1)} all-to-all(bf16[128,8,2,256]{0,2,1,3:T(2,128)(2,1)S(1)} %copy.119), channel_id=1, replica_groups=mesh['chan'=8,'frame'=16] {'frame'}, dimensions={3} | all-to-all | bytes 2097152 | tf_op jit(solution)/shard_map/all_to_all | solution.py:110
  629.5 1.2 copy.143
  (23 shorter events, 3.7 us)
Async XLA Ops:
  6.5 575.2 %all-reduce.2.cloned.1.call-start = ((), (), s32[]{:S(2)}) async-start(), calls=%async_computation.2 | async-start | bytes 8388608 | tf_op jit(solution)/shard_map/psum | solution.py:103
  581.7 3.4 copy-start
Sparse Core Ops, SparseCore 0:
  429.3 152.4 all-reduce.1
where the time goes:
time: 645 us; the launch traced here: 638 us
  other arithmetic  279 us (43%)
  waiting for transfers between devices  153 us (24%)
  blocking collectives  73.9 us (11%)
  matrix products  58.8 us (9%)
  local copies, waits for them, and re-layouts  54.7 us (8%)
  between operations  18.8 us (3%)
    another operation x1, other arithmetic  271 us
    psum x1, waiting for transfers between devices, shards(): summed = lax.psum(gram, ('chan', 'frame'))  153 us
    dot_general x8, matrix products, beamform(): jnp.dot(operator, matrix[index], preferred_element_type=jnp.float32)  35.1 us
    all_gather x1, blocking collectives, shards(): gathered = lax.all_gather(rf_data, 'chan', axis=3, tiled=True)  32.4 us
    all_to_all x1, blocking collectives, shards(): lax.all_to_all(beamed, 'frame', split_axis=0, concat_axis=3, tiled=True)  20.8 us
    all_to_all x1, blocking collectives, shards(): lax.all_to_all(applied, 'frame', split_axis=3, concat_axis=0, tiled=True)  20.7 us
    unnamed x11, local copies, waits for them, and re-layouts  18.7 us
    all_to_all x1, local copies, waits for them, and re-layouts, shards(): lax.all_to_all(beamed, 'frame', split_axis=0, concat_axis=3, tiled=True)  18.2 us
  transfers between devices with their start and end apart: 1, of which 1 were waited for; matrix products, arithmetic and copies ran while one was open for 0% of the time, Pallas kernels for 0%

commit v1 on v0

v1 whole, which is shorter than its diff:
```python
import math

import jax
import jax.numpy as jnp
from jax import lax
from jax.experimental import pallas as pl
from jax.experimental.pallas import tpu as pltpu
from jax.sharding import Mesh, PartitionSpec as P

EPSILON = 1e-06
BINS = 8
CORES = 2
F32 = jnp.float32
BF16 = jnp.bfloat16
SIN = (3.1415925800446924, -5.167706878924515, 2.5500313772531213, -0.5980451739748806, 0.0772201286897368)
COS = (0.9999999534666272, -4.934792858670076, 4.058411914063177, -1.331880160583308, 0.21969679727234584)
ROWS = 32
LANES = 256
WIDE = pltpu.CompilerParams(vmem_limit_bytes=48 * 1024 * 1024)


def horner(coefficients, z):
    total = jnp.full_like(z, coefficients[-1])
    for value in coefficients[-2::-1]:
        total = total * z + value
    return total


def operator_tile(columns, voxel, wavenumber, scale):
    delta_x = voxel[0] - columns[0]
    delta_y = voxel[1] - columns[1]
    delta_z = voxel[2] - columns[2]
    squared = delta_x * delta_x + delta_y * delta_y + delta_z * delta_z
    inverse = lax.rsqrt(squared)
    turns = (voxel[2] + squared * inverse) * wavenumber
    part = turns - jnp.round(turns)
    z = part * part
    sine = part * horner(SIN, z)
    cosine = horner(COS, z)
    double = delta_z * inverse * (2.0 * scale)
    lean = double * sine
    return 0.5 * double - lean * sine, lean * cosine


def beam_kernel(elem, vox, subbands, own, other, y_ref, keep_ref, send_ref, data, cosines, sines, places, gram):
    core = lax.axis_index("core")
    channels = elem.shape[1]
    frames = y_ref.shape[0] // 2
    half = frames // CORES
    voxels = y_ref.shape[1]
    here = pl.multiple_of(core * half, half)
    there = pl.multiple_of((1 - core) * half, half)
    blocks = own.shape[0]
    width = own.shape[-1]
    for k in range(blocks):
        for part in range(2):
            lanes = slice(k * width, (k + 1) * width)
            data[pl.ds(part * frames + here, half), lanes] = own[k, :, part].reshape(half, width)
            data[pl.ds(part * frames + there, half), lanes] = other[k, :, part].reshape(half, width)
    wavenumber = (32.0 + subbands[lax.axis_index("bin")].astype(F32)) / 64.0
    scale = 1.0 / math.sqrt(channels)
    stacked = elem[...].astype(F32)
    padded = jnp.concatenate([stacked, jnp.zeros((5, channels), F32)], axis=0)
    places[...] = jnp.transpose(padded)
    for block in range(voxels // LANES):
        lanes = slice(block * LANES, (block + 1) * LANES)
        at = pl.multiple_of(core * voxels + block * LANES, LANES)
        voxel = [vox[d : d + 1, pl.ds(at, LANES)].astype(F32) for d in range(3)]

        def tile(index, carry, voxel=voxel, lanes=lanes):
            rows = pl.ds(pl.multiple_of(index * ROWS, ROWS), ROWS)
            columns = [places[rows, d : d + 1] for d in range(3)]
            real, imag = operator_tile(columns, voxel, wavenumber, scale)
            cosines[rows, lanes] = real.astype(BF16)
            sines[rows, lanes] = imag.astype(BF16)
            return carry

        lax.fori_loop(0, channels // ROWS, tile, 0)
        first = jnp.dot(data[...], cosines[:, lanes], preferred_element_type=F32)
        second = jnp.dot(data[...], sines[:, lanes], preferred_element_type=F32)
        y_ref[:frames, lanes] = (first[:frames] + second[frames:]).astype(BF16)
        y_ref[frames:, lanes] = (first[frames:] - second[:frames]).astype(BF16)
    y = y_ref[...]
    products = lax.dot_general(y, y, (((1,), (1,)), ((), ())), preferred_element_type=F32)
    gram[...] = (products[:frames, :frames] + products[frames:, frames:]) + (
        products[:frames, frames:] - products[frames:, :frames]
    )
    keep_ref[...] = gram[pl.ds(here, half), :]
    send_ref[...] = gram[pl.ds(there, half), :]


def complex_product(left, right):
    def dot(a, b):
        return jnp.dot(a, b, preferred_element_type=F32, precision=lax.Precision.HIGHEST)

    return (
        dot(left[0], right[0]) - dot(left[1], right[1]),
        dot(left[0], right[1]) + dot(left[1], right[0]),
    )


def filter_kernel(own, other, y_ref, out_ref, gram):
    core = lax.axis_index("core")
    half, frames = own.shape
    gram[pl.ds(pl.multiple_of(core * half, half), half), :] = own[...]
    gram[pl.ds(pl.multiple_of((1 - core) * half, half), half), :] = other[...]
    both = gram[...]
    flipped = jnp.transpose(both)
    gram_re = 0.5 * (both + flipped)
    gram_im = 0.5 * (both - flipped)
    squares = jnp.sum(gram_re * gram_re + gram_im * gram_im)
    factor = 4.0 / jnp.sqrt(jnp.full((1, 1), squares + EPSILON, F32))
    mat = (gram_re * factor, gram_im * factor)
    second = complex_product(mat, mat)
    third = complex_product(second, mat)
    rows = lax.broadcasted_iota(jnp.int32, (frames, frames), 0)
    cols = lax.broadcasted_iota(jnp.int32, (frames, frames), 1)
    identity = jnp.where(rows == cols, 1.0, 0.0).astype(F32)
    real = (identity - mat[0] + 0.3 * second[0] - 0.03 * third[0]).astype(BF16)
    imag = (-mat[1] + 0.3 * second[1] - 0.03 * third[1]).astype(BF16)
    matrix = jnp.concatenate(
        [jnp.concatenate([real, imag], axis=1), jnp.concatenate([-imag, real], axis=1)], axis=0
    )
    applied = jnp.dot(matrix, y_ref[...], preferred_element_type=F32).astype(BF16)
    group = out_ref.shape[2]
    bins = out_ref.shape[0] // CORES
    for part in range(2):
        for c in range(CORES):
            for j in range(bins):
                row = part * frames + c * half + j * group
                out_ref[j * CORES + c, part] = applied[row : row + group]


def place_kernel(got, out_ref):
    group, _, bins, _ = out_ref.shape
    voxels = got.shape[-1]
    size = group * bins
    rows = lax.broadcasted_iota(jnp.int32, (size, size), 0)
    cols = lax.broadcasted_iota(jnp.int32, (size, size), 1)
    turn = jnp.where(cols == (rows % bins) * group + rows // bins, 1.0, 0.0).astype(BF16)
    for c in range(CORES):
        for part in range(2):
            block = got[:, c, part].reshape(size, voxels)
            moved = jnp.dot(turn, block, preferred_element_type=F32).astype(BF16)
            out_ref[:, part, :, c * voxels : (c + 1) * voxels] = moved.reshape(group, bins, voxels)


def shards(rf_data, elem_pos, vox_pos, subbands):
    parts, bins, group, width = rf_data.shape
    chans = elem_pos.shape[1] // width
    voxels = vox_pos.shape[1] // CORES
    frames = group * bins * CORES
    half = frames // CORES
    swap = [(0, 1), (1, 0)]
    vmem = pl.BlockSpec(memory_space=pltpu.VMEM)
    smem = pl.BlockSpec(memory_space=pltpu.SMEM)

    by_bin = jnp.broadcast_to(jnp.swapaxes(rf_data, 0, 1)[None], (chans, bins, parts, group, width))
    by_bin = by_bin.reshape(chans * bins, parts, group, width)
    own = lax.all_to_all(by_bin, ("chan", "bin"), split_axis=0, concat_axis=0, tiled=True)
    other = lax.ppermute(own, "core", swap)
    own = own.reshape(chans, bins, parts, group, width)
    other = other.reshape(chans, bins, parts, group, width)

    y, keep, send = pl.pallas_call(
        beam_kernel,
        name="beam",
        out_shape=(
            jax.ShapeDtypeStruct((2 * frames, voxels), BF16),
            jax.ShapeDtypeStruct((half, frames), F32),
            jax.ShapeDtypeStruct((half, frames), F32),
        ),
        in_specs=[vmem, vmem, smem, vmem, vmem],
        out_specs=(vmem, vmem, vmem),
        scratch_shapes=[
            pltpu.VMEM((2 * frames, chans * width), BF16),
            pltpu.VMEM((chans * width, voxels), BF16),
            pltpu.VMEM((chans * width, voxels), BF16),
            pltpu.VMEM((chans * width, 8), F32),
            pltpu.VMEM((frames, frames), F32),
        ],
        compiler_params=WIDE,
    )(elem_pos, vox_pos, subbands, own, other)

    total = keep + lax.ppermute(send, "core", swap)
    step = 1
    while step < chans:
        total = total + lax.ppermute(total, "chan", [(a, a ^ step) for a in range(chans)])
        step *= 2
    rest = lax.ppermute(total, "core", swap)

    applied = pl.pallas_call(
        filter_kernel,
        name="filter",
        out_shape=jax.ShapeDtypeStruct((bins * CORES, parts, group, voxels), BF16),
        in_specs=[vmem, vmem, vmem],
        out_specs=vmem,
        scratch_shapes=[pltpu.VMEM((frames, frames), F32)],
        compiler_params=WIDE,
    )(total, rest, y)

    got = lax.all_to_all(applied, ("bin", "core"), split_axis=0, concat_axis=0, tiled=True)
    got = got.reshape(bins, CORES, parts, group, voxels)
    return pl.pallas_call(
        place_kernel,
        name="place",
        out_shape=jax.ShapeDtypeStruct((group, parts, bins, CORES * voxels), BF16),
        in_specs=[vmem],
        out_specs=vmem,
        compiler_params=WIDE,
    )(got)


def solution(mesh):
    chans = mesh.shape["chan"]
    fine = Mesh(mesh.devices.reshape(chans, BINS, CORES), ("chan", "bin", "core"))
    return jax.shard_map(
        shards,
        mesh=fine,
        in_specs=(P(None, None, ("bin", "core"), "chan"), P(), P(None, "chan"), P()),
        out_specs=P(("bin", "core"), None, None, "chan"),
        check_vma=False,
    )
```

time: 645 us -> 96.9 us (0.15); the launches traced: 638 us -> 96.5 us
  other arithmetic: 279 us -> 0.07 us
  waiting for transfers between devices: 153 us -> 19.4 us
  matrix products: 58.8 us -> 0 us
  local copies, waits for them, and re-layouts: 54.7 us -> 1.59 us
  blocking collectives: 73.9 us -> 43.5 us
  Pallas kernels: 0 us -> 27.8 us
  between operations: 18.8 us -> 0.06 us
    another operation x3 -> x0, other arithmetic: 274 us -> none
    psum x1 -> x0, waiting for transfers between devices: 153 us -> none  [shards(): summed = lax.psum(gram, ('chan', 'frame'))]
    dot_general x18 -> x0, matrix products: 58.8 us -> none  [the longest x8 35.1 us: beamform(): jnp.dot(operator, matrix[index], preferred_element_type=jnp.float32)]
    all_gather x1 -> x0, blocking collectives: 32.4 us -> none  [shards(): gathered = lax.all_gather(rf_data, 'chan', axis=3, tiled=True)]
    pallas_call x0 -> x3, Pallas kernels: none -> 27.8 us  [the longest x1 22.7 us: shards(): pl.pallas_call(beam_kernel, name='beam', out_shape=(jax.ShapeDtypeStruct(...]
    all_to_all x2 -> x0, local copies, waits for them, and re-layouts: 19.4 us -> none  [the longest x1 18.2 us: shards(): lax.all_to_all(beamed, 'frame', split_axis=0, concat_axis=3, tiled=True)]
    ppermute x0 -> x6, waiting for transfers between devices: none -> 19.4 us  [the longest x3 14.9 us: shards(): lax.ppermute(total, 'chan', [(a, a ^ step) for a in range(chans)])]
    unnamed x11 -> x6, local copies, waits for them, and re-layouts: 18.7 us -> 0.66 us
  transfers between devices with their start and end apart: 1 -> 6, of which waited for: 1 -> 6; matrix products, arithmetic and copies ran while one was open for 0% -> 0% of each run, Pallas kernels for 0% -> 0%
where the time goes in v1:
time: 96.9 us; the launch traced here: 96.5 us
  blocking collectives  43.5 us (45%)
  Pallas kernels  27.8 us (29%)
  waiting for transfers between devices  19.4 us (20%)
  starting transfers between devices  4.09 us (4%)
  local copies, waits for them, and re-layouts  1.59 us (2%)
    all_to_all x1, blocking collectives, shards(): lax.all_to_all(by_bin, ('chan', 'bin'), split_axis=0, concat_axis=0, tile...  24.2 us
    pallas_call x1, Pallas kernels, shards(): pl.pallas_call(beam_kernel, name='beam', out_shape=(jax.ShapeDtypeStruct(...  22.7 us
    all_to_all x1, blocking collectives, shards(): lax.all_to_all(applied, ('bin', 'core'), split_axis=0, concat_axis=0, til...  19.3 us
    ppermute x3, waiting for transfers between devices, shards(): lax.ppermute(total, 'chan', [(a, a ^ step) for a in range(chans)])  14.9 us
    ppermute x3, starting transfers between devices, shards(): lax.ppermute(total, 'chan', [(a, a ^ step) for a in range(chans)])  3.79 us
    pallas_call x1, Pallas kernels, shards(): pl.pallas_call(filter_kernel, name='filter', out_shape=jax.ShapeDtypeStru...  3.72 us
  transfers between devices with their start and end apart: 6, of which 6 were waited for; matrix products, arithmetic and copies ran while one was open for 0% of the time, Pallas kernels for 0%

profile of v1, /device:TPU:0, one launch (start us, length us, event | category | flops | bytes accessed | tf_op | source)
XLA Modules:
  0.0 96.5 jit_solution(3578416936471664262)
XLA Ops:
  0.0 0.8 copy.5
  0.8 0.1 broadcast_in_dim.2
  0.9 0.0 copy-start
  0.9 0.0 copy-start.1
  1.0 24.2 %all_to_all.10 = bf16[64,2,16,128]{3,2,1,0:T(8,128)(2,1)S(1)} all-to-all(bf16[64,2,16,128]{3,2,1,0:T(8,128)(2,1)S(1)} %bitcast.8), channel_id=1, replica_groups=mesh['chan'=8,'bin'=8,'core'=2] {'chan','bin'}, dimensions={0} | all-to-all | bytes 1048576 | tf_op jit(solution)/shard_map/all_to_all | solution.py:160
  25.2 0.0 collective-permute-start
  25.2 1.9 %collective-permute-done = bf16[64,2,16,128]{3,2,1,0:T(8,128)(2,1)S(1)} collective-permute-done((bf16[64,2,16,128]{3,2,1,0:T(8,128)(2,1)S(1)}, bf16[64,2,16,128]{3,2,1,0:T(8,128)(2,1)S(1)}, u32[]{:S(2)}, u32[]{:S(2)}) %collective-permute-start) | collective-permute-done | bytes 524320 | tf_op jit(solution)/shard_map/ppermute | solution.py:161
  27.1 0.0 copy-start.2
  27.1 0.0 copy-done
  27.1 0.0 copy-done.1
  27.1 0.6 copy-done.2
  27.8 22.7 %beam.1 = (bf16[512,1024]{1,0:T(8,128)(2,1)S(1)}, f32[128,256]{1,0:T(8,128)S(1)}, f32[128,256]{1,0:T(8,128)S(1)}) custom-call(s32[3,1024]{1,0:T(4,128)S(1)} %copy-done.1, s32[3,2048]{1,0:T(4,128)S(1)} %copy-done, s32[8]{0:T(128)S(1)} %copy-done.2, bf16[8,8,2,16,128]{4,3,2,1,0:T(8,128)(2,1)S(1)} %bitcast.6, bf16[8,8,2,16,128]{4,3,2,1,0:T(8,128)(2,1)S(1)} %bitcast.7), custom_call_target="tpu_custom_call" | custom-call | tf_op jit(solution)/shard_map/beam/pallas_call | solution.py:165
  50.5 0.2 collective-permute-start.1
  50.7 1.2 %collective-permute-done.1 = f32[128,256]{1,0:T(8,128)S(1)} collective-permute-done((f32[128,256]{1,0:T(8,128)S(1)}, f32[128,256]{1,0:T(8,128)S(1)}, u32[]{:S(2)}, u32[]{:S(2)}) %collective-permute-start.1) | collective-permute-done | bytes 131104 | tf_op jit(solution)/shard_map/ppermute | solution.py:185
  51.9 0.4 collective-permute-start.2
  52.4 5.2 %collective-permute-done.2 = f32[128,256]{1,0:T(8,128)S(1)} collective-permute-done((f32[128,256]{1,0:T(8,128)S(1)}, f32[128,256]{1,0:T(8,128)S(1)}, u32[]{:S(2)}, u32[]{:S(2)}) %collective-permute-start.2) | collective-permute-done | bytes 131104 | tf_op jit(solution)/shard_map/ppermute | solution.py:188
  57.6 1.7 %collective-permute-start.3 = (f32[128,256]{1,0:T(8,128)S(1)}, f32[128,256]{1,0:T(8,128)S(1)}, u32[]{:S(2)}, u32[]{:S(2)}) collective-permute-start(f32[128,256]{1,0:T(8,128)S(1)} %add.13), channel_id=1, source_target_pairs={{0,32},{16,48},{32,0},{48,16},{64,96},{80,112},{96,64},{112,80},{1... | collective-permute-start | bytes 393224 | tf_op jit(solution)/shard_map/ppermute | solution.py:188
  59.3 4.9 %collective-permute-done.3 = f32[128,256]{1,0:T(8,128)S(1)} collective-permute-done((f32[128,256]{1,0:T(8,128)S(1)}, f32[128,256]{1,0:T(8,128)S(1)}, u32[]{:S(2)}, u32[]{:S(2)}) %collective-permute-start.3) | collective-permute-done | bytes 131104 | tf_op jit(solution)/shard_map/ppermute | solution.py:188
  64.1 1.7 %collective-permute-start.4 = (f32[128,256]{1,0:T(8,128)S(1)}, f32[128,256]{1,0:T(8,128)S(1)}, u32[]{:S(2)}, u32[]{:S(2)}) collective-permute-start(f32[128,256]{1,0:T(8,128)S(1)} %add.14), channel_id=1, source_target_pairs={{0,64},{16,80},{32,96},{48,112},{64,0},{80,16},{96,32},{112,48},{1... | collective-permute-start | bytes 393224 | tf_op jit(solution)/shard_map/ppermute | solution.py:188
  65.8 4.9 %collective-permute-done.4 = f32[128,256]{1,0:T(8,128)S(1)} collective-permute-done((f32[128,256]{1,0:T(8,128)S(1)}, f32[128,256]{1,0:T(8,128)S(1)}, u32[]{:S(2)}, u32[]{:S(2)}) %collective-permute-start.4) | collective-permute-done | bytes 131104 | tf_op jit(solution)/shard_map/ppermute | solution.py:188
  70.7 0.1 collective-permute-start.5
  70.8 1.3 %collective-permute-done.5.other = f32[128,256]{1,0:T(8,128)S(1)} collective-permute-done((f32[128,256]{1,0:T(8,128)S(1)}, f32[128,256]{1,0:T(8,128)S(1)}, u32[]{:S(2)}, u32[]{:S(2)}) %collective-permute-start.5) | collective-permute-done | bytes 131104 | tf_op jit(solution)/shard_map/ppermute | solution.py:190
  72.1 3.7 %filter.1 = bf16[16,2,16,1024]{3,2,1,0:T(8,128)(2,1)S(1)} custom-call(f32[128,256]{1,0:T(8,128)S(1)} %add.15.own, f32[128,256]{1,0:T(8,128)S(1)} %collective-permute-done.5.other, bf16[512,1024]{1,0:T(8,128)(2,1)S(1)} %get-tuple-element.10.y_ref), custom_call_target="tpu_custom_call" | custom-call | tf_op jit(solution)/shard_map/filter/pallas_call | solution.py:192
  75.9 19.3 %all_to_all.11 = bf16[16,2,16,1024]{3,2,1,0:T(8,128)(2,1)S(1)} all-to-all(bf16[16,2,16,1024]{3,2,1,0:T(8,128)(2,1)S(1)} %filter.1), channel_id=1, replica_groups=mesh['chan'=8,'bin'=8,'core'=2] {'bin','core'}, dimensions={0} | all-to-all | bytes 2097152 | tf_op jit(solution)/shard_map/all_to_all | solution.py:202
  95.2 1.4 %place.1 = bf16[16,2,8,2048]{3,2,1,0:T(8,128)(2,1)} custom-call(bf16[8,2,2,16,1024]{4,3,2,1,0:T(8,128)(2,1)S(1)} %bitcast.5), custom_call_target="tpu_custom_call" | custom-call | tf_op jit(solution)/shard_map/place/pallas_call | solution.py:204
  (4 shorter events, 0.1 us)
Async XLA Ops:
  0.9 26.2 %copy-start = (s32[3,2048]{1,0:T(4,128)S(1)}, s32[3,2048]{1,0:T(4,128)}, u32[]{:S(2)}) copy-start(s32[3,2048]{1,0:T(4,128)} %vox.1) | copy-start | bytes 73732
  0.9 26.2 %copy-start.1 = (s32[3,1024]{1,0:T(4,128)S(1)}, s32[3,1024]{1,0:T(4,128)}, u32[]{:S(2)}) copy-start(s32[3,1024]{1,0:T(4,128)} %elem.1) | copy-start | bytes 36868
  25.2 1.9 %collective-permute-start = (bf16[64,2,16,128]{3,2,1,0:T(8,128)(2,1)S(1)}, bf16[64,2,16,128]{3,2,1,0:T(8,128)(2,1)S(1)}, u32[]{:S(2)}, u32[]{:S(2)}) collective-permute-start(bf16[64,2,16,128]{3,2,1,0:T(8,128)(2,1)S(1)} %all_to_all.10), channel_id=1, source_target_pairs={{0,1},{1,0},{2,3},{3,2},{4,5},{5,4},{6,7},{7,6},{8,9},{9,8},{10,11... | collective-permute-start | bytes 1572872 | tf_op jit(solution)/shard_map/ppermute | solution.py:161
  27.1 0.7 copy-start.2
  50.5 1.4 %collective-permute-start.1 = (f32[128,256]{1,0:T(8,128)S(1)}, f32[128,256]{1,0:T(8,128)S(1)}, u32[]{:S(2)}, u32[]{:S(2)}) collective-permute-start(f32[128,256]{1,0:T(8,128)S(1)} %get-tuple-element.9), channel_id=1, source_target_pairs={{0,1},{1,0},{2,3},{3,2},{4,5},{5,4},{6,7},{7,6},{8,9},{9,8},{10,11... | collective-permute-start | bytes 393224 | tf_op jit(solution)/shard_map/ppermute | solution.py:185
  51.9 5.6 %collective-permute-start.2 = (f32[128,256]{1,0:T(8,128)S(1)}, f32[128,256]{1,0:T(8,128)S(1)}, u32[]{:S(2)}, u32[]{:S(2)}) collective-permute-start(f32[128,256]{1,0:T(8,128)S(1)} %add.12), channel_id=1, source_target_pairs={{0,16},{16,0},{32,48},{48,32},{64,80},{80,64},{96,112},{112,96},{1... | collective-permute-start | bytes 393224 | tf_op jit(solution)/shard_map/ppermute | solution.py:188
  57.6 6.6 %collective-permute-start.3 = (f32[128,256]{1,0:T(8,128)S(1)}, f32[128,256]{1,0:T(8,128)S(1)}, u32[]{:S(2)}, u32[]{:S(2)}) collective-permute-start(f32[128,256]{1,0:T(8,128)S(1)} %add.13), channel_id=1, source_target_pairs={{0,32},{16,48},{32,0},{48,16},{64,96},{80,112},{96,64},{112,80},{1... | collective-permute-start | bytes 393224 | tf_op jit(solution)/shard_map/ppermute | solution.py:188
  64.1 6.6 %collective-permute-start.4 = (f32[128,256]{1,0:T(8,128)S(1)}, f32[128,256]{1,0:T(8,128)S(1)}, u32[]{:S(2)}, u32[]{:S(2)}) collective-permute-start(f32[128,256]{1,0:T(8,128)S(1)} %add.14), channel_id=1, source_target_pairs={{0,64},{16,80},{32,96},{48,112},{64,0},{80,16},{96,32},{112,48},{1... | collective-permute-start | bytes 393224 | tf_op jit(solution)/shard_map/ppermute | solution.py:188
  70.7 1.4 %collective-permute-start.5 = (f32[128,256]{1,0:T(8,128)S(1)}, f32[128,256]{1,0:T(8,128)S(1)}, u32[]{:S(2)}, u32[]{:S(2)}) collective-permute-start(f32[128,256]{1,0:T(8,128)S(1)} %add.15.own), channel_id=1, source_target_pairs={{0,1},{1,0},{2,3},{3,2},{4,5},{5,4},{6,7},{7,6},{8,9},{9,8},{10,11... | collective-permute-start | bytes 393224 | tf_op jit(solution)/shard_map/ppermute | solution.py:190

commit v2 on v1

--- a/solution.py
+++ b/solution.py
@@ -42,9 +42,32 @@
     return 0.5 * double - lean * sine, lean * cosine
 
 
-def beam_kernel(elem, vox, subbands, own, other, y_ref, keep_ref, send_ref, data, cosines, sines, places, gram):
+def operator_kernel(elem, vox, subbands, cosines, sines, places):
     core = lax.axis_index("core")
-    channels = elem.shape[1]
+    channels, voxels = cosines.shape
+    wavenumber = (32.0 + subbands[lax.axis_index("bin")].astype(F32)) / 64.0
+    scale = 1.0 / math.sqrt(channels)
+    stacked = elem[...].astype(F32)
+    padded = jnp.concatenate([stacked, jnp.zeros((5, channels), F32)], axis=0)
+    places[...] = jnp.transpose(padded)
+    for block in range(voxels // LANES):
+        lanes = slice(block * LANES, (block + 1) * LANES)
+        at = pl.multiple_of(core * voxels + block * LANES, LANES)
+        voxel = [vox[d : d + 1, pl.ds(at, LANES)].astype(F32) for d in range(3)]
+
+        def tile(index, carry, voxel=voxel, lanes=lanes):
+            rows = pl.ds(pl.multiple_of(index * ROWS, ROWS), ROWS)
+            columns = [places[rows, d : d + 1] for d in range(3)]
+            real, imag = operator_tile(columns, voxel, wavenumber, scale)
+            cosines[rows, lanes] = real.astype(BF16)
+            sines[rows, lanes] = imag.astype(BF16)
+            return carry
+
+        lax.fori_loop(0, channels // ROWS, tile, 0)
+
+
+def beam_kernel(cosines, sines, own, other, y_ref, keep_ref, send_ref, data, gram):
+    core = lax.axis_index("core")
     frames = y_ref.shape[0] // 2
     half = frames // CORES
     voxels = y_ref.shape[1]
@@ -57,25 +80,8 @@
             lanes = slice(k * width, (k + 1) * width)
             data[pl.ds(part * frames + here, half), lanes] = own[k, :, part].reshape(half, width)
             data[pl.ds(part * frames + there, half), lanes] = other[k, :, part].reshape(half, width)
-    wavenumber = (32.0 + subbands[lax.axis_index("bin")].astype(F32)) / 64.0
-    scale = 1.0 / math.sqrt(channels)
-    stacked = elem[...].astype(F32)
-    padded = jnp.concatenate([stacked, jnp.zeros((5, channels), F32)], axis=0)
-    places[...] = jnp.transpose(padded)
     for block in range(voxels // LANES):
         lanes = slice(block * LANES, (block + 1) * LANES)
-        at = pl.multiple_of(core * voxels + block * LANES, LANES)
-        voxel = [vox[d : d + 1, pl.ds(at, LANES)].astype(F32) for d in range(3)]
-
-        def tile(index, carry, voxel=voxel, lanes=lanes):
-            rows = pl.ds(pl.multiple_of(index * ROWS, ROWS), ROWS)
-            columns = [places[rows, d : d + 1] for d in range(3)]
-            real, imag = operator_tile(columns, voxel, wavenumber, scale)
-            cosines[rows, lanes] = real.astype(BF16)
-            sines[rows, lanes] = imag.astype(BF16)
-            return carry
-
-        lax.fori_loop(0, channels // ROWS, tile, 0)
         first = jnp.dot(data[...], cosines[:, lanes], preferred_element_type=F32)
         second = jnp.dot(data[...], sines[:, lanes], preferred_element_type=F32)
         y_ref[:frames, lanes] = (first[:frames] + second[frames:]).astype(BF16)
@@ -158,6 +164,22 @@
     by_bin = jnp.broadcast_to(jnp.swapaxes(rf_data, 0, 1)[None], (chans, bins, parts, group, width))
     by_bin = by_bin.reshape(chans * bins, parts, group, width)
     own = lax.all_to_all(by_bin, ("chan", "bin"), split_axis=0, concat_axis=0, tiled=True)
+    cosines, sines = pl.pallas_call(
+        operator_kernel,
+        name="operator",
+        out_shape=(jax.ShapeDtypeStruct((chans * width, voxels), BF16),) * 2,
+        in_specs=[vmem, vmem, smem],
+        out_specs=(vmem, vmem),
+        scratch_shapes=[pltpu.VMEM((chans * width, 8), F32)],
+        compiler_params=WIDE,
+        cost_estimate=pl.CostEstimate(
+            flops=60 * chans * width * voxels,
+            transcendentals=chans * width * voxels,
+            bytes_accessed=4 * chans * width * voxels,
+        ),
+    )(elem_pos, vox_pos, subbands)
+
+    own, cosines, sines = lax.optimization_barrier((own, cosines, sines))
     other = lax.ppermute(own, "core", swap)
     own = own.reshape(chans, bins, parts, group, width)
     other = other.reshape(chans, bins, parts, group, width)
@@ -170,17 +192,14 @@
             jax.ShapeDtypeStruct((half, frames), F32),
             jax.ShapeDtypeStruct((half, frames), F32),
         ),
-        in_specs=[vmem, vmem, smem, vmem, vmem],
+        in_specs=[vmem, vmem, vmem, vmem],
         out_specs=(vmem, vmem, vmem),
         scratch_shapes=[
             pltpu.VMEM((2 * frames, chans * width), BF16),
-            pltpu.VMEM((chans * width, voxels), BF16),
-            pltpu.VMEM((chans * width, voxels), BF16),
-            pltpu.VMEM((chans * width, 8), F32),
             pltpu.VMEM((frames, frames), F32),
         ],
         compiler_params=WIDE,
-    )(elem_pos, vox_pos, subbands, own, other)
+    )(cosines, sines, own, other)
 
     total = keep + lax.ppermute(send, "core", swap)
     step = 1

time: 96.9 us -> 90.2 us (0.931)
  blocking collectives: 43.5 us -> 21.6 us
  starting transfers between devices: 4.09 us -> 19.9 us
  waiting for transfers between devices: 19.4 us -> 15.1 us
  local copies, waits for them, and re-layouts: 1.59 us -> 5.17 us
    all_to_all x1 -> x0, blocking collectives: 24.2 us -> none  [shards(): lax.all_to_all(by_bin, ('chan', 'bin'), split_axis=0, concat_axis=0, tile...]
    pallas_call x1, Pallas kernels: 22.7 us -> 5.34 us  [shards(): pl.pallas_call(beam_kernel, name='beam', out_shape=(jax.ShapeDtypeStruct(...]
    pallas_call x0 -> x1, Pallas kernels: none -> 17.3 us  [shards(): pl.pallas_call(operator_kernel, name='operator', out_shape=(jax.ShapeDtyp...]
    all_to_all x0 -> x1, starting transfers between devices: none -> 11.5 us  [shards(): lax.all_to_all(by_bin, ('chan', 'bin'), split_axis=0, concat_axis=0, tile...]
    ppermute x3, starting transfers between devices: 3.79 us -> 8.1 us  [shards(): lax.ppermute(total, 'chan', [(a, a ^ step) for a in range(chans)])]
    ppermute x3, waiting for transfers between devices: 14.9 us -> 10.6 us  [shards(): lax.ppermute(total, 'chan', [(a, a ^ step) for a in range(chans)])]
    unnamed x6 -> x8, local copies, waits for them, and re-layouts: 0.66 us -> 3.44 us
    all_to_all x1, blocking collectives: 19.3 us -> 21.6 us  [shards(): lax.all_to_all(applied, ('bin', 'core'), split_axis=0, concat_axis=0, til...]
  transfers between devices with their start and end apart: 6 -> 7, of which waited for: 6 -> 6; matrix products, arithmetic and copies ran while one was open for 0% -> 0% of each run, Pallas kernels for 0% -> 19%
where the time goes in v2:
time: 90.2 us; the launch traced here: 89.7 us
  Pallas kernels  27.7 us (31%)
  blocking collectives  21.6 us (24%)
  starting transfers between devices  19.9 us (22%)
  waiting for transfers between devices  15.1 us (17%)
  local copies, waits for them, and re-layouts  5.17 us (6%)
    all_to_all x1, blocking collectives, shards(): lax.all_to_all(applied, ('bin', 'core'), split_axis=0, concat_axis=0, til...  21.6 us
    pallas_call x1, Pallas kernels, shards(): pl.pallas_call(operator_kernel, name='operator', out_shape=(jax.ShapeDtyp...  17.3 us
    all_to_all x1, starting transfers between devices, shards(): lax.all_to_all(by_bin, ('chan', 'bin'), split_axis=0, concat_axis=0, tile...  11.5 us
    ppermute x3, waiting for transfers between devices, shards(): lax.ppermute(total, 'chan', [(a, a ^ step) for a in range(chans)])  10.6 us
    ppermute x3, starting transfers between devices, shards(): lax.ppermute(total, 'chan', [(a, a ^ step) for a in range(chans)])  8.1 us
    pallas_call x1, Pallas kernels, shards(): pl.pallas_call(beam_kernel, name='beam', out_shape=(jax.ShapeDtypeStruct(...  5.34 us
    pallas_call x1, Pallas kernels, shards(): pl.pallas_call(filter_kernel, name='filter', out_shape=jax.ShapeDtypeStru...  3.71 us
    unnamed x8, local copies, waits for them, and re-layouts  3.44 us
  transfers between devices with their start and end apart: 7, of which 6 were waited for; matrix products, arithmetic and copies ran while one was open for 0% of the time, Pallas kernels for 19%

profile of v2, /device:TPU:0, one launch (start us, length us, event | category | flops | bytes accessed | tf_op | source)
XLA Modules:
  0.0 89.7 jit_solution(2006072595438537455)
XLA Ops:
  0.0 0.8 copy.5
  0.8 0.9 broadcast_in_dim.2
  1.7 11.5 %all-to-all-start = ((bf16[64,2,16,128]{3,2,1,0:T(8,128)(2,1)}), bf16[64,2,16,128]{3,2,1,0:T(8,128)(2,1)S(1)}, u32[]{:S(2)}, u32[]{:S(2)}) async-start(bf16[64,2,16,128]{3,2,1,0:T(8,128)(2,1)} %bitcast.1), calls=%async_computation | async-start | bytes 1048576 | tf_op jit(solution)/shard_map/all_to_all | solution.py:166
  13.2 0.0 copy-start.1
  13.2 0.7 copy-done.1
  14.0 0.0 copy-start.2
  14.0 0.7 copy-done.2
  14.7 0.0 copy-start.3
  14.7 0.7 copy-done.3
  15.4 17.3 %operator.1 = (bf16[1024,1024]{1,0:T(8,128)(2,1)S(1)}, bf16[1024,1024]{1,0:T(8,128)(2,1)S(1)}) custom-call(s32[3,1024]{1,0:T(4,128)S(1)} %copy-done.2, s32[3,2048]{1,0:T(4,128)S(1)} %copy-done.1, s32[8]{0:T(128)S(1)} %copy-done.3), custom_call_target="tpu_custom_call" | custom-call | flops 62914560 | bytes 4194304 | tf_op jit(solution)/shard_map/operator/pallas_call | solution.py:167
  32.7 0.0 copy-start
  32.7 1.3 %copy-done = bf16[1024,1024]{1,0:T(8,128)(2,1)} copy-done((bf16[1024,1024]{1,0:T(8,128)(2,1)}, bf16[1024,1024]{1,0:T(8,128)(2,1)S(1)}, u32[]{:S(2)}) %copy-start) | copy-done | bytes 2097176
  34.0 0.0 all-to-all-done
  34.0 0.0 collective-permute-start
  34.0 1.9 %collective-permute-done = bf16[64,2,16,128]{3,2,1,0:T(8,128)(2,1)S(1)} collective-permute-done((bf16[64,2,16,128]{3,2,1,0:T(8,128)(2,1)S(1)}, bf16[64,2,16,128]{3,2,1,0:T(8,128)(2,1)S(1)}, u32[]{:S(2)}, u32[]{:S(2)}) %collective-permute-start) | collective-permute-done | bytes 524320 | tf_op jit(solution)/shard_map/ppermute | solution.py:183
  35.9 5.3 %beam.1 = (bf16[512,1024]{1,0:T(8,128)(2,1)S(1)}, f32[128,256]{1,0:T(8,128)S(1)}, f32[128,256]{1,0:T(8,128)S(1)}) custom-call(bf16[1024,1024]{1,0:T(8,128)(2,1)S(1)} %get-tuple-element.15.cosines, bf16[1024,1024]{1,0:T(8,128)(2,1)} %copy-done, bf16[8,8,2,16,128]{4,3,2,1,0:T(8,128)(2,1)S(1)} %bitcast.6, bf16[8,8,2,16,128]{4,3,2,1,0:T(8,128)(2,1)S(1)} %bitcast.7), custom_call_target="tpu_custom_call" | custom-call | tf_op jit(solution)/shard_map/beam/pallas_call | solution.py:187
  41.2 0.2 collective-permute-start.1
  41.5 1.2 %collective-permute-done.1 = f32[128,256]{1,0:T(8,128)S(1)} collective-permute-done((f32[128,256]{1,0:T(8,128)S(1)}, f32[128,256]{1,0:T(8,128)S(1)}, u32[]{:S(2)}, u32[]{:S(2)}) %collective-permute-start.1) | collective-permute-done | bytes 131104 | tf_op jit(solution)/shard_map/ppermute | solution.py:204
  42.7 1.7 %collective-permute-start.2 = (f32[128,256]{1,0:T(8,128)S(1)}, f32[128,256]{1,0:T(8,128)S(1)}, u32[]{:S(2)}, u32[]{:S(2)}) collective-permute-start(f32[128,256]{1,0:T(8,128)S(1)} %add.12), channel_id=1, source_target_pairs={{0,16},{16,0},{32,48},{48,32},{64,80},{80,64},{96,112},{112,96},{1... | collective-permute-start | bytes 393224 | tf_op jit(solution)/shard_map/ppermute | solution.py:207
  44.4 4.0 %collective-permute-done.2 = f32[128,256]{1,0:T(8,128)S(1)} collective-permute-done((f32[128,256]{1,0:T(8,128)S(1)}, f32[128,256]{1,0:T(8,128)S(1)}, u32[]{:S(2)}, u32[]{:S(2)}) %collective-permute-start.2) | collective-permute-done | bytes 131104 | tf_op jit(solution)/shard_map/ppermute | solution.py:207
  48.3 3.2 %collective-permute-start.3 = (f32[128,256]{1,0:T(8,128)S(1)}, f32[128,256]{1,0:T(8,128)S(1)}, u32[]{:S(2)}, u32[]{:S(2)}) collective-permute-start(f32[128,256]{1,0:T(8,128)S(1)} %add.13), channel_id=1, source_target_pairs={{0,32},{16,48},{32,0},{48,16},{64,96},{80,112},{96,64},{112,80},{1... | collective-permute-start | bytes 393224 | tf_op jit(solution)/shard_map/ppermute | solution.py:207
  51.5 3.4 %collective-permute-done.3 = f32[128,256]{1,0:T(8,128)S(1)} collective-permute-done((f32[128,256]{1,0:T(8,128)S(1)}, f32[128,256]{1,0:T(8,128)S(1)}, u32[]{:S(2)}, u32[]{:S(2)}) %collective-permute-start.3) | collective-permute-done | bytes 131104 | tf_op jit(solution)/shard_map/ppermute | solution.py:207
  54.9 3.3 %collective-permute-start.4 = (f32[128,256]{1,0:T(8,128)S(1)}, f32[128,256]{1,0:T(8,128)S(1)}, u32[]{:S(2)}, u32[]{:S(2)}) collective-permute-start(f32[128,256]{1,0:T(8,128)S(1)} %add.14), channel_id=1, source_target_pairs={{0,64},{16,80},{32,96},{48,112},{64,0},{80,16},{96,32},{112,48},{1... | collective-permute-start | bytes 393224 | tf_op jit(solution)/shard_map/ppermute | solution.py:207
  58.2 3.3 %collective-permute-done.4 = f32[128,256]{1,0:T(8,128)S(1)} collective-permute-done((f32[128,256]{1,0:T(8,128)S(1)}, f32[128,256]{1,0:T(8,128)S(1)}, u32[]{:S(2)}, u32[]{:S(2)}) %collective-permute-start.4) | collective-permute-done | bytes 131104 | tf_op jit(solution)/shard_map/ppermute | solution.py:207
  61.5 0.1 collective-permute-start.5
  61.6 1.3 %collective-permute-done.5.other = f32[128,256]{1,0:T(8,128)S(1)} collective-permute-done((f32[128,256]{1,0:T(8,128)S(1)}, f32[128,256]{1,0:T(8,128)S(1)}, u32[]{:S(2)}, u32[]{:S(2)}) %collective-permute-start.5) | collective-permute-done | bytes 131104 | tf_op jit(solution)/shard_map/ppermute | solution.py:209
  62.9 3.7 %filter.1 = bf16[16,2,16,1024]{3,2,1,0:T(8,128)(2,1)S(1)} custom-call(f32[128,256]{1,0:T(8,128)S(1)} %add.15.own, f32[128,256]{1,0:T(8,128)S(1)} %collective-permute-done.5.other, bf16[512,1024]{1,0:T(8,128)(2,1)S(1)} %get-tuple-element.20.y_ref), custom_call_target="tpu_custom_call" | custom-call | tf_op jit(solution)/shard_map/filter/pallas_call | solution.py:211
  66.6 21.6 %all_to_all.10 = bf16[16,2,16,1024]{3,2,1,0:T(8,128)(2,1)S(1)} all-to-all(bf16[16,2,16,1024]{3,2,1,0:T(8,128)(2,1)S(1)} %filter.1), channel_id=1, replica_groups=mesh['chan'=8,'bin'=8,'core'=2] {'bin','core'}, dimensions={0} | all-to-all | bytes 2097152 | tf_op jit(solution)/shard_map/all_to_all | solution.py:221
  88.3 1.4 %place.1 = bf16[16,2,8,2048]{3,2,1,0:T(8,128)(2,1)} custom-call(bf16[8,2,2,16,1024]{4,3,2,1,0:T(8,128)(2,1)S(1)} %bitcast.5), custom_call_target="tpu_custom_call" | custom-call | tf_op jit(solution)/shard_map/place/pallas_call | solution.py:223
  (4 shorter events, 0.1 us)
Async XLA Ops:
  1.7 32.3 %all-to-all-start = ((bf16[64,2,16,128]{3,2,1,0:T(8,128)(2,1)}), bf16[64,2,16,128]{3,2,1,0:T(8,128)(2,1)S(1)}, u32[]{:S(2)}, u32[]{:S(2)}) async-start(bf16[64,2,16,128]{3,2,1,0:T(8,128)(2,1)} %bitcast.1), calls=%async_computation | async-start | bytes 1048576 | tf_op jit(solution)/shard_map/all_to_all | solution.py:166
  13.2 0.8 copy-start.1
  14.0 0.7 copy-start.2
  14.7 0.7 copy-start.3
  32.7 1.3 %copy-start = (bf16[1024,1024]{1,0:T(8,128)(2,1)}, bf16[1024,1024]{1,0:T(8,128)(2,1)S(1)}, u32[]{:S(2)}) copy-start(bf16[1024,1024]{1,0:T(8,128)(2,1)S(1)} %get-tuple-element.16.sines) | copy-start | bytes 6291460
  34.0 1.9 %collective-permute-start = (bf16[64,2,16,128]{3,2,1,0:T(8,128)(2,1)S(1)}, bf16[64,2,16,128]{3,2,1,0:T(8,128)(2,1)S(1)}, u32[]{:S(2)}, u32[]{:S(2)}) collective-permute-start(bf16[64,2,16,128]{3,2,1,0:T(8,128)(2,1)S(1)} %all-to-all-done), channel_id=1, source_target_pairs={{0,1},{1,0},{2,3},{3,2},{4,5},{5,4},{6,7},{7,6},{8,9},{9,8},{10,11... | collective-permute-start | bytes 1572872 | tf_op jit(solution)/shard_map/ppermute | solution.py:183
  41.2 1.4 %collective-permute-start.1 = (f32[128,256]{1,0:T(8,128)S(1)}, f32[128,256]{1,0:T(8,128)S(1)}, u32[]{:S(2)}, u32[]{:S(2)}) collective-permute-start(f32[128,256]{1,0:T(8,128)S(1)} %get-tuple-element.19), channel_id=1, source_target_pairs={{0,1},{1,0},{2,3},{3,2},{4,5},{5,4},{6,7},{7,6},{8,9},{9,8},{10,11... | collective-permute-start | bytes 393224 | tf_op jit(solution)/shard_map/ppermute | solution.py:204
  42.7 5.6 %collective-permute-start.2 = (f32[128,256]{1,0:T(8,128)S(1)}, f32[128,256]{1,0:T(8,128)S(1)}, u32[]{:S(2)}, u32[]{:S(2)}) collective-permute-start(f32[128,256]{1,0:T(8,128)S(1)} %add.12), channel_id=1, source_target_pairs={{0,16},{16,0},{32,48},{48,32},{64,80},{80,64},{96,112},{112,96},{1... | collective-permute-start | bytes 393224 | tf_op jit(solution)/shard_map/ppermute | solution.py:207
  48.3 6.6 %collective-permute-start.3 = (f32[128,256]{1,0:T(8,128)S(1)}, f32[128,256]{1,0:T(8,128)S(1)}, u32[]{:S(2)}, u32[]{:S(2)}) collective-permute-start(f32[128,256]{1,0:T(8,128)S(1)} %add.13), channel_id=1, source_target_pairs={{0,32},{16,48},{32,0},{48,16},{64,96},{80,112},{96,64},{112,80},{1... | collective-permute-start | bytes 393224 | tf_op jit(solution)/shard_map/ppermute | solution.py:207
  54.9 6.6 %collective-permute-start.4 = (f32[128,256]{1,0:T(8,128)S(1)}, f32[128,256]{1,0:T(8,128)S(1)}, u32[]{:S(2)}, u32[]{:S(2)}) collective-permute-start(f32[128,256]{1,0:T(8,128)S(1)} %add.14), channel_id=1, source_target_pairs={{0,64},{16,80},{32,96},{48,112},{64,0},{80,16},{96,32},{112,48},{1... | collective-permute-start | bytes 393224 | tf_op jit(solution)/shard_map/ppermute | solution.py:207
  61.5 1.4 %collective-permute-start.5 = (f32[128,256]{1,0:T(8,128)S(1)}, f32[128,256]{1,0:T(8,128)S(1)}, u32[]{:S(2)}, u32[]{:S(2)}) collective-permute-start(f32[128,256]{1,0:T(8,128)S(1)} %add.15.own), channel_id=1, source_target_pairs={{0,1},{1,0},{2,3},{3,2},{4,5},{5,4},{6,7},{7,6},{8,9},{9,8},{10,11... | collective-permute-start | bytes 393224 | tf_op jit(solution)/shard_map/ppermute | solution.py:209

commit v3 on v1

v3 whole, which is shorter than its diff:
```python
import math

import jax
import jax.numpy as jnp
from jax import lax
from jax.experimental import pallas as pl
from jax.experimental.pallas import tpu as pltpu
from jax.sharding import Mesh, PartitionSpec as P

EPSILON = 1e-06
BINS = 8
CORES = 2
F32 = jnp.float32
BF16 = jnp.bfloat16
SIN = (3.1415925800446924, -5.167706878924515, 2.5500313772531213, -0.5980451739748806, 0.0772201286897368)
COS = (0.9999999534666272, -4.934792858670076, 4.058411914063177, -1.331880160583308, 0.21969679727234584)
ROUNDER = 12582912.0
ROWS = 256
LANES = 256
WIDE = pltpu.CompilerParams(vmem_limit_bytes=16 * 1024 * 1024)
VMEM = pl.BlockSpec(memory_space=pltpu.VMEM)
HBM = pl.BlockSpec(memory_space=pltpu.HBM)


def horner(coefficients, z):
    total = coefficients[-1] * z + coefficients[-2]
    for value in coefficients[-3::-1]:
        total = total * z + value
    return total


def digits(value, unit):
    high = jnp.floor(value * (1.0 / unit))
    return high, value - unit * high


def spread_kernel(rf_ref, out_ref, held, sem):
    copy = pltpu.make_async_copy(rf_ref, held, sem)
    copy.start()
    copy.wait()
    for part in range(held.shape[0]):
        block = held[part]
        for k in range(out_ref.shape[0]):
            out_ref[k, :, part] = block


def operator_kernel(elem_ref, vox_ref, bins_ref, out_ref, done_ref, elem, vox, bins, lhs_ref, sems):
    core = lax.axis_index("core")
    _, channels, voxels = out_ref.shape
    copies = [
        pltpu.make_async_copy(source, target, sems.at[n])
        for n, (source, target) in enumerate(((elem_ref, elem), (vox_ref, vox), (bins_ref, bins)))
    ]
    for copy in copies:
        copy.start()
    for copy in copies:
        copy.wait()
    wavenumber = (32.0 + bins[lax.axis_index("bin")].astype(F32)) / 64.0
    scale = 2.0 / math.sqrt(channels)

    place = elem[...].astype(F32)
    high, low = digits(jnp.sum(place * place, axis=0, keepdims=True), 16.0)
    one = jnp.ones((1, channels), F32)
    lhs = jnp.concatenate([place, high, low, one, one, 0.0 * one], axis=0)
    lhs_ref[...] = jnp.transpose(lhs).astype(BF16)
    voxel = vox[:, pl.ds(pl.multiple_of(core * voxels, voxels), voxels)].astype(F32)
    high, low = digits(jnp.sum(voxel * voxel, axis=0, keepdims=True), 64.0)
    one = jnp.ones((1, voxels), F32)
    zero = 0.0 * one
    level = voxel[2:3]
    squares = jnp.concatenate([-2.0 * voxel, 16.0 * one, one, 64.0 * high, low, zero], axis=0).astype(BF16)
    depths = jnp.concatenate([zero, zero, -1.0 * one, zero, zero, level, zero, zero], axis=0).astype(BF16)

    def tile(index, carry):
        rows = pl.ds(pl.multiple_of(index * ROWS, ROWS), ROWS)
        left = lhs_ref[rows]
        squared = jnp.dot(left, squares, preferred_element_type=F32)
        depth = jnp.dot(left, depths, preferred_element_type=F32)
        inverse = lax.rsqrt(squared)
        turns = (level + squared * inverse) * wavenumber
        part = turns - ((turns + ROUNDER) - ROUNDER)
        z = part * part
        sine = part * horner(SIN, z)
        cosine = horner(COS, z)
        double = depth * inverse * scale
        lean = double * sine
        out_ref[0, rows] = (0.5 * double - lean * sine).astype(BF16)
        out_ref[1, rows] = (lean * cosine).astype(BF16)
        return carry

    lax.fori_loop(0, channels // ROWS, tile, 0)
    done_ref[...] = jnp.zeros_like(done_ref)


def beamform(samples, operator, data):
    blocks, bins, _, group, width = samples.shape
    half = bins * group
    for k in range(blocks):
        for part in range(2):
            data[part * half : (part + 1) * half, k * width : (k + 1) * width] = samples[k, :, part].reshape(half, width)
    for block in range(operator.shape[2] // LANES):
        lanes = slice(block * LANES, (block + 1) * LANES)
        first = jnp.dot(data[...], operator[0, :, lanes], preferred_element_type=F32)
        second = jnp.dot(data[...], operator[1, :, lanes], preferred_element_type=F32)
        yield lanes, (first[:half] + second[half:]).astype(BF16), (first[half:] - second[:half]).astype(BF16)


def own_kernel(operator, samples, out_ref, data):
    half = out_ref.shape[0] // 2
    for lanes, real, imag in beamform(samples, operator, data):
        out_ref[:half, lanes] = real
        out_ref[half:, lanes] = imag


def other_kernel(operator, samples, own, y_ref, keep_ref, send_ref, data, gram):
    core = lax.axis_index("core")
    frames = y_ref.shape[0] // 2
    half = frames // CORES
    here = pl.multiple_of(core * half, half)
    there = pl.multiple_of((1 - core) * half, half)
    y_ref[pl.ds(here, half)] = own[:half]
    y_ref[pl.ds(frames + here, half)] = own[half:]
    for lanes, real, imag in beamform(samples, operator, data):
        y_ref[pl.ds(there, half), lanes] = real
        y_ref[pl.ds(frames + there, half), lanes] = imag
    y = y_ref[...]
    products = lax.dot_general(y, y, (((1,), (1,)), ((), ())), preferred_element_type=F32)
    gram[...] = (products[:frames, :frames] + products[frames:, frames:]) + (
        products[:frames, frames:] - products[frames:, :frames]
    )
    keep_ref[...] = gram[pl.ds(here, half), :]
    send_ref[...] = gram[pl.ds(there, half), :]


def halves(x):
    high = x.astype(BF16)
    return high, (x - high.astype(F32)).astype(BF16)


def product(left, right):
    left_high, left_low = halves(left)
    right_high, right_low = halves(right)
    return jnp.dot(
        jnp.concatenate([left_high, left_high, left_low], axis=1),
        jnp.concatenate([right_high, right_low, right_high], axis=0),
        preferred_element_type=F32,
    )


def unpack(packed):
    flipped = jnp.transpose(packed)
    return 0.5 * (packed + flipped), 0.5 * (packed - flipped), flipped


def filter_kernel(own, other, y_ref, out_ref, gram):
    core = lax.axis_index("core")
    half, frames = own.shape
    gram[pl.ds(pl.multiple_of(core * half, half), half), :] = own[...]
    gram[pl.ds(pl.multiple_of((1 - core) * half, half), half), :] = other[...]
    packed = gram[...]
    squares = jnp.sum(packed * packed)
    factor = 4.0 / jnp.sqrt(jnp.full((1, 1), squares + EPSILON, F32))
    mat = packed * factor
    real, imag, flipped = unpack(mat)
    left = jnp.concatenate([real, imag], axis=1)
    second = product(left, jnp.concatenate([mat, flipped], axis=0))
    third = product(left, jnp.concatenate([second, jnp.transpose(second)], axis=0))
    rows = lax.broadcasted_iota(jnp.int32, (frames, frames), 0)
    cols = lax.broadcasted_iota(jnp.int32, (frames, frames), 1)
    identity = jnp.where(rows == cols, 1.0, 0.0).astype(F32)
    real, imag, _ = unpack(identity - mat + 0.3 * second - 0.03 * third)
    real, imag = real.astype(BF16), imag.astype(BF16)
    matrix = jnp.concatenate(
        [jnp.concatenate([real, imag], axis=1), jnp.concatenate([-imag, real], axis=1)], axis=0
    )
    applied = jnp.dot(matrix, y_ref[...], preferred_element_type=F32).astype(BF16)
    group = out_ref.shape[2]
    bins = out_ref.shape[0] // CORES
    for part in range(2):
        for c in range(CORES):
            for j in range(bins):
                row = part * frames + c * half + j * group
                out_ref[j * CORES + c, part] = applied[row : row + group]


def place_kernel(got, out_ref):
    group, _, bins, _ = out_ref.shape
    voxels = got.shape[-1]
    size = group * bins
    rows = lax.broadcasted_iota(jnp.int32, (size, size), 0)
    cols = lax.broadcasted_iota(jnp.int32, (size, size), 1)
    turn = jnp.where(cols == (rows % bins) * group + rows // bins, 1.0, 0.0).astype(BF16)
    for c in range(CORES):
        for part in range(2):
            block = got[:, c, part].reshape(size, voxels)
            moved = jnp.dot(turn, block, preferred_element_type=F32).astype(BF16)
            out_ref[:, part, :, c * voxels : (c + 1) * voxels] = moved.reshape(group, bins, voxels)


def shards(rf_data, elem_pos, vox_pos, subbands):
    parts, bins, group, width = rf_data.shape
    channels = elem_pos.shape[1]
    chans = channels // width
    voxels = vox_pos.shape[1] // CORES
    frames = group * bins * CORES
    half = frames // CORES

    def shape(*dims, dtype=BF16):
        return jax.ShapeDtypeStruct(dims, dtype)

    def swap(x):
        return lax.ppermute(x, "core", [(0, 1), (1, 0)])

    def across(x, bits):
        return lax.ppermute(x, "chan", [(a, a ^ bits) for a in range(chans)])

    by_bin = pl.pallas_call(
        spread_kernel,
        name="spread",
        out_shape=shape(chans, bins, parts, group, width),
        in_specs=[HBM],
        out_specs=VMEM,
        scratch_shapes=[pltpu.VMEM(rf_data.shape, BF16), pltpu.SemaphoreType.DMA],
        compiler_params=WIDE,
    )(pltpu.with_memory_space_constraint(rf_data, pltpu.HBM))
    by_bin = by_bin.reshape(chans * bins, parts, group, width)
    own = lax.all_to_all(by_bin, ("chan", "bin"), split_axis=0, concat_axis=0, tiled=True)

    operator, done = pl.pallas_call(
        operator_kernel,
        name="operator",
        out_shape=(shape(2, channels, voxels), shape(8, 128, dtype=F32)),
        in_specs=[HBM, HBM, HBM],
        out_specs=(VMEM, VMEM),
        scratch_shapes=[
            pltpu.VMEM(elem_pos.shape, jnp.int32),
            pltpu.VMEM(vox_pos.shape, jnp.int32),
            pltpu.SMEM(subbands.shape, jnp.int32),
            pltpu.VMEM((channels, 8), BF16),
            pltpu.SemaphoreType.DMA((3,)),
        ],
        compiler_params=WIDE,
        cost_estimate=pl.CostEstimate(
            flops=60 * channels * voxels,
            transcendentals=channels * voxels,
            bytes_accessed=4 * channels * voxels,
        ),
    )(*(pltpu.with_memory_space_constraint(x, pltpu.HBM) for x in (elem_pos, vox_pos, subbands)))

    own, _ = lax.optimization_barrier((own, done))
    other = swap(own)
    own = own.reshape(chans, bins, parts, group, width)
    other = other.reshape(chans, bins, parts, group, width)

    beam_cost = pl.CostEstimate(
        flops=8 * half * channels * voxels * 2, transcendentals=0, bytes_accessed=4 * channels * voxels
    )
    mine = pl.pallas_call(
        own_kernel,
        name="beam_own",
        out_shape=shape(frames, voxels),
        in_specs=[VMEM, VMEM],
        out_specs=VMEM,
        scratch_shapes=[pltpu.VMEM((frames, channels), BF16)],
        compiler_params=WIDE,
        cost_estimate=beam_cost,
    )(operator, own)
    y, keep, send = pl.pallas_call(
        other_kernel,
        name="beam_other",
        out_shape=(shape(2 * frames, voxels), shape(half, frames, dtype=F32), shape(half, frames, dtype=F32)),
        in_specs=[VMEM, VMEM, VMEM],
        out_specs=(VMEM, VMEM, VMEM),
        scratch_shapes=[pltpu.VMEM((frames, channels), BF16), pltpu.VMEM((frames, frames), F32)],
        compiler_params=WIDE,
        cost_estimate=beam_cost,
    )(operator, other, mine)

    total = keep + swap(send)
    near, far, next_to = across(total, 1), across(total, 3), across(total, 2)
    total = total + near + far + next_to
    total = total + across(total, 4)
    rest = swap(total)

    applied = pl.pallas_call(
        filter_kernel,
        name="filter",
        out_shape=shape(bins * CORES, parts, group, voxels),
        in_specs=[VMEM, VMEM, VMEM],
        out_specs=VMEM,
        scratch_shapes=[pltpu.VMEM((frames, frames), F32)],
        compiler_params=WIDE,
    )(total, rest, y)

    got = lax.all_to_all(applied, ("bin", "core"), split_axis=0, concat_axis=0, tiled=True)
    got = got.reshape(bins, CORES, parts, group, voxels)
    return pl.pallas_call(
        place_kernel,
        name="place",
        out_shape=shape(group, parts, bins, CORES * voxels),
        in_specs=[VMEM],
        out_specs=VMEM,
        compiler_params=WIDE,
    )(got)


def solution(mesh):
    chans = mesh.shape["chan"]
    fine = Mesh(mesh.devices.reshape(chans, BINS, CORES), ("chan", "bin", "core"))
    return jax.shard_map(
        shards,
        mesh=fine,
        in_specs=(P(None, None, ("bin", "core"), "chan"), P(), P(None, "chan"), P()),
        out_specs=P(("bin", "core"), None, None, "chan"),
        check_vma=False,
    )
```

time: 96.9 us -> 78.7 us (0.81)
  Pallas kernels: 27.8 us -> 14.5 us
  waiting for transfers between devices: 19.4 us -> 14.2 us
  starting transfers between devices: 4.09 us -> 5.93 us
  local copies, waits for them, and re-layouts: 1.59 us -> 0 us
    pallas_call x3 -> x6, Pallas kernels: 27.8 us -> 14.5 us  [the longest x1 6.88 us: shards(): pl.pallas_call(operator_kernel, name='operator', out_shape=(shape(2, chan...]
    ppermute x6 -> x7, waiting for transfers between devices: 19.4 us -> 14.2 us  [the longest x4 11.9 us: across(): return lax.ppermute(x, 'chan', [(a, a ^ bits) for a in range(chans)])]
    ppermute x6 -> x7, starting transfers between devices: 4.09 us -> 5.93 us  [the longest x4 5.26 us: across(): return lax.ppermute(x, 'chan', [(a, a ^ bits) for a in range(chans)])]
  transfers between devices with their start and end apart: 6 -> 7, of which waited for: 6 -> 5; matrix products, arithmetic and copies ran while one was open for 0% -> 0% of each run, Pallas kernels for 0% -> 10%
where the time goes in v3:
time: 78.7 us; the launch traced here: 78.3 us
  blocking collectives  43.5 us (55%)
  Pallas kernels  14.5 us (18%)
  waiting for transfers between devices  14.2 us (18%)
  starting transfers between devices  5.93 us (8%)
    all_to_all x1, blocking collectives, shards(): lax.all_to_all(by_bin, ('chan', 'bin'), split_axis=0, concat_axis=0, tile...  24.2 us
    all_to_all x1, blocking collectives, shards(): lax.all_to_all(applied, ('bin', 'core'), split_axis=0, concat_axis=0, til...  19.3 us
    ppermute x4, waiting for transfers between devices, across(): return lax.ppermute(x, 'chan', [(a, a ^ bits) for a in range(chans)])  11.9 us
    pallas_call x1, Pallas kernels, shards(): pl.pallas_call(operator_kernel, name='operator', out_shape=(shape(2, chan...  6.88 us
    ppermute x4, starting transfers between devices, across(): return lax.ppermute(x, 'chan', [(a, a ^ bits) for a in range(chans)])  5.26 us
    ppermute x3, waiting for transfers between devices, swap(): return lax.ppermute(x, 'core', [(0, 1), (1, 0)])  2.32 us
    pallas_call x1, Pallas kernels, shards(): pl.pallas_call(filter_kernel, name='filter', out_shape=shape(bins * CORES...  2.1 us
    pallas_call x1, Pallas kernels, shards(): pl.pallas_call(other_kernel, name='beam_other', out_shape=(shape(2 * fram...  1.91 us
  transfers between devices with their start and end apart: 7, of which 5 were waited for; matrix products, arithmetic and copies ran while one was open for 0% of the time, Pallas kernels for 10%

profile of v3, /device:TPU:0, one launch (start us, length us, event | category | flops | bytes accessed | tf_op | source)
XLA Modules:
  0.0 78.3 jit_solution(255177776274931112)
XLA Ops:
  0.0 0.9 %spread.1 = bf16[8,8,2,16,128]{4,3,2,1,0:T(8,128)(2,1)S(1)} custom-call(bf16[2,8,16,128]{3,2,1,0:T(8,128)(2,1)} %rf_ref.1), custom_call_target="tpu_custom_call" | custom-call | tf_op jit(solution)/shard_map/spread/pallas_call | solution.py:217
  0.9 24.2 %all_to_all.10 = bf16[64,2,16,128]{3,2,1,0:T(8,128)(2,1)S(1)} all-to-all(bf16[64,2,16,128]{3,2,1,0:T(8,128)(2,1)S(1)} %bitcast.5), channel_id=1, replica_groups=mesh['chan'=8,'bin'=8,'core'=2] {'chan','bin'}, dimensions={0} | all-to-all | bytes 1048576 | tf_op jit(solution)/shard_map/all_to_all | solution.py:227
  25.2 0.0 collective-permute-start
  25.2 6.9 %operator.1 = (bf16[2,1024,1024]{2,1,0:T(8,128)(2,1)S(1)}, f32[8,128]{1,0:T(8,128)}) custom-call(s32[3,1024]{1,0:T(4,128)} %elem_ref.1, s32[3,2048]{1,0:T(4,128)} %vox_ref.1, s32[8]{0:T(128)} %bins_ref.1), custom_call_target="tpu_custom_call" | custom-call | flops 62914560 | bytes 4194304 | tf_op jit(solution)/shard_map/operator/pallas_call | solution.py:229
  32.0 1.3 %beam_own.1.own = bf16[256,1024]{1,0:T(8,128)(2,1)S(1)} custom-call(bf16[2,1024,1024]{2,1,0:T(8,128)(2,1)S(1)} %get-tuple-element.9.operator, bf16[8,8,2,16,128]{4,3,2,1,0:T(8,128)(2,1)S(1)} %bitcast.6), custom_call_target="tpu_custom_call" | custom-call | flops 2147483648 | bytes 4194304 | tf_op jit(solution)/shard_map/beam_own/pallas_call | solution.py:258
  33.3 0.0 collective-permute-done
  33.3 1.9 %beam_other.1 = (bf16[512,1024]{1,0:T(8,128)(2,1)S(1)}, f32[128,256]{1,0:T(8,128)S(1)}, f32[128,256]{1,0:T(8,128)S(1)}) custom-call(bf16[2,1024,1024]{2,1,0:T(8,128)(2,1)S(1)} %get-tuple-element.9.operator, bf16[8,8,2,16,128]{4,3,2,1,0:T(8,128)(2,1)S(1)} %bitcast.7, bf16[256,1024]{1,0:T(8,128)(2,1)S(1)} %beam_own.1.own), custom_call_target="tpu_custom_call" | custom-call | flops 2147483648 | bytes 4194304 | tf_op jit(solution)/shard_map/beam_other/pallas_call | solution.py:268
  35.2 0.6 collective-permute-start.1
  35.8 1.0 %collective-permute-done.1 = f32[128,256]{1,0:T(8,128)S(1)} collective-permute-done((f32[128,256]{1,0:T(8,128)S(1)}, f32[128,256]{1,0:T(8,128)S(1)}, u32[]{:S(2)}, u32[]{:S(2)}) %collective-permute-start.1) | collective-permute-done | bytes 131104 | tf_op jit(solution)/shard_map/ppermute | solution.py:212
  36.8 1.7 %collective-permute-start.4 = (f32[128,256]{1,0:T(8,128)S(1)}, f32[128,256]{1,0:T(8,128)S(1)}, u32[]{:S(2)}, u32[]{:S(2)}) collective-permute-start(f32[128,256]{1,0:T(8,128)S(1)} %add.15), channel_id=1, source_target_pairs={{0,32},{16,48},{32,0},{48,16},{64,96},{80,112},{96,64},{112,80},{1... | collective-permute-start | bytes 393224 | tf_op jit(solution)/shard_map/ppermute | solution.py:215
  38.5 1.4 %collective-permute-start.3 = (f32[128,256]{1,0:T(8,128)S(1)}, f32[128,256]{1,0:T(8,128)S(1)}, u32[]{:S(2)}, u32[]{:S(2)}) collective-permute-start(f32[128,256]{1,0:T(8,128)S(1)} %add.15), channel_id=1, source_target_pairs={{0,48},{16,32},{32,16},{48,0},{64,112},{80,96},{96,80},{112,64},{1... | collective-permute-start | bytes 393224 | tf_op jit(solution)/shard_map/ppermute | solution.py:215
  39.9 0.5 collective-permute-start.2
  40.4 4.3 %collective-permute-done.4 = f32[128,256]{1,0:T(8,128)S(1)} collective-permute-done((f32[128,256]{1,0:T(8,128)S(1)}, f32[128,256]{1,0:T(8,128)S(1)}, u32[]{:S(2)}, u32[]{:S(2)}) %collective-permute-start.4) | collective-permute-done | bytes 131104 | tf_op jit(solution)/shard_map/ppermute | solution.py:215
  44.7 2.2 %collective-permute-done.3 = f32[128,256]{1,0:T(8,128)S(1)} collective-permute-done((f32[128,256]{1,0:T(8,128)S(1)}, f32[128,256]{1,0:T(8,128)S(1)}, u32[]{:S(2)}, u32[]{:S(2)}) %collective-permute-start.3) | collective-permute-done | bytes 131104 | tf_op jit(solution)/shard_map/ppermute | solution.py:215
  47.0 0.0 collective-permute-done.2
  47.0 1.7 %collective-permute-start.5 = (f32[128,256]{1,0:T(8,128)S(1)}, f32[128,256]{1,0:T(8,128)S(1)}, u32[]{:S(2)}, u32[]{:S(2)}) collective-permute-start(f32[128,256]{1,0:T(8,128)S(1)} %add_add_fusion), channel_id=1, source_target_pairs={{0,64},{16,80},{32,96},{48,112},{64,0},{80,16},{96,32},{112,48},{1... | collective-permute-start | bytes 393224 | tf_op jit(solution)/shard_map/ppermute | solution.py:215
  48.7 5.3 %collective-permute-done.5 = f32[128,256]{1,0:T(8,128)S(1)} collective-permute-done((f32[128,256]{1,0:T(8,128)S(1)}, f32[128,256]{1,0:T(8,128)S(1)}, u32[]{:S(2)}, u32[]{:S(2)}) %collective-permute-start.5) | collective-permute-done | bytes 131104 | tf_op jit(solution)/shard_map/ppermute | solution.py:215
  54.1 0.1 collective-permute-start.6
  54.2 1.3 %collective-permute-done.6.other = f32[128,256]{1,0:T(8,128)S(1)} collective-permute-done((f32[128,256]{1,0:T(8,128)S(1)}, f32[128,256]{1,0:T(8,128)S(1)}, u32[]{:S(2)}, u32[]{:S(2)}) %collective-permute-start.6) | collective-permute-done | bytes 131104 | tf_op jit(solution)/shard_map/ppermute | solution.py:212
  55.5 2.1 %filter.1 = bf16[16,2,16,1024]{3,2,1,0:T(8,128)(2,1)S(1)} custom-call(f32[128,256]{1,0:T(8,128)S(1)} %add.19.own, f32[128,256]{1,0:T(8,128)S(1)} %collective-permute-done.6.other, bf16[512,1024]{1,0:T(8,128)(2,1)S(1)} %get-tuple-element.12.y_ref), custom_call_target="tpu_custom_call" | custom-call | tf_op jit(solution)/shard_map/filter/pallas_call | solution.py:285
  57.6 19.3 %all_to_all.11 = bf16[16,2,16,1024]{3,2,1,0:T(8,128)(2,1)S(1)} all-to-all(bf16[16,2,16,1024]{3,2,1,0:T(8,128)(2,1)S(1)} %filter.1), channel_id=1, replica_groups=mesh['chan'=8,'bin'=8,'core'=2] {'bin','core'}, dimensions={0} | all-to-all | bytes 2097152 | tf_op jit(solution)/shard_map/all_to_all | solution.py:295
  76.9 1.4 %place.1 = bf16[16,2,8,2048]{3,2,1,0:T(8,128)(2,1)} custom-call(bf16[8,2,2,16,1024]{4,3,2,1,0:T(8,128)(2,1)S(1)} %bitcast.4), custom_call_target="tpu_custom_call" | custom-call | tf_op jit(solution)/shard_map/place/pallas_call | solution.py:297
  (3 shorter events, 0.1 us)
Async XLA Ops:
  25.2 8.2 %collective-permute-start = (bf16[64,2,16,128]{3,2,1,0:T(8,128)(2,1)S(1)}, bf16[64,2,16,128]{3,2,1,0:T(8,128)(2,1)S(1)}, u32[]{:S(2)}, u32[]{:S(2)}) collective-permute-start(bf16[64,2,16,128]{3,2,1,0:T(8,128)(2,1)S(1)} %all_to_all.10), channel_id=1, source_target_pairs={{0,1},{1,0},{2,3},{3,2},{4,5},{5,4},{6,7},{7,6},{8,9},{9,8},{10,11... | collective-permute-start | bytes 1572872 | tf_op jit(solution)/shard_map/ppermute | solution.py:212
  35.2 1.6 %collective-permute-start.1 = (f32[128,256]{1,0:T(8,128)S(1)}, f32[128,256]{1,0:T(8,128)S(1)}, u32[]{:S(2)}, u32[]{:S(2)}) collective-permute-start(f32[128,256]{1,0:T(8,128)S(1)} %get-tuple-element.11), channel_id=1, source_target_pairs={{0,1},{1,0},{2,3},{3,2},{4,5},{5,4},{6,7},{7,6},{8,9},{9,8},{10,11... | collective-permute-start | bytes 393224 | tf_op jit(solution)/shard_map/ppermute | solution.py:212
  36.8 7.9 %collective-permute-start.4 = (f32[128,256]{1,0:T(8,128)S(1)}, f32[128,256]{1,0:T(8,128)S(1)}, u32[]{:S(2)}, u32[]{:S(2)}) collective-permute-start(f32[128,256]{1,0:T(8,128)S(1)} %add.15), channel_id=1, source_target_pairs={{0,32},{16,48},{32,0},{48,16},{64,96},{80,112},{96,64},{112,80},{1... | collective-permute-start | bytes 393224 | tf_op jit(solution)/shard_map/ppermute | solution.py:215
  38.5 8.4 %collective-permute-start.3 = (f32[128,256]{1,0:T(8,128)S(1)}, f32[128,256]{1,0:T(8,128)S(1)}, u32[]{:S(2)}, u32[]{:S(2)}) collective-permute-start(f32[128,256]{1,0:T(8,128)S(1)} %add.15), channel_id=1, source_target_pairs={{0,48},{16,32},{32,16},{48,0},{64,112},{80,96},{96,80},{112,64},{1... | collective-permute-start | bytes 393224 | tf_op jit(solution)/shard_map/ppermute | solution.py:215
  39.9 7.0 %collective-permute-start.2 = (f32[128,256]{1,0:T(8,128)S(1)}, f32[128,256]{1,0:T(8,128)S(1)}, u32[]{:S(2)}, u32[]{:S(2)}) collective-permute-start(f32[128,256]{1,0:T(8,128)S(1)} %add.15), channel_id=1, source_target_pairs={{0,16},{16,0},{32,48},{48,32},{64,80},{80,64},{96,112},{112,96},{1... | collective-permute-start | bytes 393224 | tf_op jit(solution)/shard_map/ppermute | solution.py:215
  47.0 7.0 %collective-permute-start.5 = (f32[128,256]{1,0:T(8,128)S(1)}, f32[128,256]{1,0:T(8,128)S(1)}, u32[]{:S(2)}, u32[]{:S(2)}) collective-permute-start(f32[128,256]{1,0:T(8,128)S(1)} %add_add_fusion), channel_id=1, source_target_pairs={{0,64},{16,80},{32,96},{48,112},{64,0},{80,16},{96,32},{112,48},{1... | collective-permute-start | bytes 393224 | tf_op jit(solution)/shard_map/ppermute | solution.py:215
  54.1 1.4 %collective-permute-start.6 = (f32[128,256]{1,0:T(8,128)S(1)}, f32[128,256]{1,0:T(8,128)S(1)}, u32[]{:S(2)}, u32[]{:S(2)}) collective-permute-start(f32[128,256]{1,0:T(8,128)S(1)} %add.19.own), channel_id=1, source_target_pairs={{0,1},{1,0},{2,3},{3,2},{4,5},{5,4},{6,7},{7,6},{8,9},{9,8},{10,11... | collective-permute-start | bytes 393224 | tf_op jit(solution)/shard_map/ppermute | solution.py:212

commit v4 on v3

--- a/solution.py
+++ b/solution.py
@@ -1,3 +1,4 @@
+import functools
 import math
 
 import jax
@@ -44,9 +45,10 @@
             out_ref[k, :, part] = block
 
 
-def operator_kernel(elem_ref, vox_ref, bins_ref, out_ref, done_ref, elem, vox, bins, lhs_ref, sems):
+def operator_kernel(start, elem_ref, vox_ref, bins_ref, out_ref, elem, vox, bins, lhs_ref, sems):
     core = lax.axis_index("core")
-    _, channels, voxels = out_ref.shape
+    _, share, voxels = out_ref.shape
+    channels = elem.shape[1]
     copies = [
         pltpu.make_async_copy(source, target, sems.at[n])
         for n, (source, target) in enumerate(((elem_ref, elem), (vox_ref, vox), (bins_ref, bins)))
@@ -73,7 +75,7 @@
 
     def tile(index, carry):
         rows = pl.ds(pl.multiple_of(index * ROWS, ROWS), ROWS)
-        left = lhs_ref[rows]
+        left = lhs_ref[pl.ds(pl.multiple_of(start + index * ROWS, ROWS), ROWS)]
         squared = jnp.dot(left, squares, preferred_element_type=F32)
         depth = jnp.dot(left, depths, preferred_element_type=F32)
         inverse = lax.rsqrt(squared)
@@ -88,31 +90,35 @@
         out_ref[1, rows] = (lean * cosine).astype(BF16)
         return carry
 
-    lax.fori_loop(0, channels // ROWS, tile, 0)
-    done_ref[...] = jnp.zeros_like(done_ref)
-
-
-def beamform(samples, operator, data):
+    lax.fori_loop(0, share // ROWS, tile, 0)
+
+
+def beamform(samples, upper, lower, data):
     blocks, bins, _, group, width = samples.shape
     half = bins * group
     for k in range(blocks):
         for part in range(2):
             data[part * half : (part + 1) * half, k * width : (k + 1) * width] = samples[k, :, part].reshape(half, width)
-    for block in range(operator.shape[2] // LANES):
+    share = upper.shape[1]
+
+    def applied(which, lanes):
+        left = jnp.dot(data[:, :share], upper[which, :, lanes], preferred_element_type=F32)
+        return left + jnp.dot(data[:, share:], lower[which, :, lanes], preferred_element_type=F32)
+
+    for block in range(upper.shape[2] // LANES):
         lanes = slice(block * LANES, (block + 1) * LANES)
-        first = jnp.dot(data[...], operator[0, :, lanes], preferred_element_type=F32)
-        second = jnp.dot(data[...], operator[1, :, lanes], preferred_element_type=F32)
+        first, second = applied(0, lanes), applied(1, lanes)
         yield lanes, (first[:half] + second[half:]).astype(BF16), (first[half:] - second[:half]).astype(BF16)
 
 
-def own_kernel(operator, samples, out_ref, data):
+def own_kernel(upper, lower, samples, out_ref, data):
     half = out_ref.shape[0] // 2
-    for lanes, real, imag in beamform(samples, operator, data):
+    for lanes, real, imag in beamform(samples, upper, lower, data):
         out_ref[:half, lanes] = real
         out_ref[half:, lanes] = imag
 
 
-def other_kernel(operator, samples, own, y_ref, keep_ref, send_ref, data, gram):
+def other_kernel(upper, lower, samples, own, y_ref, keep_ref, send_ref, data, gram):
     core = lax.axis_index("core")
     frames = y_ref.shape[0] // 2
     half = frames // CORES
@@ -120,7 +126,7 @@
     there = pl.multiple_of((1 - core) * half, half)
     y_ref[pl.ds(here, half)] = own[:half]
     y_ref[pl.ds(frames + here, half)] = own[half:]
-    for lanes, real, imag in beamform(samples, operator, data):
+    for lanes, real, imag in beamform(samples, upper, lower, data):
         y_ref[pl.ds(there, half), lanes] = real
         y_ref[pl.ds(frames + there, half), lanes] = imag
     y = y_ref[...]
@@ -226,29 +232,31 @@
     by_bin = by_bin.reshape(chans * bins, parts, group, width)
     own = lax.all_to_all(by_bin, ("chan", "bin"), split_axis=0, concat_axis=0, tiled=True)
 
-    operator, done = pl.pallas_call(
-        operator_kernel,
-        name="operator",
-        out_shape=(shape(2, channels, voxels), shape(8, 128, dtype=F32)),
-        in_specs=[HBM, HBM, HBM],
-        out_specs=(VMEM, VMEM),
-        scratch_shapes=[
-            pltpu.VMEM(elem_pos.shape, jnp.int32),
-            pltpu.VMEM(vox_pos.shape, jnp.int32),
-            pltpu.SMEM(subbands.shape, jnp.int32),
-            pltpu.VMEM((channels, 8), BF16),
-            pltpu.SemaphoreType.DMA((3,)),
-        ],
-        compiler_params=WIDE,
-        cost_estimate=pl.CostEstimate(
-            flops=60 * channels * voxels,
-            transcendentals=channels * voxels,
-            bytes_accessed=4 * channels * voxels,
-        ),
-    )(*(pltpu.with_memory_space_constraint(x, pltpu.HBM) for x in (elem_pos, vox_pos, subbands)))
-
-    own, _ = lax.optimization_barrier((own, done))
+    def operator(start, share, elem_pos):
+        return pl.pallas_call(
+            functools.partial(operator_kernel, start),
+            name="operator",
+            out_shape=shape(2, share, voxels),
+            in_specs=[HBM, HBM, HBM],
+            out_specs=VMEM,
+            scratch_shapes=[
+                pltpu.VMEM(elem_pos.shape, jnp.int32),
+                pltpu.VMEM(vox_pos.shape, jnp.int32),
+                pltpu.SMEM(subbands.shape, jnp.int32),
+                pltpu.VMEM((channels, 8), BF16),
+                pltpu.SemaphoreType.DMA((3,)),
+            ],
+            compiler_params=WIDE,
+            cost_estimate=pl.CostEstimate(
+                flops=60 * share * voxels, transcendentals=share * voxels, bytes_accessed=4 * share * voxels
+            ),
+        )(*(pltpu.with_memory_space_constraint(x, pltpu.HBM) for x in (elem_pos, vox_pos, subbands)))
+
+    first = 3 * channels // 4
+    upper = operator(0, first, elem_pos)
+    own, upper, elem_pos = lax.optimization_barrier((own, upper, elem_pos))
     other = swap(own)
+    lower = operator(first, channels - first, elem_pos)
     own = own.reshape(chans, bins, parts, group, width)
     other = other.reshape(chans, bins, parts, group, width)
 
@@ -259,22 +267,22 @@
         own_kernel,
         name="beam_own",
         out_shape=shape(frames, voxels),
-        in_specs=[VMEM, VMEM],
+        in_specs=[VMEM, VMEM, VMEM],
         out_specs=VMEM,
         scratch_shapes=[pltpu.VMEM((frames, channels), BF16)],
         compiler_params=WIDE,
         cost_estimate=beam_cost,
-    )(operator, own)
+    )(upper, lower, own)
     y, keep, send = pl.pallas_call(
         other_kernel,
         name="beam_other",
         out_shape=(shape(2 * frames, voxels), shape(half, frames, dtype=F32), shape(half, frames, dtype=F32)),
-        in_specs=[VMEM, VMEM, VMEM],
+        in_specs=[VMEM, VMEM, VMEM, VMEM],
         out_specs=(VMEM, VMEM, VMEM),
         scratch_shapes=[pltpu.VMEM((frames, channels), BF16), pltpu.VMEM((frames, frames), F32)],
         compiler_params=WIDE,
         cost_estimate=beam_cost,
-    )(operator, other, mine)
+    )(upper, lower, other, mine)
 
     total = keep + swap(send)
     near, far, next_to = across(total, 1), across(total, 3), across(total, 2)

time: 78.7 us -> 76.4 us (0.971)
  blocking collectives: 43.5 us -> 19.3 us
  starting transfers between devices: 5.93 us -> 17.7 us
  waiting for transfers between devices: 14.2 us -> 22 us
  Pallas kernels: 14.5 us -> 16.7 us
    all_to_all x1 -> x0, blocking collectives: 24.2 us -> none  [shards(): lax.all_to_all(by_bin, ('chan', 'bin'), split_axis=0, concat_axis=0, tile...]
    all_to_all x0 -> x1, starting transfers between devices: none -> 11.8 us  [shards(): lax.all_to_all(by_bin, ('chan', 'bin'), split_axis=0, concat_axis=0, tile...]
    all_to_all x0 -> x1, waiting for transfers between devices: none -> 7.79 us  [shards(): lax.all_to_all(by_bin, ('chan', 'bin'), split_axis=0, concat_axis=0, tile...]
    pallas_call x1, Pallas kernels: 1.25 us -> 2.3 us  [shards(): pl.pallas_call(own_kernel, name='beam_own', out_shape=shape(frames, voxel...]
    pallas_call x1, Pallas kernels: 0.91 us -> 1.71 us  [shards(): pl.pallas_call(spread_kernel, name='spread', out_shape=shape(chans, bins,...]
    pallas_call x1 -> x2, Pallas kernels: 6.88 us -> 7.24 us  [operator(): pl.pallas_call(functools.partial(operator_kernel, start), name='operator'...]
  transfers between devices with their start and end apart: 7 -> 8, of which waited for: 5 -> 6; matrix products, arithmetic and copies ran while one was open for 0% -> 0% of each run, Pallas kernels for 10% -> 13%
where the time goes in v4:
time: 76.4 us; the launch traced here: 75.8 us
  waiting for transfers between devices  22 us (29%)
  blocking collectives  19.3 us (25%)
  starting transfers between devices  17.7 us (23%)
  Pallas kernels  16.7 us (22%)
    all_to_all x1, blocking collectives, shards(): lax.all_to_all(applied, ('bin', 'core'), split_axis=0, concat_axis=0, til...  19.3 us
    ppermute x4, waiting for transfers between devices, across(): return lax.ppermute(x, 'chan', [(a, a ^ bits) for a in range(chans)])  11.9 us
    all_to_all x1, starting transfers between devices, shards(): lax.all_to_all(by_bin, ('chan', 'bin'), split_axis=0, concat_axis=0, tile...  11.8 us
    all_to_all x1, waiting for transfers between devices, shards(): lax.all_to_all(by_bin, ('chan', 'bin'), split_axis=0, concat_axis=0, tile...  7.79 us
    pallas_call x2, Pallas kernels, operator(): pl.pallas_call(functools.partial(operator_kernel, start), name='operator'...  7.24 us
    ppermute x4, starting transfers between devices, across(): return lax.ppermute(x, 'chan', [(a, a ^ bits) for a in range(chans)])  5.25 us
    ppermute x3, waiting for transfers between devices, swap(): return lax.ppermute(x, 'core', [(0, 1), (1, 0)])  2.32 us
    pallas_call x1, Pallas kernels, shards(): pl.pallas_call(own_kernel, name='beam_own', out_shape=shape(frames, voxel...  2.3 us
  transfers between devices with their start and end apart: 8, of which 6 were waited for; matrix products, arithmetic and copies ran while one was open for 0% of the time, Pallas kernels for 13%

profile of v4, /device:TPU:0, one launch (start us, length us, event | category | flops | bytes accessed | tf_op | source)
XLA Modules:
  0.0 75.8 jit_solution(12511383481691131595)
XLA Ops:
  0.0 1.7 %spread.1 = bf16[8,8,2,16,128]{4,3,2,1,0:T(8,128)(2,1)} custom-call(bf16[2,8,16,128]{3,2,1,0:T(8,128)(2,1)} %rf_ref.1), custom_call_target="tpu_custom_call" | custom-call | tf_op jit(solution)/shard_map/spread/pallas_call | solution.py:223
  1.7 11.8 %all-to-all-start = ((bf16[64,2,16,128]{3,2,1,0:T(8,128)(2,1)}), bf16[64,2,16,128]{3,2,1,0:T(8,128)(2,1)}, u32[]{:S(2)}, u32[]{:S(2)}) async-start(bf16[64,2,16,128]{3,2,1,0:T(8,128)(2,1)} %bitcast), calls=%async_computation | async-start | bytes 1048576 | tf_op jit(solution)/shard_map/all_to_all | solution.py:233
  13.5 5.0 %operator.2.upper = bf16[2,768,1024]{2,1,0:T(8,128)(2,1)S(1)} custom-call(s32[3,1024]{1,0:T(4,128)} %elem_ref.2, s32[3,2048]{1,0:T(4,128)} %vox_ref.3, s32[8]{0:T(128)} %bins_ref.3), custom_call_target="tpu_custom_call" | custom-call | flops 47185920 | bytes 3145728 | tf_op jit(solution)/shard_map/operator/pallas_call | solution.py:236
  18.5 7.8 %all-to-all-done = bf16[64,2,16,128]{3,2,1,0:T(8,128)(2,1)} async-done(((bf16[64,2,16,128]{3,2,1,0:T(8,128)(2,1)}), bf16[64,2,16,128]{3,2,1,0:T(8,128)(2,1)}, u32[]{:S(2)}, u32[]{:S(2)}) %all-to-all-start) | async-done | bytes 524320 | tf_op jit(solution)/shard_map/all_to_all | solution.py:233
  26.3 0.0 collective-permute-start
  26.3 2.3 %operator.3.lower = bf16[2,256,1024]{2,1,0:T(8,128)(2,1)S(1)} custom-call(s32[3,1024]{1,0:T(4,128)} %elem_ref.2, s32[3,2048]{1,0:T(4,128)} %vox_ref.3, s32[8]{0:T(128)} %bins_ref.3), custom_call_target="tpu_custom_call" | custom-call | flops 15728640 | bytes 1048576 | tf_op jit(solution)/shard_map/operator/pallas_call | solution.py:236
  28.5 2.3 %beam_own.1.own = bf16[256,1024]{1,0:T(8,128)(2,1)S(1)} custom-call(bf16[2,768,1024]{2,1,0:T(8,128)(2,1)S(1)} %operator.2.upper, bf16[2,256,1024]{2,1,0:T(8,128)(2,1)S(1)} %operator.3.lower, bf16[8,8,2,16,128]{4,3,2,1,0:T(8,128)(2,1)} %bitcast.2.samples), custom_call_target="tpu_custom_call" | custom-call | flops 2147483648 | bytes 4194304 | tf_op jit(solution)/shard_map/beam_own/pallas_call | solution.py:266
  30.9 0.0 collective-permute-done
  30.9 1.9 %beam_other.1 = (bf16[512,1024]{1,0:T(8,128)(2,1)S(1)}, f32[128,256]{1,0:T(8,128)S(1)}, f32[128,256]{1,0:T(8,128)S(1)}) custom-call(bf16[2,768,1024]{2,1,0:T(8,128)(2,1)S(1)} %operator.2.upper, bf16[2,256,1024]{2,1,0:T(8,128)(2,1)S(1)} %operator.3.lower, bf16[8,8,2,16,128]{4,3,2,1,0:T(8,128)(2,1)S(1)} %bitcast.5, bf16[256,1024]{1,0:T(8,128)(2,1)S(1)} %beam_own.1.own), custom_call_target="tpu_custom_call" | custom-call | flops 2147483648 | bytes 4194304 | tf_op jit(solution)/shard_map/beam_other/pallas_call | solution.py:276
  32.8 0.6 collective-permute-start.1
  33.4 1.0 %collective-permute-done.1 = f32[128,256]{1,0:T(8,128)S(1)} collective-permute-done((f32[128,256]{1,0:T(8,128)S(1)}, f32[128,256]{1,0:T(8,128)S(1)}, u32[]{:S(2)}, u32[]{:S(2)}) %collective-permute-start.1) | collective-permute-done | bytes 131104 | tf_op jit(solution)/shard_map/ppermute | solution.py:218
  34.4 1.7 %collective-permute-start.4 = (f32[128,256]{1,0:T(8,128)S(1)}, f32[128,256]{1,0:T(8,128)S(1)}, u32[]{:S(2)}, u32[]{:S(2)}) collective-permute-start(f32[128,256]{1,0:T(8,128)S(1)} %add.15), channel_id=1, source_target_pairs={{0,32},{16,48},{32,0},{48,16},{64,96},{80,112},{96,64},{112,80},{1... | collective-permute-start | bytes 393224 | tf_op jit(solution)/shard_map/ppermute | solution.py:221
  36.1 1.4 %collective-permute-start.3 = (f32[128,256]{1,0:T(8,128)S(1)}, f32[128,256]{1,0:T(8,128)S(1)}, u32[]{:S(2)}, u32[]{:S(2)}) collective-permute-start(f32[128,256]{1,0:T(8,128)S(1)} %add.15), channel_id=1, source_target_pairs={{0,48},{16,32},{32,16},{48,0},{64,112},{80,96},{96,80},{112,64},{1... | collective-permute-start | bytes 393224 | tf_op jit(solution)/shard_map/ppermute | solution.py:221
  37.5 0.5 collective-permute-start.2
  38.0 4.3 %collective-permute-done.4 = f32[128,256]{1,0:T(8,128)S(1)} collective-permute-done((f32[128,256]{1,0:T(8,128)S(1)}, f32[128,256]{1,0:T(8,128)S(1)}, u32[]{:S(2)}, u32[]{:S(2)}) %collective-permute-start.4) | collective-permute-done | bytes 131104 | tf_op jit(solution)/shard_map/ppermute | solution.py:221
  42.3 2.2 %collective-permute-done.3 = f32[128,256]{1,0:T(8,128)S(1)} collective-permute-done((f32[128,256]{1,0:T(8,128)S(1)}, f32[128,256]{1,0:T(8,128)S(1)}, u32[]{:S(2)}, u32[]{:S(2)}) %collective-permute-start.3) | collective-permute-done | bytes 131104 | tf_op jit(solution)/shard_map/ppermute | solution.py:221
  44.5 0.0 collective-permute-done.2
  44.6 1.7 %collective-permute-start.5 = (f32[128,256]{1,0:T(8,128)S(1)}, f32[128,256]{1,0:T(8,128)S(1)}, u32[]{:S(2)}, u32[]{:S(2)}) collective-permute-start(f32[128,256]{1,0:T(8,128)S(1)} %add_add_fusion), channel_id=1, source_target_pairs={{0,64},{16,80},{32,96},{48,112},{64,0},{80,16},{96,32},{112,48},{1... | collective-permute-start | bytes 393224 | tf_op jit(solution)/shard_map/ppermute | solution.py:221
  46.2 5.3 %collective-permute-done.5 = f32[128,256]{1,0:T(8,128)S(1)} collective-permute-done((f32[128,256]{1,0:T(8,128)S(1)}, f32[128,256]{1,0:T(8,128)S(1)}, u32[]{:S(2)}, u32[]{:S(2)}) %collective-permute-start.5) | collective-permute-done | bytes 131104 | tf_op jit(solution)/shard_map/ppermute | solution.py:221
  51.6 0.1 collective-permute-start.6
  51.7 1.3 %collective-permute-done.6.other = f32[128,256]{1,0:T(8,128)S(1)} collective-permute-done((f32[128,256]{1,0:T(8,128)S(1)}, f32[128,256]{1,0:T(8,128)S(1)}, u32[]{:S(2)}, u32[]{:S(2)}) %collective-permute-start.6) | collective-permute-done | bytes 131104 | tf_op jit(solution)/shard_map/ppermute | solution.py:218
  53.0 2.1 %filter.1 = bf16[16,2,16,1024]{3,2,1,0:T(8,128)(2,1)S(1)} custom-call(f32[128,256]{1,0:T(8,128)S(1)} %add.19.own, f32[128,256]{1,0:T(8,128)S(1)} %collective-permute-done.6.other, bf16[512,1024]{1,0:T(8,128)(2,1)S(1)} %get-tuple-element.16.y_ref), custom_call_target="tpu_custom_call" | custom-call | tf_op jit(solution)/shard_map/filter/pallas_call | solution.py:293
  55.2 19.3 %all_to_all.10 = bf16[16,2,16,1024]{3,2,1,0:T(8,128)(2,1)S(1)} all-to-all(bf16[16,2,16,1024]{3,2,1,0:T(8,128)(2,1)S(1)} %filter.1), channel_id=1, replica_groups=mesh['chan'=8,'bin'=8,'core'=2] {'bin','core'}, dimensions={0} | all-to-all | bytes 2097152 | tf_op jit(solution)/shard_map/all_to_all | solution.py:303
  74.4 1.4 %place.1 = bf16[16,2,8,2048]{3,2,1,0:T(8,128)(2,1)} custom-call(bf16[8,2,2,16,1024]{4,3,2,1,0:T(8,128)(2,1)S(1)} %bitcast.4), custom_call_target="tpu_custom_call" | custom-call | tf_op jit(solution)/shard_map/place/pallas_call | solution.py:305
  (3 shorter events, 0.1 us)
Async XLA Ops:
  1.7 24.6 %all-to-all-start = ((bf16[64,2,16,128]{3,2,1,0:T(8,128)(2,1)}), bf16[64,2,16,128]{3,2,1,0:T(8,128)(2,1)}, u32[]{:S(2)}, u32[]{:S(2)}) async-start(bf16[64,2,16,128]{3,2,1,0:T(8,128)(2,1)} %bitcast), calls=%async_computation | async-start | bytes 1048576 | tf_op jit(solution)/shard_map/all_to_all | solution.py:233
  26.3 4.6 %collective-permute-start = (bf16[64,2,16,128]{3,2,1,0:T(8,128)(2,1)}, bf16[64,2,16,128]{3,2,1,0:T(8,128)(2,1)S(1)}, u32[]{:S(2)}, u32[]{:S(2)}) collective-permute-start(bf16[64,2,16,128]{3,2,1,0:T(8,128)(2,1)} %all-to-all-done), channel_id=1, source_target_pairs={{0,1},{1,0},{2,3},{3,2},{4,5},{5,4},{6,7},{7,6},{8,9},{9,8},{10,11... | collective-permute-start | bytes 1572872 | tf_op jit(solution)/shard_map/ppermute | solution.py:218
  32.8 1.6 %collective-permute-start.1 = (f32[128,256]{1,0:T(8,128)S(1)}, f32[128,256]{1,0:T(8,128)S(1)}, u32[]{:S(2)}, u32[]{:S(2)}) collective-permute-start(f32[128,256]{1,0:T(8,128)S(1)} %get-tuple-element.15), channel_id=1, source_target_pairs={{0,1},{1,0},{2,3},{3,2},{4,5},{5,4},{6,7},{7,6},{8,9},{9,8},{10,11... | collective-permute-start | bytes 393224 | tf_op jit(solution)/shard_map/ppermute | solution.py:218
  34.4 7.9 %collective-permute-start.4 = (f32[128,256]{1,0:T(8,128)S(1)}, f32[128,256]{1,0:T(8,128)S(1)}, u32[]{:S(2)}, u32[]{:S(2)}) collective-permute-start(f32[128,256]{1,0:T(8,128)S(1)} %add.15), channel_id=1, source_target_pairs={{0,32},{16,48},{32,0},{48,16},{64,96},{80,112},{96,64},{112,80},{1... | collective-permute-start | bytes 393224 | tf_op jit(solution)/shard_map/ppermute | solution.py:221
  36.1 8.4 %collective-permute-start.3 = (f32[128,256]{1,0:T(8,128)S(1)}, f32[128,256]{1,0:T(8,128)S(1)}, u32[]{:S(2)}, u32[]{:S(2)}) collective-permute-start(f32[128,256]{1,0:T(8,128)S(1)} %add.15), channel_id=1, source_target_pairs={{0,48},{16,32},{32,16},{48,0},{64,112},{80,96},{96,80},{112,64},{1... | collective-permute-start | bytes 393224 | tf_op jit(solution)/shard_map/ppermute | solution.py:221
  37.5 7.0 %collective-permute-start.2 = (f32[128,256]{1,0:T(8,128)S(1)}, f32[128,256]{1,0:T(8,128)S(1)}, u32[]{:S(2)}, u32[]{:S(2)}) collective-permute-start(f32[128,256]{1,0:T(8,128)S(1)} %add.15), channel_id=1, source_target_pairs={{0,16},{16,0},{32,48},{48,32},{64,80},{80,64},{96,112},{112,96},{1... | collective-permute-start | bytes 393224 | tf_op jit(solution)/shard_map/ppermute | solution.py:221
  44.6 7.0 %collective-permute-start.5 = (f32[128,256]{1,0:T(8,128)S(1)}, f32[128,256]{1,0:T(8,128)S(1)}, u32[]{:S(2)}, u32[]{:S(2)}) collective-permute-start(f32[128,256]{1,0:T(8,128)S(1)} %add_add_fusion), channel_id=1, source_target_pairs={{0,64},{16,80},{32,96},{48,112},{64,0},{80,16},{96,32},{112,48},{1... | collective-permute-start | bytes 393224 | tf_op jit(solution)/shard_map/ppermute | solution.py:221
  51.6 1.4 %collective-permute-start.6 = (f32[128,256]{1,0:T(8,128)S(1)}, f32[128,256]{1,0:T(8,128)S(1)}, u32[]{:S(2)}, u32[]{:S(2)}) collective-permute-start(f32[128,256]{1,0:T(8,128)S(1)} %add.19.own), channel_id=1, source_target_pairs={{0,1},{1,0},{2,3},{3,2},{4,5},{5,4},{6,7},{7,6},{8,9},{9,8},{10,11... | collective-permute-start | bytes 393224 | tf_op jit(solution)/shard_map/ppermute | solution.py:218

commit v5 on v3

--- a/solution.py
+++ b/solution.py
@@ -1,3 +1,4 @@
+import functools
 import math
 
 import jax
@@ -15,7 +16,8 @@
 SIN = (3.1415925800446924, -5.167706878924515, 2.5500313772531213, -0.5980451739748806, 0.0772201286897368)
 COS = (0.9999999534666272, -4.934792858670076, 4.058411914063177, -1.331880160583308, 0.21969679727234584)
 ROUNDER = 12582912.0
-ROWS = 256
+UPPER_ROWS = 192
+LOWER_ROWS = 224
 LANES = 256
 WIDE = pltpu.CompilerParams(vmem_limit_bytes=16 * 1024 * 1024)
 VMEM = pl.BlockSpec(memory_space=pltpu.VMEM)
@@ -34,19 +36,23 @@
     return high, value - unit * high
 
 
-def spread_kernel(rf_ref, out_ref, held, sem):
-    copy = pltpu.make_async_copy(rf_ref, held, sem)
-    copy.start()
-    copy.wait()
-    for part in range(held.shape[0]):
-        block = held[part]
-        for k in range(out_ref.shape[0]):
-            out_ref[k, :, part] = block
-
-
-def operator_kernel(elem_ref, vox_ref, bins_ref, out_ref, done_ref, elem, vox, bins, lhs_ref, sems):
+def spread_kernel(rf_ref, out_ref, sems):
+    parts = rf_ref.shape[0]
+    copies = [
+        pltpu.make_async_copy(rf_ref.at[part], out_ref.at[k, :, part], sems.at[k * parts + part])
+        for k in range(out_ref.shape[0])
+        for part in range(parts)
+    ]
+    for copy in copies:
+        copy.start()
+    for copy in copies:
+        copy.wait()
+
+
+def operator_kernel(elem_ref, vox_ref, bins_ref, upper, lower, elem, vox, bins, lhs_ref, sems):
     core = lax.axis_index("core")
-    _, channels, voxels = out_ref.shape
+    voxels = upper.shape[2]
+    channels = elem.shape[1]
     copies = [
         pltpu.make_async_copy(source, target, sems.at[n])
         for n, (source, target) in enumerate(((elem_ref, elem), (vox_ref, vox), (bins_ref, bins)))
@@ -71,9 +77,9 @@
     squares = jnp.concatenate([-2.0 * voxel, 16.0 * one, one, 64.0 * high, low, zero], axis=0).astype(BF16)
     depths = jnp.concatenate([zero, zero, -1.0 * one, zero, zero, level, zero, zero], axis=0).astype(BF16)
 
-    def tile(index, carry):
-        rows = pl.ds(pl.multiple_of(index * ROWS, ROWS), ROWS)
-        left = lhs_ref[rows]
+    def tile(index, carry, out_ref, start, size):
+        rows = pl.ds(pl.multiple_of(index * size, size), size)
+        left = lhs_ref[pl.ds(pl.multiple_of(start + index * size, 16), size)]
         squared = jnp.dot(left, squares, preferred_element_type=F32)
         depth = jnp.dot(left, depths, preferred_element_type=F32)
         inverse = lax.rsqrt(squared)
@@ -88,31 +94,38 @@
         out_ref[1, rows] = (lean * cosine).astype(BF16)
         return carry
 
-    lax.fori_loop(0, channels // ROWS, tile, 0)
-    done_ref[...] = jnp.zeros_like(done_ref)
-
-
-def beamform(samples, operator, data):
+    start = 0
+    for out_ref, size in ((upper, UPPER_ROWS), (lower, LOWER_ROWS)):
+        lax.fori_loop(0, out_ref.shape[1] // size, functools.partial(tile, out_ref=out_ref, start=start, size=size), 0)
+        start += out_ref.shape[1]
+
+
+def beamform(samples, upper, lower, data):
     blocks, bins, _, group, width = samples.shape
     half = bins * group
     for k in range(blocks):
         for part in range(2):
             data[part * half : (part + 1) * half, k * width : (k + 1) * width] = samples[k, :, part].reshape(half, width)
-    for block in range(operator.shape[2] // LANES):
+    share = upper.shape[1]
+
+    def applied(which, lanes):
+        left = jnp.dot(data[:, :share], upper[which, :, lanes], preferred_element_type=F32)
+        return left + jnp.dot(data[:, share:], lower[which, :, lanes], preferred_element_type=F32)
+
+    for block in range(upper.shape[2] // LANES):
         lanes = slice(block * LANES, (block + 1) * LANES)
-        first = jnp.dot(data[...], operator[0, :, lanes], preferred_element_type=F32)
-        second = jnp.dot(data[...], operator[1, :, lanes], preferred_element_type=F32)
+        first, second = applied(0, lanes), applied(1, lanes)
         yield lanes, (first[:half] + second[half:]).astype(BF16), (first[half:] - second[:half]).astype(BF16)
 
 
-def own_kernel(operator, samples, out_ref, data):
+def own_kernel(upper, lower, samples, out_ref, data):
     half = out_ref.shape[0] // 2
-    for lanes, real, imag in beamform(samples, operator, data):
+    for lanes, real, imag in beamform(samples, upper, lower, data):
         out_ref[:half, lanes] = real
         out_ref[half:, lanes] = imag
 
 
-def other_kernel(operator, samples, own, y_ref, keep_ref, send_ref, data, gram):
+def other_kernel(upper, lower, samples, own, y_ref, keep_ref, send_ref, data, gram):
     core = lax.axis_index("core")
     frames = y_ref.shape[0] // 2
     half = frames // CORES
@@ -120,7 +133,7 @@
     there = pl.multiple_of((1 - core) * half, half)
     y_ref[pl.ds(here, half)] = own[:half]
     y_ref[pl.ds(frames + here, half)] = own[half:]
-    for lanes, real, imag in beamform(samples, operator, data):
+    for lanes, real, imag in beamform(samples, upper, lower, data):
         y_ref[pl.ds(there, half), lanes] = real
         y_ref[pl.ds(frames + there, half), lanes] = imag
     y = y_ref[...]
@@ -219,17 +232,18 @@
         name="spread",
         out_shape=shape(chans, bins, parts, group, width),
         in_specs=[HBM],
-        out_specs=VMEM,
-        scratch_shapes=[pltpu.VMEM(rf_data.shape, BF16), pltpu.SemaphoreType.DMA],
+        out_specs=HBM,
+        scratch_shapes=[pltpu.SemaphoreType.DMA((chans * parts,))],
         compiler_params=WIDE,
     )(pltpu.with_memory_space_constraint(rf_data, pltpu.HBM))
     by_bin = by_bin.reshape(chans * bins, parts, group, width)
     own = lax.all_to_all(by_bin, ("chan", "bin"), split_axis=0, concat_axis=0, tiled=True)
 
-    operator, done = pl.pallas_call(
+    share = 3 * UPPER_ROWS
+    upper, lower = pl.pallas_call(
         operator_kernel,
         name="operator",
-        out_shape=(shape(2, channels, voxels), shape(8, 128, dtype=F32)),
+        out_shape=(shape(2, share, voxels), shape(2, channels - share, voxels)),
         in_specs=[HBM, HBM, HBM],
         out_specs=(VMEM, VMEM),
         scratch_shapes=[
@@ -247,7 +261,7 @@
         ),
     )(*(pltpu.with_memory_space_constraint(x, pltpu.HBM) for x in (elem_pos, vox_pos, subbands)))
 
-    own, _ = lax.optimization_barrier((own, done))
+    own, upper, lower = lax.optimization_barrier((own, upper, lower))
     other = swap(own)
     own = own.reshape(chans, bins, parts, group, width)
     other = other.reshape(chans, bins, parts, group, width)
@@ -259,22 +273,22 @@
         own_kernel,
         name="beam_own",
         out_shape=shape(frames, voxels),
-        in_specs=[VMEM, VMEM],
+        in_specs=[VMEM, VMEM, VMEM],
         out_specs=VMEM,
         scratch_shapes=[pltpu.VMEM((frames, channels), BF16)],
         compiler_params=WIDE,
         cost_estimate=beam_cost,
-    )(operator, own)
+    )(upper, lower, own)
     y, keep, send = pl.pallas_call(
         other_kernel,
         name="beam_other",
         out_shape=(shape(2 * frames, voxels), shape(half, frames, dtype=F32), shape(half, frames, dtype=F32)),
-        in_specs=[VMEM, VMEM, VMEM],
+        in_specs=[VMEM, VMEM, VMEM, VMEM],
         out_specs=(VMEM, VMEM, VMEM),
         scratch_shapes=[pltpu.VMEM((frames, channels), BF16), pltpu.VMEM((frames, frames), F32)],
         compiler_params=WIDE,
         cost_estimate=beam_cost,
-    )(operator, other, mine)
+    )(upper, lower, other, mine)
 
     total = keep + swap(send)
     near, far, next_to = across(total, 1), across(total, 3), across(total, 2)

time: 78.7 us -> 90.5 us (1.15)
  blocking collectives: 43.5 us -> 19.3 us
  Pallas kernels: 14.5 us -> 30.8 us
  starting transfers between devices: 5.93 us -> 17.4 us
  waiting for transfers between devices: 14.2 us -> 19.6 us
  local copies, waits for them, and re-layouts: 0 us -> 2.74 us
    all_to_all x1 -> x0, blocking collectives: 24.2 us -> none  [shards(): lax.all_to_all(by_bin, ('chan', 'bin'), split_axis=0, concat_axis=0, tile...]
    pallas_call x1, Pallas kernels: 0.91 us -> 17.1 us  [shards(): pl.pallas_call(spread_kernel, name='spread', out_shape=shape(chans, bins,...]
    all_to_all x0 -> x1, starting transfers between devices: none -> 11.5 us  [shards(): lax.all_to_all(by_bin, ('chan', 'bin'), split_axis=0, concat_axis=0, tile...]
    all_to_all x0 -> x1, waiting for transfers between devices: none -> 5.32 us  [shards(): lax.all_to_all(by_bin, ('chan', 'bin'), split_axis=0, concat_axis=0, tile...]
    unnamed x0 -> x4, local copies, waits for them, and re-layouts: none -> 2.74 us
  transfers between devices with their start and end apart: 7 -> 8, of which waited for: 5 -> 6; matrix products, arithmetic and copies ran while one was open for 0% -> 0% of each run, Pallas kernels for 10% -> 9%
where the time goes in v5:
time: 90.5 us; the launch traced here: 90 us
  Pallas kernels  30.8 us (34%)
  waiting for transfers between devices  19.6 us (22%)
  blocking collectives  19.3 us (21%)
  starting transfers between devices  17.4 us (19%)
  local copies, waits for them, and re-layouts  2.74 us (3%)
    all_to_all x1, blocking collectives, shards(): lax.all_to_all(applied, ('bin', 'core'), split_axis=0, concat_axis=0, til...  19.3 us
    pallas_call x1, Pallas kernels, shards(): pl.pallas_call(spread_kernel, name='spread', out_shape=shape(chans, bins,...  17.1 us
    ppermute x4, waiting for transfers between devices, across(): return lax.ppermute(x, 'chan', [(a, a ^ bits) for a in range(chans)])  11.9 us
    all_to_all x1, starting transfers between devices, shards(): lax.all_to_all(by_bin, ('chan', 'bin'), split_axis=0, concat_axis=0, tile...  11.5 us
    pallas_call x1, Pallas kernels, shards(): pl.pallas_call(operator_kernel, name='operator', out_shape=(shape(2, shar...  6.35 us
    all_to_all x1, waiting for transfers between devices, shards(): lax.all_to_all(by_bin, ('chan', 'bin'), split_axis=0, concat_axis=0, tile...  5.32 us
    ppermute x4, starting transfers between devices, across(): return lax.ppermute(x, 'chan', [(a, a ^ bits) for a in range(chans)])  5.25 us
    unnamed x4, local copies, waits for them, and re-layouts  2.74 us
  transfers between devices with their start and end apart: 8, of which 6 were waited for; matrix products, arithmetic and copies ran while one was open for 0% of the time, Pallas kernels for 9%

profile of v5, /device:TPU:0, one launch (start us, length us, event | category | flops | bytes accessed | tf_op | source)
XLA Modules:
  0.0 90.0 jit_solution(8655477701427467763)
XLA Ops:
  0.0 17.1 %spread.1 = bf16[8,8,2,16,128]{4,3,2,1,0:T(8,128)(2,1)} custom-call(bf16[2,8,16,128]{3,2,1,0:T(8,128)(2,1)} %rf_ref.1), custom_call_target="tpu_custom_call" | custom-call | tf_op jit(solution)/shard_map/spread/pallas_call | solution.py:230
  17.1 11.5 %all-to-all-start = ((bf16[64,2,16,128]{3,2,1,0:T(8,128)(2,1)}), bf16[64,2,16,128]{3,2,1,0:T(8,128)(2,1)S(1)}, u32[]{:S(2)}, u32[]{:S(2)}) async-start(bf16[64,2,16,128]{3,2,1,0:T(8,128)(2,1)} %bitcast), calls=%async_computation | async-start | bytes 1048576 | tf_op jit(solution)/shard_map/all_to_all | solution.py:240
  28.6 6.4 %operator.1 = (bf16[2,576,1024]{2,1,0:T(8,128)(2,1)S(1)}, bf16[2,448,1024]{2,1,0:T(8,128)(2,1)S(1)}) custom-call(s32[3,1024]{1,0:T(4,128)} %elem_ref.1, s32[3,2048]{1,0:T(4,128)} %vox_ref.1, s32[8]{0:T(128)} %bins_ref.1), custom_call_target="tpu_custom_call" | custom-call | flops 62914560 | bytes 4194304 | tf_op jit(solution)/shard_map/operator/pallas_call | solution.py:243
  35.0 0.0 copy-start
  35.0 1.2 %copy-done = bf16[2,448,1024]{2,1,0:T(8,128)(2,1)} copy-done((bf16[2,448,1024]{2,1,0:T(8,128)(2,1)}, bf16[2,448,1024]{2,1,0:T(8,128)(2,1)S(1)}, u32[]{:S(2)}) %copy-start) | copy-done | bytes 1835032
  36.3 5.3 %all-to-all-done = bf16[64,2,16,128]{3,2,1,0:T(8,128)(2,1)S(1)} async-done(((bf16[64,2,16,128]{3,2,1,0:T(8,128)(2,1)}), bf16[64,2,16,128]{3,2,1,0:T(8,128)(2,1)S(1)}, u32[]{:S(2)}, u32[]{:S(2)}) %all-to-all-start) | async-done | bytes 524320 | tf_op jit(solution)/shard_map/all_to_all | solution.py:240
  41.6 0.0 collective-permute-start
  41.6 0.0 copy-start.1
  41.6 1.5 %copy-done.1 = bf16[2,448,1024]{2,1,0:T(8,128)(2,1)S(1)} copy-done((bf16[2,448,1024]{2,1,0:T(8,128)(2,1)S(1)}, bf16[2,448,1024]{2,1,0:T(8,128)(2,1)}, u32[]{:S(2)}) %copy-start.1) | copy-done | bytes 1835032
  43.1 1.6 %beam_own.1.own = bf16[256,1024]{1,0:T(8,128)(2,1)S(1)} custom-call(bf16[2,576,1024]{2,1,0:T(8,128)(2,1)S(1)} %get-tuple-element.15.upper, bf16[2,448,1024]{2,1,0:T(8,128)(2,1)S(1)} %copy-done.1, bf16[8,8,2,16,128]{4,3,2,1,0:T(8,128)(2,1)S(1)} %bitcast.5), custom_call_target="tpu_custom_call" | custom-call | flops 2147483648 | bytes 4194304 | tf_op jit(solution)/shard_map/beam_own/pallas_call | solution.py:272
  44.7 0.0 collective-permute-done
  44.7 2.3 %beam_other.1 = (bf16[512,1024]{1,0:T(8,128)(2,1)S(1)}, f32[128,256]{1,0:T(8,128)S(1)}, f32[128,256]{1,0:T(8,128)S(1)}) custom-call(bf16[2,576,1024]{2,1,0:T(8,128)(2,1)S(1)} %get-tuple-element.15.upper, bf16[2,448,1024]{2,1,0:T(8,128)(2,1)S(1)} %copy-done.1, bf16[8,8,2,16,128]{4,3,2,1,0:T(8,128)(2,1)S(1)} %bitcast.6, bf16[256,1024]{1,0:T(8,128)(2,1)S(1)} %beam_own.1.own), custom_call_target="tpu_custom_call" | custom-call | flops 2147483648 | bytes 4194304 | tf_op jit(solution)/shard_map/beam_other/pallas_call | solution.py:282
  47.0 0.6 collective-permute-start.1
  47.6 1.0 %collective-permute-done.1 = f32[128,256]{1,0:T(8,128)S(1)} collective-permute-done((f32[128,256]{1,0:T(8,128)S(1)}, f32[128,256]{1,0:T(8,128)S(1)}, u32[]{:S(2)}, u32[]{:S(2)}) %collective-permute-start.1) | collective-permute-done | bytes 131104 | tf_op jit(solution)/shard_map/ppermute | solution.py:225
  48.6 1.7 %collective-permute-start.4 = (f32[128,256]{1,0:T(8,128)S(1)}, f32[128,256]{1,0:T(8,128)S(1)}, u32[]{:S(2)}, u32[]{:S(2)}) collective-permute-start(f32[128,256]{1,0:T(8,128)S(1)} %add.15), channel_id=1, source_target_pairs={{0,32},{16,48},{32,0},{48,16},{64,96},{80,112},{96,64},{112,80},{1... | collective-permute-start | bytes 393224 | tf_op jit(solution)/shard_map/ppermute | solution.py:228
  50.3 1.4 %collective-permute-start.3 = (f32[128,256]{1,0:T(8,128)S(1)}, f32[128,256]{1,0:T(8,128)S(1)}, u32[]{:S(2)}, u32[]{:S(2)}) collective-permute-start(f32[128,256]{1,0:T(8,128)S(1)} %add.15), channel_id=1, source_target_pairs={{0,48},{16,32},{32,16},{48,0},{64,112},{80,96},{96,80},{112,64},{1... | collective-permute-start | bytes 393224 | tf_op jit(solution)/shard_map/ppermute | solution.py:228
  51.7 0.5 collective-permute-start.2
  52.2 4.3 %collective-permute-done.4 = f32[128,256]{1,0:T(8,128)S(1)} collective-permute-done((f32[128,256]{1,0:T(8,128)S(1)}, f32[128,256]{1,0:T(8,128)S(1)}, u32[]{:S(2)}, u32[]{:S(2)}) %collective-permute-start.4) | collective-permute-done | bytes 131104 | tf_op jit(solution)/shard_map/ppermute | solution.py:228
  56.5 2.2 %collective-permute-done.3 = f32[128,256]{1,0:T(8,128)S(1)} collective-permute-done((f32[128,256]{1,0:T(8,128)S(1)}, f32[128,256]{1,0:T(8,128)S(1)}, u32[]{:S(2)}, u32[]{:S(2)}) %collective-permute-start.3) | collective-permute-done | bytes 131104 | tf_op jit(solution)/shard_map/ppermute | solution.py:228
  58.7 0.0 collective-permute-done.2
  58.8 1.7 %collective-permute-start.5 = (f32[128,256]{1,0:T(8,128)S(1)}, f32[128,256]{1,0:T(8,128)S(1)}, u32[]{:S(2)}, u32[]{:S(2)}) collective-permute-start(f32[128,256]{1,0:T(8,128)S(1)} %add_add_fusion), channel_id=1, source_target_pairs={{0,64},{16,80},{32,96},{48,112},{64,0},{80,16},{96,32},{112,48},{1... | collective-permute-start | bytes 393224 | tf_op jit(solution)/shard_map/ppermute | solution.py:228
  60.4 5.3 %collective-permute-done.5 = f32[128,256]{1,0:T(8,128)S(1)} collective-permute-done((f32[128,256]{1,0:T(8,128)S(1)}, f32[128,256]{1,0:T(8,128)S(1)}, u32[]{:S(2)}, u32[]{:S(2)}) %collective-permute-start.5) | collective-permute-done | bytes 131104 | tf_op jit(solution)/shard_map/ppermute | solution.py:228
  65.8 0.1 collective-permute-start.6
  65.9 1.3 %collective-permute-done.6.other = f32[128,256]{1,0:T(8,128)S(1)} collective-permute-done((f32[128,256]{1,0:T(8,128)S(1)}, f32[128,256]{1,0:T(8,128)S(1)}, u32[]{:S(2)}, u32[]{:S(2)}) %collective-permute-start.6) | collective-permute-done | bytes 131104 | tf_op jit(solution)/shard_map/ppermute | solution.py:225
  67.2 2.1 %filter.1 = bf16[16,2,16,1024]{3,2,1,0:T(8,128)(2,1)S(1)} custom-call(f32[128,256]{1,0:T(8,128)S(1)} %add.19.own, f32[128,256]{1,0:T(8,128)S(1)} %collective-permute-done.6.other, bf16[512,1024]{1,0:T(8,128)(2,1)S(1)} %get-tuple-element.20.y_ref), custom_call_target="tpu_custom_call" | custom-call | tf_op jit(solution)/shard_map/filter/pallas_call | solution.py:299
  69.4 19.3 %all_to_all.10 = bf16[16,2,16,1024]{3,2,1,0:T(8,128)(2,1)S(1)} all-to-all(bf16[16,2,16,1024]{3,2,1,0:T(8,128)(2,1)S(1)} %filter.1), channel_id=1, replica_groups=mesh['chan'=8,'bin'=8,'core'=2] {'bin','core'}, dimensions={0} | all-to-all | bytes 2097152 | tf_op jit(solution)/shard_map/all_to_all | solution.py:309
  88.6 1.4 %place.1 = bf16[16,2,8,2048]{3,2,1,0:T(8,128)(2,1)} custom-call(bf16[8,2,2,16,1024]{4,3,2,1,0:T(8,128)(2,1)S(1)} %bitcast.4), custom_call_target="tpu_custom_call" | custom-call | tf_op jit(solution)/shard_map/place/pallas_call | solution.py:311
  (3 shorter events, 0.1 us)
Async XLA Ops:
  17.1 24.5 %all-to-all-start = ((bf16[64,2,16,128]{3,2,1,0:T(8,128)(2,1)}), bf16[64,2,16,128]{3,2,1,0:T(8,128)(2,1)S(1)}, u32[]{:S(2)}, u32[]{:S(2)}) async-start(bf16[64,2,16,128]{3,2,1,0:T(8,128)(2,1)} %bitcast), calls=%async_computation | async-start | bytes 1048576 | tf_op jit(solution)/shard_map/all_to_all | solution.py:240
  35.0 1.3 %copy-start = (bf16[2,448,1024]{2,1,0:T(8,128)(2,1)}, bf16[2,448,1024]{2,1,0:T(8,128)(2,1)S(1)}, u32[]{:S(2)}) copy-start(bf16[2,448,1024]{2,1,0:T(8,128)(2,1)S(1)} %get-tuple-element.16.lower) | copy-start | bytes 5505028
  41.6 3.1 %collective-permute-start = (bf16[64,2,16,128]{3,2,1,0:T(8,128)(2,1)S(1)}, bf16[64,2,16,128]{3,2,1,0:T(8,128)(2,1)S(1)}, u32[]{:S(2)}, u32[]{:S(2)}) collective-permute-start(bf16[64,2,16,128]{3,2,1,0:T(8,128)(2,1)S(1)} %all-to-all-done), channel_id=1, source_target_pairs={{0,1},{1,0},{2,3},{3,2},{4,5},{5,4},{6,7},{7,6},{8,9},{9,8},{10,11... | collective-permute-start | bytes 1572872 | tf_op jit(solution)/shard_map/ppermute | solution.py:225
  41.6 1.5 %copy-start.1 = (bf16[2,448,1024]{2,1,0:T(8,128)(2,1)S(1)}, bf16[2,448,1024]{2,1,0:T(8,128)(2,1)}, u32[]{:S(2)}) copy-start(bf16[2,448,1024]{2,1,0:T(8,128)(2,1)} %copy-done) | copy-start | bytes 5505028
  47.0 1.6 %collective-permute-start.1 = (f32[128,256]{1,0:T(8,128)S(1)}, f32[128,256]{1,0:T(8,128)S(1)}, u32[]{:S(2)}, u32[]{:S(2)}) collective-permute-start(f32[128,256]{1,0:T(8,128)S(1)} %get-tuple-element.19), channel_id=1, source_target_pairs={{0,1},{1,0},{2,3},{3,2},{4,5},{5,4},{6,7},{7,6},{8,9},{9,8},{10,11... | collective-permute-start | bytes 393224 | tf_op jit(solution)/shard_map/ppermute | solution.py:225
  48.6 7.9 %collective-permute-start.4 = (f32[128,256]{1,0:T(8,128)S(1)}, f32[128,256]{1,0:T(8,128)S(1)}, u32[]{:S(2)}, u32[]{:S(2)}) collective-permute-start(f32[128,256]{1,0:T(8,128)S(1)} %add.15), channel_id=1, source_target_pairs={{0,32},{16,48},{32,0},{48,16},{64,96},{80,112},{96,64},{112,80},{1... | collective-permute-start | bytes 393224 | tf_op jit(solution)/shard_map/ppermute | solution.py:228
  50.3 8.4 %collective-permute-start.3 = (f32[128,256]{1,0:T(8,128)S(1)}, f32[128,256]{1,0:T(8,128)S(1)}, u32[]{:S(2)}, u32[]{:S(2)}) collective-permute-start(f32[128,256]{1,0:T(8,128)S(1)} %add.15), channel_id=1, source_target_pairs={{0,48},{16,32},{32,16},{48,0},{64,112},{80,96},{96,80},{112,64},{1... | collective-permute-start | bytes 393224 | tf_op jit(solution)/shard_map/ppermute | solution.py:228
  51.7 7.0 %collective-permute-start.2 = (f32[128,256]{1,0:T(8,128)S(1)}, f32[128,256]{1,0:T(8,128)S(1)}, u32[]{:S(2)}, u32[]{:S(2)}) collective-permute-start(f32[128,256]{1,0:T(8,128)S(1)} %add.15), channel_id=1, source_target_pairs={{0,16},{16,0},{32,48},{48,32},{64,80},{80,64},{96,112},{112,96},{1... | collective-permute-start | bytes 393224 | tf_op jit(solution)/shard_map/ppermute | solution.py:228
  58.8 7.0 %collective-permute-start.5 = (f32[128,256]{1,0:T(8,128)S(1)}, f32[128,256]{1,0:T(8,128)S(1)}, u32[]{:S(2)}, u32[]{:S(2)}) collective-permute-start(f32[128,256]{1,0:T(8,128)S(1)} %add_add_fusion), channel_id=1, source_target_pairs={{0,64},{16,80},{32,96},{48,112},{64,0},{80,16},{96,32},{112,48},{1... | collective-permute-start | bytes 393224 | tf_op jit(solution)/shard_map/ppermute | solution.py:228
  65.8 1.4 %collective-permute-start.6 = (f32[128,256]{1,0:T(8,128)S(1)}, f32[128,256]{1,0:T(8,128)S(1)}, u32[]{:S(2)}, u32[]{:S(2)}) collective-permute-start(f32[128,256]{1,0:T(8,128)S(1)} %add.19.own), channel_id=1, source_target_pairs={{0,1},{1,0},{2,3},{3,2},{4,5},{5,4},{6,7},{7,6},{8,9},{9,8},{10,11... | collective-permute-start | bytes 393224 | tf_op jit(solution)/shard_map/ppermute | solution.py:225

commit v6 on v3

--- a/solution.py
+++ b/solution.py
@@ -1,3 +1,4 @@
+import functools
 import math
 
 import jax
@@ -44,9 +45,10 @@
             out_ref[k, :, part] = block
 
 
-def operator_kernel(elem_ref, vox_ref, bins_ref, out_ref, done_ref, elem, vox, bins, lhs_ref, sems):
+def operator_kernel(elem_ref, vox_ref, bins_ref, upper, lower_ref, elem, vox, bins, lhs_ref, lower, sems):
     core = lax.axis_index("core")
-    _, channels, voxels = out_ref.shape
+    voxels = upper.shape[2]
+    channels = elem.shape[1]
     copies = [
         pltpu.make_async_copy(source, target, sems.at[n])
         for n, (source, target) in enumerate(((elem_ref, elem), (vox_ref, vox), (bins_ref, bins)))
@@ -71,9 +73,9 @@
     squares = jnp.concatenate([-2.0 * voxel, 16.0 * one, one, 64.0 * high, low, zero], axis=0).astype(BF16)
     depths = jnp.concatenate([zero, zero, -1.0 * one, zero, zero, level, zero, zero], axis=0).astype(BF16)
 
-    def tile(index, carry):
+    def tile(index, carry, out_ref, start):
         rows = pl.ds(pl.multiple_of(index * ROWS, ROWS), ROWS)
-        left = lhs_ref[rows]
+        left = lhs_ref[pl.ds(pl.multiple_of(start + index * ROWS, ROWS), ROWS)]
         squared = jnp.dot(left, squares, preferred_element_type=F32)
         depth = jnp.dot(left, depths, preferred_element_type=F32)
         inverse = lax.rsqrt(squared)
@@ -88,31 +90,51 @@
         out_ref[1, rows] = (lean * cosine).astype(BF16)
         return carry
 
-    lax.fori_loop(0, channels // ROWS, tile, 0)
-    done_ref[...] = jnp.zeros_like(done_ref)
-
-
-def beamform(samples, operator, data):
+    share = upper.shape[1]
+    lax.fori_loop(0, (channels - share) // ROWS, functools.partial(tile, out_ref=lower, start=share), 0)
+    copy = pltpu.make_async_copy(lower, lower_ref, sems.at[3])
+    copy.start()
+    lax.fori_loop(0, share // ROWS, functools.partial(tile, out_ref=upper, start=0), 0)
+    copy.wait()
+
+
+def arrange(samples, data):
     blocks, bins, _, group, width = samples.shape
     half = bins * group
     for k in range(blocks):
         for part in range(2):
             data[part * half : (part + 1) * half, k * width : (k + 1) * width] = samples[k, :, part].reshape(half, width)
-    for block in range(operator.shape[2] // LANES):
-        lanes = slice(block * LANES, (block + 1) * LANES)
-        first = jnp.dot(data[...], operator[0, :, lanes], preferred_element_type=F32)
-        second = jnp.dot(data[...], operator[1, :, lanes], preferred_element_type=F32)
-        yield lanes, (first[:half] + second[half:]).astype(BF16), (first[half:] - second[:half]).astype(BF16)
-
-
-def own_kernel(operator, samples, out_ref, data):
+
+
+def applied(data, operator, lanes):
+    return [jnp.dot(data, operator[which, :, lanes], preferred_element_type=F32) for which in range(2)]
+
+
+def joined(first, second):
+    half = first.shape[0] // 2
+    return (first[:half] + second[half:]).astype(BF16), (first[half:] - second[:half]).astype(BF16)
+
+
+def own_kernel(upper, lower_ref, samples, out_ref, lower, data, partial, sem):
+    copy = pltpu.make_async_copy(lower_ref, lower, sem)
+    copy.start()
+    arrange(samples, data)
     half = out_ref.shape[0] // 2
-    for lanes, real, imag in beamform(samples, operator, data):
-        out_ref[:half, lanes] = real
-        out_ref[half:, lanes] = imag
-
-
-def other_kernel(operator, samples, own, y_ref, keep_ref, send_ref, data, gram):
+    share = upper.shape[1]
+    blocks = [slice(n, n + LANES) for n in range(0, upper.shape[2], LANES)]
+    for lanes in blocks:
+        first, second = applied(data[:, :share], upper, lanes)
+        partial[0, :, lanes] = first
+        partial[1, :, lanes] = second
+    copy.wait()
+    for lanes in blocks:
+        first, second = applied(data[:, share:], lower, lanes)
+        out_ref[:half, lanes], out_ref[half:, lanes] = joined(
+            partial[0, :, lanes] + first, partial[1, :, lanes] + second
+        )
+
+
+def other_kernel(upper, lower, samples, own, y_ref, keep_ref, send_ref, data, gram):
     core = lax.axis_index("core")
     frames = y_ref.shape[0] // 2
     half = frames // CORES
@@ -120,9 +142,15 @@
     there = pl.multiple_of((1 - core) * half, half)
     y_ref[pl.ds(here, half)] = own[:half]
     y_ref[pl.ds(frames + here, half)] = own[half:]
-    for lanes, real, imag in beamform(samples, operator, data):
-        y_ref[pl.ds(there, half), lanes] = real
-        y_ref[pl.ds(frames + there, half), lanes] = imag
+    arrange(samples, data)
+    share = upper.shape[1]
+    for n in range(0, upper.shape[2], LANES):
+        lanes = slice(n, n + LANES)
+        first, second = applied(data[:, :share], upper, lanes)
+        more, further = applied(data[:, share:], lower, lanes)
+        y_ref[pl.ds(there, half), lanes], y_ref[pl.ds(frames + there, half), lanes] = joined(
+            first + more, second + further
+        )
     y = y_ref[...]
     products = lax.dot_general(y, y, (((1,), (1,)), ((), ())), preferred_element_type=F32)
     gram[...] = (products[:frames, :frames] + products[frames:, frames:]) + (
@@ -226,18 +254,20 @@
     by_bin = by_bin.reshape(chans * bins, parts, group, width)
     own = lax.all_to_all(by_bin, ("chan", "bin"), split_axis=0, concat_axis=0, tiled=True)
 
-    operator, done = pl.pallas_call(
+    share = channels // 2
+    upper, lower = pl.pallas_call(
         operator_kernel,
         name="operator",
-        out_shape=(shape(2, channels, voxels), shape(8, 128, dtype=F32)),
+        out_shape=(shape(2, share, voxels), pltpu.HBM((2, channels - share, voxels), BF16)),
         in_specs=[HBM, HBM, HBM],
-        out_specs=(VMEM, VMEM),
+        out_specs=(VMEM, HBM),
         scratch_shapes=[
             pltpu.VMEM(elem_pos.shape, jnp.int32),
             pltpu.VMEM(vox_pos.shape, jnp.int32),
             pltpu.SMEM(subbands.shape, jnp.int32),
             pltpu.VMEM((channels, 8), BF16),
-            pltpu.SemaphoreType.DMA((3,)),
+            pltpu.VMEM((2, channels - share, voxels), BF16),
+            pltpu.SemaphoreType.DMA((4,)),
         ],
         compiler_params=WIDE,
         cost_estimate=pl.CostEstimate(
@@ -247,7 +277,7 @@
         ),
     )(*(pltpu.with_memory_space_constraint(x, pltpu.HBM) for x in (elem_pos, vox_pos, subbands)))
 
-    own, _ = lax.optimization_barrier((own, done))
+    own, upper, lower = lax.optimization_barrier((own, upper, lower))
     other = swap(own)
     own = own.reshape(chans, bins, parts, group, width)
     other = other.reshape(chans, bins, parts, group, width)
@@ -255,26 +285,30 @@
     beam_cost = pl.CostEstimate(
         flops=8 * half * channels * voxels * 2, transcendentals=0, bytes_accessed=4 * channels * voxels
     )
-    mine = pl.pallas_call(
+    mine, lower = pl.pallas_call(
         own_kernel,
         name="beam_own",
-        out_shape=shape(frames, voxels),
-        in_specs=[VMEM, VMEM],
-        out_specs=VMEM,
-        scratch_shapes=[pltpu.VMEM((frames, channels), BF16)],
+        out_shape=(shape(frames, voxels), shape(2, channels - share, voxels)),
+        in_specs=[VMEM, HBM, VMEM],
+        out_specs=(VMEM, VMEM),
+        scratch_shapes=[
+            pltpu.VMEM((frames, channels), BF16),
+            pltpu.VMEM((2, frames, voxels), F32),
+            pltpu.SemaphoreType.DMA,
+        ],
         compiler_params=WIDE,
         cost_estimate=beam_cost,
-    )(operator, own)
+    )(upper, pltpu.with_memory_space_constraint(lower, pltpu.HBM), own)
     y, keep, send = pl.pallas_call(
         other_kernel,
         name="beam_other",
         out_shape=(shape(2 * frames, voxels), shape(half, frames, dtype=F32), shape(half, frames, dtype=F32)),
-        in_specs=[VMEM, VMEM, VMEM],
+        in_specs=[VMEM, VMEM, VMEM, VMEM],
         out_specs=(VMEM, VMEM, VMEM),
         scratch_shapes=[pltpu.VMEM((frames, channels), BF16), pltpu.VMEM((frames, frames), F32)],
         compiler_params=WIDE,
         cost_estimate=beam_cost,
-    )(operator, other, mine)
+    )(upper, lower, other, mine)
 
     total = keep + swap(send)
     near, far, next_to = across(total, 1), across(total, 3), across(total, 2)

time: 78.7 us -> 74 us (0.940)
  blocking collectives: 43.5 us -> 19.3 us
  starting transfers between devices: 5.93 us -> 17.4 us
  waiting for transfers between devices: 14.2 us -> 20.9 us
  Pallas kernels: 14.5 us -> 15.7 us
    all_to_all x1 -> x0, blocking collectives: 24.2 us -> none  [shards(): lax.all_to_all(by_bin, ('chan', 'bin'), split_axis=0, concat_axis=0, tile...]
    all_to_all x0 -> x1, starting transfers between devices: none -> 11.5 us  [shards(): lax.all_to_all(by_bin, ('chan', 'bin'), split_axis=0, concat_axis=0, tile...]
    all_to_all x0 -> x1, waiting for transfers between devices: none -> 6.69 us  [shards(): lax.all_to_all(by_bin, ('chan', 'bin'), split_axis=0, concat_axis=0, tile...]
    pallas_call x1, Pallas kernels: 0.91 us -> 1.71 us  [shards(): pl.pallas_call(spread_kernel, name='spread', out_shape=shape(chans, bins,...]
  transfers between devices with their start and end apart: 7 -> 8, of which waited for: 5 -> 6; matrix products, arithmetic and copies ran while one was open for 0% -> 0% of each run, Pallas kernels for 10% -> 12%
where the time goes in v6:
time: 74 us; the launch traced here: 73.5 us
  waiting for transfers between devices  20.9 us (28%)
  blocking collectives  19.3 us (26%)
  starting transfers between devices  17.4 us (24%)
  Pallas kernels  15.7 us (21%)
    all_to_all x1, blocking collectives, shards(): lax.all_to_all(applied, ('bin', 'core'), split_axis=0, concat_axis=0, til...  19.3 us
    ppermute x4, waiting for transfers between devices, across(): return lax.ppermute(x, 'chan', [(a, a ^ bits) for a in range(chans)])  11.9 us
    all_to_all x1, starting transfers between devices, shards(): lax.all_to_all(by_bin, ('chan', 'bin'), split_axis=0, concat_axis=0, tile...  11.5 us
    all_to_all x1, waiting for transfers between devices, shards(): lax.all_to_all(by_bin, ('chan', 'bin'), split_axis=0, concat_axis=0, tile...  6.69 us
    pallas_call x1, Pallas kernels, shards(): pl.pallas_call(operator_kernel, name='operator', out_shape=(shape(2, shar...  6.24 us
    ppermute x4, starting transfers between devices, across(): return lax.ppermute(x, 'chan', [(a, a ^ bits) for a in range(chans)])  5.25 us
    ppermute x3, waiting for transfers between devices, swap(): return lax.ppermute(x, 'core', [(0, 1), (1, 0)])  2.32 us
    pallas_call x1, Pallas kernels, shards(): pl.pallas_call(own_kernel, name='beam_own', out_shape=(shape(frames, voxe...  2.31 us
  transfers between devices with their start and end apart: 8, of which 6 were waited for; matrix products, arithmetic and copies ran while one was open for 0% of the time, Pallas kernels for 12%

profile of v6, /device:TPU:0, one launch (start us, length us, event | category | flops | bytes accessed | tf_op | source)
XLA Modules:
  0.0 73.5 jit_solution(6983430616591141866)
XLA Ops:
  0.0 1.7 %spread.1 = bf16[8,8,2,16,128]{4,3,2,1,0:T(8,128)(2,1)} custom-call(bf16[2,8,16,128]{3,2,1,0:T(8,128)(2,1)} %rf_ref.1), custom_call_target="tpu_custom_call" | custom-call | tf_op jit(solution)/shard_map/spread/pallas_call | solution.py:245
  1.7 11.5 %all-to-all-start = ((bf16[64,2,16,128]{3,2,1,0:T(8,128)(2,1)}), bf16[64,2,16,128]{3,2,1,0:T(8,128)(2,1)S(1)}, u32[]{:S(2)}, u32[]{:S(2)}) async-start(bf16[64,2,16,128]{3,2,1,0:T(8,128)(2,1)} %bitcast), calls=%async_computation | async-start | bytes 1048576 | tf_op jit(solution)/shard_map/all_to_all | solution.py:255
  13.2 6.2 %operator.1 = (bf16[2,512,1024]{2,1,0:T(8,128)(2,1)S(1)}, bf16[2,512,1024]{2,1,0:T(8,128)(2,1)}) custom-call(s32[3,1024]{1,0:T(4,128)} %elem_ref.1, s32[3,2048]{1,0:T(4,128)} %vox_ref.1, s32[8]{0:T(128)} %bins_ref.1), custom_call_target="tpu_custom_call" | custom-call | flops 62914560 | bytes 4194304 | tf_op jit(solution)/shard_map/operator/pallas_call | solution.py:258
  19.5 6.7 %all-to-all-done = bf16[64,2,16,128]{3,2,1,0:T(8,128)(2,1)S(1)} async-done(((bf16[64,2,16,128]{3,2,1,0:T(8,128)(2,1)}), bf16[64,2,16,128]{3,2,1,0:T(8,128)(2,1)S(1)}, u32[]{:S(2)}, u32[]{:S(2)}) %all-to-all-start) | async-done | bytes 524320 | tf_op jit(solution)/shard_map/all_to_all | solution.py:255
  26.2 0.0 collective-permute-start
  26.2 2.3 %beam_own.1 = (bf16[256,1024]{1,0:T(8,128)(2,1)S(1)}, bf16[2,512,1024]{2,1,0:T(8,128)(2,1)S(1)}) custom-call(bf16[2,512,1024]{2,1,0:T(8,128)(2,1)S(1)} %get-tuple-element.17.upper, bf16[2,512,1024]{2,1,0:T(8,128)(2,1)} %get-tuple-element.18.lower_ref, bf16[8,8,2,16,128]{4,3,2,1,0:T(8,128)(2,1)S(1)} %bitcast.5), custom_call_target="tpu_custom_call" | custom-call | flops 2147483648 | bytes 4194304 | tf_op jit(solution)/shard_map/beam_own/pallas_call | solution.py:288
  28.5 0.0 collective-permute-done
  28.5 1.9 %beam_other.1 = (bf16[512,1024]{1,0:T(8,128)(2,1)S(1)}, f32[128,256]{1,0:T(8,128)S(1)}, f32[128,256]{1,0:T(8,128)S(1)}) custom-call(bf16[2,512,1024]{2,1,0:T(8,128)(2,1)S(1)} %get-tuple-element.17.upper, bf16[2,512,1024]{2,1,0:T(8,128)(2,1)S(1)} %get-tuple-element.20.lower, bf16[8,8,2,16,128]{4,3,2,1,0:T(8,128)(2,1)S(1)} %bitcast.6, ...), custom_call_target="tpu_custom_call" | custom-call | flops 2147483648 | bytes 4194304 | tf_op jit(solution)/shard_map/beam_other/pallas_call | solution.py:302
  30.4 0.6 collective-permute-start.1
  31.0 1.0 %collective-permute-done.1 = f32[128,256]{1,0:T(8,128)S(1)} collective-permute-done((f32[128,256]{1,0:T(8,128)S(1)}, f32[128,256]{1,0:T(8,128)S(1)}, u32[]{:S(2)}, u32[]{:S(2)}) %collective-permute-start.1) | collective-permute-done | bytes 131104 | tf_op jit(solution)/shard_map/ppermute | solution.py:240
  32.0 1.7 %collective-permute-start.4 = (f32[128,256]{1,0:T(8,128)S(1)}, f32[128,256]{1,0:T(8,128)S(1)}, u32[]{:S(2)}, u32[]{:S(2)}) collective-permute-start(f32[128,256]{1,0:T(8,128)S(1)} %add.15), channel_id=1, source_target_pairs={{0,32},{16,48},{32,0},{48,16},{64,96},{80,112},{96,64},{112,80},{1... | collective-permute-start | bytes 393224 | tf_op jit(solution)/shard_map/ppermute | solution.py:243
  33.8 1.4 %collective-permute-start.3 = (f32[128,256]{1,0:T(8,128)S(1)}, f32[128,256]{1,0:T(8,128)S(1)}, u32[]{:S(2)}, u32[]{:S(2)}) collective-permute-start(f32[128,256]{1,0:T(8,128)S(1)} %add.15), channel_id=1, source_target_pairs={{0,48},{16,32},{32,16},{48,0},{64,112},{80,96},{96,80},{112,64},{1... | collective-permute-start | bytes 393224 | tf_op jit(solution)/shard_map/ppermute | solution.py:243
  35.2 0.5 collective-permute-start.2
  35.6 4.3 %collective-permute-done.4 = f32[128,256]{1,0:T(8,128)S(1)} collective-permute-done((f32[128,256]{1,0:T(8,128)S(1)}, f32[128,256]{1,0:T(8,128)S(1)}, u32[]{:S(2)}, u32[]{:S(2)}) %collective-permute-start.4) | collective-permute-done | bytes 131104 | tf_op jit(solution)/shard_map/ppermute | solution.py:243
  40.0 2.2 %collective-permute-done.3 = f32[128,256]{1,0:T(8,128)S(1)} collective-permute-done((f32[128,256]{1,0:T(8,128)S(1)}, f32[128,256]{1,0:T(8,128)S(1)}, u32[]{:S(2)}, u32[]{:S(2)}) %collective-permute-start.3) | collective-permute-done | bytes 131104 | tf_op jit(solution)/shard_map/ppermute | solution.py:243
  42.2 0.0 collective-permute-done.2
  42.2 1.7 %collective-permute-start.5 = (f32[128,256]{1,0:T(8,128)S(1)}, f32[128,256]{1,0:T(8,128)S(1)}, u32[]{:S(2)}, u32[]{:S(2)}) collective-permute-start(f32[128,256]{1,0:T(8,128)S(1)} %add_add_fusion), channel_id=1, source_target_pairs={{0,64},{16,80},{32,96},{48,112},{64,0},{80,16},{96,32},{112,48},{1... | collective-permute-start | bytes 393224 | tf_op jit(solution)/shard_map/ppermute | solution.py:243
  43.9 5.3 %collective-permute-done.5 = f32[128,256]{1,0:T(8,128)S(1)} collective-permute-done((f32[128,256]{1,0:T(8,128)S(1)}, f32[128,256]{1,0:T(8,128)S(1)}, u32[]{:S(2)}, u32[]{:S(2)}) %collective-permute-start.5) | collective-permute-done | bytes 131104 | tf_op jit(solution)/shard_map/ppermute | solution.py:243
  49.3 0.1 collective-permute-start.6
  49.4 1.3 %collective-permute-done.6.other = f32[128,256]{1,0:T(8,128)S(1)} collective-permute-done((f32[128,256]{1,0:T(8,128)S(1)}, f32[128,256]{1,0:T(8,128)S(1)}, u32[]{:S(2)}, u32[]{:S(2)}) %collective-permute-start.6) | collective-permute-done | bytes 131104 | tf_op jit(solution)/shard_map/ppermute | solution.py:240
  50.7 2.1 %filter.1 = bf16[16,2,16,1024]{3,2,1,0:T(8,128)(2,1)S(1)} custom-call(f32[128,256]{1,0:T(8,128)S(1)} %add.19.own, f32[128,256]{1,0:T(8,128)S(1)} %collective-permute-done.6.other, bf16[512,1024]{1,0:T(8,128)(2,1)S(1)} %get-tuple-element.24.y_ref), custom_call_target="tpu_custom_call" | custom-call | tf_op jit(solution)/shard_map/filter/pallas_call | solution.py:319
  52.8 19.3 %all_to_all.10 = bf16[16,2,16,1024]{3,2,1,0:T(8,128)(2,1)S(1)} all-to-all(bf16[16,2,16,1024]{3,2,1,0:T(8,128)(2,1)S(1)} %filter.1), channel_id=1, replica_groups=mesh['chan'=8,'bin'=8,'core'=2] {'bin','core'}, dimensions={0} | all-to-all | bytes 2097152 | tf_op jit(solution)/shard_map/all_to_all | solution.py:329
  72.1 1.4 %place.1 = bf16[16,2,8,2048]{3,2,1,0:T(8,128)(2,1)} custom-call(bf16[8,2,2,16,1024]{4,3,2,1,0:T(8,128)(2,1)S(1)} %bitcast.4), custom_call_target="tpu_custom_call" | custom-call | tf_op jit(solution)/shard_map/place/pallas_call | solution.py:331
  (3 shorter events, 0.1 us)
Async XLA Ops:
  1.7 24.5 %all-to-all-start = ((bf16[64,2,16,128]{3,2,1,0:T(8,128)(2,1)}), bf16[64,2,16,128]{3,2,1,0:T(8,128)(2,1)S(1)}, u32[]{:S(2)}, u32[]{:S(2)}) async-start(bf16[64,2,16,128]{3,2,1,0:T(8,128)(2,1)} %bitcast), calls=%async_computation | async-start | bytes 1048576 | tf_op jit(solution)/shard_map/all_to_all | solution.py:255
  26.2 2.3 %collective-permute-start = (bf16[64,2,16,128]{3,2,1,0:T(8,128)(2,1)S(1)}, bf16[64,2,16,128]{3,2,1,0:T(8,128)(2,1)S(1)}, u32[]{:S(2)}, u32[]{:S(2)}) collective-permute-start(bf16[64,2,16,128]{3,2,1,0:T(8,128)(2,1)S(1)} %all-to-all-done), channel_id=1, source_target_pairs={{0,1},{1,0},{2,3},{3,2},{4,5},{5,4},{6,7},{7,6},{8,9},{9,8},{10,11... | collective-permute-start | bytes 1572872 | tf_op jit(solution)/shard_map/ppermute | solution.py:240
  30.4 1.6 %collective-permute-start.1 = (f32[128,256]{1,0:T(8,128)S(1)}, f32[128,256]{1,0:T(8,128)S(1)}, u32[]{:S(2)}, u32[]{:S(2)}) collective-permute-start(f32[128,256]{1,0:T(8,128)S(1)} %get-tuple-element.23), channel_id=1, source_target_pairs={{0,1},{1,0},{2,3},{3,2},{4,5},{5,4},{6,7},{7,6},{8,9},{9,8},{10,11... | collective-permute-start | bytes 393224 | tf_op jit(solution)/shard_map/ppermute | solution.py:240
  32.0 7.9 %collective-permute-start.4 = (f32[128,256]{1,0:T(8,128)S(1)}, f32[128,256]{1,0:T(8,128)S(1)}, u32[]{:S(2)}, u32[]{:S(2)}) collective-permute-start(f32[128,256]{1,0:T(8,128)S(1)} %add.15), channel_id=1, source_target_pairs={{0,32},{16,48},{32,0},{48,16},{64,96},{80,112},{96,64},{112,80},{1... | collective-permute-start | bytes 393224 | tf_op jit(solution)/shard_map/ppermute | solution.py:243
  33.8 8.4 %collective-permute-start.3 = (f32[128,256]{1,0:T(8,128)S(1)}, f32[128,256]{1,0:T(8,128)S(1)}, u32[]{:S(2)}, u32[]{:S(2)}) collective-permute-start(f32[128,256]{1,0:T(8,128)S(1)} %add.15), channel_id=1, source_target_pairs={{0,48},{16,32},{32,16},{48,0},{64,112},{80,96},{96,80},{112,64},{1... | collective-permute-start | bytes 393224 | tf_op jit(solution)/shard_map/ppermute | solution.py:243
  35.2 7.0 %collective-permute-start.2 = (f32[128,256]{1,0:T(8,128)S(1)}, f32[128,256]{1,0:T(8,128)S(1)}, u32[]{:S(2)}, u32[]{:S(2)}) collective-permute-start(f32[128,256]{1,0:T(8,128)S(1)} %add.15), channel_id=1, source_target_pairs={{0,16},{16,0},{32,48},{48,32},{64,80},{80,64},{96,112},{112,96},{1... | collective-permute-start | bytes 393224 | tf_op jit(solution)/shard_map/ppermute | solution.py:243
  42.2 7.0 %collective-permute-start.5 = (f32[128,256]{1,0:T(8,128)S(1)}, f32[128,256]{1,0:T(8,128)S(1)}, u32[]{:S(2)}, u32[]{:S(2)}) collective-permute-start(f32[128,256]{1,0:T(8,128)S(1)} %add_add_fusion), channel_id=1, source_target_pairs={{0,64},{16,80},{32,96},{48,112},{64,0},{80,16},{96,32},{112,48},{1... | collective-permute-start | bytes 393224 | tf_op jit(solution)/shard_map/ppermute | solution.py:243
  49.3 1.4 %collective-permute-start.6 = (f32[128,256]{1,0:T(8,128)S(1)}, f32[128,256]{1,0:T(8,128)S(1)}, u32[]{:S(2)}, u32[]{:S(2)}) collective-permute-start(f32[128,256]{1,0:T(8,128)S(1)} %add.19.own), channel_id=1, source_target_pairs={{0,1},{1,0},{2,3},{3,2},{4,5},{5,4},{6,7},{7,6},{8,9},{9,8},{10,11... | collective-permute-start | bytes 393224 | tf_op jit(solution)/shard_map/ppermute | solution.py:240

commit v7 on v6

--- a/solution.py
+++ b/solution.py
@@ -35,14 +35,21 @@
     return high, value - unit * high
 
 
-def spread_kernel(rf_ref, out_ref, held, sem):
-    copy = pltpu.make_async_copy(rf_ref, held, sem)
+def spread_kernel(rf_ref, out_ref, held, sems):
+    parts, bins = held.shape[:2]
+    chans = out_ref.shape[0] // bins
+    copy = pltpu.make_async_copy(rf_ref, held, sems.at[chans * parts])
     copy.start()
     copy.wait()
-    for part in range(held.shape[0]):
-        block = held[part]
-        for k in range(out_ref.shape[0]):
-            out_ref[k, :, part] = block
+    copies = [
+        pltpu.make_async_copy(held.at[part], out_ref.at[k * bins : (k + 1) * bins, part], sems.at[k * parts + part])
+        for k in range(chans)
+        for part in range(parts)
+    ]
+    for copy in copies:
+        copy.start()
+    for copy in copies:
+        copy.wait()
 
 
 def operator_kernel(elem_ref, vox_ref, bins_ref, upper, lower_ref, elem, vox, bins, lhs_ref, lower, sems):
@@ -245,13 +252,12 @@
     by_bin = pl.pallas_call(
         spread_kernel,
         name="spread",
-        out_shape=shape(chans, bins, parts, group, width),
+        out_shape=shape(chans * bins, parts, group, width),
         in_specs=[HBM],
-        out_specs=VMEM,
-        scratch_shapes=[pltpu.VMEM(rf_data.shape, BF16), pltpu.SemaphoreType.DMA],
+        out_specs=HBM,
+        scratch_shapes=[pltpu.VMEM(rf_data.shape, BF16), pltpu.SemaphoreType.DMA((chans * parts + 1,))],
         compiler_params=WIDE,
     )(pltpu.with_memory_space_constraint(rf_data, pltpu.HBM))
-    by_bin = by_bin.reshape(chans * bins, parts, group, width)
     own = lax.all_to_all(by_bin, ("chan", "bin"), split_axis=0, concat_axis=0, tiled=True)
 
     share = channels // 2
@@ -311,9 +317,9 @@
     )(upper, lower, other, mine)
 
     total = keep + swap(send)
-    near, far, next_to = across(total, 1), across(total, 3), across(total, 2)
-    total = total + near + far + next_to
-    total = total + across(total, 4)
+    narrow = total.astype(BF16)
+    total = total + sum(across(narrow, bits).astype(F32) for bits in (1, 3, 2))
+    total = total + across(total.astype(BF16), 4).astype(F32)
     rest = swap(total)
 
     applied = pl.pallas_call(

time: 74 us -> 70.4 us (0.951)
  waiting for transfers between devices: 20.9 us -> 16.7 us
    ppermute x4, waiting for transfers between devices: 11.9 us -> 7.69 us  [across(): return lax.ppermute(x, 'chan', [(a, a ^ bits) for a in range(chans)])]
where the time goes in v7:
time: 70.4 us; the launch traced here: 69.9 us
  blocking collectives  19.6 us (28%)
  starting transfers between devices  17.7 us (25%)
  waiting for transfers between devices  16.7 us (24%)
  Pallas kernels  15.8 us (22%)
    all_to_all x1, blocking collectives, shards(): lax.all_to_all(applied, ('bin', 'core'), split_axis=0, concat_axis=0, til...  19.6 us
    all_to_all x1, starting transfers between devices, shards(): lax.all_to_all(by_bin, ('chan', 'bin'), split_axis=0, concat_axis=0, tile...  11.5 us
    ppermute x4, waiting for transfers between devices, across(): return lax.ppermute(x, 'chan', [(a, a ^ bits) for a in range(chans)])  7.69 us
    all_to_all x1, waiting for transfers between devices, shards(): lax.all_to_all(by_bin, ('chan', 'bin'), split_axis=0, concat_axis=0, tile...  6.67 us
    pallas_call x1, Pallas kernels, shards(): pl.pallas_call(operator_kernel, name='operator', out_shape=(shape(2, shar...  6.26 us
    ppermute x4, starting transfers between devices, across(): return lax.ppermute(x, 'chan', [(a, a ^ bits) for a in range(chans)])  5.53 us
    ppermute x3, waiting for transfers between devices, swap(): return lax.ppermute(x, 'core', [(0, 1), (1, 0)])  2.32 us
    pallas_call x1, Pallas kernels, shards(): pl.pallas_call(own_kernel, name='beam_own', out_shape=(shape(frames, voxe...  2.31 us
  transfers between devices with their start and end apart: 8, of which 6 were waited for; matrix products, arithmetic and copies ran while one was open for 0% of the time, Pallas kernels for 12%

profile of v7, /device:TPU:0, one launch (start us, length us, event | category | flops | bytes accessed | tf_op | source)
XLA Modules:
  0.0 69.9 jit_solution(3087855175655671133)
XLA Ops:
  0.0 1.8 %spread.1 = bf16[64,2,16,128]{3,2,1,0:T(8,128)(2,1)} custom-call(bf16[2,8,16,128]{3,2,1,0:T(8,128)(2,1)} %rf_ref.1), custom_call_target="tpu_custom_call" | custom-call | tf_op jit(solution)/shard_map/spread/pallas_call | solution.py:252
  1.8 11.5 %all-to-all-start = ((bf16[64,2,16,128]{3,2,1,0:T(8,128)(2,1)}), bf16[64,2,16,128]{3,2,1,0:T(8,128)(2,1)S(1)}, u32[]{:S(2)}, u32[]{:S(2)}) async-start(bf16[64,2,16,128]{3,2,1,0:T(8,128)(2,1)} %spread.1), calls=%async_computation | async-start | bytes 1048576 | tf_op jit(solution)/shard_map/all_to_all | solution.py:261
  13.3 6.3 %operator.1 = (bf16[2,512,1024]{2,1,0:T(8,128)(2,1)S(1)}, bf16[2,512,1024]{2,1,0:T(8,128)(2,1)}) custom-call(s32[3,1024]{1,0:T(4,128)} %elem_ref.1, s32[3,2048]{1,0:T(4,128)} %vox_ref.1, s32[8]{0:T(128)} %bins_ref.1), custom_call_target="tpu_custom_call" | custom-call | flops 62914560 | bytes 4194304 | tf_op jit(solution)/shard_map/operator/pallas_call | solution.py:264
  19.6 6.7 %all-to-all-done = bf16[64,2,16,128]{3,2,1,0:T(8,128)(2,1)S(1)} async-done(((bf16[64,2,16,128]{3,2,1,0:T(8,128)(2,1)}), bf16[64,2,16,128]{3,2,1,0:T(8,128)(2,1)S(1)}, u32[]{:S(2)}, u32[]{:S(2)}) %all-to-all-start) | async-done | bytes 524320 | tf_op jit(solution)/shard_map/all_to_all | solution.py:261
  26.2 0.0 collective-permute-start
  26.2 2.3 %beam_own.1 = (bf16[256,1024]{1,0:T(8,128)(2,1)S(1)}, bf16[2,512,1024]{2,1,0:T(8,128)(2,1)S(1)}) custom-call(bf16[2,512,1024]{2,1,0:T(8,128)(2,1)S(1)} %get-tuple-element.17.upper, bf16[2,512,1024]{2,1,0:T(8,128)(2,1)} %get-tuple-element.18.lower_ref, bf16[8,8,2,16,128]{4,3,2,1,0:T(8,128)(2,1)S(1)} %bitcast.4), custom_call_target="tpu_custom_call" | custom-call | flops 2147483648 | bytes 4194304 | tf_op jit(solution)/shard_map/beam_own/pallas_call | solution.py:294
  28.5 0.0 collective-permute-done
  28.6 1.9 %beam_other.1 = (bf16[512,1024]{1,0:T(8,128)(2,1)S(1)}, f32[128,256]{1,0:T(8,128)S(1)}, f32[128,256]{1,0:T(8,128)S(1)}) custom-call(bf16[2,512,1024]{2,1,0:T(8,128)(2,1)S(1)} %get-tuple-element.17.upper, bf16[2,512,1024]{2,1,0:T(8,128)(2,1)S(1)} %get-tuple-element.20.lower, bf16[8,8,2,16,128]{4,3,2,1,0:T(8,128)(2,1)S(1)} %bitcast.5, ...), custom_call_target="tpu_custom_call" | custom-call | flops 2147483648 | bytes 4194304 | tf_op jit(solution)/shard_map/beam_other/pallas_call | solution.py:308
  30.5 0.6 collective-permute-start.1
  31.1 1.0 %collective-permute-done.1 = f32[128,256]{1,0:T(8,128)S(1)} collective-permute-done((f32[128,256]{1,0:T(8,128)S(1)}, f32[128,256]{1,0:T(8,128)S(1)}, u32[]{:S(2)}, u32[]{:S(2)}) %collective-permute-start.1) | collective-permute-done | bytes 131104 | tf_op jit(solution)/shard_map/ppermute | solution.py:247
  32.1 1.7 %collective-permute-start.4 = (bf16[128,256]{1,0:T(8,128)(2,1)S(1)}, bf16[128,256]{1,0:T(8,128)(2,1)S(1)}, u32[]{:S(2)}, u32[]{:S(2)}) collective-permute-start(bf16[128,256]{1,0:T(8,128)(2,1)S(1)} %get-tuple-element.25), channel_id=1, source_target_pairs={{0,32},{16,48},{32,0},{48,16},{64,96},{80,112},{96,64},{112,80},{1... | collective-permute-start | bytes 196616 | tf_op jit(solution)/shard_map/ppermute | solution.py:250
  33.8 1.4 %collective-permute-start.3 = (bf16[128,256]{1,0:T(8,128)(2,1)S(1)}, bf16[128,256]{1,0:T(8,128)(2,1)S(1)}, u32[]{:S(2)}, u32[]{:S(2)}) collective-permute-start(bf16[128,256]{1,0:T(8,128)(2,1)S(1)} %get-tuple-element.25), channel_id=1, source_target_pairs={{0,48},{16,32},{32,16},{48,0},{64,112},{80,96},{96,80},{112,64},{1... | collective-permute-start | bytes 196616 | tf_op jit(solution)/shard_map/ppermute | solution.py:250
  35.2 0.5 collective-permute-start.2
  35.7 2.4 %collective-permute-done.4 = bf16[128,256]{1,0:T(8,128)(2,1)S(1)} collective-permute-done((bf16[128,256]{1,0:T(8,128)(2,1)S(1)}, bf16[128,256]{1,0:T(8,128)(2,1)S(1)}, u32[]{:S(2)}, u32[]{:S(2)}) %collective-permute-start.4) | collective-permute-done | bytes 65568 | tf_op jit(solution)/shard_map/ppermute | solution.py:250
  38.1 1.4 %collective-permute-done.3 = bf16[128,256]{1,0:T(8,128)(2,1)S(1)} collective-permute-done((bf16[128,256]{1,0:T(8,128)(2,1)S(1)}, bf16[128,256]{1,0:T(8,128)(2,1)S(1)}, u32[]{:S(2)}, u32[]{:S(2)}) %collective-permute-start.3) | collective-permute-done | bytes 65568 | tf_op jit(solution)/shard_map/ppermute | solution.py:250
  39.4 0.0 collective-permute-done.2
  39.5 1.9 %collective-permute-start.5 = (bf16[128,256]{1,0:T(8,128)(2,1)S(1)}, bf16[128,256]{1,0:T(8,128)(2,1)S(1)}, u32[]{:S(2)}, u32[]{:S(2)}) collective-permute-start(bf16[128,256]{1,0:T(8,128)(2,1)S(1)} %fusion), channel_id=1, source_target_pairs={{0,64},{16,80},{32,96},{48,112},{64,0},{80,16},{96,32},{112,48},{1... | collective-permute-start | bytes 196616 | tf_op jit(solution)/shard_map/ppermute | solution.py:250
  41.5 3.9 %collective-permute-done.5 = bf16[128,256]{1,0:T(8,128)(2,1)S(1)} collective-permute-done((bf16[128,256]{1,0:T(8,128)(2,1)S(1)}, bf16[128,256]{1,0:T(8,128)(2,1)S(1)}, u32[]{:S(2)}, u32[]{:S(2)}) %collective-permute-start.5) | collective-permute-done | bytes 65568 | tf_op jit(solution)/shard_map/ppermute | solution.py:250
  45.4 0.1 collective-permute-start.6
  45.5 1.3 %collective-permute-done.6.other = f32[128,256]{1,0:T(8,128)S(1)} collective-permute-done((f32[128,256]{1,0:T(8,128)S(1)}, f32[128,256]{1,0:T(8,128)S(1)}, u32[]{:S(2)}, u32[]{:S(2)}) %collective-permute-start.6) | collective-permute-done | bytes 131104 | tf_op jit(solution)/shard_map/ppermute | solution.py:247
  46.8 2.1 %filter.1 = bf16[16,2,16,1024]{3,2,1,0:T(8,128)(2,1)S(1)} custom-call(f32[128,256]{1,0:T(8,128)S(1)} %convert_add_fusion.own, f32[128,256]{1,0:T(8,128)S(1)} %collective-permute-done.6.other, bf16[512,1024]{1,0:T(8,128)(2,1)S(1)} %get-tuple-element.24.y_ref), custom_call_target="tpu_custom_call" | custom-call | tf_op jit(solution)/shard_map/filter/pallas_call | solution.py:325
  48.9 19.6 %all_to_all.10 = bf16[16,2,16,1024]{3,2,1,0:T(8,128)(2,1)S(1)} all-to-all(bf16[16,2,16,1024]{3,2,1,0:T(8,128)(2,1)S(1)} %filter.1), channel_id=1, replica_groups=mesh['chan'=8,'bin'=8,'core'=2] {'bin','core'}, dimensions={0} | all-to-all | bytes 2097152 | tf_op jit(solution)/shard_map/all_to_all | solution.py:335
  68.5 1.4 %place.1 = bf16[16,2,8,2048]{3,2,1,0:T(8,128)(2,1)} custom-call(bf16[8,2,2,16,1024]{4,3,2,1,0:T(8,128)(2,1)S(1)} %bitcast.3), custom_call_target="tpu_custom_call" | custom-call | tf_op jit(solution)/shard_map/place/pallas_call | solution.py:337
  (3 shorter events, 0.1 us)
Async XLA Ops:
  1.8 24.5 %all-to-all-start = ((bf16[64,2,16,128]{3,2,1,0:T(8,128)(2,1)}), bf16[64,2,16,128]{3,2,1,0:T(8,128)(2,1)S(1)}, u32[]{:S(2)}, u32[]{:S(2)}) async-start(bf16[64,2,16,128]{3,2,1,0:T(8,128)(2,1)} %spread.1), calls=%async_computation | async-start | bytes 1048576 | tf_op jit(solution)/shard_map/all_to_all | solution.py:261
  26.2 2.3 %collective-permute-start = (bf16[64,2,16,128]{3,2,1,0:T(8,128)(2,1)S(1)}, bf16[64,2,16,128]{3,2,1,0:T(8,128)(2,1)S(1)}, u32[]{:S(2)}, u32[]{:S(2)}) collective-permute-start(bf16[64,2,16,128]{3,2,1,0:T(8,128)(2,1)S(1)} %all-to-all-done), channel_id=1, source_target_pairs={{0,1},{1,0},{2,3},{3,2},{4,5},{5,4},{6,7},{7,6},{8,9},{9,8},{10,11... | collective-permute-start | bytes 1572872 | tf_op jit(solution)/shard_map/ppermute | solution.py:247
  30.5 1.6 %collective-permute-start.1 = (f32[128,256]{1,0:T(8,128)S(1)}, f32[128,256]{1,0:T(8,128)S(1)}, u32[]{:S(2)}, u32[]{:S(2)}) collective-permute-start(f32[128,256]{1,0:T(8,128)S(1)} %get-tuple-element.23), channel_id=1, source_target_pairs={{0,1},{1,0},{2,3},{3,2},{4,5},{5,4},{6,7},{7,6},{8,9},{9,8},{10,11... | collective-permute-start | bytes 393224 | tf_op jit(solution)/shard_map/ppermute | solution.py:247
  32.1 6.0 %collective-permute-start.4 = (bf16[128,256]{1,0:T(8,128)(2,1)S(1)}, bf16[128,256]{1,0:T(8,128)(2,1)S(1)}, u32[]{:S(2)}, u32[]{:S(2)}) collective-permute-start(bf16[128,256]{1,0:T(8,128)(2,1)S(1)} %get-tuple-element.25), channel_id=1, source_target_pairs={{0,32},{16,48},{32,0},{48,16},{64,96},{80,112},{96,64},{112,80},{1... | collective-permute-start | bytes 196616 | tf_op jit(solution)/shard_map/ppermute | solution.py:250
  33.8 5.6 %collective-permute-start.3 = (bf16[128,256]{1,0:T(8,128)(2,1)S(1)}, bf16[128,256]{1,0:T(8,128)(2,1)S(1)}, u32[]{:S(2)}, u32[]{:S(2)}) collective-permute-start(bf16[128,256]{1,0:T(8,128)(2,1)S(1)} %get-tuple-element.25), channel_id=1, source_target_pairs={{0,48},{16,32},{32,16},{48,0},{64,112},{80,96},{96,80},{112,64},{1... | collective-permute-start | bytes 196616 | tf_op jit(solution)/shard_map/ppermute | solution.py:250
  35.2 4.3 %collective-permute-start.2 = (bf16[128,256]{1,0:T(8,128)(2,1)S(1)}, bf16[128,256]{1,0:T(8,128)(2,1)S(1)}, u32[]{:S(2)}, u32[]{:S(2)}) collective-permute-start(bf16[128,256]{1,0:T(8,128)(2,1)S(1)} %get-tuple-element.25), channel_id=1, source_target_pairs={{0,16},{16,0},{32,48},{48,32},{64,80},{80,64},{96,112},{112,96},{1... | collective-permute-start | bytes 196616 | tf_op jit(solution)/shard_map/ppermute | solution.py:250
  39.5 5.8 %collective-permute-start.5 = (bf16[128,256]{1,0:T(8,128)(2,1)S(1)}, bf16[128,256]{1,0:T(8,128)(2,1)S(1)}, u32[]{:S(2)}, u32[]{:S(2)}) collective-permute-start(bf16[128,256]{1,0:T(8,128)(2,1)S(1)} %fusion), channel_id=1, source_target_pairs={{0,64},{16,80},{32,96},{48,112},{64,0},{80,16},{96,32},{112,48},{1... | collective-permute-start | bytes 196616 | tf_op jit(solution)/shard_map/ppermute | solution.py:250
  45.4 1.4 %collective-permute-start.6 = (f32[128,256]{1,0:T(8,128)S(1)}, f32[128,256]{1,0:T(8,128)S(1)}, u32[]{:S(2)}, u32[]{:S(2)}) collective-permute-start(f32[128,256]{1,0:T(8,128)S(1)} %convert_add_fusion.own), channel_id=1, source_target_pairs={{0,1},{1,0},{2,3},{3,2},{4,5},{5,4},{6,7},{7,6},{8,9},{9,8},{10,11... | collective-permute-start | bytes 393224 | tf_op jit(solution)/shard_map/ppermute | solution.py:247

commit v8 on v7

--- a/solution.py
+++ b/solution.py
@@ -16,7 +16,7 @@
 SIN = (3.1415925800446924, -5.167706878924515, 2.5500313772531213, -0.5980451739748806, 0.0772201286897368)
 COS = (0.9999999534666272, -4.934792858670076, 4.058411914063177, -1.331880160583308, 0.21969679727234584)
 ROUNDER = 12582912.0
-ROWS = 256
+ROWS = 512
 LANES = 256
 WIDE = pltpu.CompilerParams(vmem_limit_bytes=16 * 1024 * 1024)
 VMEM = pl.BlockSpec(memory_space=pltpu.VMEM)
@@ -54,8 +54,9 @@
 
 def operator_kernel(elem_ref, vox_ref, bins_ref, upper, lower_ref, elem, vox, bins, lhs_ref, lower, sems):
     core = lax.axis_index("core")
-    voxels = upper.shape[2]
     channels = elem.shape[1]
+    share = upper.shape[2]
+    voxels = share + lower.shape[2]
     copies = [
         pltpu.make_async_copy(source, target, sems.at[n])
         for n, (source, target) in enumerate(((elem_ref, elem), (vox_ref, vox), (bins_ref, bins)))
@@ -80,13 +81,13 @@
     squares = jnp.concatenate([-2.0 * voxel, 16.0 * one, one, 64.0 * high, low, zero], axis=0).astype(BF16)
     depths = jnp.concatenate([zero, zero, -1.0 * one, zero, zero, level, zero, zero], axis=0).astype(BF16)
 
-    def tile(index, carry, out_ref, start):
+    def tile(index, carry, out_ref, lanes):
         rows = pl.ds(pl.multiple_of(index * ROWS, ROWS), ROWS)
-        left = lhs_ref[pl.ds(pl.multiple_of(start + index * ROWS, ROWS), ROWS)]
-        squared = jnp.dot(left, squares, preferred_element_type=F32)
-        depth = jnp.dot(left, depths, preferred_element_type=F32)
+        left = lhs_ref[rows]
+        squared = jnp.dot(left, squares[:, lanes], preferred_element_type=F32)
+        depth = jnp.dot(left, depths[:, lanes], preferred_element_type=F32)
         inverse = lax.rsqrt(squared)
-        turns = (level + squared * inverse) * wavenumber
+        turns = (level[:, lanes] + squared * inverse) * wavenumber
         part = turns - ((turns + ROUNDER) - ROUNDER)
         z = part * part
         sine = part * horner(SIN, z)
@@ -97,11 +98,10 @@
         out_ref[1, rows] = (lean * cosine).astype(BF16)
         return carry
 
-    share = upper.shape[1]
-    lax.fori_loop(0, (channels - share) // ROWS, functools.partial(tile, out_ref=lower, start=share), 0)
+    lax.fori_loop(0, channels // ROWS, functools.partial(tile, out_ref=lower, lanes=slice(share, voxels)), 0)
     copy = pltpu.make_async_copy(lower, lower_ref, sems.at[3])
     copy.start()
-    lax.fori_loop(0, share // ROWS, functools.partial(tile, out_ref=upper, start=0), 0)
+    lax.fori_loop(0, channels // ROWS, functools.partial(tile, out_ref=upper, lanes=slice(0, share)), 0)
     copy.wait()
 
 
@@ -113,32 +113,27 @@
             data[part * half : (part + 1) * half, k * width : (k + 1) * width] = samples[k, :, part].reshape(half, width)
 
 
-def applied(data, operator, lanes):
-    return [jnp.dot(data, operator[which, :, lanes], preferred_element_type=F32) for which in range(2)]
-
-
-def joined(first, second):
-    half = first.shape[0] // 2
-    return (first[:half] + second[half:]).astype(BF16), (first[half:] - second[:half]).astype(BF16)
-
-
-def own_kernel(upper, lower_ref, samples, out_ref, lower, data, partial, sem):
+def beamform(data, operator, start):
+    half = data.shape[0] // 2
+    for n in range(0, operator.shape[2], LANES):
+        first, second = (
+            jnp.dot(data[...], operator[which, :, n : n + LANES], preferred_element_type=F32) for which in range(2)
+        )
+        real = (first[:half] + second[half:]).astype(BF16)
+        imag = (first[half:] - second[:half]).astype(BF16)
+        yield slice(start + n, start + n + LANES), real, imag
+
+
+def own_kernel(upper, lower_ref, samples, out_ref, lower, data, sem):
     copy = pltpu.make_async_copy(lower_ref, lower, sem)
     copy.start()
     arrange(samples, data)
     half = out_ref.shape[0] // 2
-    share = upper.shape[1]
-    blocks = [slice(n, n + LANES) for n in range(0, upper.shape[2], LANES)]
-    for lanes in blocks:
-        first, second = applied(data[:, :share], upper, lanes)
-        partial[0, :, lanes] = first
-        partial[1, :, lanes] = second
+    for lanes, real, imag in beamform(data, upper, 0):
+        out_ref[:half, lanes], out_ref[half:, lanes] = real, imag
     copy.wait()
-    for lanes in blocks:
-        first, second = applied(data[:, share:], lower, lanes)
-        out_ref[:half, lanes], out_ref[half:, lanes] = joined(
-            partial[0, :, lanes] + first, partial[1, :, lanes] + second
-        )
+    for lanes, real, imag in beamform(data, lower, upper.shape[2]):
+        out_ref[:half, lanes], out_ref[half:, lanes] = real, imag
 
 
 def other_kernel(upper, lower, samples, own, y_ref, keep_ref, send_ref, data, gram):
@@ -150,14 +145,9 @@
     y_ref[pl.ds(here, half)] = own[:half]
     y_ref[pl.ds(frames + here, half)] = own[half:]
     arrange(samples, data)
-    share = upper.shape[1]
-    for n in range(0, upper.shape[2], LANES):
-        lanes = slice(n, n + LANES)
-        first, second = applied(data[:, :share], upper, lanes)
-        more, further = applied(data[:, share:], lower, lanes)
-        y_ref[pl.ds(there, half), lanes], y_ref[pl.ds(frames + there, half), lanes] = joined(
-            first + more, second + further
-        )
+    for operator, start in ((upper, 0), (lower, upper.shape[2])):
+        for lanes, real, imag in beamform(data, operator, start):
+            y_ref[pl.ds(there, half), lanes], y_ref[pl.ds(frames + there, half), lanes] = real, imag
     y = y_ref[...]
     products = lax.dot_general(y, y, (((1,), (1,)), ((), ())), preferred_element_type=F32)
     gram[...] = (products[:frames, :frames] + products[frames:, frames:]) + (
@@ -187,7 +177,7 @@
     return 0.5 * (packed + flipped), 0.5 * (packed - flipped), flipped
 
 
-def filter_kernel(own, other, y_ref, out_ref, gram):
+def filter_kernel(own, other, y_ref, peer_ref, out_ref, gram, kept):
     core = lax.axis_index("core")
     half, frames = own.shape
     gram[pl.ds(pl.multiple_of(core * half, half), half), :] = own[...]
@@ -204,32 +194,32 @@
     cols = lax.broadcasted_iota(jnp.int32, (frames, frames), 1)
     identity = jnp.where(rows == cols, 1.0, 0.0).astype(F32)
     real, imag, _ = unpack(identity - mat + 0.3 * second - 0.03 * third)
-    real, imag = real.astype(BF16), imag.astype(BF16)
+    kept[0] = real.astype(BF16)
+    kept[1] = imag.astype(BF16)
+    real, imag = (kept[part, pl.ds(pl.multiple_of(core * half, half), half)] for part in range(2))
     matrix = jnp.concatenate(
         [jnp.concatenate([real, imag], axis=1), jnp.concatenate([-imag, real], axis=1)], axis=0
     )
-    applied = jnp.dot(matrix, y_ref[...], preferred_element_type=F32).astype(BF16)
-    group = out_ref.shape[2]
-    bins = out_ref.shape[0] // CORES
-    for part in range(2):
-        for c in range(CORES):
+    bins, parts, group, _ = out_ref.shape
+    voxels = y_ref.shape[1]
+    for source, place in ((y_ref, core), (peer_ref, 1 - core)):
+        lanes = pl.ds(pl.multiple_of(place * voxels, voxels), voxels)
+        applied = jnp.dot(matrix, source[...], preferred_element_type=F32).astype(BF16)
+        for part in range(parts):
             for j in range(bins):
-                row = part * frames + c * half + j * group
-                out_ref[j * CORES + c, part] = applied[row : row + group]
+                row = part * half + j * group
+                out_ref[j, part, :, lanes] = applied[row : row + group]
 
 
 def place_kernel(got, out_ref):
-    group, _, bins, _ = out_ref.shape
-    voxels = got.shape[-1]
+    bins, parts, group, voxels = got.shape
     size = group * bins
     rows = lax.broadcasted_iota(jnp.int32, (size, size), 0)
     cols = lax.broadcasted_iota(jnp.int32, (size, size), 1)
     turn = jnp.where(cols == (rows % bins) * group + rows // bins, 1.0, 0.0).astype(BF16)
-    for c in range(CORES):
-        for part in range(2):
-            block = got[:, c, part].reshape(size, voxels)
-            moved = jnp.dot(turn, block, preferred_element_type=F32).astype(BF16)
-            out_ref[:, part, :, c * voxels : (c + 1) * voxels] = moved.reshape(group, bins, voxels)
+    for part in range(parts):
+        moved = jnp.dot(turn, got[:, part].reshape(size, voxels), preferred_element_type=F32).astype(BF16)
+        out_ref[:, part] = moved.reshape(group, bins, voxels)
 
 
 def shards(rf_data, elem_pos, vox_pos, subbands):
@@ -260,11 +250,11 @@
     )(pltpu.with_memory_space_constraint(rf_data, pltpu.HBM))
     own = lax.all_to_all(by_bin, ("chan", "bin"), split_axis=0, concat_axis=0, tiled=True)
 
-    share = channels // 2
+    share = voxels // 2
     upper, lower = pl.pallas_call(
         operator_kernel,
         name="operator",
-        out_shape=(shape(2, share, voxels), pltpu.HBM((2, channels - share, voxels), BF16)),
+        out_shape=(shape(2, channels, share), pltpu.HBM((2, channels, voxels - share), BF16)),
         in_specs=[HBM, HBM, HBM],
         out_specs=(VMEM, HBM),
         scratch_shapes=[
@@ -272,7 +262,7 @@
             pltpu.VMEM(vox_pos.shape, jnp.int32),
             pltpu.SMEM(subbands.shape, jnp.int32),
             pltpu.VMEM((channels, 8), BF16),
-            pltpu.VMEM((2, channels - share, voxels), BF16),
+            pltpu.VMEM((2, channels, voxels - share), BF16),
             pltpu.SemaphoreType.DMA((4,)),
         ],
         compiler_params=WIDE,
@@ -294,12 +284,11 @@
     mine, lower = pl.pallas_call(
         own_kernel,
         name="beam_own",
-        out_shape=(shape(frames, voxels), shape(2, channels - share, voxels)),
+        out_shape=(shape(frames, voxels), shape(2, channels, voxels - share)),
         in_specs=[VMEM, HBM, VMEM],
         out_specs=(VMEM, VMEM),
         scratch_shapes=[
             pltpu.VMEM((frames, channels), BF16),
-            pltpu.VMEM((2, frames, voxels), F32),
             pltpu.SemaphoreType.DMA,
         ],
         compiler_params=WIDE,
@@ -317,6 +306,8 @@
     )(upper, lower, other, mine)
 
     total = keep + swap(send)
+    total, y = lax.optimization_barrier((total, y))
+    peer = swap(y)
     narrow = total.astype(BF16)
     total = total + sum(across(narrow, bits).astype(F32) for bits in (1, 3, 2))
     total = total + across(total.astype(BF16), 4).astype(F32)
@@ -325,15 +316,14 @@
     applied = pl.pallas_call(
         filter_kernel,
         name="filter",
-        out_shape=shape(bins * CORES, parts, group, voxels),
-        in_specs=[VMEM, VMEM, VMEM],
+        out_shape=shape(bins, parts, group, CORES * voxels),
+        in_specs=[VMEM] * 4,
         out_specs=VMEM,
-        scratch_shapes=[pltpu.VMEM((frames, frames), F32)],
-        compiler_params=WIDE,
-    )(total, rest, y)
-
-    got = lax.all_to_all(applied, ("bin", "core"), split_axis=0, concat_axis=0, tiled=True)
-    got = got.reshape(bins, CORES, parts, group, voxels)
+        scratch_shapes=[pltpu.VMEM((frames, frames), F32), pltpu.VMEM((2, frames, frames), BF16)],
+        compiler_params=WIDE,
+    )(total, rest, y, peer)
+
+    got = lax.all_to_all(applied, "bin", split_axis=0, concat_axis=0, tiled=True)
     return pl.pallas_call(
         place_kernel,
         name="place",

time: 70.4 us -> 69.9 us (level)
  blocking collectives: 19.6 us -> 18.6 us
    all_to_all x1, blocking collectives: 19.6 us -> 18.6 us  [shards(): lax.all_to_all(applied, 'bin', split_axis=0, concat_axis=0, tiled=True)]
    ppermute x3 -> x4, waiting for transfers between devices: 2.32 us -> 2.33 us  [swap(): return lax.ppermute(x, 'core', [(0, 1), (1, 0)])]
  transfers between devices with their start and end apart: 8 -> 9, of which waited for: 6 -> 7; matrix products, arithmetic and copies ran while one was open for 0% -> 0% of each run, Pallas kernels for 12% -> 12%
where the time goes in v8:
time: 69.9 us; the launch traced here: 69.5 us
  blocking collectives  18.6 us (27%)
  starting transfers between devices  18.1 us (26%)
  waiting for transfers between devices  16.8 us (24%)
  Pallas kernels  15.8 us (23%)
    all_to_all x1, blocking collectives, shards(): lax.all_to_all(applied, 'bin', split_axis=0, concat_axis=0, tiled=True)  18.6 us
    all_to_all x1, starting transfers between devices, shards(): lax.all_to_all(by_bin, ('chan', 'bin'), split_axis=0, concat_axis=0, tile...  11.5 us
    ppermute x4, waiting for transfers between devices, across(): return lax.ppermute(x, 'chan', [(a, a ^ bits) for a in range(chans)])  7.71 us
    all_to_all x1, waiting for transfers between devices, shards(): lax.all_to_all(by_bin, ('chan', 'bin'), split_axis=0, concat_axis=0, tile...  6.71 us
    pallas_call x1, Pallas kernels, shards(): pl.pallas_call(operator_kernel, name='operator', out_shape=(shape(2, chan...  6.21 us
    ppermute x4, starting transfers between devices, across(): return lax.ppermute(x, 'chan', [(a, a ^ bits) for a in range(chans)])  5.51 us
    pallas_call x1, Pallas kernels, shards(): pl.pallas_call(own_kernel, name='beam_own', out_shape=(shape(frames, voxe...  2.41 us
    ppermute x4, waiting for transfers between devices, swap(): return lax.ppermute(x, 'core', [(0, 1), (1, 0)])  2.33 us
  transfers between devices with their start and end apart: 9, of which 7 were waited for; matrix products, arithmetic and copies ran while one was open for 0% of the time, Pallas kernels for 12%

profile of v8, /device:TPU:0, one launch (start us, length us, event | category | flops | bytes accessed | tf_op | source)
XLA Modules:
  0.0 69.5 jit_solution(838472469294868335)
XLA Ops:
  0.0 1.8 %spread.1 = bf16[64,2,16,128]{3,2,1,0:T(8,128)(2,1)} custom-call(bf16[2,8,16,128]{3,2,1,0:T(8,128)(2,1)} %rf_ref.1), custom_call_target="tpu_custom_call" | custom-call | tf_op jit(solution)/shard_map/spread/pallas_call | solution.py:242
  1.8 11.5 %all-to-all-start = ((bf16[64,2,16,128]{3,2,1,0:T(8,128)(2,1)}), bf16[64,2,16,128]{3,2,1,0:T(8,128)(2,1)S(1)}, u32[]{:S(2)}, u32[]{:S(2)}) async-start(bf16[64,2,16,128]{3,2,1,0:T(8,128)(2,1)} %spread.1), calls=%async_computation | async-start | bytes 1048576 | tf_op jit(solution)/shard_map/all_to_all | solution.py:251
  13.3 6.2 %operator.1 = (bf16[2,1024,512]{2,1,0:T(8,128)(2,1)S(1)}, bf16[2,1024,512]{2,1,0:T(8,128)(2,1)}) custom-call(s32[3,1024]{1,0:T(4,128)} %elem_ref.1, s32[3,2048]{1,0:T(4,128)} %vox_ref.1, s32[8]{0:T(128)} %bins_ref.1), custom_call_target="tpu_custom_call" | custom-call | flops 62914560 | bytes 4194304 | tf_op jit(solution)/shard_map/operator/pallas_call | solution.py:254
  19.5 6.7 %all-to-all-done = bf16[64,2,16,128]{3,2,1,0:T(8,128)(2,1)S(1)} async-done(((bf16[64,2,16,128]{3,2,1,0:T(8,128)(2,1)}), bf16[64,2,16,128]{3,2,1,0:T(8,128)(2,1)S(1)}, u32[]{:S(2)}, u32[]{:S(2)}) %all-to-all-start) | async-done | bytes 524320 | tf_op jit(solution)/shard_map/all_to_all | solution.py:251
  26.2 0.0 collective-permute-start
  26.2 2.4 %beam_own.1 = (bf16[256,1024]{1,0:T(8,128)(2,1)S(1)}, bf16[2,1024,512]{2,1,0:T(8,128)(2,1)S(1)}) custom-call(bf16[2,1024,512]{2,1,0:T(8,128)(2,1)S(1)} %get-tuple-element.19.upper, bf16[2,1024,512]{2,1,0:T(8,128)(2,1)} %get-tuple-element.20.lower_ref, bf16[8,8,2,16,128]{4,3,2,1,0:T(8,128)(2,1)S(1)} %bitcast.2), custom_call_target="tpu_custom_call" | custom-call | flops 2147483648 | bytes 4194304 | tf_op jit(solution)/shard_map/beam_own/pallas_call | solution.py:284
  28.6 0.0 collective-permute-done
  28.7 1.9 %beam_other.1 = (bf16[512,1024]{1,0:T(8,128)(2,1)S(1)}, f32[128,256]{1,0:T(8,128)S(1)}, f32[128,256]{1,0:T(8,128)S(1)}) custom-call(bf16[2,1024,512]{2,1,0:T(8,128)(2,1)S(1)} %get-tuple-element.19.upper, bf16[2,1024,512]{2,1,0:T(8,128)(2,1)S(1)} %get-tuple-element.22.lower, bf16[8,8,2,16,128]{4,3,2,1,0:T(8,128)(2,1)S(1)} %bitcast.3, ...), custom_call_target="tpu_custom_call" | custom-call | flops 2147483648 | bytes 4194304 | tf_op jit(solution)/shard_map/beam_other/pallas_call | solution.py:297
  30.6 0.6 collective-permute-start.1
  31.1 1.0 %collective-permute-done.1 = f32[128,256]{1,0:T(8,128)S(1)} collective-permute-done((f32[128,256]{1,0:T(8,128)S(1)}, f32[128,256]{1,0:T(8,128)S(1)}, u32[]{:S(2)}, u32[]{:S(2)}) %collective-permute-start.1) | collective-permute-done | bytes 131104 | tf_op jit(solution)/shard_map/ppermute | solution.py:237
  32.2 0.4 collective-permute-start.7
  32.6 1.7 %collective-permute-start.4 = (bf16[128,256]{1,0:T(8,128)(2,1)S(1)}, bf16[128,256]{1,0:T(8,128)(2,1)S(1)}, u32[]{:S(2)}, u32[]{:S(2)}) collective-permute-start(bf16[128,256]{1,0:T(8,128)(2,1)S(1)} %convert_element_type.18), channel_id=1, source_target_pairs={{0,32},{16,48},{32,0},{48,16},{64,96},{80,112},{96,64},{112,80},{1... | collective-permute-start | bytes 196616 | tf_op jit(solution)/shard_map/ppermute | solution.py:240
  34.3 1.4 %collective-permute-start.3 = (bf16[128,256]{1,0:T(8,128)(2,1)S(1)}, bf16[128,256]{1,0:T(8,128)(2,1)S(1)}, u32[]{:S(2)}, u32[]{:S(2)}) collective-permute-start(bf16[128,256]{1,0:T(8,128)(2,1)S(1)} %convert_element_type.18), channel_id=1, source_target_pairs={{0,48},{16,32},{32,16},{48,0},{64,112},{80,96},{96,80},{112,64},{1... | collective-permute-start | bytes 196616 | tf_op jit(solution)/shard_map/ppermute | solution.py:240
  35.7 0.5 collective-permute-start.2
  36.2 2.3 %collective-permute-done.4 = bf16[128,256]{1,0:T(8,128)(2,1)S(1)} collective-permute-done((bf16[128,256]{1,0:T(8,128)(2,1)S(1)}, bf16[128,256]{1,0:T(8,128)(2,1)S(1)}, u32[]{:S(2)}, u32[]{:S(2)}) %collective-permute-start.4) | collective-permute-done | bytes 65568 | tf_op jit(solution)/shard_map/ppermute | solution.py:240
  38.5 1.4 %collective-permute-done.3 = bf16[128,256]{1,0:T(8,128)(2,1)S(1)} collective-permute-done((bf16[128,256]{1,0:T(8,128)(2,1)S(1)}, bf16[128,256]{1,0:T(8,128)(2,1)S(1)}, u32[]{:S(2)}, u32[]{:S(2)}) %collective-permute-start.3) | collective-permute-done | bytes 65568 | tf_op jit(solution)/shard_map/ppermute | solution.py:240
  39.9 0.1 collective-permute-done.2
  40.0 1.9 %collective-permute-start.5 = (bf16[128,256]{1,0:T(8,128)(2,1)S(1)}, bf16[128,256]{1,0:T(8,128)(2,1)S(1)}, u32[]{:S(2)}, u32[]{:S(2)}) collective-permute-start(bf16[128,256]{1,0:T(8,128)(2,1)S(1)} %fusion), channel_id=1, source_target_pairs={{0,64},{16,80},{32,96},{48,112},{64,0},{80,16},{96,32},{112,48},{1... | collective-permute-start | bytes 196616 | tf_op jit(solution)/shard_map/ppermute | solution.py:240
  42.0 3.9 %collective-permute-done.5 = bf16[128,256]{1,0:T(8,128)(2,1)S(1)} collective-permute-done((bf16[128,256]{1,0:T(8,128)(2,1)S(1)}, bf16[128,256]{1,0:T(8,128)(2,1)S(1)}, u32[]{:S(2)}, u32[]{:S(2)}) %collective-permute-start.5) | collective-permute-done | bytes 65568 | tf_op jit(solution)/shard_map/ppermute | solution.py:240
  45.9 0.1 collective-permute-start.6
  46.0 1.3 %collective-permute-done.6.other = f32[128,256]{1,0:T(8,128)S(1)} collective-permute-done((f32[128,256]{1,0:T(8,128)S(1)}, f32[128,256]{1,0:T(8,128)S(1)}, u32[]{:S(2)}, u32[]{:S(2)}) %collective-permute-start.6) | collective-permute-done | bytes 131104 | tf_op jit(solution)/shard_map/ppermute | solution.py:237
  47.3 0.0 collective-permute-done.7.peer_ref
  47.3 2.1 %filter.1 = bf16[8,2,16,2048]{3,2,1,0:T(8,128)(2,1)S(1)} custom-call(f32[128,256]{1,0:T(8,128)S(1)} %convert_add_fusion.own, f32[128,256]{1,0:T(8,128)S(1)} %collective-permute-done.6.other, bf16[512,1024]{1,0:T(8,128)(2,1)S(1)} %get-tuple-element.28.y_ref, bf16[512,1024]{1,0:T(8,128)(2,1)S(1)} %collective-permute-done.7.peer_ref), custom_call_target="tpu_custom_call" | custom-call | tf_op jit(solution)/shard_map/filter/pallas_call | solution.py:316
  49.5 18.6 %all_to_all.10.got = bf16[8,2,16,2048]{3,2,1,0:T(8,128)(2,1)S(1)} all-to-all(bf16[8,2,16,2048]{3,2,1,0:T(8,128)(2,1)S(1)} %filter.1), channel_id=1, replica_groups=mesh['chan'=8,'bin'=8,'core'=2] {'bin'}, dimensions={0} | all-to-all | bytes 2097152 | tf_op jit(solution)/shard_map/all_to_all | solution.py:326
  68.1 1.4 %place.1 = bf16[16,2,8,2048]{3,2,1,0:T(8,128)(2,1)} custom-call(bf16[8,2,16,2048]{3,2,1,0:T(8,128)(2,1)S(1)} %all_to_all.10.got), custom_call_target="tpu_custom_call" | custom-call | tf_op jit(solution)/shard_map/place/pallas_call | solution.py:327
  (4 shorter events, 0.1 us)
Async XLA Ops:
  1.8 24.5 %all-to-all-start = ((bf16[64,2,16,128]{3,2,1,0:T(8,128)(2,1)}), bf16[64,2,16,128]{3,2,1,0:T(8,128)(2,1)S(1)}, u32[]{:S(2)}, u32[]{:S(2)}) async-start(bf16[64,2,16,128]{3,2,1,0:T(8,128)(2,1)} %spread.1), calls=%async_computation | async-start | bytes 1048576 | tf_op jit(solution)/shard_map/all_to_all | solution.py:251
  26.2 2.4 %collective-permute-start = (bf16[64,2,16,128]{3,2,1,0:T(8,128)(2,1)S(1)}, bf16[64,2,16,128]{3,2,1,0:T(8,128)(2,1)S(1)}, u32[]{:S(2)}, u32[]{:S(2)}) collective-permute-start(bf16[64,2,16,128]{3,2,1,0:T(8,128)(2,1)S(1)} %all-to-all-done), channel_id=1, source_target_pairs={{0,1},{1,0},{2,3},{3,2},{4,5},{5,4},{6,7},{7,6},{8,9},{9,8},{10,11... | collective-permute-start | bytes 1572872 | tf_op jit(solution)/shard_map/ppermute | solution.py:237
  30.6 1.6 %collective-permute-start.1 = (f32[128,256]{1,0:T(8,128)S(1)}, f32[128,256]{1,0:T(8,128)S(1)}, u32[]{:S(2)}, u32[]{:S(2)}) collective-permute-start(f32[128,256]{1,0:T(8,128)S(1)} %get-tuple-element.25), channel_id=1, source_target_pairs={{0,1},{1,0},{2,3},{3,2},{4,5},{5,4},{6,7},{7,6},{8,9},{9,8},{10,11... | collective-permute-start | bytes 393224 | tf_op jit(solution)/shard_map/ppermute | solution.py:237
  32.2 15.2 %collective-permute-start.7 = (bf16[512,1024]{1,0:T(8,128)(2,1)S(1)}, bf16[512,1024]{1,0:T(8,128)(2,1)S(1)}, u32[]{:S(2)}, u32[]{:S(2)}) collective-permute-start(bf16[512,1024]{1,0:T(8,128)(2,1)S(1)} %get-tuple-element.28.y_ref), channel_id=1, source_target_pairs={{0,1},{1,0},{2,3},{3,2},{4,5},{5,4},{6,7},{7,6},{8,9},{9,8},{10,11... | collective-permute-start | bytes 3145736 | tf_op jit(solution)/shard_map/ppermute | solution.py:237
  32.6 5.9 %collective-permute-start.4 = (bf16[128,256]{1,0:T(8,128)(2,1)S(1)}, bf16[128,256]{1,0:T(8,128)(2,1)S(1)}, u32[]{:S(2)}, u32[]{:S(2)}) collective-permute-start(bf16[128,256]{1,0:T(8,128)(2,1)S(1)} %convert_element_type.18), channel_id=1, source_target_pairs={{0,32},{16,48},{32,0},{48,16},{64,96},{80,112},{96,64},{112,80},{1... | collective-permute-start | bytes 196616 | tf_op jit(solution)/shard_map/ppermute | solution.py:240
  34.3 5.6 %collective-permute-start.3 = (bf16[128,256]{1,0:T(8,128)(2,1)S(1)}, bf16[128,256]{1,0:T(8,128)(2,1)S(1)}, u32[]{:S(2)}, u32[]{:S(2)}) collective-permute-start(bf16[128,256]{1,0:T(8,128)(2,1)S(1)} %convert_element_type.18), channel_id=1, source_target_pairs={{0,48},{16,32},{32,16},{48,0},{64,112},{80,96},{96,80},{112,64},{1... | collective-permute-start | bytes 196616 | tf_op jit(solution)/shard_map/ppermute | solution.py:240
  35.7 4.3 %collective-permute-start.2 = (bf16[128,256]{1,0:T(8,128)(2,1)S(1)}, bf16[128,256]{1,0:T(8,128)(2,1)S(1)}, u32[]{:S(2)}, u32[]{:S(2)}) collective-permute-start(bf16[128,256]{1,0:T(8,128)(2,1)S(1)} %convert_element_type.18), channel_id=1, source_target_pairs={{0,16},{16,0},{32,48},{48,32},{64,80},{80,64},{96,112},{112,96},{1... | collective-permute-start | bytes 196616 | tf_op jit(solution)/shard_map/ppermute | solution.py:240
  40.0 5.8 %collective-permute-start.5 = (bf16[128,256]{1,0:T(8,128)(2,1)S(1)}, bf16[128,256]{1,0:T(8,128)(2,1)S(1)}, u32[]{:S(2)}, u32[]{:S(2)}) collective-permute-start(bf16[128,256]{1,0:T(8,128)(2,1)S(1)} %fusion), channel_id=1, source_target_pairs={{0,64},{16,80},{32,96},{48,112},{64,0},{80,16},{96,32},{112,48},{1... | collective-permute-start | bytes 196616 | tf_op jit(solution)/shard_map/ppermute | solution.py:240
  45.9 1.4 %collective-permute-start.6 = (f32[128,256]{1,0:T(8,128)S(1)}, f32[128,256]{1,0:T(8,128)S(1)}, u32[]{:S(2)}, u32[]{:S(2)}) collective-permute-start(f32[128,256]{1,0:T(8,128)S(1)} %convert_add_fusion.own), channel_id=1, source_target_pairs={{0,1},{1,0},{2,3},{3,2},{4,5},{5,4},{6,7},{7,6},{8,9},{9,8},{10,11... | collective-permute-start | bytes 393224 | tf_op jit(solution)/shard_map/ppermute | solution.py:237

commit v9 on v8

--- a/solution.py
+++ b/solution.py
@@ -18,6 +18,7 @@
 ROUNDER = 12582912.0
 ROWS = 512
 LANES = 256
+PLACED = 512
 WIDE = pltpu.CompilerParams(vmem_limit_bytes=16 * 1024 * 1024)
 VMEM = pl.BlockSpec(memory_space=pltpu.VMEM)
 HBM = pl.BlockSpec(memory_space=pltpu.HBM)
@@ -177,23 +178,22 @@
     return 0.5 * (packed + flipped), 0.5 * (packed - flipped), flipped
 
 
-def filter_kernel(own, other, y_ref, peer_ref, out_ref, gram, kept):
+def filter_kernel(mine, far, twin, far_twin, y_ref, peer_ref, out_ref, gram, kept):
     core = lax.axis_index("core")
-    half, frames = own.shape
-    gram[pl.ds(pl.multiple_of(core * half, half), half), :] = own[...]
-    gram[pl.ds(pl.multiple_of((1 - core) * half, half), half), :] = other[...]
+    half, frames = mine.shape
+    gram[pl.ds(pl.multiple_of(core * half, half), half), :] = mine[...] + far[...].astype(F32)
+    gram[pl.ds(pl.multiple_of((1 - core) * half, half), half), :] = twin[...] + far_twin[...].astype(F32)
     packed = gram[...]
     squares = jnp.sum(packed * packed)
     factor = 4.0 / jnp.sqrt(jnp.full((1, 1), squares + EPSILON, F32))
-    mat = packed * factor
-    real, imag, flipped = unpack(mat)
+    real, imag, flipped = unpack(packed)
     left = jnp.concatenate([real, imag], axis=1)
-    second = product(left, jnp.concatenate([mat, flipped], axis=0))
-    third = product(left, jnp.concatenate([second, jnp.transpose(second)], axis=0))
+    second = product(left, jnp.concatenate([packed, flipped], axis=0)) * (factor * factor)
+    third = product(left, jnp.concatenate([second, jnp.transpose(second)], axis=0)) * factor
     rows = lax.broadcasted_iota(jnp.int32, (frames, frames), 0)
     cols = lax.broadcasted_iota(jnp.int32, (frames, frames), 1)
     identity = jnp.where(rows == cols, 1.0, 0.0).astype(F32)
-    real, imag, _ = unpack(identity - mat + 0.3 * second - 0.03 * third)
+    real, imag, _ = unpack(identity - factor * packed + 0.3 * second - 0.03 * third)
     kept[0] = real.astype(BF16)
     kept[1] = imag.astype(BF16)
     real, imag = (kept[part, pl.ds(pl.multiple_of(core * half, half), half)] for part in range(2))
@@ -212,14 +212,17 @@
 
 
 def place_kernel(got, out_ref):
-    bins, parts, group, voxels = got.shape
+    bins, parts, group, _ = got.shape
+    width = out_ref.shape[3]
     size = group * bins
     rows = lax.broadcasted_iota(jnp.int32, (size, size), 0)
     cols = lax.broadcasted_iota(jnp.int32, (size, size), 1)
     turn = jnp.where(cols == (rows % bins) * group + rows // bins, 1.0, 0.0).astype(BF16)
+    lanes = pl.ds(pl.multiple_of(pl.program_id(0) * width, width), width)
     for part in range(parts):
-        moved = jnp.dot(turn, got[:, part].reshape(size, voxels), preferred_element_type=F32).astype(BF16)
-        out_ref[:, part] = moved.reshape(group, bins, voxels)
+        block = got[:, part, :, lanes].reshape(size, width)
+        moved = jnp.dot(turn, block, preferred_element_type=F32).astype(BF16)
+        out_ref[:, part] = moved.reshape(group, bins, width)
 
 
 def shards(rf_data, elem_pos, vox_pos, subbands):
@@ -310,26 +313,31 @@
     peer = swap(y)
     narrow = total.astype(BF16)
     total = total + sum(across(narrow, bits).astype(F32) for bits in (1, 3, 2))
-    total = total + across(total.astype(BF16), 4).astype(F32)
-    rest = swap(total)
+    narrow = total.astype(BF16)
+    far = across(narrow, 4)
+    far_twin = lax.ppermute(
+        narrow, ("chan", "core"), [(2 * a + c, 2 * (a ^ 4) + 1 - c) for a in range(chans) for c in range(CORES)]
+    )
+    twin = swap(total)
 
     applied = pl.pallas_call(
         filter_kernel,
         name="filter",
         out_shape=shape(bins, parts, group, CORES * voxels),
-        in_specs=[VMEM] * 4,
+        in_specs=[VMEM] * 6,
         out_specs=VMEM,
         scratch_shapes=[pltpu.VMEM((frames, frames), F32), pltpu.VMEM((2, frames, frames), BF16)],
         compiler_params=WIDE,
-    )(total, rest, y, peer)
+    )(total, far, twin, far_twin, y, peer)
 
     got = lax.all_to_all(applied, "bin", split_axis=0, concat_axis=0, tiled=True)
     return pl.pallas_call(
         place_kernel,
         name="place",
+        grid=(CORES * voxels // PLACED,),
         out_shape=shape(group, parts, bins, CORES * voxels),
         in_specs=[VMEM],
-        out_specs=VMEM,
+        out_specs=pl.BlockSpec((group, parts, bins, PLACED), lambda n: (0, 0, 0, n)),
         compiler_params=WIDE,
     )(got)
 

time: 69.9 us -> 70 us (level)
  starting transfers between devices: 18.1 us -> 19.8 us
  waiting for transfers between devices: 16.8 us -> 15.6 us
  blocking collectives: 18.6 us -> 17.7 us
    ppermute x0 -> x1, starting transfers between devices: none -> 1.98 us  [shards(): lax.ppermute(narrow, ('chan', 'core'), [(2 * a + c, 2 * (a ^ 4) + 1 - c)...]
    ppermute x0 -> x1, waiting for transfers between devices: none -> 1.77 us  [shards(): lax.ppermute(narrow, ('chan', 'core'), [(2 * a + c, 2 * (a ^ 4) + 1 - c)...]
    ppermute x4, waiting for transfers between devices: 7.71 us -> 6.13 us  [across(): return lax.ppermute(x, 'chan', [(a, a ^ bits) for a in range(chans)])]
    ppermute x4, waiting for transfers between devices: 2.33 us -> 0.99 us  [swap(): return lax.ppermute(x, 'core', [(0, 1), (1, 0)])]
    all_to_all x1, blocking collectives: 18.6 us -> 17.7 us  [shards(): lax.all_to_all(applied, 'bin', split_axis=0, concat_axis=0, tiled=True)]
  transfers between devices with their start and end apart: 9 -> 10, of which waited for: 7 -> 7; matrix products, arithmetic and copies ran while one was open for 0% -> 0% of each run, Pallas kernels for 12% -> 12%
where the time goes in v9:
time: 70 us; the launch traced here: 69.6 us
  starting transfers between devices  19.8 us (28%)
  blocking collectives  17.7 us (25%)
  Pallas kernels  16.4 us (23%)
  waiting for transfers between devices  15.6 us (22%)
    all_to_all x1, blocking collectives, shards(): lax.all_to_all(applied, 'bin', split_axis=0, concat_axis=0, tiled=True)  17.7 us
    all_to_all x1, starting transfers between devices, shards(): lax.all_to_all(by_bin, ('chan', 'bin'), split_axis=0, concat_axis=0, tile...  11.5 us
    all_to_all x1, waiting for transfers between devices, shards(): lax.all_to_all(by_bin, ('chan', 'bin'), split_axis=0, concat_axis=0, tile...  6.71 us
    pallas_call x1, Pallas kernels, shards(): pl.pallas_call(operator_kernel, name='operator', out_shape=(shape(2, chan...  6.21 us
    ppermute x4, waiting for transfers between devices, across(): return lax.ppermute(x, 'chan', [(a, a ^ bits) for a in range(chans)])  6.13 us
    ppermute x4, starting transfers between devices, across(): return lax.ppermute(x, 'chan', [(a, a ^ bits) for a in range(chans)])  5.24 us
    pallas_call x1, Pallas kernels, shards(): pl.pallas_call(own_kernel, name='beam_own', out_shape=(shape(frames, voxe...  2.41 us
    pallas_call x1, Pallas kernels, shards(): pl.pallas_call(place_kernel, name='place', grid=(CORES * voxels // PLACED...  2.06 us
  transfers between devices with their start and end apart: 10, of which 7 were waited for; matrix products, arithmetic and copies ran while one was open for 0% of the time, Pallas kernels for 12%

profile of v9, /device:TPU:0, one launch (start us, length us, event | category | flops | bytes accessed | tf_op | source)
XLA Modules:
  0.0 69.6 jit_solution(5173509914963499462)
XLA Ops:
  0.0 1.8 %spread.1 = bf16[64,2,16,128]{3,2,1,0:T(8,128)(2,1)} custom-call(bf16[2,8,16,128]{3,2,1,0:T(8,128)(2,1)} %rf_ref.1), custom_call_target="tpu_custom_call" | custom-call | tf_op jit(solution)/shard_map/spread/pallas_call | solution.py:245
  1.8 11.5 %all-to-all-start = ((bf16[64,2,16,128]{3,2,1,0:T(8,128)(2,1)}), bf16[64,2,16,128]{3,2,1,0:T(8,128)(2,1)S(1)}, u32[]{:S(2)}, u32[]{:S(2)}) async-start(bf16[64,2,16,128]{3,2,1,0:T(8,128)(2,1)} %spread.1), calls=%async_computation | async-start | bytes 1048576 | tf_op jit(solution)/shard_map/all_to_all | solution.py:254
  13.3 6.2 %operator.1 = (bf16[2,1024,512]{2,1,0:T(8,128)(2,1)S(1)}, bf16[2,1024,512]{2,1,0:T(8,128)(2,1)}) custom-call(s32[3,1024]{1,0:T(4,128)} %elem_ref.1, s32[3,2048]{1,0:T(4,128)} %vox_ref.1, s32[8]{0:T(128)} %bins_ref.1), custom_call_target="tpu_custom_call" | custom-call | flops 62914560 | bytes 4194304 | tf_op jit(solution)/shard_map/operator/pallas_call | solution.py:257
  19.5 6.7 %all-to-all-done = bf16[64,2,16,128]{3,2,1,0:T(8,128)(2,1)S(1)} async-done(((bf16[64,2,16,128]{3,2,1,0:T(8,128)(2,1)}), bf16[64,2,16,128]{3,2,1,0:T(8,128)(2,1)S(1)}, u32[]{:S(2)}, u32[]{:S(2)}) %all-to-all-start) | async-done | bytes 524320 | tf_op jit(solution)/shard_map/all_to_all | solution.py:254
  26.2 0.0 collective-permute-start
  26.2 2.4 %beam_own.1 = (bf16[256,1024]{1,0:T(8,128)(2,1)S(1)}, bf16[2,1024,512]{2,1,0:T(8,128)(2,1)S(1)}) custom-call(bf16[2,1024,512]{2,1,0:T(8,128)(2,1)S(1)} %get-tuple-element.19.upper, bf16[2,1024,512]{2,1,0:T(8,128)(2,1)} %get-tuple-element.20.lower_ref, bf16[8,8,2,16,128]{4,3,2,1,0:T(8,128)(2,1)S(1)} %bitcast.2), custom_call_target="tpu_custom_call" | custom-call | flops 2147483648 | bytes 4194304 | tf_op jit(solution)/shard_map/beam_own/pallas_call | solution.py:287
  28.6 0.0 collective-permute-done
  28.7 1.9 %beam_other.1 = (bf16[512,1024]{1,0:T(8,128)(2,1)S(1)}, f32[128,256]{1,0:T(8,128)S(1)}, f32[128,256]{1,0:T(8,128)S(1)}) custom-call(bf16[2,1024,512]{2,1,0:T(8,128)(2,1)S(1)} %get-tuple-element.19.upper, bf16[2,1024,512]{2,1,0:T(8,128)(2,1)S(1)} %get-tuple-element.22.lower, bf16[8,8,2,16,128]{4,3,2,1,0:T(8,128)(2,1)S(1)} %bitcast.3, ...), custom_call_target="tpu_custom_call" | custom-call | flops 2147483648 | bytes 4194304 | tf_op jit(solution)/shard_map/beam_other/pallas_call | solution.py:300
  30.6 0.6 collective-permute-start.1
  31.1 1.0 %collective-permute-done.1 = f32[128,256]{1,0:T(8,128)S(1)} collective-permute-done((f32[128,256]{1,0:T(8,128)S(1)}, f32[128,256]{1,0:T(8,128)S(1)}, u32[]{:S(2)}, u32[]{:S(2)}) %collective-permute-start.1) | collective-permute-done | bytes 131104 | tf_op jit(solution)/shard_map/ppermute | solution.py:240
  32.2 0.4 collective-permute-start.8
  32.6 1.7 %collective-permute-start.4 = (bf16[128,256]{1,0:T(8,128)(2,1)S(1)}, bf16[128,256]{1,0:T(8,128)(2,1)S(1)}, u32[]{:S(2)}, u32[]{:S(2)}) collective-permute-start(bf16[128,256]{1,0:T(8,128)(2,1)S(1)} %convert_element_type.15), channel_id=1, source_target_pairs={{0,32},{16,48},{32,0},{48,16},{64,96},{80,112},{96,64},{112,80},{1... | collective-permute-start | bytes 196616 | tf_op jit(solution)/shard_map/ppermute | solution.py:243
  34.3 1.4 %collective-permute-start.3 = (bf16[128,256]{1,0:T(8,128)(2,1)S(1)}, bf16[128,256]{1,0:T(8,128)(2,1)S(1)}, u32[]{:S(2)}, u32[]{:S(2)}) collective-permute-start(bf16[128,256]{1,0:T(8,128)(2,1)S(1)} %convert_element_type.15), channel_id=1, source_target_pairs={{0,48},{16,32},{32,16},{48,0},{64,112},{80,96},{96,80},{112,64},{1... | collective-permute-start | bytes 196616 | tf_op jit(solution)/shard_map/ppermute | solution.py:243
  35.7 0.5 collective-permute-start.2
  36.2 2.3 %collective-permute-done.4 = bf16[128,256]{1,0:T(8,128)(2,1)S(1)} collective-permute-done((bf16[128,256]{1,0:T(8,128)(2,1)S(1)}, bf16[128,256]{1,0:T(8,128)(2,1)S(1)}, u32[]{:S(2)}, u32[]{:S(2)}) %collective-permute-start.4) | collective-permute-done | bytes 65568 | tf_op jit(solution)/shard_map/ppermute | solution.py:243
  38.5 1.4 %collective-permute-done.3 = bf16[128,256]{1,0:T(8,128)(2,1)S(1)} collective-permute-done((bf16[128,256]{1,0:T(8,128)(2,1)S(1)}, bf16[128,256]{1,0:T(8,128)(2,1)S(1)}, u32[]{:S(2)}, u32[]{:S(2)}) %collective-permute-start.3) | collective-permute-done | bytes 65568 | tf_op jit(solution)/shard_map/ppermute | solution.py:243
  39.9 0.1 collective-permute-done.2
  40.0 0.1 collective-permute-start.6
  40.1 2.0 %collective-permute-start.7 = (bf16[128,256]{1,0:T(8,128)(2,1)S(1)}, bf16[128,256]{1,0:T(8,128)(2,1)S(1)}, u32[]{:S(2)}, u32[]{:S(2)}) collective-permute-start(bf16[128,256]{1,0:T(8,128)(2,1)S(1)} %get-tuple-element.29), channel_id=1, source_target_pairs={{0,65},{1,64},{16,81},{17,80},{32,97},{33,96},{48,113},{49,112},{6... | collective-permute-start | bytes 196616 | tf_op jit(solution)/shard_map/ppermute | solution.py:318
  42.1 1.7 %collective-permute-start.5 = (bf16[128,256]{1,0:T(8,128)(2,1)S(1)}, bf16[128,256]{1,0:T(8,128)(2,1)S(1)}, u32[]{:S(2)}, u32[]{:S(2)}) collective-permute-start(bf16[128,256]{1,0:T(8,128)(2,1)S(1)} %get-tuple-element.29), channel_id=1, source_target_pairs={{0,64},{16,80},{32,96},{48,112},{64,0},{80,16},{96,32},{112,48},{1... | collective-permute-start | bytes 196616 | tf_op jit(solution)/shard_map/ppermute | solution.py:243
  43.8 1.8 %collective-permute-done.7.far_twin = bf16[128,256]{1,0:T(8,128)(2,1)S(1)} collective-permute-done((bf16[128,256]{1,0:T(8,128)(2,1)S(1)}, bf16[128,256]{1,0:T(8,128)(2,1)S(1)}, u32[]{:S(2)}, u32[]{:S(2)}) %collective-permute-start.7) | collective-permute-done | bytes 65568 | tf_op jit(solution)/shard_map/ppermute | solution.py:318
  45.5 2.3 %collective-permute-done.5.far = bf16[128,256]{1,0:T(8,128)(2,1)S(1)} collective-permute-done((bf16[128,256]{1,0:T(8,128)(2,1)S(1)}, bf16[128,256]{1,0:T(8,128)(2,1)S(1)}, u32[]{:S(2)}, u32[]{:S(2)}) %collective-permute-start.5) | collective-permute-done | bytes 65568 | tf_op jit(solution)/shard_map/ppermute | solution.py:243
  47.9 0.0 collective-permute-done.6.twin
  47.9 0.0 collective-permute-done.8.peer_ref
  47.9 2.0 %filter.1 = bf16[8,2,16,2048]{3,2,1,0:T(8,128)(2,1)S(1)} custom-call(f32[128,256]{1,0:T(8,128)S(1)} %get-tuple-element.30.mine, bf16[128,256]{1,0:T(8,128)(2,1)S(1)} %collective-permute-done.5.far, f32[128,256]{1,0:T(8,128)S(1)} %collective-permute-done.6.twin, bf16[128,256]{1,0:T(8,128)(2,1)S(1)} %collective-permute-done.7.far_twin, ...), custom_call_target="tpu_custom_call" | custom-call | tf_op jit(solution)/shard_map/filter/pallas_call | solution.py:323
  49.9 17.7 %all_to_all.10.got = bf16[8,2,16,2048]{3,2,1,0:T(8,128)(2,1)S(1)} all-to-all(bf16[8,2,16,2048]{3,2,1,0:T(8,128)(2,1)S(1)} %filter.1), channel_id=1, replica_groups=mesh['chan'=8,'bin'=8,'core'=2] {'bin'}, dimensions={0} | all-to-all | bytes 2097152 | tf_op jit(solution)/shard_map/all_to_all | solution.py:333
  67.5 2.1 %place.1 = bf16[16,2,8,2048]{3,2,1,0:T(8,128)(2,1)} custom-call(bf16[8,2,16,2048]{3,2,1,0:T(8,128)(2,1)S(1)} %all_to_all.10.got), custom_call_target="tpu_custom_call" | custom-call | tf_op jit(solution)/shard_map/place/pallas_call | solution.py:334
  (3 shorter events, 0.1 us)
Async XLA Ops:
  1.8 24.5 %all-to-all-start = ((bf16[64,2,16,128]{3,2,1,0:T(8,128)(2,1)}), bf16[64,2,16,128]{3,2,1,0:T(8,128)(2,1)S(1)}, u32[]{:S(2)}, u32[]{:S(2)}) async-start(bf16[64,2,16,128]{3,2,1,0:T(8,128)(2,1)} %spread.1), calls=%async_computation | async-start | bytes 1048576 | tf_op jit(solution)/shard_map/all_to_all | solution.py:254
  26.2 2.4 %collective-permute-start = (bf16[64,2,16,128]{3,2,1,0:T(8,128)(2,1)S(1)}, bf16[64,2,16,128]{3,2,1,0:T(8,128)(2,1)S(1)}, u32[]{:S(2)}, u32[]{:S(2)}) collective-permute-start(bf16[64,2,16,128]{3,2,1,0:T(8,128)(2,1)S(1)} %all-to-all-done), channel_id=1, source_target_pairs={{0,1},{1,0},{2,3},{3,2},{4,5},{5,4},{6,7},{7,6},{8,9},{9,8},{10,11... | collective-permute-start | bytes 1572872 | tf_op jit(solution)/shard_map/ppermute | solution.py:240
  30.6 1.6 %collective-permute-start.1 = (f32[128,256]{1,0:T(8,128)S(1)}, f32[128,256]{1,0:T(8,128)S(1)}, u32[]{:S(2)}, u32[]{:S(2)}) collective-permute-start(f32[128,256]{1,0:T(8,128)S(1)} %get-tuple-element.25), channel_id=1, source_target_pairs={{0,1},{1,0},{2,3},{3,2},{4,5},{5,4},{6,7},{7,6},{8,9},{9,8},{10,11... | collective-permute-start | bytes 393224 | tf_op jit(solution)/shard_map/ppermute | solution.py:240
  32.2 15.7 %collective-permute-start.8 = (bf16[512,1024]{1,0:T(8,128)(2,1)S(1)}, bf16[512,1024]{1,0:T(8,128)(2,1)S(1)}, u32[]{:S(2)}, u32[]{:S(2)}) collective-permute-start(bf16[512,1024]{1,0:T(8,128)(2,1)S(1)} %get-tuple-element.28.y_ref), channel_id=1, source_target_pairs={{0,1},{1,0},{2,3},{3,2},{4,5},{5,4},{6,7},{7,6},{8,9},{9,8},{10,11... | collective-permute-start | bytes 3145736 | tf_op jit(solution)/shard_map/ppermute | solution.py:240
  32.6 5.9 %collective-permute-start.4 = (bf16[128,256]{1,0:T(8,128)(2,1)S(1)}, bf16[128,256]{1,0:T(8,128)(2,1)S(1)}, u32[]{:S(2)}, u32[]{:S(2)}) collective-permute-start(bf16[128,256]{1,0:T(8,128)(2,1)S(1)} %convert_element_type.15), channel_id=1, source_target_pairs={{0,32},{16,48},{32,0},{48,16},{64,96},{80,112},{96,64},{112,80},{1... | collective-permute-start | bytes 196616 | tf_op jit(solution)/shard_map/ppermute | solution.py:243
  34.3 5.6 %collective-permute-start.3 = (bf16[128,256]{1,0:T(8,128)(2,1)S(1)}, bf16[128,256]{1,0:T(8,128)(2,1)S(1)}, u32[]{:S(2)}, u32[]{:S(2)}) collective-permute-start(bf16[128,256]{1,0:T(8,128)(2,1)S(1)} %convert_element_type.15), channel_id=1, source_target_pairs={{0,48},{16,32},{32,16},{48,0},{64,112},{80,96},{96,80},{112,64},{1... | collective-permute-start | bytes 196616 | tf_op jit(solution)/shard_map/ppermute | solution.py:243
  35.7 4.3 %collective-permute-start.2 = (bf16[128,256]{1,0:T(8,128)(2,1)S(1)}, bf16[128,256]{1,0:T(8,128)(2,1)S(1)}, u32[]{:S(2)}, u32[]{:S(2)}) collective-permute-start(bf16[128,256]{1,0:T(8,128)(2,1)S(1)} %convert_element_type.15), channel_id=1, source_target_pairs={{0,16},{16,0},{32,48},{48,32},{64,80},{80,64},{96,112},{112,96},{1... | collective-permute-start | bytes 196616 | tf_op jit(solution)/shard_map/ppermute | solution.py:243
  40.0 7.8 %collective-permute-start.6 = (f32[128,256]{1,0:T(8,128)S(1)}, f32[128,256]{1,0:T(8,128)S(1)}, u32[]{:S(2)}, u32[]{:S(2)}) collective-permute-start(f32[128,256]{1,0:T(8,128)S(1)} %get-tuple-element.30.mine), channel_id=1, source_target_pairs={{0,1},{1,0},{2,3},{3,2},{4,5},{5,4},{6,7},{7,6},{8,9},{9,8},{10,11... | collective-permute-start | bytes 393224 | tf_op jit(solution)/shard_map/ppermute | solution.py:240
  40.1 5.4 %collective-permute-start.7 = (bf16[128,256]{1,0:T(8,128)(2,1)S(1)}, bf16[128,256]{1,0:T(8,128)(2,1)S(1)}, u32[]{:S(2)}, u32[]{:S(2)}) collective-permute-start(bf16[128,256]{1,0:T(8,128)(2,1)S(1)} %get-tuple-element.29), channel_id=1, source_target_pairs={{0,65},{1,64},{16,81},{17,80},{32,97},{33,96},{48,113},{49,112},{6... | collective-permute-start | bytes 196616 | tf_op jit(solution)/shard_map/ppermute | solution.py:318
  42.1 5.8 %collective-permute-start.5 = (bf16[128,256]{1,0:T(8,128)(2,1)S(1)}, bf16[128,256]{1,0:T(8,128)(2,1)S(1)}, u32[]{:S(2)}, u32[]{:S(2)}) collective-permute-start(bf16[128,256]{1,0:T(8,128)(2,1)S(1)} %get-tuple-element.29), channel_id=1, source_target_pairs={{0,64},{16,80},{32,96},{48,112},{64,0},{80,16},{96,32},{112,48},{1... | collective-permute-start | bytes 196616 | tf_op jit(solution)/shard_map/ppermute | solution.py:243

commit v10 on v9

--- a/solution.py
+++ b/solution.py
@@ -18,7 +18,6 @@
 ROUNDER = 12582912.0
 ROWS = 512
 LANES = 256
-PLACED = 512
 WIDE = pltpu.CompilerParams(vmem_limit_bytes=16 * 1024 * 1024)
 VMEM = pl.BlockSpec(memory_space=pltpu.VMEM)
 HBM = pl.BlockSpec(memory_space=pltpu.HBM)
@@ -211,18 +210,21 @@
                 out_ref[j, part, :, lanes] = applied[row : row + group]
 
 
-def place_kernel(got, out_ref):
-    bins, parts, group, _ = got.shape
-    width = out_ref.shape[3]
+def place_kernel(got, out_ref, held, sems):
+    bins, parts, group, voxels = got.shape
     size = group * bins
     rows = lax.broadcasted_iota(jnp.int32, (size, size), 0)
     cols = lax.broadcasted_iota(jnp.int32, (size, size), 1)
     turn = jnp.where(cols == (rows % bins) * group + rows // bins, 1.0, 0.0).astype(BF16)
-    lanes = pl.ds(pl.multiple_of(pl.program_id(0) * width, width), width)
+    copies = [
+        pltpu.make_async_copy(held.at[part], out_ref.at[:, part], sems.at[part]) for part in range(parts)
+    ]
     for part in range(parts):
-        block = got[:, part, :, lanes].reshape(size, width)
-        moved = jnp.dot(turn, block, preferred_element_type=F32).astype(BF16)
-        out_ref[:, part] = moved.reshape(group, bins, width)
+        moved = jnp.dot(turn, got[:, part].reshape(size, voxels), preferred_element_type=F32).astype(BF16)
+        held[part] = moved.reshape(group, bins, voxels)
+        copies[part].start()
+    for copy in copies:
+        copy.wait()
 
 
 def shards(rf_data, elem_pos, vox_pos, subbands):
@@ -334,10 +336,13 @@
     return pl.pallas_call(
         place_kernel,
         name="place",
-        grid=(CORES * voxels // PLACED,),
         out_shape=shape(group, parts, bins, CORES * voxels),
         in_specs=[VMEM],
-        out_specs=pl.BlockSpec((group, parts, bins, PLACED), lambda n: (0, 0, 0, n)),
+        out_specs=HBM,
+        scratch_shapes=[
+            pltpu.VMEM((parts, group, bins, CORES * voxels), BF16),
+            pltpu.SemaphoreType.DMA((parts,)),
+        ],
         compiler_params=WIDE,
     )(got)
 

time: 70 us -> 69.2 us (0.989)
  Pallas kernels: 16.4 us -> 15.6 us
    pallas_call x1, Pallas kernels: 2.06 us -> 1.27 us  [shards(): pl.pallas_call(place_kernel, name='place', out_shape=shape(group, parts,...]
  transfers between devices with their start and end apart: 10 -> 10, of which waited for: 7 -> 7; matrix products, arithmetic and copies ran while one was open for 0% -> 0% of each run, Pallas kernels for 12% -> 13%
where the time goes in v10:
time: 69.2 us; the launch traced here: 68.8 us
  starting transfers between devices  19.8 us (29%)
  blocking collectives  17.7 us (26%)
  Pallas kernels  15.6 us (23%)
  waiting for transfers between devices  15.6 us (23%)
    all_to_all x1, blocking collectives, shards(): lax.all_to_all(applied, 'bin', split_axis=0, concat_axis=0, tiled=True)  17.7 us
    all_to_all x1, starting transfers between devices, shards(): lax.all_to_all(by_bin, ('chan', 'bin'), split_axis=0, concat_axis=0, tile...  11.5 us
    all_to_all x1, waiting for transfers between devices, shards(): lax.all_to_all(by_bin, ('chan', 'bin'), split_axis=0, concat_axis=0, tile...  6.71 us
    pallas_call x1, Pallas kernels, shards(): pl.pallas_call(operator_kernel, name='operator', out_shape=(shape(2, chan...  6.21 us
    ppermute x4, waiting for transfers between devices, across(): return lax.ppermute(x, 'chan', [(a, a ^ bits) for a in range(chans)])  6.13 us
    ppermute x4, starting transfers between devices, across(): return lax.ppermute(x, 'chan', [(a, a ^ bits) for a in range(chans)])  5.24 us
    pallas_call x1, Pallas kernels, shards(): pl.pallas_call(own_kernel, name='beam_own', out_shape=(shape(frames, voxe...  2.41 us
    pallas_call x1, Pallas kernels, shards(): pl.pallas_call(filter_kernel, name='filter', out_shape=shape(bins, parts,...  2 us
  transfers between devices with their start and end apart: 10, of which 7 were waited for; matrix products, arithmetic and copies ran while one was open for 0% of the time, Pallas kernels for 13%

profile of v10, /device:TPU:0, one launch (start us, length us, event | category | flops | bytes accessed | tf_op | source)
XLA Modules:
  0.0 68.8 jit_solution(1780846066510333163)
XLA Ops:
  0.0 1.8 %spread.1 = bf16[64,2,16,128]{3,2,1,0:T(8,128)(2,1)} custom-call(bf16[2,8,16,128]{3,2,1,0:T(8,128)(2,1)} %rf_ref.1), custom_call_target="tpu_custom_call" | custom-call | tf_op jit(solution)/shard_map/spread/pallas_call | solution.py:247
  1.8 11.5 %all-to-all-start = ((bf16[64,2,16,128]{3,2,1,0:T(8,128)(2,1)}), bf16[64,2,16,128]{3,2,1,0:T(8,128)(2,1)S(1)}, u32[]{:S(2)}, u32[]{:S(2)}) async-start(bf16[64,2,16,128]{3,2,1,0:T(8,128)(2,1)} %spread.1), calls=%async_computation | async-start | bytes 1048576 | tf_op jit(solution)/shard_map/all_to_all | solution.py:256
  13.3 6.2 %operator.1 = (bf16[2,1024,512]{2,1,0:T(8,128)(2,1)S(1)}, bf16[2,1024,512]{2,1,0:T(8,128)(2,1)}) custom-call(s32[3,1024]{1,0:T(4,128)} %elem_ref.1, s32[3,2048]{1,0:T(4,128)} %vox_ref.1, s32[8]{0:T(128)} %bins_ref.1), custom_call_target="tpu_custom_call" | custom-call | flops 62914560 | bytes 4194304 | tf_op jit(solution)/shard_map/operator/pallas_call | solution.py:259
  19.5 6.7 %all-to-all-done = bf16[64,2,16,128]{3,2,1,0:T(8,128)(2,1)S(1)} async-done(((bf16[64,2,16,128]{3,2,1,0:T(8,128)(2,1)}), bf16[64,2,16,128]{3,2,1,0:T(8,128)(2,1)S(1)}, u32[]{:S(2)}, u32[]{:S(2)}) %all-to-all-start) | async-done | bytes 524320 | tf_op jit(solution)/shard_map/all_to_all | solution.py:256
  26.2 0.0 collective-permute-start
  26.2 2.4 %beam_own.1 = (bf16[256,1024]{1,0:T(8,128)(2,1)S(1)}, bf16[2,1024,512]{2,1,0:T(8,128)(2,1)S(1)}) custom-call(bf16[2,1024,512]{2,1,0:T(8,128)(2,1)S(1)} %get-tuple-element.19.upper, bf16[2,1024,512]{2,1,0:T(8,128)(2,1)} %get-tuple-element.20.lower_ref, bf16[8,8,2,16,128]{4,3,2,1,0:T(8,128)(2,1)S(1)} %bitcast.2), custom_call_target="tpu_custom_call" | custom-call | flops 2147483648 | bytes 4194304 | tf_op jit(solution)/shard_map/beam_own/pallas_call | solution.py:289
  28.6 0.0 collective-permute-done
  28.7 1.9 %beam_other.1 = (bf16[512,1024]{1,0:T(8,128)(2,1)S(1)}, f32[128,256]{1,0:T(8,128)S(1)}, f32[128,256]{1,0:T(8,128)S(1)}) custom-call(bf16[2,1024,512]{2,1,0:T(8,128)(2,1)S(1)} %get-tuple-element.19.upper, bf16[2,1024,512]{2,1,0:T(8,128)(2,1)S(1)} %get-tuple-element.22.lower, bf16[8,8,2,16,128]{4,3,2,1,0:T(8,128)(2,1)S(1)} %bitcast.3, ...), custom_call_target="tpu_custom_call" | custom-call | flops 2147483648 | bytes 4194304 | tf_op jit(solution)/shard_map/beam_other/pallas_call | solution.py:302
  30.6 0.6 collective-permute-start.1
  31.1 1.0 %collective-permute-done.1 = f32[128,256]{1,0:T(8,128)S(1)} collective-permute-done((f32[128,256]{1,0:T(8,128)S(1)}, f32[128,256]{1,0:T(8,128)S(1)}, u32[]{:S(2)}, u32[]{:S(2)}) %collective-permute-start.1) | collective-permute-done | bytes 131104 | tf_op jit(solution)/shard_map/ppermute | solution.py:242
  32.2 0.4 collective-permute-start.8
  32.6 1.7 %collective-permute-start.4 = (bf16[128,256]{1,0:T(8,128)(2,1)S(1)}, bf16[128,256]{1,0:T(8,128)(2,1)S(1)}, u32[]{:S(2)}, u32[]{:S(2)}) collective-permute-start(bf16[128,256]{1,0:T(8,128)(2,1)S(1)} %convert_element_type.15), channel_id=1, source_target_pairs={{0,32},{16,48},{32,0},{48,16},{64,96},{80,112},{96,64},{112,80},{1... | collective-permute-start | bytes 196616 | tf_op jit(solution)/shard_map/ppermute | solution.py:245
  34.3 1.4 %collective-permute-start.3 = (bf16[128,256]{1,0:T(8,128)(2,1)S(1)}, bf16[128,256]{1,0:T(8,128)(2,1)S(1)}, u32[]{:S(2)}, u32[]{:S(2)}) collective-permute-start(bf16[128,256]{1,0:T(8,128)(2,1)S(1)} %convert_element_type.15), channel_id=1, source_target_pairs={{0,48},{16,32},{32,16},{48,0},{64,112},{80,96},{96,80},{112,64},{1... | collective-permute-start | bytes 196616 | tf_op jit(solution)/shard_map/ppermute | solution.py:245
  35.7 0.5 collective-permute-start.2
  36.2 2.3 %collective-permute-done.4 = bf16[128,256]{1,0:T(8,128)(2,1)S(1)} collective-permute-done((bf16[128,256]{1,0:T(8,128)(2,1)S(1)}, bf16[128,256]{1,0:T(8,128)(2,1)S(1)}, u32[]{:S(2)}, u32[]{:S(2)}) %collective-permute-start.4) | collective-permute-done | bytes 65568 | tf_op jit(solution)/shard_map/ppermute | solution.py:245
  38.5 1.4 %collective-permute-done.3 = bf16[128,256]{1,0:T(8,128)(2,1)S(1)} collective-permute-done((bf16[128,256]{1,0:T(8,128)(2,1)S(1)}, bf16[128,256]{1,0:T(8,128)(2,1)S(1)}, u32[]{:S(2)}, u32[]{:S(2)}) %collective-permute-start.3) | collective-permute-done | bytes 65568 | tf_op jit(solution)/shard_map/ppermute | solution.py:245
  39.9 0.1 collective-permute-done.2
  40.0 0.1 collective-permute-start.6
  40.1 2.0 %collective-permute-start.7 = (bf16[128,256]{1,0:T(8,128)(2,1)S(1)}, bf16[128,256]{1,0:T(8,128)(2,1)S(1)}, u32[]{:S(2)}, u32[]{:S(2)}) collective-permute-start(bf16[128,256]{1,0:T(8,128)(2,1)S(1)} %get-tuple-element.29), channel_id=1, source_target_pairs={{0,65},{1,64},{16,81},{17,80},{32,97},{33,96},{48,113},{49,112},{6... | collective-permute-start | bytes 196616 | tf_op jit(solution)/shard_map/ppermute | solution.py:320
  42.1 1.7 %collective-permute-start.5 = (bf16[128,256]{1,0:T(8,128)(2,1)S(1)}, bf16[128,256]{1,0:T(8,128)(2,1)S(1)}, u32[]{:S(2)}, u32[]{:S(2)}) collective-permute-start(bf16[128,256]{1,0:T(8,128)(2,1)S(1)} %get-tuple-element.29), channel_id=1, source_target_pairs={{0,64},{16,80},{32,96},{48,112},{64,0},{80,16},{96,32},{112,48},{1... | collective-permute-start | bytes 196616 | tf_op jit(solution)/shard_map/ppermute | solution.py:245
  43.8 1.8 %collective-permute-done.7.far_twin = bf16[128,256]{1,0:T(8,128)(2,1)S(1)} collective-permute-done((bf16[128,256]{1,0:T(8,128)(2,1)S(1)}, bf16[128,256]{1,0:T(8,128)(2,1)S(1)}, u32[]{:S(2)}, u32[]{:S(2)}) %collective-permute-start.7) | collective-permute-done | bytes 65568 | tf_op jit(solution)/shard_map/ppermute | solution.py:320
  45.5 2.3 %collective-permute-done.5.far = bf16[128,256]{1,0:T(8,128)(2,1)S(1)} collective-permute-done((bf16[128,256]{1,0:T(8,128)(2,1)S(1)}, bf16[128,256]{1,0:T(8,128)(2,1)S(1)}, u32[]{:S(2)}, u32[]{:S(2)}) %collective-permute-start.5) | collective-permute-done | bytes 65568 | tf_op jit(solution)/shard_map/ppermute | solution.py:245
  47.9 0.0 collective-permute-done.6.twin
  47.9 0.0 collective-permute-done.8.peer_ref
  47.9 2.0 %filter.1 = bf16[8,2,16,2048]{3,2,1,0:T(8,128)(2,1)S(1)} custom-call(f32[128,256]{1,0:T(8,128)S(1)} %get-tuple-element.30.mine, bf16[128,256]{1,0:T(8,128)(2,1)S(1)} %collective-permute-done.5.far, f32[128,256]{1,0:T(8,128)S(1)} %collective-permute-done.6.twin, bf16[128,256]{1,0:T(8,128)(2,1)S(1)} %collective-permute-done.7.far_twin, ...), custom_call_target="tpu_custom_call" | custom-call | tf_op jit(solution)/shard_map/filter/pallas_call | solution.py:325
  49.9 17.7 %all_to_all.10.got = bf16[8,2,16,2048]{3,2,1,0:T(8,128)(2,1)S(1)} all-to-all(bf16[8,2,16,2048]{3,2,1,0:T(8,128)(2,1)S(1)} %filter.1), channel_id=1, replica_groups=mesh['chan'=8,'bin'=8,'core'=2] {'bin'}, dimensions={0} | all-to-all | bytes 2097152 | tf_op jit(solution)/shard_map/all_to_all | solution.py:335
  67.5 1.3 %place.1 = bf16[16,2,8,2048]{3,2,1,0:T(8,128)(2,1)} custom-call(bf16[8,2,16,2048]{3,2,1,0:T(8,128)(2,1)S(1)} %all_to_all.10.got), custom_call_target="tpu_custom_call" | custom-call | tf_op jit(solution)/shard_map/place/pallas_call | solution.py:336
  (3 shorter events, 0.1 us)
Async XLA Ops:
  1.8 24.5 %all-to-all-start = ((bf16[64,2,16,128]{3,2,1,0:T(8,128)(2,1)}), bf16[64,2,16,128]{3,2,1,0:T(8,128)(2,1)S(1)}, u32[]{:S(2)}, u32[]{:S(2)}) async-start(bf16[64,2,16,128]{3,2,1,0:T(8,128)(2,1)} %spread.1), calls=%async_computation | async-start | bytes 1048576 | tf_op jit(solution)/shard_map/all_to_all | solution.py:256
  26.2 2.4 %collective-permute-start = (bf16[64,2,16,128]{3,2,1,0:T(8,128)(2,1)S(1)}, bf16[64,2,16,128]{3,2,1,0:T(8,128)(2,1)S(1)}, u32[]{:S(2)}, u32[]{:S(2)}) collective-permute-start(bf16[64,2,16,128]{3,2,1,0:T(8,128)(2,1)S(1)} %all-to-all-done), channel_id=1, source_target_pairs={{0,1},{1,0},{2,3},{3,2},{4,5},{5,4},{6,7},{7,6},{8,9},{9,8},{10,11... | collective-permute-start | bytes 1572872 | tf_op jit(solution)/shard_map/ppermute | solution.py:242
  30.6 1.6 %collective-permute-start.1 = (f32[128,256]{1,0:T(8,128)S(1)}, f32[128,256]{1,0:T(8,128)S(1)}, u32[]{:S(2)}, u32[]{:S(2)}) collective-permute-start(f32[128,256]{1,0:T(8,128)S(1)} %get-tuple-element.25), channel_id=1, source_target_pairs={{0,1},{1,0},{2,3},{3,2},{4,5},{5,4},{6,7},{7,6},{8,9},{9,8},{10,11... | collective-permute-start | bytes 393224 | tf_op jit(solution)/shard_map/ppermute | solution.py:242
  32.2 15.7 %collective-permute-start.8 = (bf16[512,1024]{1,0:T(8,128)(2,1)S(1)}, bf16[512,1024]{1,0:T(8,128)(2,1)S(1)}, u32[]{:S(2)}, u32[]{:S(2)}) collective-permute-start(bf16[512,1024]{1,0:T(8,128)(2,1)S(1)} %get-tuple-element.28.y_ref), channel_id=1, source_target_pairs={{0,1},{1,0},{2,3},{3,2},{4,5},{5,4},{6,7},{7,6},{8,9},{9,8},{10,11... | collective-permute-start | bytes 3145736 | tf_op jit(solution)/shard_map/ppermute | solution.py:242
  32.6 5.9 %collective-permute-start.4 = (bf16[128,256]{1,0:T(8,128)(2,1)S(1)}, bf16[128,256]{1,0:T(8,128)(2,1)S(1)}, u32[]{:S(2)}, u32[]{:S(2)}) collective-permute-start(bf16[128,256]{1,0:T(8,128)(2,1)S(1)} %convert_element_type.15), channel_id=1, source_target_pairs={{0,32},{16,48},{32,0},{48,16},{64,96},{80,112},{96,64},{112,80},{1... | collective-permute-start | bytes 196616 | tf_op jit(solution)/shard_map/ppermute | solution.py:245
  34.3 5.6 %collective-permute-start.3 = (bf16[128,256]{1,0:T(8,128)(2,1)S(1)}, bf16[128,256]{1,0:T(8,128)(2,1)S(1)}, u32[]{:S(2)}, u32[]{:S(2)}) collective-permute-start(bf16[128,256]{1,0:T(8,128)(2,1)S(1)} %convert_element_type.15), channel_id=1, source_target_pairs={{0,48},{16,32},{32,16},{48,0},{64,112},{80,96},{96,80},{112,64},{1... | collective-permute-start | bytes 196616 | tf_op jit(solution)/shard_map/ppermute | solution.py:245
  35.7 4.3 %collective-permute-start.2 = (bf16[128,256]{1,0:T(8,128)(2,1)S(1)}, bf16[128,256]{1,0:T(8,128)(2,1)S(1)}, u32[]{:S(2)}, u32[]{:S(2)}) collective-permute-start(bf16[128,256]{1,0:T(8,128)(2,1)S(1)} %convert_element_type.15), channel_id=1, source_target_pairs={{0,16},{16,0},{32,48},{48,32},{64,80},{80,64},{96,112},{112,96},{1... | collective-permute-start | bytes 196616 | tf_op jit(solution)/shard_map/ppermute | solution.py:245
  40.0 7.8 %collective-permute-start.6 = (f32[128,256]{1,0:T(8,128)S(1)}, f32[128,256]{1,0:T(8,128)S(1)}, u32[]{:S(2)}, u32[]{:S(2)}) collective-permute-start(f32[128,256]{1,0:T(8,128)S(1)} %get-tuple-element.30.mine), channel_id=1, source_target_pairs={{0,1},{1,0},{2,3},{3,2},{4,5},{5,4},{6,7},{7,6},{8,9},{9,8},{10,11... | collective-permute-start | bytes 393224 | tf_op jit(solution)/shard_map/ppermute | solution.py:242
  40.1 5.4 %collective-permute-start.7 = (bf16[128,256]{1,0:T(8,128)(2,1)S(1)}, bf16[128,256]{1,0:T(8,128)(2,1)S(1)}, u32[]{:S(2)}, u32[]{:S(2)}) collective-permute-start(bf16[128,256]{1,0:T(8,128)(2,1)S(1)} %get-tuple-element.29), channel_id=1, source_target_pairs={{0,65},{1,64},{16,81},{17,80},{32,97},{33,96},{48,113},{49,112},{6... | collective-permute-start | bytes 196616 | tf_op jit(solution)/shard_map/ppermute | solution.py:320
  42.1 5.8 %collective-permute-start.5 = (bf16[128,256]{1,0:T(8,128)(2,1)S(1)}, bf16[128,256]{1,0:T(8,128)(2,1)S(1)}, u32[]{:S(2)}, u32[]{:S(2)}) collective-permute-start(bf16[128,256]{1,0:T(8,128)(2,1)S(1)} %get-tuple-element.29), channel_id=1, source_target_pairs={{0,64},{16,80},{32,96},{48,112},{64,0},{80,16},{96,32},{112,48},{1... | collective-permute-start | bytes 196616 | tf_op jit(solution)/shard_map/ppermute | solution.py:245

commit v11 on v10

--- a/solution.py
+++ b/solution.py
@@ -18,6 +18,7 @@
 ROUNDER = 12582912.0
 ROWS = 512
 LANES = 256
+IN_FLIGHT = 5
 WIDE = pltpu.CompilerParams(vmem_limit_bytes=16 * 1024 * 1024)
 VMEM = pl.BlockSpec(memory_space=pltpu.VMEM)
 HBM = pl.BlockSpec(memory_space=pltpu.HBM)
@@ -177,8 +178,9 @@
     return 0.5 * (packed + flipped), 0.5 * (packed - flipped), flipped
 
 
-def filter_kernel(mine, far, twin, far_twin, y_ref, peer_ref, out_ref, gram, kept):
+def filter_kernel(mine, far, twin, far_twin, y_ref, peer_ref, *refs):
     core = lax.axis_index("core")
+    *out_refs, gram, kept = refs
     half, frames = mine.shape
     gram[pl.ds(pl.multiple_of(core * half, half), half), :] = mine[...] + far[...].astype(F32)
     gram[pl.ds(pl.multiple_of((1 - core) * half, half), half), :] = twin[...] + far_twin[...].astype(F32)
@@ -195,32 +197,40 @@
     real, imag, _ = unpack(identity - factor * packed + 0.3 * second - 0.03 * third)
     kept[0] = real.astype(BF16)
     kept[1] = imag.astype(BF16)
-    real, imag = (kept[part, pl.ds(pl.multiple_of(core * half, half), half)] for part in range(2))
+    parts, group, _ = out_refs[0].shape
+    index = lax.axis_index("bin")
+    starts = [pl.multiple_of(core * half + (index ^ m) * group, group) for m in range(len(out_refs))]
+    real, imag = (
+        jnp.concatenate([kept[part, pl.ds(start, group)] for start in starts], axis=0) for part in range(parts)
+    )
     matrix = jnp.concatenate(
         [jnp.concatenate([real, imag], axis=1), jnp.concatenate([-imag, real], axis=1)], axis=0
     )
-    bins, parts, group, _ = out_ref.shape
     voxels = y_ref.shape[1]
     for source, place in ((y_ref, core), (peer_ref, 1 - core)):
         lanes = pl.ds(pl.multiple_of(place * voxels, voxels), voxels)
         applied = jnp.dot(matrix, source[...], preferred_element_type=F32).astype(BF16)
         for part in range(parts):
-            for j in range(bins):
-                row = part * half + j * group
-                out_ref[j, part, :, lanes] = applied[row : row + group]
-
-
-def place_kernel(got, out_ref, held, sems):
-    bins, parts, group, voxels = got.shape
+            for m, out_ref in enumerate(out_refs):
+                row = part * half + m * group
+                out_ref[part, :, lanes] = applied[row : row + group]
+
+
+def place_kernel(*refs):
+    *got, out_ref, held, sems = refs
+    bins = len(got)
+    parts, group, voxels = got[0].shape
     size = group * bins
     rows = lax.broadcasted_iota(jnp.int32, (size, size), 0)
     cols = lax.broadcasted_iota(jnp.int32, (size, size), 1)
-    turn = jnp.where(cols == (rows % bins) * group + rows // bins, 1.0, 0.0).astype(BF16)
+    slots = (rows % bins) ^ lax.axis_index("bin")
+    turn = jnp.where(cols == slots * group + rows // bins, 1.0, 0.0).astype(BF16)
     copies = [
         pltpu.make_async_copy(held.at[part], out_ref.at[:, part], sems.at[part]) for part in range(parts)
     ]
     for part in range(parts):
-        moved = jnp.dot(turn, got[:, part].reshape(size, voxels), preferred_element_type=F32).astype(BF16)
+        block = jnp.concatenate([piece[part] for piece in got], axis=0)
+        moved = jnp.dot(turn, block, preferred_element_type=F32).astype(BF16)
         held[part] = moved.reshape(group, bins, voxels)
         copies[part].start()
     for copy in copies:
@@ -322,29 +332,37 @@
     )
     twin = swap(total)
 
-    applied = pl.pallas_call(
+    pieces = pl.pallas_call(
         filter_kernel,
         name="filter",
-        out_shape=shape(bins, parts, group, CORES * voxels),
+        out_shape=(shape(parts, group, CORES * voxels),) * bins,
         in_specs=[VMEM] * 6,
-        out_specs=VMEM,
+        out_specs=(VMEM,) * bins,
         scratch_shapes=[pltpu.VMEM((frames, frames), F32), pltpu.VMEM((2, frames, frames), BF16)],
         compiler_params=WIDE,
     )(total, far, twin, far_twin, y, peer)
 
-    got = lax.all_to_all(applied, "bin", split_axis=0, concat_axis=0, tiled=True)
+    got = {0: pieces[0]}
+    order = [5, 4, 7, 3, 6, 2, 1]
+    for n, m in enumerate(order):
+        piece = pieces[m]
+        if n >= IN_FLIGHT:
+            earlier = order[n - IN_FLIGHT]
+            piece, got[earlier] = lax.optimization_barrier((piece, got[earlier]))
+        got[m] = lax.ppermute(piece, "bin", [(a, a ^ m) for a in range(bins)])
+
     return pl.pallas_call(
         place_kernel,
         name="place",
         out_shape=shape(group, parts, bins, CORES * voxels),
-        in_specs=[VMEM],
+        in_specs=[VMEM] * bins,
         out_specs=HBM,
         scratch_shapes=[
             pltpu.VMEM((parts, group, bins, CORES * voxels), BF16),
             pltpu.SemaphoreType.DMA((parts,)),
         ],
         compiler_params=WIDE,
-    )(got)
+    )(*(got[m] for m in range(bins)))
 
 
 def solution(mesh):

time: 69.2 us -> 69.5 us (level); the launches traced: 68.8 us -> 68.3 us
  blocking collectives: 17.7 us -> 0 us
  starting transfers between devices: 19.8 us -> 30.6 us
  waiting for transfers between devices: 15.6 us -> 21.9 us
    all_to_all x1 -> x0, blocking collectives: 17.7 us -> none  [shards(): lax.all_to_all(applied, 'bin', split_axis=0, concat_axis=0, tiled=True)]
    ppermute x0 -> x7, starting transfers between devices: none -> 10.8 us  [shards(): got[m] = lax.ppermute(piece, 'bin', [(a, a ^ m) for a in range(bins)])]
    ppermute x0 -> x7, waiting for transfers between devices: none -> 6.33 us  [shards(): got[m] = lax.ppermute(piece, 'bin', [(a, a ^ m) for a in range(bins)])]
  transfers between devices with their start and end apart: 10 -> 17, of which waited for: 7 -> 12; matrix products, arithmetic and copies ran while one was open for 0% -> 0% of each run, Pallas kernels for 13% -> 13%
where the time goes in v11:
time: 69.5 us; the launch traced here: 68.3 us
  starting transfers between devices  30.6 us (44%)
  waiting for transfers between devices  21.9 us (32%)
  Pallas kernels  15.6 us (22%)
    all_to_all x1, starting transfers between devices, shards(): lax.all_to_all(by_bin, ('chan', 'bin'), split_axis=0, concat_axis=0, tile...  11.5 us
    ppermute x7, starting transfers between devices, shards(): got[m] = lax.ppermute(piece, 'bin', [(a, a ^ m) for a in range(bins)])  10.8 us
    all_to_all x1, waiting for transfers between devices, shards(): lax.all_to_all(by_bin, ('chan', 'bin'), split_axis=0, concat_axis=0, tile...  6.71 us
    ppermute x7, waiting for transfers between devices, shards(): got[m] = lax.ppermute(piece, 'bin', [(a, a ^ m) for a in range(bins)])  6.33 us
    pallas_call x1, Pallas kernels, shards(): pl.pallas_call(operator_kernel, name='operator', out_shape=(shape(2, chan...  6.21 us
    ppermute x4, waiting for transfers between devices, across(): return lax.ppermute(x, 'chan', [(a, a ^ bits) for a in range(chans)])  6.13 us
    ppermute x4, starting transfers between devices, across(): return lax.ppermute(x, 'chan', [(a, a ^ bits) for a in range(chans)])  5.24 us
    pallas_call x1, Pallas kernels, shards(): pl.pallas_call(own_kernel, name='beam_own', out_shape=(shape(frames, voxe...  2.41 us
  transfers between devices with their start and end apart: 17, of which 12 were waited for; matrix products, arithmetic and copies ran while one was open for 0% of the time, Pallas kernels for 13%

profile of v11, /device:TPU:0, one launch (start us, length us, event | category | flops | bytes accessed | tf_op | source)
XLA Modules:
  0.0 68.3 jit_solution(9420990873523015636)
XLA Ops:
  0.0 1.8 %spread.1 = bf16[64,2,16,128]{3,2,1,0:T(8,128)(2,1)} custom-call(bf16[2,8,16,128]{3,2,1,0:T(8,128)(2,1)} %rf_ref.1), custom_call_target="tpu_custom_call" | custom-call | tf_op jit(solution)/shard_map/spread/pallas_call | solution.py:257
  1.8 11.5 %all-to-all-start = ((bf16[64,2,16,128]{3,2,1,0:T(8,128)(2,1)}), bf16[64,2,16,128]{3,2,1,0:T(8,128)(2,1)S(1)}, u32[]{:S(2)}, u32[]{:S(2)}) async-start(bf16[64,2,16,128]{3,2,1,0:T(8,128)(2,1)} %spread.1), calls=%async_computation | async-start | bytes 1048576 | tf_op jit(solution)/shard_map/all_to_all | solution.py:266
  13.3 6.2 %operator.1 = (bf16[2,1024,512]{2,1,0:T(8,128)(2,1)S(1)}, bf16[2,1024,512]{2,1,0:T(8,128)(2,1)}) custom-call(s32[3,1024]{1,0:T(4,128)} %elem_ref.1, s32[3,2048]{1,0:T(4,128)} %vox_ref.1, s32[8]{0:T(128)} %bins_ref.1), custom_call_target="tpu_custom_call" | custom-call | flops 62914560 | bytes 4194304 | tf_op jit(solution)/shard_map/operator/pallas_call | solution.py:269
  19.5 6.7 %all-to-all-done = bf16[64,2,16,128]{3,2,1,0:T(8,128)(2,1)S(1)} async-done(((bf16[64,2,16,128]{3,2,1,0:T(8,128)(2,1)}), bf16[64,2,16,128]{3,2,1,0:T(8,128)(2,1)S(1)}, u32[]{:S(2)}, u32[]{:S(2)}) %all-to-all-start) | async-done | bytes 524320 | tf_op jit(solution)/shard_map/all_to_all | solution.py:266
  26.2 2.4 %beam_own.1 = (bf16[256,1024]{1,0:T(8,128)(2,1)S(1)}, bf16[2,1024,512]{2,1,0:T(8,128)(2,1)S(1)}) custom-call(bf16[2,1024,512]{2,1,0:T(8,128)(2,1)S(1)} %get-tuple-element.31.upper, bf16[2,1024,512]{2,1,0:T(8,128)(2,1)} %get-tuple-element.32.lower_ref, bf16[8,8,2,16,128]{4,3,2,1,0:T(8,128)(2,1)S(1)} %bitcast.2), custom_call_target="tpu_custom_call" | custom-call | flops 2147483648 | bytes 4194304 | tf_op jit(solution)/shard_map/beam_own/pallas_call | solution.py:299
  28.7 1.9 %beam_other.1 = (bf16[512,1024]{1,0:T(8,128)(2,1)S(1)}, f32[128,256]{1,0:T(8,128)S(1)}, f32[128,256]{1,0:T(8,128)S(1)}) custom-call(bf16[2,1024,512]{2,1,0:T(8,128)(2,1)S(1)} %get-tuple-element.31.upper, bf16[2,1024,512]{2,1,0:T(8,128)(2,1)S(1)} %get-tuple-element.34.lower, bf16[8,8,2,16,128]{4,3,2,1,0:T(8,128)(2,1)S(1)} %bitcast.3, ...), custom_call_target="tpu_custom_call" | custom-call | flops 2147483648 | bytes 4194304 | tf_op jit(solution)/shard_map/beam_other/pallas_call | solution.py:312
  30.6 0.6 collective-permute-start.1
  31.1 1.0 %collective-permute-done.1 = f32[128,256]{1,0:T(8,128)S(1)} collective-permute-done((f32[128,256]{1,0:T(8,128)S(1)}, f32[128,256]{1,0:T(8,128)S(1)}, u32[]{:S(2)}, u32[]{:S(2)}) %collective-permute-start.1) | collective-permute-done | bytes 131104 | tf_op jit(solution)/shard_map/ppermute | solution.py:252
  32.2 0.4 collective-permute-start.8
  32.6 1.7 %collective-permute-start.4 = (bf16[128,256]{1,0:T(8,128)(2,1)S(1)}, bf16[128,256]{1,0:T(8,128)(2,1)S(1)}, u32[]{:S(2)}, u32[]{:S(2)}) collective-permute-start(bf16[128,256]{1,0:T(8,128)(2,1)S(1)} %convert_element_type.15), channel_id=1, source_target_pairs={{0,32},{16,48},{32,0},{48,16},{64,96},{80,112},{96,64},{112,80},{1... | collective-permute-start | bytes 196616 | tf_op jit(solution)/shard_map/ppermute | solution.py:255
  34.3 1.4 %collective-permute-start.3 = (bf16[128,256]{1,0:T(8,128)(2,1)S(1)}, bf16[128,256]{1,0:T(8,128)(2,1)S(1)}, u32[]{:S(2)}, u32[]{:S(2)}) collective-permute-start(bf16[128,256]{1,0:T(8,128)(2,1)S(1)} %convert_element_type.15), channel_id=1, source_target_pairs={{0,48},{16,32},{32,16},{48,0},{64,112},{80,96},{96,80},{112,64},{1... | collective-permute-start | bytes 196616 | tf_op jit(solution)/shard_map/ppermute | solution.py:255
  35.7 0.5 collective-permute-start.2
  36.2 2.3 %collective-permute-done.4 = bf16[128,256]{1,0:T(8,128)(2,1)S(1)} collective-permute-done((bf16[128,256]{1,0:T(8,128)(2,1)S(1)}, bf16[128,256]{1,0:T(8,128)(2,1)S(1)}, u32[]{:S(2)}, u32[]{:S(2)}) %collective-permute-start.4) | collective-permute-done | bytes 65568 | tf_op jit(solution)/shard_map/ppermute | solution.py:255
  38.5 1.4 %collective-permute-done.3 = bf16[128,256]{1,0:T(8,128)(2,1)S(1)} collective-permute-done((bf16[128,256]{1,0:T(8,128)(2,1)S(1)}, bf16[128,256]{1,0:T(8,128)(2,1)S(1)}, u32[]{:S(2)}, u32[]{:S(2)}) %collective-permute-start.3) | collective-permute-done | bytes 65568 | tf_op jit(solution)/shard_map/ppermute | solution.py:255
  40.1 2.0 %collective-permute-start.7 = (bf16[128,256]{1,0:T(8,128)(2,1)S(1)}, bf16[128,256]{1,0:T(8,128)(2,1)S(1)}, u32[]{:S(2)}, u32[]{:S(2)}) collective-permute-start(bf16[128,256]{1,0:T(8,128)(2,1)S(1)} %get-tuple-element.53), channel_id=1, source_target_pairs={{0,65},{1,64},{16,81},{17,80},{32,97},{33,96},{48,113},{49,112},{6... | collective-permute-start | bytes 196616 | tf_op jit(solution)/shard_map/ppermute | solution.py:330
  42.1 1.7 %collective-permute-start.5 = (bf16[128,256]{1,0:T(8,128)(2,1)S(1)}, bf16[128,256]{1,0:T(8,128)(2,1)S(1)}, u32[]{:S(2)}, u32[]{:S(2)}) collective-permute-start(bf16[128,256]{1,0:T(8,128)(2,1)S(1)} %get-tuple-element.53), channel_id=1, source_target_pairs={{0,64},{16,80},{32,96},{48,112},{64,0},{80,16},{96,32},{112,48},{1... | collective-permute-start | bytes 196616 | tf_op jit(solution)/shard_map/ppermute | solution.py:255
  43.8 1.8 %collective-permute-done.7.far_twin = bf16[128,256]{1,0:T(8,128)(2,1)S(1)} collective-permute-done((bf16[128,256]{1,0:T(8,128)(2,1)S(1)}, bf16[128,256]{1,0:T(8,128)(2,1)S(1)}, u32[]{:S(2)}, u32[]{:S(2)}) %collective-permute-start.7) | collective-permute-done | bytes 65568 | tf_op jit(solution)/shard_map/ppermute | solution.py:330
  45.5 2.3 %collective-permute-done.5.far = bf16[128,256]{1,0:T(8,128)(2,1)S(1)} collective-permute-done((bf16[128,256]{1,0:T(8,128)(2,1)S(1)}, bf16[128,256]{1,0:T(8,128)(2,1)S(1)}, u32[]{:S(2)}, u32[]{:S(2)}) %collective-permute-start.5) | collective-permute-done | bytes 65568 | tf_op jit(solution)/shard_map/ppermute | solution.py:255
  47.9 2.0 %filter.1 = (bf16[2,16,2048]{2,1,0:T(8,128)(2,1)S(1)}, bf16[2,16,2048]{2,1,0:T(8,128)(2,1)S(1)}, bf16[2,16,2048]{2,1,0:T(8,128)(2,1)S(1)}, bf16[2,16,2048]{2,1,0...) custom-call(f32[128,256]{1,0:T(8,128)S(1)} %get-tuple-element.54.min, ...), custom_call_target="tpu_custom_call" | custom-call | tf_op jit(solution)/shard_map/filter/pallas_call | solution.py:335
  49.9 1.1 %collective-permute-start.9 = (bf16[2,16,2048]{2,1,0:T(8,128)(2,1)S(1)}, bf16[2,16,2048]{2,1,0:T(8,128)(2,1)S(1)}, u32[]{:S(2)}, u32[]{:S(2)}) collective-permute-start(bf16[2,16,2048]{2,1,0:T(8,128)(2,1)S(1)} %get-tuple-element.43), channel_id=1, source_target_pairs={{0,8},{2,10},{4,12},{6,14},{8,0},{10,2},{12,4},{14,6},{1,9},{3,11}... | collective-permute-start | bytes 393224 | tf_op jit(solution)/shard_map/ppermute | solution.py:352
  51.0 2.1 %collective-permute-start.11 = (bf16[2,16,2048]{2,1,0:T(8,128)(2,1)S(1)}, bf16[2,16,2048]{2,1,0:T(8,128)(2,1)S(1)}, u32[]{:S(2)}, u32[]{:S(2)}) collective-permute-start(bf16[2,16,2048]{2,1,0:T(8,128)(2,1)S(1)} %get-tuple-element.46), channel_id=1, source_target_pairs={{0,10},{2,8},{4,14},{6,12},{8,2},{10,0},{12,6},{14,4},{1,11},{3,9}... | collective-permute-start | bytes 393224 | tf_op jit(solution)/shard_map/ppermute | solution.py:352
  53.0 2.0 %collective-permute-start.13 = (bf16[2,16,2048]{2,1,0:T(8,128)(2,1)S(1)}, bf16[2,16,2048]{2,1,0:T(8,128)(2,1)S(1)}, u32[]{:S(2)}, u32[]{:S(2)}) collective-permute-start(bf16[2,16,2048]{2,1,0:T(8,128)(2,1)S(1)} %get-tuple-element.48), channel_id=1, source_target_pairs={{0,6},{2,4},{4,2},{6,0},{8,14},{10,12},{12,10},{14,8},{1,7},{3,5},... | collective-permute-start | bytes 393224 | tf_op jit(solution)/shard_map/ppermute | solution.py:352
  55.0 0.9 %collective-permute-start.14 = (bf16[2,16,2048]{2,1,0:T(8,128)(2,1)S(1)}, bf16[2,16,2048]{2,1,0:T(8,128)(2,1)S(1)}, u32[]{:S(2)}, u32[]{:S(2)}) collective-permute-start(bf16[2,16,2048]{2,1,0:T(8,128)(2,1)S(1)} %get-tuple-element.51), channel_id=1, source_target_pairs={{0,12},{2,14},{4,8},{6,10},{8,4},{10,6},{12,0},{14,2},{1,13},{3,15... | collective-permute-start | bytes 393224 | tf_op jit(solution)/shard_map/ppermute | solution.py:352
  56.0 1.9 %collective-permute-start.15 = (bf16[2,16,2048]{2,1,0:T(8,128)(2,1)S(1)}, bf16[2,16,2048]{2,1,0:T(8,128)(2,1)S(1)}, u32[]{:S(2)}, u32[]{:S(2)}) collective-permute-start(bf16[2,16,2048]{2,1,0:T(8,128)(2,1)S(1)} %get-tuple-element.52), channel_id=1, source_target_pairs={{0,14},{2,12},{4,10},{6,8},{8,6},{10,4},{12,2},{14,0},{1,15},{3,13... | collective-permute-start | bytes 393224 | tf_op jit(solution)/shard_map/ppermute | solution.py:352
  57.8 1.9 %collective-permute-start.10 = (bf16[2,16,2048]{2,1,0:T(8,128)(2,1)S(1)}, bf16[2,16,2048]{2,1,0:T(8,128)(2,1)S(1)}, u32[]{:S(2)}, u32[]{:S(2)}) collective-permute-start(bf16[2,16,2048]{2,1,0:T(8,128)(2,1)S(1)} %get-tuple-element.44), channel_id=1, source_target_pairs={{0,2},{2,0},{4,6},{6,4},{8,10},{10,8},{12,14},{14,12},{1,3},{3,1},... | collective-permute-start | bytes 393224 | tf_op jit(solution)/shard_map/ppermute | solution.py:352
  59.7 1.0 %collective-permute-done.11.refs_5_ = bf16[2,16,2048]{2,1,0:T(8,128)(2,1)S(1)} collective-permute-done((bf16[2,16,2048]{2,1,0:T(8,128)(2,1)S(1)}, bf16[2,16,2048]{2,1,0:T(8,128)(2,1)S(1)}, u32[]{:S(2)}, u32[]{:S(2)}) %collective-permute-start.11) | collective-permute-done | bytes 131104 | tf_op jit(solution)/shard_map/ppermute | solution.py:352
  60.7 0.9 %collective-permute-start.12 = (bf16[2,16,2048]{2,1,0:T(8,128)(2,1)S(1)}, bf16[2,16,2048]{2,1,0:T(8,128)(2,1)S(1)}, u32[]{:S(2)}, u32[]{:S(2)}) collective-permute-start(bf16[2,16,2048]{2,1,0:T(8,128)(2,1)S(1)} %get-tuple-element.47), channel_id=1, source_target_pairs={{0,4},{2,6},{4,0},{6,2},{8,12},{10,14},{12,8},{14,10},{1,5},{3,7},... | collective-permute-start | bytes 393224 | tf_op jit(solution)/shard_map/ppermute | solution.py:352
  61.6 0.2 collective-permute-done.13.refs_3_
  61.9 1.0 %collective-permute-done.14.refs_6_ = bf16[2,16,2048]{2,1,0:T(8,128)(2,1)S(1)} collective-permute-done((bf16[2,16,2048]{2,1,0:T(8,128)(2,1)S(1)}, bf16[2,16,2048]{2,1,0:T(8,128)(2,1)S(1)}, u32[]{:S(2)}, u32[]{:S(2)}) %collective-permute-start.14) | collective-permute-done | bytes 131104 | tf_op jit(solution)/shard_map/ppermute | solution.py:352
  62.9 1.6 %collective-permute-done.15.refs_7_ = bf16[2,16,2048]{2,1,0:T(8,128)(2,1)S(1)} collective-permute-done((bf16[2,16,2048]{2,1,0:T(8,128)(2,1)S(1)}, bf16[2,16,2048]{2,1,0:T(8,128)(2,1)S(1)}, u32[]{:S(2)}, u32[]{:S(2)}) %collective-permute-start.15) | collective-permute-done | bytes 131104 | tf_op jit(solution)/shard_map/ppermute | solution.py:352
  64.5 2.5 %collective-permute-done.10.refs_1_ = bf16[2,16,2048]{2,1,0:T(8,128)(2,1)S(1)} collective-permute-done((bf16[2,16,2048]{2,1,0:T(8,128)(2,1)S(1)}, bf16[2,16,2048]{2,1,0:T(8,128)(2,1)S(1)}, u32[]{:S(2)}, u32[]{:S(2)}) %collective-permute-start.10) | collective-permute-done | bytes 131104 | tf_op jit(solution)/shard_map/ppermute | solution.py:352
  67.0 1.3 %place.1 = bf16[16,2,8,2048]{3,2,1,0:T(8,128)(2,1)} custom-call(bf16[2,16,2048]{2,1,0:T(8,128)(2,1)S(1)} %get-tuple-element.41.refs_0_, bf16[2,16,2048]{2,1,0:T(8,128)(2,1)S(1)} %collective-permute-done.10.refs_1_, bf16[2,16,2048]{2,1,0:T(8,128)(2,1)S(1)} %collective-permute-done.12.refs_2_, bf16[2,16,2048]{2,1,0:T(8,128)(2,1)S(1)} %collective-permute-done.13.refs_3_, ...), custom_call_target="tpu_custom_call" | custom-call | tf_op jit(solution)/shard_map/place/pallas_call | solution.py:354
  (11 shorter events, 0.3 us)
Async XLA Ops:
  1.8 24.5 %all-to-all-start = ((bf16[64,2,16,128]{3,2,1,0:T(8,128)(2,1)}), bf16[64,2,16,128]{3,2,1,0:T(8,128)(2,1)S(1)}, u32[]{:S(2)}, u32[]{:S(2)}) async-start(bf16[64,2,16,128]{3,2,1,0:T(8,128)(2,1)} %spread.1), calls=%async_computation | async-start | bytes 1048576 | tf_op jit(solution)/shard_map/all_to_all | solution.py:266
  26.2 2.4 %collective-permute-start = (bf16[64,2,16,128]{3,2,1,0:T(8,128)(2,1)S(1)}, bf16[64,2,16,128]{3,2,1,0:T(8,128)(2,1)S(1)}, u32[]{:S(2)}, u32[]{:S(2)}) collective-permute-start(bf16[64,2,16,128]{3,2,1,0:T(8,128)(2,1)S(1)} %all-to-all-done), channel_id=1, source_target_pairs={{0,1},{1,0},{2,3},{3,2},{4,5},{5,4},{6,7},{7,6},{8,9},{9,8},{10,11... | collective-permute-start | bytes 1572872 | tf_op jit(solution)/shard_map/ppermute | solution.py:252
  30.6 1.6 %collective-permute-start.1 = (f32[128,256]{1,0:T(8,128)S(1)}, f32[128,256]{1,0:T(8,128)S(1)}, u32[]{:S(2)}, u32[]{:S(2)}) collective-permute-start(f32[128,256]{1,0:T(8,128)S(1)} %get-tuple-element.37), channel_id=1, source_target_pairs={{0,1},{1,0},{2,3},{3,2},{4,5},{5,4},{6,7},{7,6},{8,9},{9,8},{10,11... | collective-permute-start | bytes 393224 | tf_op jit(solution)/shard_map/ppermute | solution.py:252
  32.2 15.7 %collective-permute-start.8 = (bf16[512,1024]{1,0:T(8,128)(2,1)S(1)}, bf16[512,1024]{1,0:T(8,128)(2,1)S(1)}, u32[]{:S(2)}, u32[]{:S(2)}) collective-permute-start(bf16[512,1024]{1,0:T(8,128)(2,1)S(1)} %get-tuple-element.40.y_ref), channel_id=1, source_target_pairs={{0,1},{1,0},{2,3},{3,2},{4,5},{5,4},{6,7},{7,6},{8,9},{9,8},{10,11... | collective-permute-start | bytes 3145736 | tf_op jit(solution)/shard_map/ppermute | solution.py:252
  32.6 5.9 %collective-permute-start.4 = (bf16[128,256]{1,0:T(8,128)(2,1)S(1)}, bf16[128,256]{1,0:T(8,128)(2,1)S(1)}, u32[]{:S(2)}, u32[]{:S(2)}) collective-permute-start(bf16[128,256]{1,0:T(8,128)(2,1)S(1)} %convert_element_type.15), channel_id=1, source_target_pairs={{0,32},{16,48},{32,0},{48,16},{64,96},{80,112},{96,64},{112,80},{1... | collective-permute-start | bytes 196616 | tf_op jit(solution)/shard_map/ppermute | solution.py:255
  34.3 5.6 %collective-permute-start.3 = (bf16[128,256]{1,0:T(8,128)(2,1)S(1)}, bf16[128,256]{1,0:T(8,128)(2,1)S(1)}, u32[]{:S(2)}, u32[]{:S(2)}) collective-permute-start(bf16[128,256]{1,0:T(8,128)(2,1)S(1)} %convert_element_type.15), channel_id=1, source_target_pairs={{0,48},{16,32},{32,16},{48,0},{64,112},{80,96},{96,80},{112,64},{1... | collective-permute-start | bytes 196616 | tf_op jit(solution)/shard_map/ppermute | solution.py:255
  35.7 4.3 %collective-permute-start.2 = (bf16[128,256]{1,0:T(8,128)(2,1)S(1)}, bf16[128,256]{1,0:T(8,128)(2,1)S(1)}, u32[]{:S(2)}, u32[]{:S(2)}) collective-permute-start(bf16[128,256]{1,0:T(8,128)(2,1)S(1)} %convert_element_type.15), channel_id=1, source_target_pairs={{0,16},{16,0},{32,48},{48,32},{64,80},{80,64},{96,112},{112,96},{1... | collective-permute-start | bytes 196616 | tf_op jit(solution)/shard_map/ppermute | solution.py:255
  40.0 7.8 %collective-permute-start.6 = (f32[128,256]{1,0:T(8,128)S(1)}, f32[128,256]{1,0:T(8,128)S(1)}, u32[]{:S(2)}, u32[]{:S(2)}) collective-permute-start(f32[128,256]{1,0:T(8,128)S(1)} %get-tuple-element.54.mine), channel_id=1, source_target_pairs={{0,1},{1,0},{2,3},{3,2},{4,5},{5,4},{6,7},{7,6},{8,9},{9,8},{10,11... | collective-permute-start | bytes 393224 | tf_op jit(solution)/shard_map/ppermute | solution.py:252
  40.1 5.4 %collective-permute-start.7 = (bf16[128,256]{1,0:T(8,128)(2,1)S(1)}, bf16[128,256]{1,0:T(8,128)(2,1)S(1)}, u32[]{:S(2)}, u32[]{:S(2)}) collective-permute-start(bf16[128,256]{1,0:T(8,128)(2,1)S(1)} %get-tuple-element.53), channel_id=1, source_target_pairs={{0,65},{1,64},{16,81},{17,80},{32,97},{33,96},{48,113},{49,112},{6... | collective-permute-start | bytes 196616 | tf_op jit(solution)/shard_map/ppermute | solution.py:330
  42.1 5.8 %collective-permute-start.5 = (bf16[128,256]{1,0:T(8,128)(2,1)S(1)}, bf16[128,256]{1,0:T(8,128)(2,1)S(1)}, u32[]{:S(2)}, u32[]{:S(2)}) collective-permute-start(bf16[128,256]{1,0:T(8,128)(2,1)S(1)} %get-tuple-element.53), channel_id=1, source_target_pairs={{0,64},{16,80},{32,96},{48,112},{64,0},{80,16},{96,32},{112,48},{1... | collective-permute-start | bytes 196616 | tf_op jit(solution)/shard_map/ppermute | solution.py:255
  49.9 8.0 %collective-permute-start.9 = (bf16[2,16,2048]{2,1,0:T(8,128)(2,1)S(1)}, bf16[2,16,2048]{2,1,0:T(8,128)(2,1)S(1)}, u32[]{:S(2)}, u32[]{:S(2)}) collective-permute-start(bf16[2,16,2048]{2,1,0:T(8,128)(2,1)S(1)} %get-tuple-element.43), channel_id=1, source_target_pairs={{0,8},{2,10},{4,12},{6,14},{8,0},{10,2},{12,4},{14,6},{1,9},{3,11}... | collective-permute-start | bytes 393224 | tf_op jit(solution)/shard_map/ppermute | solution.py:352
  51.0 9.7 %collective-permute-start.11 = (bf16[2,16,2048]{2,1,0:T(8,128)(2,1)S(1)}, bf16[2,16,2048]{2,1,0:T(8,128)(2,1)S(1)}, u32[]{:S(2)}, u32[]{:S(2)}) collective-permute-start(bf16[2,16,2048]{2,1,0:T(8,128)(2,1)S(1)} %get-tuple-element.46), channel_id=1, source_target_pairs={{0,10},{2,8},{4,14},{6,12},{8,2},{10,0},{12,6},{14,4},{1,11},{3,9}... | collective-permute-start | bytes 393224 | tf_op jit(solution)/shard_map/ppermute | solution.py:352
  53.0 8.8 %collective-permute-start.13 = (bf16[2,16,2048]{2,1,0:T(8,128)(2,1)S(1)}, bf16[2,16,2048]{2,1,0:T(8,128)(2,1)S(1)}, u32[]{:S(2)}, u32[]{:S(2)}) collective-permute-start(bf16[2,16,2048]{2,1,0:T(8,128)(2,1)S(1)} %get-tuple-element.48), channel_id=1, source_target_pairs={{0,6},{2,4},{4,2},{6,0},{8,14},{10,12},{12,10},{14,8},{1,7},{3,5},... | collective-permute-start | bytes 393224 | tf_op jit(solution)/shard_map/ppermute | solution.py:352
  55.0 7.9 %collective-permute-start.14 = (bf16[2,16,2048]{2,1,0:T(8,128)(2,1)S(1)}, bf16[2,16,2048]{2,1,0:T(8,128)(2,1)S(1)}, u32[]{:S(2)}, u32[]{:S(2)}) collective-permute-start(bf16[2,16,2048]{2,1,0:T(8,128)(2,1)S(1)} %get-tuple-element.51), channel_id=1, source_target_pairs={{0,12},{2,14},{4,8},{6,10},{8,4},{10,6},{12,0},{14,2},{1,13},{3,15... | collective-permute-start | bytes 393224 | tf_op jit(solution)/shard_map/ppermute | solution.py:352
  56.0 8.5 %collective-permute-start.15 = (bf16[2,16,2048]{2,1,0:T(8,128)(2,1)S(1)}, bf16[2,16,2048]{2,1,0:T(8,128)(2,1)S(1)}, u32[]{:S(2)}, u32[]{:S(2)}) collective-permute-start(bf16[2,16,2048]{2,1,0:T(8,128)(2,1)S(1)} %get-tuple-element.52), channel_id=1, source_target_pairs={{0,14},{2,12},{4,10},{6,8},{8,6},{10,4},{12,2},{14,0},{1,15},{3,13... | collective-permute-start | bytes 393224 | tf_op jit(solution)/shard_map/ppermute | solution.py:352
  57.8 9.2 %collective-permute-start.10 = (bf16[2,16,2048]{2,1,0:T(8,128)(2,1)S(1)}, bf16[2,16,2048]{2,1,0:T(8,128)(2,1)S(1)}, u32[]{:S(2)}, u32[]{:S(2)}) collective-permute-start(bf16[2,16,2048]{2,1,0:T(8,128)(2,1)S(1)} %get-tuple-element.44), channel_id=1, source_target_pairs={{0,2},{2,0},{4,6},{6,4},{8,10},{10,8},{12,14},{14,12},{1,3},{3,1},... | collective-permute-start | bytes 393224 | tf_op jit(solution)/shard_map/ppermute | solution.py:352
  60.7 6.3 %collective-permute-start.12 = (bf16[2,16,2048]{2,1,0:T(8,128)(2,1)S(1)}, bf16[2,16,2048]{2,1,0:T(8,128)(2,1)S(1)}, u32[]{:S(2)}, u32[]{:S(2)}) collective-permute-start(bf16[2,16,2048]{2,1,0:T(8,128)(2,1)S(1)} %get-tuple-element.47), channel_id=1, source_target_pairs={{0,4},{2,6},{4,0},{6,2},{8,12},{10,14},{12,8},{14,10},{1,5},{3,7},... | collective-permute-start | bytes 393224 | tf_op jit(solution)/shard_map/ppermute | solution.py:352

commit v12 on v10

--- a/solution.py
+++ b/solution.py
@@ -136,7 +136,7 @@
         out_ref[:half, lanes], out_ref[half:, lanes] = real, imag
 
 
-def other_kernel(upper, lower, samples, own, y_ref, keep_ref, send_ref, data, gram):
+def other_kernel(upper, lower, samples, own, y_ref, gram_ref, data):
     core = lax.axis_index("core")
     frames = y_ref.shape[0] // 2
     half = frames // CORES
@@ -150,11 +150,9 @@
             y_ref[pl.ds(there, half), lanes], y_ref[pl.ds(frames + there, half), lanes] = real, imag
     y = y_ref[...]
     products = lax.dot_general(y, y, (((1,), (1,)), ((), ())), preferred_element_type=F32)
-    gram[...] = (products[:frames, :frames] + products[frames:, frames:]) + (
+    gram_ref[...] = (products[:frames, :frames] + products[frames:, frames:]) + (
         products[:frames, frames:] - products[frames:, :frames]
     )
-    keep_ref[...] = gram[pl.ds(here, half), :]
-    send_ref[...] = gram[pl.ds(there, half), :]
 
 
 def halves(x):
@@ -177,12 +175,11 @@
     return 0.5 * (packed + flipped), 0.5 * (packed - flipped), flipped
 
 
-def filter_kernel(mine, far, twin, far_twin, y_ref, peer_ref, out_ref, gram, kept):
+def filter_kernel(near, far, y_ref, peer_ref, out_ref, kept):
     core = lax.axis_index("core")
-    half, frames = mine.shape
-    gram[pl.ds(pl.multiple_of(core * half, half), half), :] = mine[...] + far[...].astype(F32)
-    gram[pl.ds(pl.multiple_of((1 - core) * half, half), half), :] = twin[...] + far_twin[...].astype(F32)
-    packed = gram[...]
+    frames = near.shape[0]
+    half = frames // CORES
+    packed = near[...] + far[...].astype(F32)
     squares = jnp.sum(packed * packed)
     factor = 4.0 / jnp.sqrt(jnp.full((1, 1), squares + EPSILON, F32))
     real, imag, flipped = unpack(packed)
@@ -241,9 +238,6 @@
     def swap(x):
         return lax.ppermute(x, "core", [(0, 1), (1, 0)])
 
-    def across(x, bits):
-        return lax.ppermute(x, "chan", [(a, a ^ bits) for a in range(chans)])
-
     by_bin = pl.pallas_call(
         spread_kernel,
         name="spread",
@@ -299,38 +293,37 @@
         compiler_params=WIDE,
         cost_estimate=beam_cost,
     )(upper, pltpu.with_memory_space_constraint(lower, pltpu.HBM), own)
-    y, keep, send = pl.pallas_call(
+    y, gram = pl.pallas_call(
         other_kernel,
         name="beam_other",
-        out_shape=(shape(2 * frames, voxels), shape(half, frames, dtype=F32), shape(half, frames, dtype=F32)),
+        out_shape=(shape(2 * frames, voxels), shape(frames, frames, dtype=F32)),
         in_specs=[VMEM, VMEM, VMEM, VMEM],
-        out_specs=(VMEM, VMEM, VMEM),
-        scratch_shapes=[pltpu.VMEM((frames, channels), BF16), pltpu.VMEM((frames, frames), F32)],
+        out_specs=(VMEM, VMEM),
+        scratch_shapes=[pltpu.VMEM((frames, channels), BF16)],
         compiler_params=WIDE,
         cost_estimate=beam_cost,
     )(upper, lower, other, mine)
 
-    total = keep + swap(send)
+    total = gram + swap(gram)
     total, y = lax.optimization_barrier((total, y))
     peer = swap(y)
     narrow = total.astype(BF16)
-    total = total + sum(across(narrow, bits).astype(F32) for bits in (1, 3, 2))
-    narrow = total.astype(BF16)
-    far = across(narrow, 4)
-    far_twin = lax.ppermute(
-        narrow, ("chan", "core"), [(2 * a + c, 2 * (a ^ 4) + 1 - c) for a in range(chans) for c in range(CORES)]
-    )
-    twin = swap(total)
+    beside = lax.ppermute(
+        narrow, ("chan", "core"), [(2 * a + c, 2 * (a ^ (3 if c else 1)) + c) for a in range(chans) for c in range(CORES)]
+    )
+    across = lax.ppermute(narrow, "chan", [(a, a ^ 2) for a in range(chans)])
+    total = total + (beside.astype(F32) + swap(beside).astype(F32)) + across.astype(F32)
+    far = lax.ppermute(total.astype(BF16), "chan", [(a, a ^ 4) for a in range(chans)])
 
     applied = pl.pallas_call(
         filter_kernel,
         name="filter",
         out_shape=shape(bins, parts, group, CORES * voxels),
-        in_specs=[VMEM] * 6,
+        in_specs=[VMEM] * 4,
         out_specs=VMEM,
-        scratch_shapes=[pltpu.VMEM((frames, frames), F32), pltpu.VMEM((2, frames, frames), BF16)],
-        compiler_params=WIDE,
-    )(total, far, twin, far_twin, y, peer)
+        scratch_shapes=[pltpu.VMEM((2, frames, frames), BF16)],
+        compiler_params=WIDE,
+    )(total, far, y, peer)
 
     got = lax.all_to_all(applied, "bin", split_axis=0, concat_axis=0, tiled=True)
     return pl.pallas_call(

time: 69.2 us -> 70.8 us (1.023)
  waiting for transfers between devices: 15.6 us -> 18.6 us
  starting transfers between devices: 19.8 us -> 17.5 us
  blocking collectives: 17.7 us -> 18.6 us
    ppermute x5 -> x3, waiting for transfers between devices: 7.9 us -> 10.7 us  [the longest x1 4.97 us: shards(): lax.ppermute(total.astype(BF16), 'chan', [(a, a ^ 4) for a in range(chans)])]
    ppermute x5 -> x3, starting transfers between devices: 7.21 us -> 5 us  [the longest x1 2.91 us: shards(): across = lax.ppermute(narrow, 'chan', [(a, a ^ 2) for a in range(chans)])]
    all_to_all x1, blocking collectives: 17.7 us -> 18.6 us  [shards(): lax.all_to_all(applied, 'bin', split_axis=0, concat_axis=0, tiled=True)]
  transfers between devices with their start and end apart: 10 -> 8, of which waited for: 7 -> 5; matrix products, arithmetic and copies ran while one was open for 0% -> 0% of each run, Pallas kernels for 13% -> 12%
where the time goes in v12:
time: 70.8 us; the launch traced here: 70.4 us
  waiting for transfers between devices  18.6 us (26%)
  blocking collectives  18.6 us (26%)
  starting transfers between devices  17.5 us (25%)
  Pallas kernels  15.5 us (22%)
    all_to_all x1, blocking collectives, shards(): lax.all_to_all(applied, 'bin', split_axis=0, concat_axis=0, tiled=True)  18.6 us
    all_to_all x1, starting transfers between devices, shards(): lax.all_to_all(by_bin, ('chan', 'bin'), split_axis=0, concat_axis=0, tile...  11.5 us
    all_to_all x1, waiting for transfers between devices, shards(): lax.all_to_all(by_bin, ('chan', 'bin'), split_axis=0, concat_axis=0, tile...  6.71 us
    pallas_call x1, Pallas kernels, shards(): pl.pallas_call(operator_kernel, name='operator', out_shape=(shape(2, chan...  6.21 us
    ppermute x1, waiting for transfers between devices, shards(): lax.ppermute(total.astype(BF16), 'chan', [(a, a ^ 4) for a in range(chans)])  4.97 us
    ppermute x1, waiting for transfers between devices, shards(): across = lax.ppermute(narrow, 'chan', [(a, a ^ 2) for a in range(chans)])  3.58 us
    ppermute x1, starting transfers between devices, shards(): across = lax.ppermute(narrow, 'chan', [(a, a ^ 2) for a in range(chans)])  2.91 us
    pallas_call x1, Pallas kernels, shards(): pl.pallas_call(own_kernel, name='beam_own', out_shape=(shape(frames, voxe...  2.41 us
  transfers between devices with their start and end apart: 8, of which 5 were waited for; matrix products, arithmetic and copies ran while one was open for 0% of the time, Pallas kernels for 12%

profile of v12, /device:TPU:0, one launch (start us, length us, event | category | flops | bytes accessed | tf_op | source)
XLA Modules:
  0.0 70.4 jit_solution(8079910043719749732)
XLA Ops:
  0.0 1.8 %spread.1 = bf16[64,2,16,128]{3,2,1,0:T(8,128)(2,1)} custom-call(bf16[2,8,16,128]{3,2,1,0:T(8,128)(2,1)} %rf_ref.1), custom_call_target="tpu_custom_call" | custom-call | tf_op jit(solution)/shard_map/spread/pallas_call | solution.py:241
  1.8 11.5 %all-to-all-start = ((bf16[64,2,16,128]{3,2,1,0:T(8,128)(2,1)}), bf16[64,2,16,128]{3,2,1,0:T(8,128)(2,1)S(1)}, u32[]{:S(2)}, u32[]{:S(2)}) async-start(bf16[64,2,16,128]{3,2,1,0:T(8,128)(2,1)} %spread.1), calls=%async_computation | async-start | bytes 1048576 | tf_op jit(solution)/shard_map/all_to_all | solution.py:250
  13.3 6.2 %operator.1 = (bf16[2,1024,512]{2,1,0:T(8,128)(2,1)S(1)}, bf16[2,1024,512]{2,1,0:T(8,128)(2,1)}) custom-call(s32[3,1024]{1,0:T(4,128)} %elem_ref.1, s32[3,2048]{1,0:T(4,128)} %vox_ref.1, s32[8]{0:T(128)} %bins_ref.1), custom_call_target="tpu_custom_call" | custom-call | flops 62914560 | bytes 4194304 | tf_op jit(solution)/shard_map/operator/pallas_call | solution.py:253
  19.5 6.7 %all-to-all-done = bf16[64,2,16,128]{3,2,1,0:T(8,128)(2,1)S(1)} async-done(((bf16[64,2,16,128]{3,2,1,0:T(8,128)(2,1)}), bf16[64,2,16,128]{3,2,1,0:T(8,128)(2,1)S(1)}, u32[]{:S(2)}, u32[]{:S(2)}) %all-to-all-start) | async-done | bytes 524320 | tf_op jit(solution)/shard_map/all_to_all | solution.py:250
  26.2 0.0 collective-permute-start
  26.2 2.4 %beam_own.1 = (bf16[256,1024]{1,0:T(8,128)(2,1)S(1)}, bf16[2,1024,512]{2,1,0:T(8,128)(2,1)S(1)}) custom-call(bf16[2,1024,512]{2,1,0:T(8,128)(2,1)S(1)} %get-tuple-element.18.upper, bf16[2,1024,512]{2,1,0:T(8,128)(2,1)} %get-tuple-element.19.lower_ref, bf16[8,8,2,16,128]{4,3,2,1,0:T(8,128)(2,1)S(1)} %bitcast.2), custom_call_target="tpu_custom_call" | custom-call | flops 2147483648 | bytes 4194304 | tf_op jit(solution)/shard_map/beam_own/pallas_call | solution.py:283
  28.6 0.0 collective-permute-done
  28.7 1.9 %beam_other.1 = (bf16[512,1024]{1,0:T(8,128)(2,1)S(1)}, f32[256,256]{1,0:T(8,128)S(1)}) custom-call(bf16[2,1024,512]{2,1,0:T(8,128)(2,1)S(1)} %get-tuple-element.18.upper, bf16[2,1024,512]{2,1,0:T(8,128)(2,1)S(1)} %get-tuple-element.21.lower, bf16[8,8,2,16,128]{4,3,2,1,0:T(8,128)(2,1)S(1)} %bitcast.3, bf16[256,1024]{1,0:T(8,128)(2,1)S(1)} %get-tuple-element.22.own), custom_call_target="tpu_custom_call" | custom-call | flops 2147483648 | bytes 4194304 | tf_op jit(solution)/shard_map/beam_other/pallas_call | solution.py:296
  30.5 0.6 collective-permute-start.1
  31.1 1.2 %collective-permute-done.1 = f32[256,256]{1,0:T(8,128)S(1)} collective-permute-done((f32[256,256]{1,0:T(8,128)S(1)}, f32[256,256]{1,0:T(8,128)S(1)}, u32[]{:S(2)}, u32[]{:S(2)}) %collective-permute-start.1) | collective-permute-done | bytes 262176 | tf_op jit(solution)/shard_map/ppermute | solution.py:239
  32.3 0.5 collective-permute-start.6
  32.8 0.4 collective-permute-start.2
  33.2 2.9 %collective-permute-start.4 = (bf16[256,256]{1,0:T(8,128)(2,1)S(1)}, bf16[256,256]{1,0:T(8,128)(2,1)S(1)}, u32[]{:S(2)}, u32[]{:S(2)}) collective-permute-start(bf16[256,256]{1,0:T(8,128)(2,1)S(1)} %convert_element_type.15), channel_id=1, source_target_pairs={{0,32},{16,48},{32,0},{48,16},{64,96},{80,112},{96,64},{112,80},{1... | collective-permute-start | bytes 393224 | tf_op jit(solution)/shard_map/ppermute | solution.py:314
  36.1 2.2 %collective-permute-done.2 = bf16[256,256]{1,0:T(8,128)(2,1)S(1)} collective-permute-done((bf16[256,256]{1,0:T(8,128)(2,1)S(1)}, bf16[256,256]{1,0:T(8,128)(2,1)S(1)}, u32[]{:S(2)}, u32[]{:S(2)}) %collective-permute-start.2) | collective-permute-done | bytes 131104 | tf_op jit(solution)/shard_map/ppermute | solution.py:311
  38.3 0.0 collective-permute-start.3
  38.3 3.6 %collective-permute-done.4 = bf16[256,256]{1,0:T(8,128)(2,1)S(1)} collective-permute-done((bf16[256,256]{1,0:T(8,128)(2,1)S(1)}, bf16[256,256]{1,0:T(8,128)(2,1)S(1)}, u32[]{:S(2)}, u32[]{:S(2)}) %collective-permute-start.4) | collective-permute-done | bytes 131104 | tf_op jit(solution)/shard_map/ppermute | solution.py:314
  41.9 0.0 collective-permute-done.3
  41.9 0.1 fusion
  41.9 1.7 %collective-permute-start.5 = (bf16[256,256]{1,0:T(8,128)(2,1)S(1)}, bf16[256,256]{1,0:T(8,128)(2,1)S(1)}, u32[]{:S(2)}, u32[]{:S(2)}) collective-permute-start(bf16[256,256]{1,0:T(8,128)(2,1)S(1)} %get-tuple-element.27), channel_id=1, source_target_pairs={{0,64},{16,80},{32,96},{48,112},{64,0},{80,16},{96,32},{112,48},{1... | collective-permute-start | bytes 393224 | tf_op jit(solution)/shard_map/ppermute | solution.py:316
  43.6 5.0 %collective-permute-done.5.far = bf16[256,256]{1,0:T(8,128)(2,1)S(1)} collective-permute-done((bf16[256,256]{1,0:T(8,128)(2,1)S(1)}, bf16[256,256]{1,0:T(8,128)(2,1)S(1)}, u32[]{:S(2)}, u32[]{:S(2)}) %collective-permute-start.5) | collective-permute-done | bytes 131104 | tf_op jit(solution)/shard_map/ppermute | solution.py:316
  48.6 0.0 collective-permute-done.6.peer_ref
  48.6 2.0 %filter.1 = bf16[8,2,16,2048]{3,2,1,0:T(8,128)(2,1)S(1)} custom-call(f32[256,256]{1,0:T(8,128)S(1)} %get-tuple-element.28.near, bf16[256,256]{1,0:T(8,128)(2,1)S(1)} %collective-permute-done.5.far, bf16[512,1024]{1,0:T(8,128)(2,1)S(1)} %get-tuple-element.26.y_ref, bf16[512,1024]{1,0:T(8,128)(2,1)S(1)} %collective-permute-done.6.peer_ref), custom_call_target="tpu_custom_call" | custom-call | tf_op jit(solution)/shard_map/filter/pallas_call | solution.py:318
  50.5 18.6 %all_to_all.10.got = bf16[8,2,16,2048]{3,2,1,0:T(8,128)(2,1)S(1)} all-to-all(bf16[8,2,16,2048]{3,2,1,0:T(8,128)(2,1)S(1)} %filter.1), channel_id=1, replica_groups=mesh['chan'=8,'bin'=8,'core'=2] {'bin'}, dimensions={0} | all-to-all | bytes 2097152 | tf_op jit(solution)/shard_map/all_to_all | solution.py:328
  69.2 1.3 %place.1 = bf16[16,2,8,2048]{3,2,1,0:T(8,128)(2,1)} custom-call(bf16[8,2,16,2048]{3,2,1,0:T(8,128)(2,1)S(1)} %all_to_all.10.got), custom_call_target="tpu_custom_call" | custom-call | tf_op jit(solution)/shard_map/place/pallas_call | solution.py:329
  (2 shorter events, 0.0 us)
Async XLA Ops:
  1.8 24.5 %all-to-all-start = ((bf16[64,2,16,128]{3,2,1,0:T(8,128)(2,1)}), bf16[64,2,16,128]{3,2,1,0:T(8,128)(2,1)S(1)}, u32[]{:S(2)}, u32[]{:S(2)}) async-start(bf16[64,2,16,128]{3,2,1,0:T(8,128)(2,1)} %spread.1), calls=%async_computation | async-start | bytes 1048576 | tf_op jit(solution)/shard_map/all_to_all | solution.py:250
  26.2 2.4 %collective-permute-start = (bf16[64,2,16,128]{3,2,1,0:T(8,128)(2,1)S(1)}, bf16[64,2,16,128]{3,2,1,0:T(8,128)(2,1)S(1)}, u32[]{:S(2)}, u32[]{:S(2)}) collective-permute-start(bf16[64,2,16,128]{3,2,1,0:T(8,128)(2,1)S(1)} %all-to-all-done), channel_id=1, source_target_pairs={{0,1},{1,0},{2,3},{3,2},{4,5},{5,4},{6,7},{7,6},{8,9},{9,8},{10,11... | collective-permute-start | bytes 1572872 | tf_op jit(solution)/shard_map/ppermute | solution.py:239
  30.5 1.7 %collective-permute-start.1 = (f32[256,256]{1,0:T(8,128)S(1)}, f32[256,256]{1,0:T(8,128)S(1)}, u32[]{:S(2)}, u32[]{:S(2)}) collective-permute-start(f32[256,256]{1,0:T(8,128)S(1)} %get-tuple-element.23), channel_id=1, source_target_pairs={{0,1},{1,0},{2,3},{3,2},{4,5},{5,4},{6,7},{7,6},{8,9},{9,8},{10,11... | collective-permute-start | bytes 786440 | tf_op jit(solution)/shard_map/ppermute | solution.py:239
  32.3 16.3 %collective-permute-start.6 = (bf16[512,1024]{1,0:T(8,128)(2,1)S(1)}, bf16[512,1024]{1,0:T(8,128)(2,1)S(1)}, u32[]{:S(2)}, u32[]{:S(2)}) collective-permute-start(bf16[512,1024]{1,0:T(8,128)(2,1)S(1)} %get-tuple-element.26.y_ref), channel_id=1, source_target_pairs={{0,1},{1,0},{2,3},{3,2},{4,5},{5,4},{6,7},{7,6},{8,9},{9,8},{10,11... | collective-permute-start | bytes 3145736 | tf_op jit(solution)/shard_map/ppermute | solution.py:239
  32.8 5.5 %collective-permute-start.2 = (bf16[256,256]{1,0:T(8,128)(2,1)S(1)}, bf16[256,256]{1,0:T(8,128)(2,1)S(1)}, u32[]{:S(2)}, u32[]{:S(2)}) collective-permute-start(bf16[256,256]{1,0:T(8,128)(2,1)S(1)} %convert_element_type.15), channel_id=1, source_target_pairs={{0,16},{1,49},{16,0},{17,33},{32,48},{33,17},{48,32},{49,1},{64,80... | collective-permute-start | bytes 393224 | tf_op jit(solution)/shard_map/ppermute | solution.py:311
  33.2 8.7 %collective-permute-start.4 = (bf16[256,256]{1,0:T(8,128)(2,1)S(1)}, bf16[256,256]{1,0:T(8,128)(2,1)S(1)}, u32[]{:S(2)}, u32[]{:S(2)}) collective-permute-start(bf16[256,256]{1,0:T(8,128)(2,1)S(1)} %convert_element_type.15), channel_id=1, source_target_pairs={{0,32},{16,48},{32,0},{48,16},{64,96},{80,112},{96,64},{112,80},{1... | collective-permute-start | bytes 393224 | tf_op jit(solution)/shard_map/ppermute | solution.py:314
  38.3 3.6 %collective-permute-start.3 = (bf16[256,256]{1,0:T(8,128)(2,1)S(1)}, bf16[256,256]{1,0:T(8,128)(2,1)S(1)}, u32[]{:S(2)}, u32[]{:S(2)}) collective-permute-start(bf16[256,256]{1,0:T(8,128)(2,1)S(1)} %collective-permute-done.2), channel_id=1, source_target_pairs={{0,1},{1,0},{2,3},{3,2},{4,5},{5,4},{6,7},{7,6},{8,9},{9,8},{10,11... | collective-permute-start | bytes 393224 | tf_op jit(solution)/shard_map/ppermute | solution.py:239
  41.9 6.6 %collective-permute-start.5 = (bf16[256,256]{1,0:T(8,128)(2,1)S(1)}, bf16[256,256]{1,0:T(8,128)(2,1)S(1)}, u32[]{:S(2)}, u32[]{:S(2)}) collective-permute-start(bf16[256,256]{1,0:T(8,128)(2,1)S(1)} %get-tuple-element.27), channel_id=1, source_target_pairs={{0,64},{16,80},{32,96},{48,112},{64,0},{80,16},{96,32},{112,48},{1... | collective-permute-start | bytes 393224 | tf_op jit(solution)/shard_map/ppermute | solution.py:316

commit v13 on v10

--- a/solution.py
+++ b/solution.py
@@ -13,8 +13,15 @@
 CORES = 2
 F32 = jnp.float32
 BF16 = jnp.bfloat16
-SIN = (3.1415925800446924, -5.167706878924515, 2.5500313772531213, -0.5980451739748806, 0.0772201286897368)
-COS = (0.9999999534666272, -4.934792858670076, 4.058411914063177, -1.331880160583308, 0.21969679727234584)
+ROOT = math.sqrt(2.0)
+SIN = tuple(
+    ROOT * c
+    for c in (3.1415925800446924, -5.167706878924515, 2.5500313772531213, -0.5980451739748806, 0.0772201286897368)
+)
+COS = tuple(
+    ROOT * c
+    for c in (0.9999999534666272, -4.934792858670076, 4.058411914063177, -1.331880160583308, 0.21969679727234584)
+)
 ROUNDER = 12582912.0
 ROWS = 512
 LANES = 256
@@ -35,71 +42,77 @@
     return high, value - unit * high
 
 
-def spread_kernel(rf_ref, out_ref, held, sems):
+def spread_kernel(
+    rf_ref, elem_ref, vox_ref, bins_ref, out_ref, lhs_ref, rhs_ref, wave_ref, held, elem, vox, numbers, sems
+):
     parts, bins = held.shape[:2]
     chans = out_ref.shape[0] // bins
-    copy = pltpu.make_async_copy(rf_ref, held, sems.at[chans * parts])
-    copy.start()
-    copy.wait()
+    reads = [
+        pltpu.make_async_copy(source, target, sems.at[n])
+        for n, (source, target) in enumerate(
+            ((rf_ref, held), (elem_ref, elem), (vox_ref, vox), (bins_ref, numbers))
+        )
+    ]
+    for copy in reads:
+        copy.start()
+    reads[0].wait()
     copies = [
-        pltpu.make_async_copy(held.at[part], out_ref.at[k * bins : (k + 1) * bins, part], sems.at[k * parts + part])
+        pltpu.make_async_copy(
+            held.at[part], out_ref.at[k * bins : (k + 1) * bins, part], sems.at[4 + k * parts + part]
+        )
         for k in range(chans)
         for part in range(parts)
     ]
     for copy in copies:
         copy.start()
-    for copy in copies:
+    for copy in reads[1:]:
         copy.wait()
 
-
-def operator_kernel(elem_ref, vox_ref, bins_ref, upper, lower_ref, elem, vox, bins, lhs_ref, lower, sems):
-    core = lax.axis_index("core")
     channels = elem.shape[1]
-    share = upper.shape[2]
-    voxels = share + lower.shape[2]
-    copies = [
-        pltpu.make_async_copy(source, target, sems.at[n])
-        for n, (source, target) in enumerate(((elem_ref, elem), (vox_ref, vox), (bins_ref, bins)))
-    ]
-    for copy in copies:
-        copy.start()
-    for copy in copies:
-        copy.wait()
-    wavenumber = (32.0 + bins[lax.axis_index("bin")].astype(F32)) / 64.0
-    scale = 2.0 / math.sqrt(channels)
-
     place = elem[...].astype(F32)
     high, low = digits(jnp.sum(place * place, axis=0, keepdims=True), 16.0)
     one = jnp.ones((1, channels), F32)
-    lhs = jnp.concatenate([place, high, low, one, one, 0.0 * one], axis=0)
-    lhs_ref[...] = jnp.transpose(lhs).astype(BF16)
-    voxel = vox[:, pl.ds(pl.multiple_of(core * voxels, voxels), voxels)].astype(F32)
+    lhs_ref[...] = jnp.transpose(jnp.concatenate([place, high, low, one, one, 0.0 * one], axis=0)).astype(BF16)
+    voxels = wave_ref.shape[1]
+    voxel = vox[:, pl.ds(pl.multiple_of(lax.axis_index("core") * voxels, voxels), voxels)].astype(F32)
     high, low = digits(jnp.sum(voxel * voxel, axis=0, keepdims=True), 64.0)
     one = jnp.ones((1, voxels), F32)
     zero = 0.0 * one
-    level = voxel[2:3]
-    squares = jnp.concatenate([-2.0 * voxel, 16.0 * one, one, 64.0 * high, low, zero], axis=0).astype(BF16)
-    depths = jnp.concatenate([zero, zero, -1.0 * one, zero, zero, level, zero, zero], axis=0).astype(BF16)
+    wave_ref[0:1] = voxel[2:3]
+    wave_ref[1:2] = one * ((32.0 + numbers[lax.axis_index("bin")].astype(F32)) / 64.0)
+    rhs_ref[0] = jnp.concatenate([-2.0 * voxel, 16.0 * one, one, 64.0 * high, low, zero], axis=0).astype(BF16)
+    scale = 1.0 / math.sqrt(channels)
+    rhs_ref[1] = jnp.concatenate(
+        [zero, zero, -scale * one, zero, zero, scale * voxel[2:3], zero, zero], axis=0
+    ).astype(BF16)
+    for copy in copies:
+        copy.wait()
+
+
+def operator_kernel(lhs_ref, rhs_ref, wave_ref, upper, lower_ref, lower, sem):
+    channels = lhs_ref.shape[0]
+    share = upper.shape[2]
+    voxels = share + lower.shape[2]
 
     def tile(index, carry, out_ref, lanes):
         rows = pl.ds(pl.multiple_of(index * ROWS, ROWS), ROWS)
         left = lhs_ref[rows]
-        squared = jnp.dot(left, squares[:, lanes], preferred_element_type=F32)
-        depth = jnp.dot(left, depths[:, lanes], preferred_element_type=F32)
+        squared = jnp.dot(left, rhs_ref[0, :, lanes], preferred_element_type=F32)
+        depth = jnp.dot(left, rhs_ref[1, :, lanes], preferred_element_type=F32)
         inverse = lax.rsqrt(squared)
-        turns = (level[:, lanes] + squared * inverse) * wavenumber
+        turns = (wave_ref[0:1, lanes] + squared * inverse) * wave_ref[1:2, lanes]
         part = turns - ((turns + ROUNDER) - ROUNDER)
         z = part * part
         sine = part * horner(SIN, z)
         cosine = horner(COS, z)
-        double = depth * inverse * scale
-        lean = double * sine
-        out_ref[0, rows] = (0.5 * double - lean * sine).astype(BF16)
+        weight = depth * inverse
+        lean = weight * sine
+        out_ref[0, rows] = (weight - lean * sine).astype(BF16)
         out_ref[1, rows] = (lean * cosine).astype(BF16)
         return carry
 
     lax.fori_loop(0, channels // ROWS, functools.partial(tile, out_ref=lower, lanes=slice(share, voxels)), 0)
-    copy = pltpu.make_async_copy(lower, lower_ref, sems.at[3])
+    copy = pltpu.make_async_copy(lower, lower_ref, sem)
     copy.start()
     lax.fori_loop(0, channels // ROWS, functools.partial(tile, out_ref=upper, lanes=slice(0, share)), 0)
     copy.wait()
@@ -177,11 +190,11 @@
     return 0.5 * (packed + flipped), 0.5 * (packed - flipped), flipped
 
 
-def filter_kernel(mine, far, twin, far_twin, y_ref, peer_ref, out_ref, gram, kept):
+def filter_kernel(mine, twin, y_ref, peer_ref, out_ref, gram, kept):
     core = lax.axis_index("core")
     half, frames = mine.shape
-    gram[pl.ds(pl.multiple_of(core * half, half), half), :] = mine[...] + far[...].astype(F32)
-    gram[pl.ds(pl.multiple_of((1 - core) * half, half), half), :] = twin[...] + far_twin[...].astype(F32)
+    gram[pl.ds(pl.multiple_of(core * half, half), half), :] = mine[...]
+    gram[pl.ds(pl.multiple_of((1 - core) * half, half), half), :] = twin[...]
     packed = gram[...]
     squares = jnp.sum(packed * packed)
     factor = 4.0 / jnp.sqrt(jnp.full((1, 1), squares + EPSILON, F32))
@@ -244,15 +257,29 @@
     def across(x, bits):
         return lax.ppermute(x, "chan", [(a, a ^ bits) for a in range(chans)])
 
-    by_bin = pl.pallas_call(
+    def in_hbm(x):
+        return pltpu.with_memory_space_constraint(x, pltpu.HBM)
+
+    by_bin, lhs, rhs, wave = pl.pallas_call(
         spread_kernel,
         name="spread",
-        out_shape=shape(chans * bins, parts, group, width),
-        in_specs=[HBM],
-        out_specs=HBM,
-        scratch_shapes=[pltpu.VMEM(rf_data.shape, BF16), pltpu.SemaphoreType.DMA((chans * parts + 1,))],
-        compiler_params=WIDE,
-    )(pltpu.with_memory_space_constraint(rf_data, pltpu.HBM))
+        out_shape=(
+            shape(chans * bins, parts, group, width),
+            shape(channels, 8),
+            shape(2, 8, voxels),
+            shape(2, voxels, dtype=F32),
+        ),
+        in_specs=[HBM] * 4,
+        out_specs=(HBM, VMEM, VMEM, VMEM),
+        scratch_shapes=[
+            pltpu.VMEM(rf_data.shape, BF16),
+            pltpu.VMEM(elem_pos.shape, jnp.int32),
+            pltpu.VMEM(vox_pos.shape, jnp.int32),
+            pltpu.SMEM(subbands.shape, jnp.int32),
+            pltpu.SemaphoreType.DMA((chans * parts + 4,)),
+        ],
+        compiler_params=WIDE,
+    )(in_hbm(rf_data), in_hbm(elem_pos), in_hbm(vox_pos), in_hbm(subbands))
     own = lax.all_to_all(by_bin, ("chan", "bin"), split_axis=0, concat_axis=0, tiled=True)
 
     share = voxels // 2
@@ -260,15 +287,11 @@
         operator_kernel,
         name="operator",
         out_shape=(shape(2, channels, share), pltpu.HBM((2, channels, voxels - share), BF16)),
-        in_specs=[HBM, HBM, HBM],
+        in_specs=[VMEM, VMEM, VMEM],
         out_specs=(VMEM, HBM),
         scratch_shapes=[
-            pltpu.VMEM(elem_pos.shape, jnp.int32),
-            pltpu.VMEM(vox_pos.shape, jnp.int32),
-            pltpu.SMEM(subbands.shape, jnp.int32),
-            pltpu.VMEM((channels, 8), BF16),
             pltpu.VMEM((2, channels, voxels - share), BF16),
-            pltpu.SemaphoreType.DMA((4,)),
+            pltpu.SemaphoreType.DMA,
         ],
         compiler_params=WIDE,
         cost_estimate=pl.CostEstimate(
@@ -276,7 +299,7 @@
             transcendentals=channels * voxels,
             bytes_accessed=4 * channels * voxels,
         ),
-    )(*(pltpu.with_memory_space_constraint(x, pltpu.HBM) for x in (elem_pos, vox_pos, subbands)))
+    )(lhs, rhs, wave)
 
     own, upper, lower = lax.optimization_barrier((own, upper, lower))
     other = swap(own)
@@ -298,7 +321,7 @@
         ],
         compiler_params=WIDE,
         cost_estimate=beam_cost,
-    )(upper, pltpu.with_memory_space_constraint(lower, pltpu.HBM), own)
+    )(upper, in_hbm(lower), own)
     y, keep, send = pl.pallas_call(
         other_kernel,
         name="beam_other",
@@ -315,22 +338,18 @@
     peer = swap(y)
     narrow = total.astype(BF16)
     total = total + sum(across(narrow, bits).astype(F32) for bits in (1, 3, 2))
-    narrow = total.astype(BF16)
-    far = across(narrow, 4)
-    far_twin = lax.ppermute(
-        narrow, ("chan", "core"), [(2 * a + c, 2 * (a ^ 4) + 1 - c) for a in range(chans) for c in range(CORES)]
-    )
-    twin = swap(total)
+    total = total + across(total.astype(BF16), 4).astype(F32)
+    rest = swap(total)
 
     applied = pl.pallas_call(
         filter_kernel,
         name="filter",
         out_shape=shape(bins, parts, group, CORES * voxels),
-        in_specs=[VMEM] * 6,
+        in_specs=[VMEM] * 4,
         out_specs=VMEM,
         scratch_shapes=[pltpu.VMEM((frames, frames), F32), pltpu.VMEM((2, frames, frames), BF16)],
         compiler_params=WIDE,
-    )(total, far, twin, far_twin, y, peer)
+    )(total, rest, y, peer)
 
     got = lax.all_to_all(applied, "bin", split_axis=0, concat_axis=0, tiled=True)
     return pl.pallas_call(

time: 69.2 us -> 69.6 us (level)
  waiting for transfers between devices: 15.6 us -> 17.9 us
  starting transfers between devices: 19.8 us -> 18.1 us
  Pallas kernels: 15.6 us -> 14.4 us
  blocking collectives: 17.7 us -> 18.6 us
    ppermute x1 -> x0, starting transfers between devices: 1.98 us -> none  [shards(): lax.ppermute(narrow, ('chan', 'core'), [(2 * a + c, 2 * (a ^ 4) + 1 - c)...]
    ppermute x1 -> x0, waiting for transfers between devices: 1.77 us -> none  [shards(): lax.ppermute(narrow, ('chan', 'core'), [(2 * a + c, 2 * (a ^ 4) + 1 - c)...]
    ppermute x4, waiting for transfers between devices: 6.13 us -> 7.71 us  [across(): return lax.ppermute(x, 'chan', [(a, a ^ bits) for a in range(chans)])]
    ppermute x4, waiting for transfers between devices: 0.99 us -> 2.33 us  [swap(): return lax.ppermute(x, 'core', [(0, 1), (1, 0)])]
    pallas_call x1, Pallas kernels: 6.21 us -> 5.05 us  [shards(): pl.pallas_call(operator_kernel, name='operator', out_shape=(shape(2, chan...]
    all_to_all x1, waiting for transfers between devices: 6.71 us -> 7.88 us  [shards(): lax.all_to_all(by_bin, ('chan', 'bin'), split_axis=0, concat_axis=0, tile...]
    all_to_all x1, blocking collectives: 17.7 us -> 18.6 us  [shards(): lax.all_to_all(applied, 'bin', split_axis=0, concat_axis=0, tiled=True)]
  transfers between devices with their start and end apart: 10 -> 9, of which waited for: 7 -> 7; matrix products, arithmetic and copies ran while one was open for 0% -> 0% of each run, Pallas kernels for 13% -> 11%
where the time goes in v13:
time: 69.6 us; the launch traced here: 69.3 us
  blocking collectives  18.6 us (27%)
  starting transfers between devices  18.1 us (26%)
  waiting for transfers between devices  17.9 us (26%)
  Pallas kernels  14.4 us (21%)
    all_to_all x1, blocking collectives, shards(): lax.all_to_all(applied, 'bin', split_axis=0, concat_axis=0, tiled=True)  18.6 us
    all_to_all x1, starting transfers between devices, shards(): lax.all_to_all(by_bin, ('chan', 'bin'), split_axis=0, concat_axis=0, tile...  11.5 us
    all_to_all x1, waiting for transfers between devices, shards(): lax.all_to_all(by_bin, ('chan', 'bin'), split_axis=0, concat_axis=0, tile...  7.88 us
    ppermute x4, waiting for transfers between devices, across(): return lax.ppermute(x, 'chan', [(a, a ^ bits) for a in range(chans)])  7.71 us
    ppermute x4, starting transfers between devices, across(): return lax.ppermute(x, 'chan', [(a, a ^ bits) for a in range(chans)])  5.51 us
    pallas_call x1, Pallas kernels, shards(): pl.pallas_call(operator_kernel, name='operator', out_shape=(shape(2, chan...  5.05 us
    pallas_call x1, Pallas kernels, shards(): pl.pallas_call(own_kernel, name='beam_own', out_shape=(shape(frames, voxe...  2.41 us
    ppermute x4, waiting for transfers between devices, swap(): return lax.ppermute(x, 'core', [(0, 1), (1, 0)])  2.33 us
  transfers between devices with their start and end apart: 9, of which 7 were waited for; matrix products, arithmetic and copies ran while one was open for 0% of the time, Pallas kernels for 11%

profile of v13, /device:TPU:0, one launch (start us, length us, event | category | flops | bytes accessed | tf_op | source)
XLA Modules:
  0.0 69.3 jit_solution(5245049246866949179)
XLA Ops:
  0.0 1.8 %spread.1 = (bf16[64,2,16,128]{3,2,1,0:T(8,128)(2,1)}, bf16[1024,8]{1,0:T(8,128)(2,1)S(1)}, bf16[2,8,1024]{2,1,0:T(8,128)(2,1)S(1)}, f32[2,1024]{1,0:T(2,128)S(1)}) custom-call(bf16[2,8,16,128]{3,2,1,0:T(8,128)(2,1)} %rf_ref.1, s32[3,1024]{1,0:T(4,128)} %elem_ref.1, s32[3,2048]{1,0:T(4,128)} %vox_ref.1, s32[8]{0:T(128)} %bins_ref.1), custom_call_target="tpu_custom_call" | custom-call | tf_op jit(solution)/shard_map/spread/pallas_call | solution.py:263
  1.8 11.5 %all-to-all-start = ((bf16[64,2,16,128]{3,2,1,0:T(8,128)(2,1)}), bf16[64,2,16,128]{3,2,1,0:T(8,128)(2,1)S(1)}, u32[]{:S(2)}, u32[]{:S(2)}) async-start(bf16[64,2,16,128]{3,2,1,0:T(8,128)(2,1)} %get-tuple-element.21), calls=%async_computation | async-start | bytes 1048576 | tf_op jit(solution)/shard_map/all_to_all | solution.py:283
  13.3 5.1 %operator.1 = (bf16[2,1024,512]{2,1,0:T(8,128)(2,1)S(1)}, bf16[2,1024,512]{2,1,0:T(8,128)(2,1)}) custom-call(bf16[1024,8]{1,0:T(8,128)(2,1)S(1)} %get-tuple-element.22.lhs_ref, bf16[2,8,1024]{2,1,0:T(8,128)(2,1)S(1)} %get-tuple-element.23.rhs_ref, f32[2,1024]{1,0:T(2,128)S(1)} %get-tuple-element.24.wave_ref), custom_call_target="tpu_custom_call" | custom-call | flops 62914560 | bytes 4194304 | tf_op jit(solution)/shard_map/operator/pallas_call | solution.py:286
  18.4 7.9 %all-to-all-done = bf16[64,2,16,128]{3,2,1,0:T(8,128)(2,1)S(1)} async-done(((bf16[64,2,16,128]{3,2,1,0:T(8,128)(2,1)}), bf16[64,2,16,128]{3,2,1,0:T(8,128)(2,1)S(1)}, u32[]{:S(2)}, u32[]{:S(2)}) %all-to-all-start) | async-done | bytes 524320 | tf_op jit(solution)/shard_map/all_to_all | solution.py:283
  26.3 0.0 collective-permute-start
  26.3 2.4 %beam_own.1 = (bf16[256,1024]{1,0:T(8,128)(2,1)S(1)}, bf16[2,1024,512]{2,1,0:T(8,128)(2,1)S(1)}) custom-call(bf16[2,1024,512]{2,1,0:T(8,128)(2,1)S(1)} %get-tuple-element.27.upper, bf16[2,1024,512]{2,1,0:T(8,128)(2,1)} %get-tuple-element.28.lower_ref, bf16[8,8,2,16,128]{4,3,2,1,0:T(8,128)(2,1)S(1)} %bitcast.2), custom_call_target="tpu_custom_call" | custom-call | flops 2147483648 | bytes 4194304 | tf_op jit(solution)/shard_map/beam_own/pallas_call | solution.py:312
  28.7 0.0 collective-permute-done
  28.7 1.9 %beam_other.1 = (bf16[512,1024]{1,0:T(8,128)(2,1)S(1)}, f32[128,256]{1,0:T(8,128)S(1)}, f32[128,256]{1,0:T(8,128)S(1)}) custom-call(bf16[2,1024,512]{2,1,0:T(8,128)(2,1)S(1)} %get-tuple-element.27.upper, bf16[2,1024,512]{2,1,0:T(8,128)(2,1)S(1)} %get-tuple-element.30.lower, bf16[8,8,2,16,128]{4,3,2,1,0:T(8,128)(2,1)S(1)} %bitcast.3, ...), custom_call_target="tpu_custom_call" | custom-call | flops 2147483648 | bytes 4194304 | tf_op jit(solution)/shard_map/beam_other/pallas_call | solution.py:325
  30.6 0.6 collective-permute-start.1
  31.2 1.0 %collective-permute-done.1 = f32[128,256]{1,0:T(8,128)S(1)} collective-permute-done((f32[128,256]{1,0:T(8,128)S(1)}, f32[128,256]{1,0:T(8,128)S(1)}, u32[]{:S(2)}, u32[]{:S(2)}) %collective-permute-start.1) | collective-permute-done | bytes 131104 | tf_op jit(solution)/shard_map/ppermute | solution.py:255
  32.2 0.4 collective-permute-start.7
  32.6 1.7 %collective-permute-start.4 = (bf16[128,256]{1,0:T(8,128)(2,1)S(1)}, bf16[128,256]{1,0:T(8,128)(2,1)S(1)}, u32[]{:S(2)}, u32[]{:S(2)}) collective-permute-start(bf16[128,256]{1,0:T(8,128)(2,1)S(1)} %convert_element_type.18), channel_id=1, source_target_pairs={{0,32},{16,48},{32,0},{48,16},{64,96},{80,112},{96,64},{112,80},{1... | collective-permute-start | bytes 196616 | tf_op jit(solution)/shard_map/ppermute | solution.py:258
  34.3 1.4 %collective-permute-start.3 = (bf16[128,256]{1,0:T(8,128)(2,1)S(1)}, bf16[128,256]{1,0:T(8,128)(2,1)S(1)}, u32[]{:S(2)}, u32[]{:S(2)}) collective-permute-start(bf16[128,256]{1,0:T(8,128)(2,1)S(1)} %convert_element_type.18), channel_id=1, source_target_pairs={{0,48},{16,32},{32,16},{48,0},{64,112},{80,96},{96,80},{112,64},{1... | collective-permute-start | bytes 196616 | tf_op jit(solution)/shard_map/ppermute | solution.py:258
  35.7 0.5 collective-permute-start.2
  36.2 2.3 %collective-permute-done.4 = bf16[128,256]{1,0:T(8,128)(2,1)S(1)} collective-permute-done((bf16[128,256]{1,0:T(8,128)(2,1)S(1)}, bf16[128,256]{1,0:T(8,128)(2,1)S(1)}, u32[]{:S(2)}, u32[]{:S(2)}) %collective-permute-start.4) | collective-permute-done | bytes 65568 | tf_op jit(solution)/shard_map/ppermute | solution.py:258
  38.5 1.4 %collective-permute-done.3 = bf16[128,256]{1,0:T(8,128)(2,1)S(1)} collective-permute-done((bf16[128,256]{1,0:T(8,128)(2,1)S(1)}, bf16[128,256]{1,0:T(8,128)(2,1)S(1)}, u32[]{:S(2)}, u32[]{:S(2)}) %collective-permute-start.3) | collective-permute-done | bytes 65568 | tf_op jit(solution)/shard_map/ppermute | solution.py:258
  39.9 0.1 collective-permute-done.2
  40.0 1.9 %collective-permute-start.5 = (bf16[128,256]{1,0:T(8,128)(2,1)S(1)}, bf16[128,256]{1,0:T(8,128)(2,1)S(1)}, u32[]{:S(2)}, u32[]{:S(2)}) collective-permute-start(bf16[128,256]{1,0:T(8,128)(2,1)S(1)} %fusion), channel_id=1, source_target_pairs={{0,64},{16,80},{32,96},{48,112},{64,0},{80,16},{96,32},{112,48},{1... | collective-permute-start | bytes 196616 | tf_op jit(solution)/shard_map/ppermute | solution.py:258
  42.0 3.9 %collective-permute-done.5 = bf16[128,256]{1,0:T(8,128)(2,1)S(1)} collective-permute-done((bf16[128,256]{1,0:T(8,128)(2,1)S(1)}, bf16[128,256]{1,0:T(8,128)(2,1)S(1)}, u32[]{:S(2)}, u32[]{:S(2)}) %collective-permute-start.5) | collective-permute-done | bytes 65568 | tf_op jit(solution)/shard_map/ppermute | solution.py:258
  45.9 0.1 collective-permute-start.6
  46.0 1.3 %collective-permute-done.6.twin = f32[128,256]{1,0:T(8,128)S(1)} collective-permute-done((f32[128,256]{1,0:T(8,128)S(1)}, f32[128,256]{1,0:T(8,128)S(1)}, u32[]{:S(2)}, u32[]{:S(2)}) %collective-permute-start.6) | collective-permute-done | bytes 131104 | tf_op jit(solution)/shard_map/ppermute | solution.py:255
  47.4 0.0 collective-permute-done.7.peer_ref
  47.4 2.0 %filter.1 = bf16[8,2,16,2048]{3,2,1,0:T(8,128)(2,1)S(1)} custom-call(f32[128,256]{1,0:T(8,128)S(1)} %convert_add_fusion.mine, f32[128,256]{1,0:T(8,128)S(1)} %collective-permute-done.6.twin, bf16[512,1024]{1,0:T(8,128)(2,1)S(1)} %get-tuple-element.36.y_ref, bf16[512,1024]{1,0:T(8,128)(2,1)S(1)} %collective-permute-done.7.peer_ref), custom_call_target="tpu_custom_call" | custom-call | tf_op jit(solution)/shard_map/filter/pallas_call | solution.py:344
  49.4 18.6 %all_to_all.10.got = bf16[8,2,16,2048]{3,2,1,0:T(8,128)(2,1)S(1)} all-to-all(bf16[8,2,16,2048]{3,2,1,0:T(8,128)(2,1)S(1)} %filter.1), channel_id=1, replica_groups=mesh['chan'=8,'bin'=8,'core'=2] {'bin'}, dimensions={0} | all-to-all | bytes 2097152 | tf_op jit(solution)/shard_map/all_to_all | solution.py:354
  68.0 1.3 %place.1 = bf16[16,2,8,2048]{3,2,1,0:T(8,128)(2,1)} custom-call(bf16[8,2,16,2048]{3,2,1,0:T(8,128)(2,1)S(1)} %all_to_all.10.got), custom_call_target="tpu_custom_call" | custom-call | tf_op jit(solution)/shard_map/place/pallas_call | solution.py:355
  (4 shorter events, 0.1 us)
Async XLA Ops:
  1.8 24.5 %all-to-all-start = ((bf16[64,2,16,128]{3,2,1,0:T(8,128)(2,1)}), bf16[64,2,16,128]{3,2,1,0:T(8,128)(2,1)S(1)}, u32[]{:S(2)}, u32[]{:S(2)}) async-start(bf16[64,2,16,128]{3,2,1,0:T(8,128)(2,1)} %get-tuple-element.21), calls=%async_computation | async-start | bytes 1048576 | tf_op jit(solution)/shard_map/all_to_all | solution.py:283
  26.3 2.4 %collective-permute-start = (bf16[64,2,16,128]{3,2,1,0:T(8,128)(2,1)S(1)}, bf16[64,2,16,128]{3,2,1,0:T(8,128)(2,1)S(1)}, u32[]{:S(2)}, u32[]{:S(2)}) collective-permute-start(bf16[64,2,16,128]{3,2,1,0:T(8,128)(2,1)S(1)} %all-to-all-done), channel_id=1, source_target_pairs={{0,1},{1,0},{2,3},{3,2},{4,5},{5,4},{6,7},{7,6},{8,9},{9,8},{10,11... | collective-permute-start | bytes 1572872 | tf_op jit(solution)/shard_map/ppermute | solution.py:255
  30.6 1.6 %collective-permute-start.1 = (f32[128,256]{1,0:T(8,128)S(1)}, f32[128,256]{1,0:T(8,128)S(1)}, u32[]{:S(2)}, u32[]{:S(2)}) collective-permute-start(f32[128,256]{1,0:T(8,128)S(1)} %get-tuple-element.33), channel_id=1, source_target_pairs={{0,1},{1,0},{2,3},{3,2},{4,5},{5,4},{6,7},{7,6},{8,9},{9,8},{10,11... | collective-permute-start | bytes 393224 | tf_op jit(solution)/shard_map/ppermute | solution.py:255
  32.2 15.2 %collective-permute-start.7 = (bf16[512,1024]{1,0:T(8,128)(2,1)S(1)}, bf16[512,1024]{1,0:T(8,128)(2,1)S(1)}, u32[]{:S(2)}, u32[]{:S(2)}) collective-permute-start(bf16[512,1024]{1,0:T(8,128)(2,1)S(1)} %get-tuple-element.36.y_ref), channel_id=1, source_target_pairs={{0,1},{1,0},{2,3},{3,2},{4,5},{5,4},{6,7},{7,6},{8,9},{9,8},{10,11... | collective-permute-start | bytes 3145736 | tf_op jit(solution)/shard_map/ppermute | solution.py:255
  32.6 5.9 %collective-permute-start.4 = (bf16[128,256]{1,0:T(8,128)(2,1)S(1)}, bf16[128,256]{1,0:T(8,128)(2,1)S(1)}, u32[]{:S(2)}, u32[]{:S(2)}) collective-permute-start(bf16[128,256]{1,0:T(8,128)(2,1)S(1)} %convert_element_type.18), channel_id=1, source_target_pairs={{0,32},{16,48},{32,0},{48,16},{64,96},{80,112},{96,64},{112,80},{1... | collective-permute-start | bytes 196616 | tf_op jit(solution)/shard_map/ppermute | solution.py:258
  34.3 5.6 %collective-permute-start.3 = (bf16[128,256]{1,0:T(8,128)(2,1)S(1)}, bf16[128,256]{1,0:T(8,128)(2,1)S(1)}, u32[]{:S(2)}, u32[]{:S(2)}) collective-permute-start(bf16[128,256]{1,0:T(8,128)(2,1)S(1)} %convert_element_type.18), channel_id=1, source_target_pairs={{0,48},{16,32},{32,16},{48,0},{64,112},{80,96},{96,80},{112,64},{1... | collective-permute-start | bytes 196616 | tf_op jit(solution)/shard_map/ppermute | solution.py:258
  35.7 4.3 %collective-permute-start.2 = (bf16[128,256]{1,0:T(8,128)(2,1)S(1)}, bf16[128,256]{1,0:T(8,128)(2,1)S(1)}, u32[]{:S(2)}, u32[]{:S(2)}) collective-permute-start(bf16[128,256]{1,0:T(8,128)(2,1)S(1)} %convert_element_type.18), channel_id=1, source_target_pairs={{0,16},{16,0},{32,48},{48,32},{64,80},{80,64},{96,112},{112,96},{1... | collective-permute-start | bytes 196616 | tf_op jit(solution)/shard_map/ppermute | solution.py:258
  40.0 5.8 %collective-permute-start.5 = (bf16[128,256]{1,0:T(8,128)(2,1)S(1)}, bf16[128,256]{1,0:T(8,128)(2,1)S(1)}, u32[]{:S(2)}, u32[]{:S(2)}) collective-permute-start(bf16[128,256]{1,0:T(8,128)(2,1)S(1)} %fusion), channel_id=1, source_target_pairs={{0,64},{16,80},{32,96},{48,112},{64,0},{80,16},{96,32},{112,48},{1... | collective-permute-start | bytes 196616 | tf_op jit(solution)/shard_map/ppermute | solution.py:258
  45.9 1.4 %collective-permute-start.6 = (f32[128,256]{1,0:T(8,128)S(1)}, f32[128,256]{1,0:T(8,128)S(1)}, u32[]{:S(2)}, u32[]{:S(2)}) collective-permute-start(f32[128,256]{1,0:T(8,128)S(1)} %convert_add_fusion.mine), channel_id=1, source_target_pairs={{0,1},{1,0},{2,3},{3,2},{4,5},{5,4},{6,7},{7,6},{8,9},{9,8},{10,11... | collective-permute-start | bytes 393224 | tf_op jit(solution)/shard_map/ppermute | solution.py:255

commit v14 on v13

--- a/solution.py
+++ b/solution.py
@@ -190,11 +190,11 @@
     return 0.5 * (packed + flipped), 0.5 * (packed - flipped), flipped
 
 
-def filter_kernel(mine, twin, y_ref, peer_ref, out_ref, gram, kept):
+def filter_kernel(mine, far, twin, far_twin, y_ref, peer_ref, out_ref, gram, kept):
     core = lax.axis_index("core")
     half, frames = mine.shape
-    gram[pl.ds(pl.multiple_of(core * half, half), half), :] = mine[...]
-    gram[pl.ds(pl.multiple_of((1 - core) * half, half), half), :] = twin[...]
+    gram[pl.ds(pl.multiple_of(core * half, half), half), :] = mine[...] + far[...].astype(F32)
+    gram[pl.ds(pl.multiple_of((1 - core) * half, half), half), :] = twin[...] + far_twin[...].astype(F32)
     packed = gram[...]
     squares = jnp.sum(packed * packed)
     factor = 4.0 / jnp.sqrt(jnp.full((1, 1), squares + EPSILON, F32))
@@ -338,18 +338,22 @@
     peer = swap(y)
     narrow = total.astype(BF16)
     total = total + sum(across(narrow, bits).astype(F32) for bits in (1, 3, 2))
-    total = total + across(total.astype(BF16), 4).astype(F32)
-    rest = swap(total)
+    narrow = total.astype(BF16)
+    far = across(narrow, 4)
+    far_twin = lax.ppermute(
+        narrow, ("chan", "core"), [(2 * a + c, 2 * (a ^ 4) + 1 - c) for a in range(chans) for c in range(CORES)]
+    )
+    twin = swap(total)
 
     applied = pl.pallas_call(
         filter_kernel,
         name="filter",
         out_shape=shape(bins, parts, group, CORES * voxels),
-        in_specs=[VMEM] * 4,
+        in_specs=[VMEM] * 6,
         out_specs=VMEM,
         scratch_shapes=[pltpu.VMEM((frames, frames), F32), pltpu.VMEM((2, frames, frames), BF16)],
         compiler_params=WIDE,
-    )(total, rest, y, peer)
+    )(total, far, twin, far_twin, y, peer)
 
     got = lax.all_to_all(applied, "bin", split_axis=0, concat_axis=0, tiled=True)
     return pl.pallas_call(

time: 69.6 us -> 69.1 us (level)
  starting transfers between devices: 18.1 us -> 19.8 us
  waiting for transfers between devices: 17.9 us -> 16.8 us
  blocking collectives: 18.6 us -> 17.7 us
    ppermute x0 -> x1, starting transfers between devices: none -> 1.97 us  [shards(): lax.ppermute(narrow, ('chan', 'core'), [(2 * a + c, 2 * (a ^ 4) + 1 - c)...]
    ppermute x0 -> x1, waiting for transfers between devices: none -> 1.77 us  [shards(): lax.ppermute(narrow, ('chan', 'core'), [(2 * a + c, 2 * (a ^ 4) + 1 - c)...]
    ppermute x4, waiting for transfers between devices: 7.71 us -> 6.12 us  [across(): return lax.ppermute(x, 'chan', [(a, a ^ bits) for a in range(chans)])]
    ppermute x4, waiting for transfers between devices: 2.33 us -> 0.99 us  [swap(): return lax.ppermute(x, 'core', [(0, 1), (1, 0)])]
    all_to_all x1, blocking collectives: 18.6 us -> 17.7 us  [shards(): lax.all_to_all(applied, 'bin', split_axis=0, concat_axis=0, tiled=True)]
  transfers between devices with their start and end apart: 9 -> 10, of which waited for: 7 -> 7; matrix products, arithmetic and copies ran while one was open for 0% -> 0% of each run, Pallas kernels for 11% -> 11%
where the time goes in v14:
time: 69.1 us; the launch traced here: 68.8 us
  starting transfers between devices  19.8 us (29%)
  blocking collectives  17.7 us (26%)
  waiting for transfers between devices  16.8 us (24%)
  Pallas kernels  14.4 us (21%)
    all_to_all x1, blocking collectives, shards(): lax.all_to_all(applied, 'bin', split_axis=0, concat_axis=0, tiled=True)  17.7 us
    all_to_all x1, starting transfers between devices, shards(): lax.all_to_all(by_bin, ('chan', 'bin'), split_axis=0, concat_axis=0, tile...  11.5 us
    all_to_all x1, waiting for transfers between devices, shards(): lax.all_to_all(by_bin, ('chan', 'bin'), split_axis=0, concat_axis=0, tile...  7.88 us
    ppermute x4, waiting for transfers between devices, across(): return lax.ppermute(x, 'chan', [(a, a ^ bits) for a in range(chans)])  6.12 us
    ppermute x4, starting transfers between devices, across(): return lax.ppermute(x, 'chan', [(a, a ^ bits) for a in range(chans)])  5.24 us
    pallas_call x1, Pallas kernels, shards(): pl.pallas_call(operator_kernel, name='operator', out_shape=(shape(2, chan...  5.05 us
    pallas_call x1, Pallas kernels, shards(): pl.pallas_call(own_kernel, name='beam_own', out_shape=(shape(frames, voxe...  2.41 us
    pallas_call x1, Pallas kernels, shards(): pl.pallas_call(filter_kernel, name='filter', out_shape=shape(bins, parts,...  2 us
  transfers between devices with their start and end apart: 10, of which 7 were waited for; matrix products, arithmetic and copies ran while one was open for 0% of the time, Pallas kernels for 11%

profile of v14, /device:TPU:0, one launch (start us, length us, event | category | flops | bytes accessed | tf_op | source)
XLA Modules:
  0.0 68.8 jit_solution(7007500716854798314)
XLA Ops:
  0.0 1.8 %spread.1 = (bf16[64,2,16,128]{3,2,1,0:T(8,128)(2,1)}, bf16[1024,8]{1,0:T(8,128)(2,1)S(1)}, bf16[2,8,1024]{2,1,0:T(8,128)(2,1)S(1)}, f32[2,1024]{1,0:T(2,128)S(1)}) custom-call(bf16[2,8,16,128]{3,2,1,0:T(8,128)(2,1)} %rf_ref.1, s32[3,1024]{1,0:T(4,128)} %elem_ref.1, s32[3,2048]{1,0:T(4,128)} %vox_ref.1, s32[8]{0:T(128)} %bins_ref.1), custom_call_target="tpu_custom_call" | custom-call | tf_op jit(solution)/shard_map/spread/pallas_call | solution.py:263
  1.8 11.5 %all-to-all-start = ((bf16[64,2,16,128]{3,2,1,0:T(8,128)(2,1)}), bf16[64,2,16,128]{3,2,1,0:T(8,128)(2,1)S(1)}, u32[]{:S(2)}, u32[]{:S(2)}) async-start(bf16[64,2,16,128]{3,2,1,0:T(8,128)(2,1)} %get-tuple-element.21), calls=%async_computation | async-start | bytes 1048576 | tf_op jit(solution)/shard_map/all_to_all | solution.py:283
  13.3 5.1 %operator.1 = (bf16[2,1024,512]{2,1,0:T(8,128)(2,1)S(1)}, bf16[2,1024,512]{2,1,0:T(8,128)(2,1)}) custom-call(bf16[1024,8]{1,0:T(8,128)(2,1)S(1)} %get-tuple-element.22.lhs_ref, bf16[2,8,1024]{2,1,0:T(8,128)(2,1)S(1)} %get-tuple-element.23.rhs_ref, f32[2,1024]{1,0:T(2,128)S(1)} %get-tuple-element.24.wave_ref), custom_call_target="tpu_custom_call" | custom-call | flops 62914560 | bytes 4194304 | tf_op jit(solution)/shard_map/operator/pallas_call | solution.py:286
  18.4 7.9 %all-to-all-done = bf16[64,2,16,128]{3,2,1,0:T(8,128)(2,1)S(1)} async-done(((bf16[64,2,16,128]{3,2,1,0:T(8,128)(2,1)}), bf16[64,2,16,128]{3,2,1,0:T(8,128)(2,1)S(1)}, u32[]{:S(2)}, u32[]{:S(2)}) %all-to-all-start) | async-done | bytes 524320 | tf_op jit(solution)/shard_map/all_to_all | solution.py:283
  26.3 0.0 collective-permute-start
  26.3 2.4 %beam_own.1 = (bf16[256,1024]{1,0:T(8,128)(2,1)S(1)}, bf16[2,1024,512]{2,1,0:T(8,128)(2,1)S(1)}) custom-call(bf16[2,1024,512]{2,1,0:T(8,128)(2,1)S(1)} %get-tuple-element.27.upper, bf16[2,1024,512]{2,1,0:T(8,128)(2,1)} %get-tuple-element.28.lower_ref, bf16[8,8,2,16,128]{4,3,2,1,0:T(8,128)(2,1)S(1)} %bitcast.2), custom_call_target="tpu_custom_call" | custom-call | flops 2147483648 | bytes 4194304 | tf_op jit(solution)/shard_map/beam_own/pallas_call | solution.py:312
  28.7 0.0 collective-permute-done
  28.7 1.9 %beam_other.1 = (bf16[512,1024]{1,0:T(8,128)(2,1)S(1)}, f32[128,256]{1,0:T(8,128)S(1)}, f32[128,256]{1,0:T(8,128)S(1)}) custom-call(bf16[2,1024,512]{2,1,0:T(8,128)(2,1)S(1)} %get-tuple-element.27.upper, bf16[2,1024,512]{2,1,0:T(8,128)(2,1)S(1)} %get-tuple-element.30.lower, bf16[8,8,2,16,128]{4,3,2,1,0:T(8,128)(2,1)S(1)} %bitcast.3, ...), custom_call_target="tpu_custom_call" | custom-call | flops 2147483648 | bytes 4194304 | tf_op jit(solution)/shard_map/beam_other/pallas_call | solution.py:325
  30.6 0.6 collective-permute-start.1
  31.2 1.0 %collective-permute-done.1 = f32[128,256]{1,0:T(8,128)S(1)} collective-permute-done((f32[128,256]{1,0:T(8,128)S(1)}, f32[128,256]{1,0:T(8,128)S(1)}, u32[]{:S(2)}, u32[]{:S(2)}) %collective-permute-start.1) | collective-permute-done | bytes 131104 | tf_op jit(solution)/shard_map/ppermute | solution.py:255
  32.2 0.4 collective-permute-start.8
  32.6 1.7 %collective-permute-start.4 = (bf16[128,256]{1,0:T(8,128)(2,1)S(1)}, bf16[128,256]{1,0:T(8,128)(2,1)S(1)}, u32[]{:S(2)}, u32[]{:S(2)}) collective-permute-start(bf16[128,256]{1,0:T(8,128)(2,1)S(1)} %convert_element_type.15), channel_id=1, source_target_pairs={{0,32},{16,48},{32,0},{48,16},{64,96},{80,112},{96,64},{112,80},{1... | collective-permute-start | bytes 196616 | tf_op jit(solution)/shard_map/ppermute | solution.py:258
  34.3 1.4 %collective-permute-start.3 = (bf16[128,256]{1,0:T(8,128)(2,1)S(1)}, bf16[128,256]{1,0:T(8,128)(2,1)S(1)}, u32[]{:S(2)}, u32[]{:S(2)}) collective-permute-start(bf16[128,256]{1,0:T(8,128)(2,1)S(1)} %convert_element_type.15), channel_id=1, source_target_pairs={{0,48},{16,32},{32,16},{48,0},{64,112},{80,96},{96,80},{112,64},{1... | collective-permute-start | bytes 196616 | tf_op jit(solution)/shard_map/ppermute | solution.py:258
  35.7 0.5 collective-permute-start.2
  36.2 2.3 %collective-permute-done.4 = bf16[128,256]{1,0:T(8,128)(2,1)S(1)} collective-permute-done((bf16[128,256]{1,0:T(8,128)(2,1)S(1)}, bf16[128,256]{1,0:T(8,128)(2,1)S(1)}, u32[]{:S(2)}, u32[]{:S(2)}) %collective-permute-start.4) | collective-permute-done | bytes 65568 | tf_op jit(solution)/shard_map/ppermute | solution.py:258
  38.5 1.4 %collective-permute-done.3 = bf16[128,256]{1,0:T(8,128)(2,1)S(1)} collective-permute-done((bf16[128,256]{1,0:T(8,128)(2,1)S(1)}, bf16[128,256]{1,0:T(8,128)(2,1)S(1)}, u32[]{:S(2)}, u32[]{:S(2)}) %collective-permute-start.3) | collective-permute-done | bytes 65568 | tf_op jit(solution)/shard_map/ppermute | solution.py:258
  39.9 0.1 collective-permute-done.2
  40.0 0.1 collective-permute-start.6
  40.1 2.0 %collective-permute-start.7 = (bf16[128,256]{1,0:T(8,128)(2,1)S(1)}, bf16[128,256]{1,0:T(8,128)(2,1)S(1)}, u32[]{:S(2)}, u32[]{:S(2)}) collective-permute-start(bf16[128,256]{1,0:T(8,128)(2,1)S(1)} %get-tuple-element.37), channel_id=1, source_target_pairs={{0,65},{1,64},{16,81},{17,80},{32,97},{33,96},{48,113},{49,112},{6... | collective-permute-start | bytes 196616 | tf_op jit(solution)/shard_map/ppermute | solution.py:343
  42.1 1.7 %collective-permute-start.5 = (bf16[128,256]{1,0:T(8,128)(2,1)S(1)}, bf16[128,256]{1,0:T(8,128)(2,1)S(1)}, u32[]{:S(2)}, u32[]{:S(2)}) collective-permute-start(bf16[128,256]{1,0:T(8,128)(2,1)S(1)} %get-tuple-element.37), channel_id=1, source_target_pairs={{0,64},{16,80},{32,96},{48,112},{64,0},{80,16},{96,32},{112,48},{1... | collective-permute-start | bytes 196616 | tf_op jit(solution)/shard_map/ppermute | solution.py:258
  43.8 1.8 %collective-permute-done.7.far_twin = bf16[128,256]{1,0:T(8,128)(2,1)S(1)} collective-permute-done((bf16[128,256]{1,0:T(8,128)(2,1)S(1)}, bf16[128,256]{1,0:T(8,128)(2,1)S(1)}, u32[]{:S(2)}, u32[]{:S(2)}) %collective-permute-start.7) | collective-permute-done | bytes 65568 | tf_op jit(solution)/shard_map/ppermute | solution.py:343
  45.6 2.3 %collective-permute-done.5.far = bf16[128,256]{1,0:T(8,128)(2,1)S(1)} collective-permute-done((bf16[128,256]{1,0:T(8,128)(2,1)S(1)}, bf16[128,256]{1,0:T(8,128)(2,1)S(1)}, u32[]{:S(2)}, u32[]{:S(2)}) %collective-permute-start.5) | collective-permute-done | bytes 65568 | tf_op jit(solution)/shard_map/ppermute | solution.py:258
  47.9 0.0 collective-permute-done.6.twin
  47.9 0.0 collective-permute-done.8.peer_ref
  47.9 2.0 %filter.1 = bf16[8,2,16,2048]{3,2,1,0:T(8,128)(2,1)S(1)} custom-call(f32[128,256]{1,0:T(8,128)S(1)} %get-tuple-element.38.mine, bf16[128,256]{1,0:T(8,128)(2,1)S(1)} %collective-permute-done.5.far, f32[128,256]{1,0:T(8,128)S(1)} %collective-permute-done.6.twin, bf16[128,256]{1,0:T(8,128)(2,1)S(1)} %collective-permute-done.7.far_twin, ...), custom_call_target="tpu_custom_call" | custom-call | tf_op jit(solution)/shard_map/filter/pallas_call | solution.py:348
  49.9 17.7 %all_to_all.10.got = bf16[8,2,16,2048]{3,2,1,0:T(8,128)(2,1)S(1)} all-to-all(bf16[8,2,16,2048]{3,2,1,0:T(8,128)(2,1)S(1)} %filter.1), channel_id=1, replica_groups=mesh['chan'=8,'bin'=8,'core'=2] {'bin'}, dimensions={0} | all-to-all | bytes 2097152 | tf_op jit(solution)/shard_map/all_to_all | solution.py:358
  67.6 1.3 %place.1 = bf16[16,2,8,2048]{3,2,1,0:T(8,128)(2,1)} custom-call(bf16[8,2,16,2048]{3,2,1,0:T(8,128)(2,1)S(1)} %all_to_all.10.got), custom_call_target="tpu_custom_call" | custom-call | tf_op jit(solution)/shard_map/place/pallas_call | solution.py:359
  (3 shorter events, 0.1 us)
Async XLA Ops:
  1.8 24.5 %all-to-all-start = ((bf16[64,2,16,128]{3,2,1,0:T(8,128)(2,1)}), bf16[64,2,16,128]{3,2,1,0:T(8,128)(2,1)S(1)}, u32[]{:S(2)}, u32[]{:S(2)}) async-start(bf16[64,2,16,128]{3,2,1,0:T(8,128)(2,1)} %get-tuple-element.21), calls=%async_computation | async-start | bytes 1048576 | tf_op jit(solution)/shard_map/all_to_all | solution.py:283
  26.3 2.4 %collective-permute-start = (bf16[64,2,16,128]{3,2,1,0:T(8,128)(2,1)S(1)}, bf16[64,2,16,128]{3,2,1,0:T(8,128)(2,1)S(1)}, u32[]{:S(2)}, u32[]{:S(2)}) collective-permute-start(bf16[64,2,16,128]{3,2,1,0:T(8,128)(2,1)S(1)} %all-to-all-done), channel_id=1, source_target_pairs={{0,1},{1,0},{2,3},{3,2},{4,5},{5,4},{6,7},{7,6},{8,9},{9,8},{10,11... | collective-permute-start | bytes 1572872 | tf_op jit(solution)/shard_map/ppermute | solution.py:255
  30.6 1.6 %collective-permute-start.1 = (f32[128,256]{1,0:T(8,128)S(1)}, f32[128,256]{1,0:T(8,128)S(1)}, u32[]{:S(2)}, u32[]{:S(2)}) collective-permute-start(f32[128,256]{1,0:T(8,128)S(1)} %get-tuple-element.33), channel_id=1, source_target_pairs={{0,1},{1,0},{2,3},{3,2},{4,5},{5,4},{6,7},{7,6},{8,9},{9,8},{10,11... | collective-permute-start | bytes 393224 | tf_op jit(solution)/shard_map/ppermute | solution.py:255
  32.2 15.7 %collective-permute-start.8 = (bf16[512,1024]{1,0:T(8,128)(2,1)S(1)}, bf16[512,1024]{1,0:T(8,128)(2,1)S(1)}, u32[]{:S(2)}, u32[]{:S(2)}) collective-permute-start(bf16[512,1024]{1,0:T(8,128)(2,1)S(1)} %get-tuple-element.36.y_ref), channel_id=1, source_target_pairs={{0,1},{1,0},{2,3},{3,2},{4,5},{5,4},{6,7},{7,6},{8,9},{9,8},{10,11... | collective-permute-start | bytes 3145736 | tf_op jit(solution)/shard_map/ppermute | solution.py:255
  32.6 5.9 %collective-permute-start.4 = (bf16[128,256]{1,0:T(8,128)(2,1)S(1)}, bf16[128,256]{1,0:T(8,128)(2,1)S(1)}, u32[]{:S(2)}, u32[]{:S(2)}) collective-permute-start(bf16[128,256]{1,0:T(8,128)(2,1)S(1)} %convert_element_type.15), channel_id=1, source_target_pairs={{0,32},{16,48},{32,0},{48,16},{64,96},{80,112},{96,64},{112,80},{1... | collective-permute-start | bytes 196616 | tf_op jit(solution)/shard_map/ppermute | solution.py:258
  34.3 5.6 %collective-permute-start.3 = (bf16[128,256]{1,0:T(8,128)(2,1)S(1)}, bf16[128,256]{1,0:T(8,128)(2,1)S(1)}, u32[]{:S(2)}, u32[]{:S(2)}) collective-permute-start(bf16[128,256]{1,0:T(8,128)(2,1)S(1)} %convert_element_type.15), channel_id=1, source_target_pairs={{0,48},{16,32},{32,16},{48,0},{64,112},{80,96},{96,80},{112,64},{1... | collective-permute-start | bytes 196616 | tf_op jit(solution)/shard_map/ppermute | solution.py:258
  35.7 4.3 %collective-permute-start.2 = (bf16[128,256]{1,0:T(8,128)(2,1)S(1)}, bf16[128,256]{1,0:T(8,128)(2,1)S(1)}, u32[]{:S(2)}, u32[]{:S(2)}) collective-permute-start(bf16[128,256]{1,0:T(8,128)(2,1)S(1)} %convert_element_type.15), channel_id=1, source_target_pairs={{0,16},{16,0},{32,48},{48,32},{64,80},{80,64},{96,112},{112,96},{1... | collective-permute-start | bytes 196616 | tf_op jit(solution)/shard_map/ppermute | solution.py:258
  40.0 7.8 %collective-permute-start.6 = (f32[128,256]{1,0:T(8,128)S(1)}, f32[128,256]{1,0:T(8,128)S(1)}, u32[]{:S(2)}, u32[]{:S(2)}) collective-permute-start(f32[128,256]{1,0:T(8,128)S(1)} %get-tuple-element.38.mine), channel_id=1, source_target_pairs={{0,1},{1,0},{2,3},{3,2},{4,5},{5,4},{6,7},{7,6},{8,9},{9,8},{10,11... | collective-permute-start | bytes 393224 | tf_op jit(solution)/shard_map/ppermute | solution.py:255
  40.1 5.4 %collective-permute-start.7 = (bf16[128,256]{1,0:T(8,128)(2,1)S(1)}, bf16[128,256]{1,0:T(8,128)(2,1)S(1)}, u32[]{:S(2)}, u32[]{:S(2)}) collective-permute-start(bf16[128,256]{1,0:T(8,128)(2,1)S(1)} %get-tuple-element.37), channel_id=1, source_target_pairs={{0,65},{1,64},{16,81},{17,80},{32,97},{33,96},{48,113},{49,112},{6... | collective-permute-start | bytes 196616 | tf_op jit(solution)/shard_map/ppermute | solution.py:343
  42.1 5.8 %collective-permute-start.5 = (bf16[128,256]{1,0:T(8,128)(2,1)S(1)}, bf16[128,256]{1,0:T(8,128)(2,1)S(1)}, u32[]{:S(2)}, u32[]{:S(2)}) collective-permute-start(bf16[128,256]{1,0:T(8,128)(2,1)S(1)} %get-tuple-element.37), channel_id=1, source_target_pairs={{0,64},{16,80},{32,96},{48,112},{64,0},{80,16},{96,32},{112,48},{1... | collective-permute-start | bytes 196616 | tf_op jit(solution)/shard_map/ppermute | solution.py:258

commit v15 on v14

--- a/solution.py
+++ b/solution.py
@@ -149,7 +149,22 @@
         out_ref[:half, lanes], out_ref[half:, lanes] = real, imag
 
 
-def other_kernel(upper, lower, samples, own, y_ref, keep_ref, send_ref, data, gram):
+def gram_rows(y_ref, start):
+    frames = y_ref.shape[0] // 2
+    half = frames // CORES
+    left = jnp.concatenate([y_ref[pl.ds(start, half)], y_ref[pl.ds(frames + start, half)]], axis=0)
+    products = lax.dot_general(left, y_ref[...], (((1,), (1,)), ((), ())), preferred_element_type=F32)
+    return (products[:half, :frames] + products[half:, frames:]) + (
+        products[:half, frames:] - products[half:, :frames]
+    )
+
+
+def keep_kernel(y_ref, out_ref):
+    half = out_ref.shape[0]
+    out_ref[...] = gram_rows(y_ref, pl.multiple_of(lax.axis_index("core") * half, half))
+
+
+def other_kernel(upper, lower, samples, own, y_ref, send_ref, data):
     core = lax.axis_index("core")
     frames = y_ref.shape[0] // 2
     half = frames // CORES
@@ -161,13 +176,7 @@
     for operator, start in ((upper, 0), (lower, upper.shape[2])):
         for lanes, real, imag in beamform(data, operator, start):
             y_ref[pl.ds(there, half), lanes], y_ref[pl.ds(frames + there, half), lanes] = real, imag
-    y = y_ref[...]
-    products = lax.dot_general(y, y, (((1,), (1,)), ((), ())), preferred_element_type=F32)
-    gram[...] = (products[:frames, :frames] + products[frames:, frames:]) + (
-        products[:frames, frames:] - products[frames:, :frames]
-    )
-    keep_ref[...] = gram[pl.ds(here, half), :]
-    send_ref[...] = gram[pl.ds(there, half), :]
+    send_ref[...] = gram_rows(y_ref, there)
 
 
 def halves(x):
@@ -176,12 +185,9 @@
 
 
 def product(left, right):
-    left_high, left_low = halves(left)
-    right_high, right_low = halves(right)
+    left = left.astype(BF16)
     return jnp.dot(
-        jnp.concatenate([left_high, left_high, left_low], axis=1),
-        jnp.concatenate([right_high, right_low, right_high], axis=0),
-        preferred_element_type=F32,
+        jnp.concatenate([left, left], axis=1), jnp.concatenate(halves(right), axis=0), preferred_element_type=F32
     )
 
 
@@ -201,7 +207,8 @@
     real, imag, flipped = unpack(packed)
     left = jnp.concatenate([real, imag], axis=1)
     second = product(left, jnp.concatenate([packed, flipped], axis=0)) * (factor * factor)
-    third = product(left, jnp.concatenate([second, jnp.transpose(second)], axis=0)) * factor
+    right = jnp.concatenate([second, jnp.transpose(second)], axis=0).astype(BF16)
+    third = jnp.dot(left.astype(BF16), right, preferred_element_type=F32) * factor
     rows = lax.broadcasted_iota(jnp.int32, (frames, frames), 0)
     cols = lax.broadcasted_iota(jnp.int32, (frames, frames), 1)
     identity = jnp.where(rows == cols, 1.0, 0.0).astype(F32)
@@ -322,18 +329,30 @@
         compiler_params=WIDE,
         cost_estimate=beam_cost,
     )(upper, in_hbm(lower), own)
-    y, keep, send = pl.pallas_call(
+    y, send = pl.pallas_call(
         other_kernel,
         name="beam_other",
-        out_shape=(shape(2 * frames, voxels), shape(half, frames, dtype=F32), shape(half, frames, dtype=F32)),
+        out_shape=(shape(2 * frames, voxels), shape(half, frames, dtype=F32)),
         in_specs=[VMEM, VMEM, VMEM, VMEM],
-        out_specs=(VMEM, VMEM, VMEM),
-        scratch_shapes=[pltpu.VMEM((frames, channels), BF16), pltpu.VMEM((frames, frames), F32)],
+        out_specs=(VMEM, VMEM),
+        scratch_shapes=[pltpu.VMEM((frames, channels), BF16)],
         compiler_params=WIDE,
         cost_estimate=beam_cost,
     )(upper, lower, other, mine)
 
-    total = keep + swap(send)
+    sent = swap(send)
+    keep = pl.pallas_call(
+        keep_kernel,
+        name="gram_keep",
+        out_shape=shape(half, frames, dtype=F32),
+        in_specs=[VMEM],
+        out_specs=VMEM,
+        compiler_params=WIDE,
+        cost_estimate=pl.CostEstimate(
+            flops=8 * half * frames * voxels, transcendentals=0, bytes_accessed=4 * frames * voxels
+        ),
+    )(y)
+    total = keep + sent
     total, y = lax.optimization_barrier((total, y))
     peer = swap(y)
     narrow = total.astype(BF16)

time: 69.1 us -> 68.9 us (level)
  transfers between devices with their start and end apart: 10 -> 10, of which waited for: 7 -> 7; matrix products, arithmetic and copies ran while one was open for 0% -> 0% of each run, Pallas kernels for 11% -> 12%
where the time goes in v15:
time: 68.9 us; the launch traced here: 68.6 us
  starting transfers between devices  19.8 us (29%)
  blocking collectives  17.7 us (26%)
  waiting for transfers between devices  16.3 us (24%)
  Pallas kernels  14.6 us (21%)
    all_to_all x1, blocking collectives, shards(): lax.all_to_all(applied, 'bin', split_axis=0, concat_axis=0, tiled=True)  17.7 us
    all_to_all x1, starting transfers between devices, shards(): lax.all_to_all(by_bin, ('chan', 'bin'), split_axis=0, concat_axis=0, tile...  11.5 us
    all_to_all x1, waiting for transfers between devices, shards(): lax.all_to_all(by_bin, ('chan', 'bin'), split_axis=0, concat_axis=0, tile...  7.88 us
    ppermute x4, waiting for transfers between devices, across(): return lax.ppermute(x, 'chan', [(a, a ^ bits) for a in range(chans)])  6.12 us
    ppermute x4, starting transfers between devices, across(): return lax.ppermute(x, 'chan', [(a, a ^ bits) for a in range(chans)])  5.24 us
    pallas_call x1, Pallas kernels, shards(): pl.pallas_call(operator_kernel, name='operator', out_shape=(shape(2, chan...  5.05 us
    pallas_call x1, Pallas kernels, shards(): pl.pallas_call(own_kernel, name='beam_own', out_shape=(shape(frames, voxe...  2.41 us
    pallas_call x1, Pallas kernels, shards(): pl.pallas_call(other_kernel, name='beam_other', out_shape=(shape(2 * fram...  2.07 us
  transfers between devices with their start and end apart: 10, of which 7 were waited for; matrix products, arithmetic and copies ran while one was open for 0% of the time, Pallas kernels for 12%

profile of v15, /device:TPU:0, one launch (start us, length us, event | category | flops | bytes accessed | tf_op | source)
XLA Modules:
  0.0 68.6 jit_solution(13623846799513266466)
XLA Ops:
  0.0 1.8 %spread.1 = (bf16[64,2,16,128]{3,2,1,0:T(8,128)(2,1)}, bf16[1024,8]{1,0:T(8,128)(2,1)S(1)}, bf16[2,8,1024]{2,1,0:T(8,128)(2,1)S(1)}, f32[2,1024]{1,0:T(2,128)S(1)}) custom-call(bf16[2,8,16,128]{3,2,1,0:T(8,128)(2,1)} %rf_ref.1, s32[3,1024]{1,0:T(4,128)} %elem_ref.1, s32[3,2048]{1,0:T(4,128)} %vox_ref.1, s32[8]{0:T(128)} %bins_ref.1), custom_call_target="tpu_custom_call" | custom-call | tf_op jit(solution)/shard_map/spread/pallas_call | solution.py:270
  1.8 11.5 %all-to-all-start = ((bf16[64,2,16,128]{3,2,1,0:T(8,128)(2,1)}), bf16[64,2,16,128]{3,2,1,0:T(8,128)(2,1)S(1)}, u32[]{:S(2)}, u32[]{:S(2)}) async-start(bf16[64,2,16,128]{3,2,1,0:T(8,128)(2,1)} %get-tuple-element.20), calls=%async_computation | async-start | bytes 1048576 | tf_op jit(solution)/shard_map/all_to_all | solution.py:290
  13.3 5.1 %operator.1 = (bf16[2,1024,512]{2,1,0:T(8,128)(2,1)S(1)}, bf16[2,1024,512]{2,1,0:T(8,128)(2,1)}) custom-call(bf16[1024,8]{1,0:T(8,128)(2,1)S(1)} %get-tuple-element.21.lhs_ref, bf16[2,8,1024]{2,1,0:T(8,128)(2,1)S(1)} %get-tuple-element.22.rhs_ref, f32[2,1024]{1,0:T(2,128)S(1)} %get-tuple-element.23.wave_ref), custom_call_target="tpu_custom_call" | custom-call | flops 62914560 | bytes 4194304 | tf_op jit(solution)/shard_map/operator/pallas_call | solution.py:293
  18.4 7.9 %all-to-all-done = bf16[64,2,16,128]{3,2,1,0:T(8,128)(2,1)S(1)} async-done(((bf16[64,2,16,128]{3,2,1,0:T(8,128)(2,1)}), bf16[64,2,16,128]{3,2,1,0:T(8,128)(2,1)S(1)}, u32[]{:S(2)}, u32[]{:S(2)}) %all-to-all-start) | async-done | bytes 524320 | tf_op jit(solution)/shard_map/all_to_all | solution.py:290
  26.3 0.0 collective-permute-start
  26.3 2.4 %beam_own.1 = (bf16[256,1024]{1,0:T(8,128)(2,1)S(1)}, bf16[2,1024,512]{2,1,0:T(8,128)(2,1)S(1)}) custom-call(bf16[2,1024,512]{2,1,0:T(8,128)(2,1)S(1)} %get-tuple-element.26.upper, bf16[2,1024,512]{2,1,0:T(8,128)(2,1)} %get-tuple-element.27.lower_ref, bf16[8,8,2,16,128]{4,3,2,1,0:T(8,128)(2,1)S(1)} %bitcast.2), custom_call_target="tpu_custom_call" | custom-call | flops 2147483648 | bytes 4194304 | tf_op jit(solution)/shard_map/beam_own/pallas_call | solution.py:319
  28.7 0.0 collective-permute-done
  28.7 2.1 %beam_other.1 = (bf16[512,1024]{1,0:T(8,128)(2,1)S(1)}, f32[128,256]{1,0:T(8,128)S(1)}) custom-call(bf16[2,1024,512]{2,1,0:T(8,128)(2,1)S(1)} %get-tuple-element.26.upper, bf16[2,1024,512]{2,1,0:T(8,128)(2,1)S(1)} %get-tuple-element.29.lower, bf16[8,8,2,16,128]{4,3,2,1,0:T(8,128)(2,1)S(1)} %bitcast.3, bf16[256,1024]{1,0:T(8,128)(2,1)S(1)} %get-tuple-element.30.own), custom_call_target="tpu_custom_call" | custom-call | flops 2147483648 | bytes 4194304 | tf_op jit(solution)/shard_map/beam_other/pallas_call | solution.py:332
  30.8 0.6 collective-permute-start.1
  31.4 0.5 gram_keep.1
  31.8 0.5 collective-permute-done.1
  32.4 0.4 collective-permute-start.8
  32.8 1.7 %collective-permute-start.4 = (bf16[128,256]{1,0:T(8,128)(2,1)S(1)}, bf16[128,256]{1,0:T(8,128)(2,1)S(1)}, u32[]{:S(2)}, u32[]{:S(2)}) collective-permute-start(bf16[128,256]{1,0:T(8,128)(2,1)S(1)} %convert_element_type.15), channel_id=1, source_target_pairs={{0,32},{16,48},{32,0},{48,16},{64,96},{80,112},{96,64},{112,80},{1... | collective-permute-start | bytes 196616 | tf_op jit(solution)/shard_map/ppermute | solution.py:265
  34.5 1.4 %collective-permute-start.3 = (bf16[128,256]{1,0:T(8,128)(2,1)S(1)}, bf16[128,256]{1,0:T(8,128)(2,1)S(1)}, u32[]{:S(2)}, u32[]{:S(2)}) collective-permute-start(bf16[128,256]{1,0:T(8,128)(2,1)S(1)} %convert_element_type.15), channel_id=1, source_target_pairs={{0,48},{16,32},{32,16},{48,0},{64,112},{80,96},{96,80},{112,64},{1... | collective-permute-start | bytes 196616 | tf_op jit(solution)/shard_map/ppermute | solution.py:265
  35.9 0.5 collective-permute-start.2
  36.4 2.3 %collective-permute-done.4 = bf16[128,256]{1,0:T(8,128)(2,1)S(1)} collective-permute-done((bf16[128,256]{1,0:T(8,128)(2,1)S(1)}, bf16[128,256]{1,0:T(8,128)(2,1)S(1)}, u32[]{:S(2)}, u32[]{:S(2)}) %collective-permute-start.4) | collective-permute-done | bytes 65568 | tf_op jit(solution)/shard_map/ppermute | solution.py:265
  38.7 1.4 %collective-permute-done.3 = bf16[128,256]{1,0:T(8,128)(2,1)S(1)} collective-permute-done((bf16[128,256]{1,0:T(8,128)(2,1)S(1)}, bf16[128,256]{1,0:T(8,128)(2,1)S(1)}, u32[]{:S(2)}, u32[]{:S(2)}) %collective-permute-start.3) | collective-permute-done | bytes 65568 | tf_op jit(solution)/shard_map/ppermute | solution.py:265
  40.1 0.1 collective-permute-done.2
  40.2 0.1 collective-permute-start.6
  40.3 2.0 %collective-permute-start.7 = (bf16[128,256]{1,0:T(8,128)(2,1)S(1)}, bf16[128,256]{1,0:T(8,128)(2,1)S(1)}, u32[]{:S(2)}, u32[]{:S(2)}) collective-permute-start(bf16[128,256]{1,0:T(8,128)(2,1)S(1)} %get-tuple-element.35), channel_id=1, source_target_pairs={{0,65},{1,64},{16,81},{17,80},{32,97},{33,96},{48,113},{49,112},{6... | collective-permute-start | bytes 196616 | tf_op jit(solution)/shard_map/ppermute | solution.py:362
  42.3 1.7 %collective-permute-start.5 = (bf16[128,256]{1,0:T(8,128)(2,1)S(1)}, bf16[128,256]{1,0:T(8,128)(2,1)S(1)}, u32[]{:S(2)}, u32[]{:S(2)}) collective-permute-start(bf16[128,256]{1,0:T(8,128)(2,1)S(1)} %get-tuple-element.35), channel_id=1, source_target_pairs={{0,64},{16,80},{32,96},{48,112},{64,0},{80,16},{96,32},{112,48},{1... | collective-permute-start | bytes 196616 | tf_op jit(solution)/shard_map/ppermute | solution.py:265
  44.0 1.8 %collective-permute-done.7.far_twin = bf16[128,256]{1,0:T(8,128)(2,1)S(1)} collective-permute-done((bf16[128,256]{1,0:T(8,128)(2,1)S(1)}, bf16[128,256]{1,0:T(8,128)(2,1)S(1)}, u32[]{:S(2)}, u32[]{:S(2)}) %collective-permute-start.7) | collective-permute-done | bytes 65568 | tf_op jit(solution)/shard_map/ppermute | solution.py:362
  45.7 2.3 %collective-permute-done.5.far = bf16[128,256]{1,0:T(8,128)(2,1)S(1)} collective-permute-done((bf16[128,256]{1,0:T(8,128)(2,1)S(1)}, bf16[128,256]{1,0:T(8,128)(2,1)S(1)}, u32[]{:S(2)}, u32[]{:S(2)}) %collective-permute-start.5) | collective-permute-done | bytes 65568 | tf_op jit(solution)/shard_map/ppermute | solution.py:265
  48.1 0.0 collective-permute-done.6.twin
  48.1 0.0 collective-permute-done.8.peer_ref
  48.1 1.6 %filter.1 = bf16[8,2,16,2048]{3,2,1,0:T(8,128)(2,1)S(1)} custom-call(f32[128,256]{1,0:T(8,128)S(1)} %get-tuple-element.36.mine, bf16[128,256]{1,0:T(8,128)(2,1)S(1)} %collective-permute-done.5.far, f32[128,256]{1,0:T(8,128)S(1)} %collective-permute-done.6.twin, bf16[128,256]{1,0:T(8,128)(2,1)S(1)} %collective-permute-done.7.far_twin, ...), custom_call_target="tpu_custom_call" | custom-call | tf_op jit(solution)/shard_map/filter/pallas_call | solution.py:367
  49.6 17.7 %all_to_all.10.got = bf16[8,2,16,2048]{3,2,1,0:T(8,128)(2,1)S(1)} all-to-all(bf16[8,2,16,2048]{3,2,1,0:T(8,128)(2,1)S(1)} %filter.1), channel_id=1, replica_groups=mesh['chan'=8,'bin'=8,'core'=2] {'bin'}, dimensions={0} | all-to-all | bytes 2097152 | tf_op jit(solution)/shard_map/all_to_all | solution.py:377
  67.3 1.3 %place.1 = bf16[16,2,8,2048]{3,2,1,0:T(8,128)(2,1)} custom-call(bf16[8,2,16,2048]{3,2,1,0:T(8,128)(2,1)S(1)} %all_to_all.10.got), custom_call_target="tpu_custom_call" | custom-call | tf_op jit(solution)/shard_map/place/pallas_call | solution.py:378
  (3 shorter events, 0.1 us)
Async XLA Ops:
  1.8 24.5 %all-to-all-start = ((bf16[64,2,16,128]{3,2,1,0:T(8,128)(2,1)}), bf16[64,2,16,128]{3,2,1,0:T(8,128)(2,1)S(1)}, u32[]{:S(2)}, u32[]{:S(2)}) async-start(bf16[64,2,16,128]{3,2,1,0:T(8,128)(2,1)} %get-tuple-element.20), calls=%async_computation | async-start | bytes 1048576 | tf_op jit(solution)/shard_map/all_to_all | solution.py:290
  26.3 2.4 %collective-permute-start = (bf16[64,2,16,128]{3,2,1,0:T(8,128)(2,1)S(1)}, bf16[64,2,16,128]{3,2,1,0:T(8,128)(2,1)S(1)}, u32[]{:S(2)}, u32[]{:S(2)}) collective-permute-start(bf16[64,2,16,128]{3,2,1,0:T(8,128)(2,1)S(1)} %all-to-all-done), channel_id=1, source_target_pairs={{0,1},{1,0},{2,3},{3,2},{4,5},{5,4},{6,7},{7,6},{8,9},{9,8},{10,11... | collective-permute-start | bytes 1572872 | tf_op jit(solution)/shard_map/ppermute | solution.py:262
  30.8 1.6 %collective-permute-start.1 = (f32[128,256]{1,0:T(8,128)S(1)}, f32[128,256]{1,0:T(8,128)S(1)}, u32[]{:S(2)}, u32[]{:S(2)}) collective-permute-start(f32[128,256]{1,0:T(8,128)S(1)} %get-tuple-element.32), channel_id=1, source_target_pairs={{0,1},{1,0},{2,3},{3,2},{4,5},{5,4},{6,7},{7,6},{8,9},{9,8},{10,11... | collective-permute-start | bytes 393224 | tf_op jit(solution)/shard_map/ppermute | solution.py:262
  32.4 15.7 %collective-permute-start.8 = (bf16[512,1024]{1,0:T(8,128)(2,1)S(1)}, bf16[512,1024]{1,0:T(8,128)(2,1)S(1)}, u32[]{:S(2)}, u32[]{:S(2)}) collective-permute-start(bf16[512,1024]{1,0:T(8,128)(2,1)S(1)} %get-tuple-element.34.y_ref), channel_id=1, source_target_pairs={{0,1},{1,0},{2,3},{3,2},{4,5},{5,4},{6,7},{7,6},{8,9},{9,8},{10,11... | collective-permute-start | bytes 3145736 | tf_op jit(solution)/shard_map/ppermute | solution.py:262
  32.8 5.9 %collective-permute-start.4 = (bf16[128,256]{1,0:T(8,128)(2,1)S(1)}, bf16[128,256]{1,0:T(8,128)(2,1)S(1)}, u32[]{:S(2)}, u32[]{:S(2)}) collective-permute-start(bf16[128,256]{1,0:T(8,128)(2,1)S(1)} %convert_element_type.15), channel_id=1, source_target_pairs={{0,32},{16,48},{32,0},{48,16},{64,96},{80,112},{96,64},{112,80},{1... | collective-permute-start | bytes 196616 | tf_op jit(solution)/shard_map/ppermute | solution.py:265
  34.5 5.6 %collective-permute-start.3 = (bf16[128,256]{1,0:T(8,128)(2,1)S(1)}, bf16[128,256]{1,0:T(8,128)(2,1)S(1)}, u32[]{:S(2)}, u32[]{:S(2)}) collective-permute-start(bf16[128,256]{1,0:T(8,128)(2,1)S(1)} %convert_element_type.15), channel_id=1, source_target_pairs={{0,48},{16,32},{32,16},{48,0},{64,112},{80,96},{96,80},{112,64},{1... | collective-permute-start | bytes 196616 | tf_op jit(solution)/shard_map/ppermute | solution.py:265
  35.9 4.3 %collective-permute-start.2 = (bf16[128,256]{1,0:T(8,128)(2,1)S(1)}, bf16[128,256]{1,0:T(8,128)(2,1)S(1)}, u32[]{:S(2)}, u32[]{:S(2)}) collective-permute-start(bf16[128,256]{1,0:T(8,128)(2,1)S(1)} %convert_element_type.15), channel_id=1, source_target_pairs={{0,16},{16,0},{32,48},{48,32},{64,80},{80,64},{96,112},{112,96},{1... | collective-permute-start | bytes 196616 | tf_op jit(solution)/shard_map/ppermute | solution.py:265
  40.2 7.8 %collective-permute-start.6 = (f32[128,256]{1,0:T(8,128)S(1)}, f32[128,256]{1,0:T(8,128)S(1)}, u32[]{:S(2)}, u32[]{:S(2)}) collective-permute-start(f32[128,256]{1,0:T(8,128)S(1)} %get-tuple-element.36.mine), channel_id=1, source_target_pairs={{0,1},{1,0},{2,3},{3,2},{4,5},{5,4},{6,7},{7,6},{8,9},{9,8},{10,11... | collective-permute-start | bytes 393224 | tf_op jit(solution)/shard_map/ppermute | solution.py:262
  40.3 5.4 %collective-permute-start.7 = (bf16[128,256]{1,0:T(8,128)(2,1)S(1)}, bf16[128,256]{1,0:T(8,128)(2,1)S(1)}, u32[]{:S(2)}, u32[]{:S(2)}) collective-permute-start(bf16[128,256]{1,0:T(8,128)(2,1)S(1)} %get-tuple-element.35), channel_id=1, source_target_pairs={{0,65},{1,64},{16,81},{17,80},{32,97},{33,96},{48,113},{49,112},{6... | collective-permute-start | bytes 196616 | tf_op jit(solution)/shard_map/ppermute | solution.py:362
  42.3 5.8 %collective-permute-start.5 = (bf16[128,256]{1,0:T(8,128)(2,1)S(1)}, bf16[128,256]{1,0:T(8,128)(2,1)S(1)}, u32[]{:S(2)}, u32[]{:S(2)}) collective-permute-start(bf16[128,256]{1,0:T(8,128)(2,1)S(1)} %get-tuple-element.35), channel_id=1, source_target_pairs={{0,64},{16,80},{32,96},{48,112},{64,0},{80,16},{96,32},{112,48},{1... | collective-permute-start | bytes 196616 | tf_op jit(solution)/shard_map/ppermute | solution.py:265

commit v16 on v14

--- a/solution.py
+++ b/solution.py
@@ -176,12 +176,9 @@
 
 
 def product(left, right):
-    left_high, left_low = halves(left)
-    right_high, right_low = halves(right)
+    left = left.astype(BF16)
     return jnp.dot(
-        jnp.concatenate([left_high, left_high, left_low], axis=1),
-        jnp.concatenate([right_high, right_low, right_high], axis=0),
-        preferred_element_type=F32,
+        jnp.concatenate([left, left], axis=1), jnp.concatenate(halves(right), axis=0), preferred_element_type=F32
     )
 
 
@@ -201,7 +198,8 @@
     real, imag, flipped = unpack(packed)
     left = jnp.concatenate([real, imag], axis=1)
     second = product(left, jnp.concatenate([packed, flipped], axis=0)) * (factor * factor)
-    third = product(left, jnp.concatenate([second, jnp.transpose(second)], axis=0)) * factor
+    right = jnp.concatenate([second, jnp.transpose(second)], axis=0).astype(BF16)
+    third = jnp.dot(left.astype(BF16), right, preferred_element_type=F32) * factor
     rows = lax.broadcasted_iota(jnp.int32, (frames, frames), 0)
     cols = lax.broadcasted_iota(jnp.int32, (frames, frames), 1)
     identity = jnp.where(rows == cols, 1.0, 0.0).astype(F32)

time: 69.1 us -> 68.7 us (level)
  no operation moved by 1% of the time
where the time goes in v16:
time: 68.7 us; the launch traced here: 68.4 us
  starting transfers between devices  19.8 us (29%)
  blocking collectives  17.7 us (26%)
  waiting for transfers between devices  16.8 us (24%)
  Pallas kernels  14 us (20%)
    all_to_all x1, blocking collectives, shards(): lax.all_to_all(applied, 'bin', split_axis=0, concat_axis=0, tiled=True)  17.7 us
    all_to_all x1, starting transfers between devices, shards(): lax.all_to_all(by_bin, ('chan', 'bin'), split_axis=0, concat_axis=0, tile...  11.5 us
    all_to_all x1, waiting for transfers between devices, shards(): lax.all_to_all(by_bin, ('chan', 'bin'), split_axis=0, concat_axis=0, tile...  7.88 us
    ppermute x4, waiting for transfers between devices, across(): return lax.ppermute(x, 'chan', [(a, a ^ bits) for a in range(chans)])  6.12 us
    ppermute x4, starting transfers between devices, across(): return lax.ppermute(x, 'chan', [(a, a ^ bits) for a in range(chans)])  5.24 us
    pallas_call x1, Pallas kernels, shards(): pl.pallas_call(operator_kernel, name='operator', out_shape=(shape(2, chan...  5.05 us
    pallas_call x1, Pallas kernels, shards(): pl.pallas_call(own_kernel, name='beam_own', out_shape=(shape(frames, voxe...  2.41 us
    ppermute x1, starting transfers between devices, shards(): lax.ppermute(narrow, ('chan', 'core'), [(2 * a + c, 2 * (a ^ 4) + 1 - c)...  1.97 us
  transfers between devices with their start and end apart: 10, of which 7 were waited for; matrix products, arithmetic and copies ran while one was open for 0% of the time, Pallas kernels for 11%

profile of v16, /device:TPU:0, one launch (start us, length us, event | category | flops | bytes accessed | tf_op | source)
XLA Modules:
  0.0 68.4 jit_solution(8206427866522578371)
XLA Ops:
  0.0 1.8 %spread.1 = (bf16[64,2,16,128]{3,2,1,0:T(8,128)(2,1)}, bf16[1024,8]{1,0:T(8,128)(2,1)S(1)}, bf16[2,8,1024]{2,1,0:T(8,128)(2,1)S(1)}, f32[2,1024]{1,0:T(2,128)S(1)}) custom-call(bf16[2,8,16,128]{3,2,1,0:T(8,128)(2,1)} %rf_ref.1, s32[3,1024]{1,0:T(4,128)} %elem_ref.1, s32[3,2048]{1,0:T(4,128)} %vox_ref.1, s32[8]{0:T(128)} %bins_ref.1), custom_call_target="tpu_custom_call" | custom-call | tf_op jit(solution)/shard_map/spread/pallas_call | solution.py:261
  1.8 11.5 %all-to-all-start = ((bf16[64,2,16,128]{3,2,1,0:T(8,128)(2,1)}), bf16[64,2,16,128]{3,2,1,0:T(8,128)(2,1)S(1)}, u32[]{:S(2)}, u32[]{:S(2)}) async-start(bf16[64,2,16,128]{3,2,1,0:T(8,128)(2,1)} %get-tuple-element.21), calls=%async_computation | async-start | bytes 1048576 | tf_op jit(solution)/shard_map/all_to_all | solution.py:281
  13.3 5.1 %operator.1 = (bf16[2,1024,512]{2,1,0:T(8,128)(2,1)S(1)}, bf16[2,1024,512]{2,1,0:T(8,128)(2,1)}) custom-call(bf16[1024,8]{1,0:T(8,128)(2,1)S(1)} %get-tuple-element.22.lhs_ref, bf16[2,8,1024]{2,1,0:T(8,128)(2,1)S(1)} %get-tuple-element.23.rhs_ref, f32[2,1024]{1,0:T(2,128)S(1)} %get-tuple-element.24.wave_ref), custom_call_target="tpu_custom_call" | custom-call | flops 62914560 | bytes 4194304 | tf_op jit(solution)/shard_map/operator/pallas_call | solution.py:284
  18.4 7.9 %all-to-all-done = bf16[64,2,16,128]{3,2,1,0:T(8,128)(2,1)S(1)} async-done(((bf16[64,2,16,128]{3,2,1,0:T(8,128)(2,1)}), bf16[64,2,16,128]{3,2,1,0:T(8,128)(2,1)S(1)}, u32[]{:S(2)}, u32[]{:S(2)}) %all-to-all-start) | async-done | bytes 524320 | tf_op jit(solution)/shard_map/all_to_all | solution.py:281
  26.3 0.0 collective-permute-start
  26.3 2.4 %beam_own.1 = (bf16[256,1024]{1,0:T(8,128)(2,1)S(1)}, bf16[2,1024,512]{2,1,0:T(8,128)(2,1)S(1)}) custom-call(bf16[2,1024,512]{2,1,0:T(8,128)(2,1)S(1)} %get-tuple-element.27.upper, bf16[2,1024,512]{2,1,0:T(8,128)(2,1)} %get-tuple-element.28.lower_ref, bf16[8,8,2,16,128]{4,3,2,1,0:T(8,128)(2,1)S(1)} %bitcast.2), custom_call_target="tpu_custom_call" | custom-call | flops 2147483648 | bytes 4194304 | tf_op jit(solution)/shard_map/beam_own/pallas_call | solution.py:310
  28.7 0.0 collective-permute-done
  28.7 1.9 %beam_other.1 = (bf16[512,1024]{1,0:T(8,128)(2,1)S(1)}, f32[128,256]{1,0:T(8,128)S(1)}, f32[128,256]{1,0:T(8,128)S(1)}) custom-call(bf16[2,1024,512]{2,1,0:T(8,128)(2,1)S(1)} %get-tuple-element.27.upper, bf16[2,1024,512]{2,1,0:T(8,128)(2,1)S(1)} %get-tuple-element.30.lower, bf16[8,8,2,16,128]{4,3,2,1,0:T(8,128)(2,1)S(1)} %bitcast.3, ...), custom_call_target="tpu_custom_call" | custom-call | flops 2147483648 | bytes 4194304 | tf_op jit(solution)/shard_map/beam_other/pallas_call | solution.py:323
  30.6 0.6 collective-permute-start.1
  31.2 1.0 %collective-permute-done.1 = f32[128,256]{1,0:T(8,128)S(1)} collective-permute-done((f32[128,256]{1,0:T(8,128)S(1)}, f32[128,256]{1,0:T(8,128)S(1)}, u32[]{:S(2)}, u32[]{:S(2)}) %collective-permute-start.1) | collective-permute-done | bytes 131104 | tf_op jit(solution)/shard_map/ppermute | solution.py:253
  32.2 0.4 collective-permute-start.8
  32.6 1.7 %collective-permute-start.4 = (bf16[128,256]{1,0:T(8,128)(2,1)S(1)}, bf16[128,256]{1,0:T(8,128)(2,1)S(1)}, u32[]{:S(2)}, u32[]{:S(2)}) collective-permute-start(bf16[128,256]{1,0:T(8,128)(2,1)S(1)} %convert_element_type.15), channel_id=1, source_target_pairs={{0,32},{16,48},{32,0},{48,16},{64,96},{80,112},{96,64},{112,80},{1... | collective-permute-start | bytes 196616 | tf_op jit(solution)/shard_map/ppermute | solution.py:256
  34.3 1.4 %collective-permute-start.3 = (bf16[128,256]{1,0:T(8,128)(2,1)S(1)}, bf16[128,256]{1,0:T(8,128)(2,1)S(1)}, u32[]{:S(2)}, u32[]{:S(2)}) collective-permute-start(bf16[128,256]{1,0:T(8,128)(2,1)S(1)} %convert_element_type.15), channel_id=1, source_target_pairs={{0,48},{16,32},{32,16},{48,0},{64,112},{80,96},{96,80},{112,64},{1... | collective-permute-start | bytes 196616 | tf_op jit(solution)/shard_map/ppermute | solution.py:256
  35.7 0.5 collective-permute-start.2
  36.2 2.3 %collective-permute-done.4 = bf16[128,256]{1,0:T(8,128)(2,1)S(1)} collective-permute-done((bf16[128,256]{1,0:T(8,128)(2,1)S(1)}, bf16[128,256]{1,0:T(8,128)(2,1)S(1)}, u32[]{:S(2)}, u32[]{:S(2)}) %collective-permute-start.4) | collective-permute-done | bytes 65568 | tf_op jit(solution)/shard_map/ppermute | solution.py:256
  38.5 1.4 %collective-permute-done.3 = bf16[128,256]{1,0:T(8,128)(2,1)S(1)} collective-permute-done((bf16[128,256]{1,0:T(8,128)(2,1)S(1)}, bf16[128,256]{1,0:T(8,128)(2,1)S(1)}, u32[]{:S(2)}, u32[]{:S(2)}) %collective-permute-start.3) | collective-permute-done | bytes 65568 | tf_op jit(solution)/shard_map/ppermute | solution.py:256
  39.9 0.1 collective-permute-done.2
  40.0 0.1 collective-permute-start.6
  40.1 2.0 %collective-permute-start.7 = (bf16[128,256]{1,0:T(8,128)(2,1)S(1)}, bf16[128,256]{1,0:T(8,128)(2,1)S(1)}, u32[]{:S(2)}, u32[]{:S(2)}) collective-permute-start(bf16[128,256]{1,0:T(8,128)(2,1)S(1)} %get-tuple-element.37), channel_id=1, source_target_pairs={{0,65},{1,64},{16,81},{17,80},{32,97},{33,96},{48,113},{49,112},{6... | collective-permute-start | bytes 196616 | tf_op jit(solution)/shard_map/ppermute | solution.py:341
  42.1 1.7 %collective-permute-start.5 = (bf16[128,256]{1,0:T(8,128)(2,1)S(1)}, bf16[128,256]{1,0:T(8,128)(2,1)S(1)}, u32[]{:S(2)}, u32[]{:S(2)}) collective-permute-start(bf16[128,256]{1,0:T(8,128)(2,1)S(1)} %get-tuple-element.37), channel_id=1, source_target_pairs={{0,64},{16,80},{32,96},{48,112},{64,0},{80,16},{96,32},{112,48},{1... | collective-permute-start | bytes 196616 | tf_op jit(solution)/shard_map/ppermute | solution.py:256
  43.8 1.8 %collective-permute-done.7.far_twin = bf16[128,256]{1,0:T(8,128)(2,1)S(1)} collective-permute-done((bf16[128,256]{1,0:T(8,128)(2,1)S(1)}, bf16[128,256]{1,0:T(8,128)(2,1)S(1)}, u32[]{:S(2)}, u32[]{:S(2)}) %collective-permute-start.7) | collective-permute-done | bytes 65568 | tf_op jit(solution)/shard_map/ppermute | solution.py:341
  45.6 2.3 %collective-permute-done.5.far = bf16[128,256]{1,0:T(8,128)(2,1)S(1)} collective-permute-done((bf16[128,256]{1,0:T(8,128)(2,1)S(1)}, bf16[128,256]{1,0:T(8,128)(2,1)S(1)}, u32[]{:S(2)}, u32[]{:S(2)}) %collective-permute-start.5) | collective-permute-done | bytes 65568 | tf_op jit(solution)/shard_map/ppermute | solution.py:256
  47.9 0.0 collective-permute-done.6.twin
  47.9 0.0 collective-permute-done.8.peer_ref
  47.9 1.6 %filter.1 = bf16[8,2,16,2048]{3,2,1,0:T(8,128)(2,1)S(1)} custom-call(f32[128,256]{1,0:T(8,128)S(1)} %get-tuple-element.38.mine, bf16[128,256]{1,0:T(8,128)(2,1)S(1)} %collective-permute-done.5.far, f32[128,256]{1,0:T(8,128)S(1)} %collective-permute-done.6.twin, bf16[128,256]{1,0:T(8,128)(2,1)S(1)} %collective-permute-done.7.far_twin, ...), custom_call_target="tpu_custom_call" | custom-call | tf_op jit(solution)/shard_map/filter/pallas_call | solution.py:346
  49.5 17.7 %all_to_all.10.got = bf16[8,2,16,2048]{3,2,1,0:T(8,128)(2,1)S(1)} all-to-all(bf16[8,2,16,2048]{3,2,1,0:T(8,128)(2,1)S(1)} %filter.1), channel_id=1, replica_groups=mesh['chan'=8,'bin'=8,'core'=2] {'bin'}, dimensions={0} | all-to-all | bytes 2097152 | tf_op jit(solution)/shard_map/all_to_all | solution.py:356
  67.1 1.3 %place.1 = bf16[16,2,8,2048]{3,2,1,0:T(8,128)(2,1)} custom-call(bf16[8,2,16,2048]{3,2,1,0:T(8,128)(2,1)S(1)} %all_to_all.10.got), custom_call_target="tpu_custom_call" | custom-call | tf_op jit(solution)/shard_map/place/pallas_call | solution.py:357
  (3 shorter events, 0.1 us)
Async XLA Ops:
  1.8 24.5 %all-to-all-start = ((bf16[64,2,16,128]{3,2,1,0:T(8,128)(2,1)}), bf16[64,2,16,128]{3,2,1,0:T(8,128)(2,1)S(1)}, u32[]{:S(2)}, u32[]{:S(2)}) async-start(bf16[64,2,16,128]{3,2,1,0:T(8,128)(2,1)} %get-tuple-element.21), calls=%async_computation | async-start | bytes 1048576 | tf_op jit(solution)/shard_map/all_to_all | solution.py:281
  26.3 2.4 %collective-permute-start = (bf16[64,2,16,128]{3,2,1,0:T(8,128)(2,1)S(1)}, bf16[64,2,16,128]{3,2,1,0:T(8,128)(2,1)S(1)}, u32[]{:S(2)}, u32[]{:S(2)}) collective-permute-start(bf16[64,2,16,128]{3,2,1,0:T(8,128)(2,1)S(1)} %all-to-all-done), channel_id=1, source_target_pairs={{0,1},{1,0},{2,3},{3,2},{4,5},{5,4},{6,7},{7,6},{8,9},{9,8},{10,11... | collective-permute-start | bytes 1572872 | tf_op jit(solution)/shard_map/ppermute | solution.py:253
  30.6 1.6 %collective-permute-start.1 = (f32[128,256]{1,0:T(8,128)S(1)}, f32[128,256]{1,0:T(8,128)S(1)}, u32[]{:S(2)}, u32[]{:S(2)}) collective-permute-start(f32[128,256]{1,0:T(8,128)S(1)} %get-tuple-element.33), channel_id=1, source_target_pairs={{0,1},{1,0},{2,3},{3,2},{4,5},{5,4},{6,7},{7,6},{8,9},{9,8},{10,11... | collective-permute-start | bytes 393224 | tf_op jit(solution)/shard_map/ppermute | solution.py:253
  32.2 15.7 %collective-permute-start.8 = (bf16[512,1024]{1,0:T(8,128)(2,1)S(1)}, bf16[512,1024]{1,0:T(8,128)(2,1)S(1)}, u32[]{:S(2)}, u32[]{:S(2)}) collective-permute-start(bf16[512,1024]{1,0:T(8,128)(2,1)S(1)} %get-tuple-element.36.y_ref), channel_id=1, source_target_pairs={{0,1},{1,0},{2,3},{3,2},{4,5},{5,4},{6,7},{7,6},{8,9},{9,8},{10,11... | collective-permute-start | bytes 3145736 | tf_op jit(solution)/shard_map/ppermute | solution.py:253
  32.6 5.9 %collective-permute-start.4 = (bf16[128,256]{1,0:T(8,128)(2,1)S(1)}, bf16[128,256]{1,0:T(8,128)(2,1)S(1)}, u32[]{:S(2)}, u32[]{:S(2)}) collective-permute-start(bf16[128,256]{1,0:T(8,128)(2,1)S(1)} %convert_element_type.15), channel_id=1, source_target_pairs={{0,32},{16,48},{32,0},{48,16},{64,96},{80,112},{96,64},{112,80},{1... | collective-permute-start | bytes 196616 | tf_op jit(solution)/shard_map/ppermute | solution.py:256
  34.3 5.6 %collective-permute-start.3 = (bf16[128,256]{1,0:T(8,128)(2,1)S(1)}, bf16[128,256]{1,0:T(8,128)(2,1)S(1)}, u32[]{:S(2)}, u32[]{:S(2)}) collective-permute-start(bf16[128,256]{1,0:T(8,128)(2,1)S(1)} %convert_element_type.15), channel_id=1, source_target_pairs={{0,48},{16,32},{32,16},{48,0},{64,112},{80,96},{96,80},{112,64},{1... | collective-permute-start | bytes 196616 | tf_op jit(solution)/shard_map/ppermute | solution.py:256
  35.7 4.3 %collective-permute-start.2 = (bf16[128,256]{1,0:T(8,128)(2,1)S(1)}, bf16[128,256]{1,0:T(8,128)(2,1)S(1)}, u32[]{:S(2)}, u32[]{:S(2)}) collective-permute-start(bf16[128,256]{1,0:T(8,128)(2,1)S(1)} %convert_element_type.15), channel_id=1, source_target_pairs={{0,16},{16,0},{32,48},{48,32},{64,80},{80,64},{96,112},{112,96},{1... | collective-permute-start | bytes 196616 | tf_op jit(solution)/shard_map/ppermute | solution.py:256
  40.0 7.8 %collective-permute-start.6 = (f32[128,256]{1,0:T(8,128)S(1)}, f32[128,256]{1,0:T(8,128)S(1)}, u32[]{:S(2)}, u32[]{:S(2)}) collective-permute-start(f32[128,256]{1,0:T(8,128)S(1)} %get-tuple-element.38.mine), channel_id=1, source_target_pairs={{0,1},{1,0},{2,3},{3,2},{4,5},{5,4},{6,7},{7,6},{8,9},{9,8},{10,11... | collective-permute-start | bytes 393224 | tf_op jit(solution)/shard_map/ppermute | solution.py:253
  40.1 5.4 %collective-permute-start.7 = (bf16[128,256]{1,0:T(8,128)(2,1)S(1)}, bf16[128,256]{1,0:T(8,128)(2,1)S(1)}, u32[]{:S(2)}, u32[]{:S(2)}) collective-permute-start(bf16[128,256]{1,0:T(8,128)(2,1)S(1)} %get-tuple-element.37), channel_id=1, source_target_pairs={{0,65},{1,64},{16,81},{17,80},{32,97},{33,96},{48,113},{49,112},{6... | collective-permute-start | bytes 196616 | tf_op jit(solution)/shard_map/ppermute | solution.py:341
  42.1 5.8 %collective-permute-start.5 = (bf16[128,256]{1,0:T(8,128)(2,1)S(1)}, bf16[128,256]{1,0:T(8,128)(2,1)S(1)}, u32[]{:S(2)}, u32[]{:S(2)}) collective-permute-start(bf16[128,256]{1,0:T(8,128)(2,1)S(1)} %get-tuple-element.37), channel_id=1, source_target_pairs={{0,64},{16,80},{32,96},{48,112},{64,0},{80,16},{96,32},{112,48},{1... | collective-permute-start | bytes 196616 | tf_op jit(solution)/shard_map/ppermute | solution.py:256

commit v17 on v16

--- a/solution.py
+++ b/solution.py
@@ -24,7 +24,7 @@
 )
 ROUNDER = 12582912.0
 ROWS = 512
-LANES = 256
+LANES = 512
 WIDE = pltpu.CompilerParams(vmem_limit_bytes=16 * 1024 * 1024)
 VMEM = pl.BlockSpec(memory_space=pltpu.VMEM)
 HBM = pl.BlockSpec(memory_space=pltpu.HBM)

time: 68.7 us -> 68.7 us (level)
  no operation moved by 1% of the time
where the time goes in v17:
time: 68.7 us; the launch traced here: 68.4 us
  starting transfers between devices  19.8 us (29%)
  blocking collectives  17.7 us (26%)
  waiting for transfers between devices  16.8 us (24%)
  Pallas kernels  14 us (20%)
    all_to_all x1, blocking collectives, shards(): lax.all_to_all(applied, 'bin', split_axis=0, concat_axis=0, tiled=True)  17.7 us
    all_to_all x1, starting transfers between devices, shards(): lax.all_to_all(by_bin, ('chan', 'bin'), split_axis=0, concat_axis=0, tile...  11.5 us
    all_to_all x1, waiting for transfers between devices, shards(): lax.all_to_all(by_bin, ('chan', 'bin'), split_axis=0, concat_axis=0, tile...  7.88 us
    ppermute x4, waiting for transfers between devices, across(): return lax.ppermute(x, 'chan', [(a, a ^ bits) for a in range(chans)])  6.12 us
    ppermute x4, starting transfers between devices, across(): return lax.ppermute(x, 'chan', [(a, a ^ bits) for a in range(chans)])  5.24 us
    pallas_call x1, Pallas kernels, shards(): pl.pallas_call(operator_kernel, name='operator', out_shape=(shape(2, chan...  5.05 us
    pallas_call x1, Pallas kernels, shards(): pl.pallas_call(own_kernel, name='beam_own', out_shape=(shape(frames, voxe...  2.41 us
    ppermute x1, starting transfers between devices, shards(): lax.ppermute(narrow, ('chan', 'core'), [(2 * a + c, 2 * (a ^ 4) + 1 - c)...  1.97 us
  transfers between devices with their start and end apart: 10, of which 7 were waited for; matrix products, arithmetic and copies ran while one was open for 0% of the time, Pallas kernels for 11%

profile of v17, /device:TPU:0, one launch (start us, length us, event | category | flops | bytes accessed | tf_op | source)
XLA Modules:
  0.0 68.4 jit_solution(8206427866522578371)
XLA Ops:
  0.0 1.8 %spread.1 = (bf16[64,2,16,128]{3,2,1,0:T(8,128)(2,1)}, bf16[1024,8]{1,0:T(8,128)(2,1)S(1)}, bf16[2,8,1024]{2,1,0:T(8,128)(2,1)S(1)}, f32[2,1024]{1,0:T(2,128)S(1)}) custom-call(bf16[2,8,16,128]{3,2,1,0:T(8,128)(2,1)} %rf_ref.1, s32[3,1024]{1,0:T(4,128)} %elem_ref.1, s32[3,2048]{1,0:T(4,128)} %vox_ref.1, s32[8]{0:T(128)} %bins_ref.1), custom_call_target="tpu_custom_call" | custom-call | tf_op jit(solution)/shard_map/spread/pallas_call | solution.py:261
  1.8 11.5 %all-to-all-start = ((bf16[64,2,16,128]{3,2,1,0:T(8,128)(2,1)}), bf16[64,2,16,128]{3,2,1,0:T(8,128)(2,1)S(1)}, u32[]{:S(2)}, u32[]{:S(2)}) async-start(bf16[64,2,16,128]{3,2,1,0:T(8,128)(2,1)} %get-tuple-element.21), calls=%async_computation | async-start | bytes 1048576 | tf_op jit(solution)/shard_map/all_to_all | solution.py:281
  13.3 5.1 %operator.1 = (bf16[2,1024,512]{2,1,0:T(8,128)(2,1)S(1)}, bf16[2,1024,512]{2,1,0:T(8,128)(2,1)}) custom-call(bf16[1024,8]{1,0:T(8,128)(2,1)S(1)} %get-tuple-element.22.lhs_ref, bf16[2,8,1024]{2,1,0:T(8,128)(2,1)S(1)} %get-tuple-element.23.rhs_ref, f32[2,1024]{1,0:T(2,128)S(1)} %get-tuple-element.24.wave_ref), custom_call_target="tpu_custom_call" | custom-call | flops 62914560 | bytes 4194304 | tf_op jit(solution)/shard_map/operator/pallas_call | solution.py:284
  18.4 7.9 %all-to-all-done = bf16[64,2,16,128]{3,2,1,0:T(8,128)(2,1)S(1)} async-done(((bf16[64,2,16,128]{3,2,1,0:T(8,128)(2,1)}), bf16[64,2,16,128]{3,2,1,0:T(8,128)(2,1)S(1)}, u32[]{:S(2)}, u32[]{:S(2)}) %all-to-all-start) | async-done | bytes 524320 | tf_op jit(solution)/shard_map/all_to_all | solution.py:281
  26.3 0.0 collective-permute-start
  26.3 2.4 %beam_own.1 = (bf16[256,1024]{1,0:T(8,128)(2,1)S(1)}, bf16[2,1024,512]{2,1,0:T(8,128)(2,1)S(1)}) custom-call(bf16[2,1024,512]{2,1,0:T(8,128)(2,1)S(1)} %get-tuple-element.27.upper, bf16[2,1024,512]{2,1,0:T(8,128)(2,1)} %get-tuple-element.28.lower_ref, bf16[8,8,2,16,128]{4,3,2,1,0:T(8,128)(2,1)S(1)} %bitcast.2), custom_call_target="tpu_custom_call" | custom-call | flops 2147483648 | bytes 4194304 | tf_op jit(solution)/shard_map/beam_own/pallas_call | solution.py:310
  28.7 0.0 collective-permute-done
  28.7 1.9 %beam_other.1 = (bf16[512,1024]{1,0:T(8,128)(2,1)S(1)}, f32[128,256]{1,0:T(8,128)S(1)}, f32[128,256]{1,0:T(8,128)S(1)}) custom-call(bf16[2,1024,512]{2,1,0:T(8,128)(2,1)S(1)} %get-tuple-element.27.upper, bf16[2,1024,512]{2,1,0:T(8,128)(2,1)S(1)} %get-tuple-element.30.lower, bf16[8,8,2,16,128]{4,3,2,1,0:T(8,128)(2,1)S(1)} %bitcast.3, ...), custom_call_target="tpu_custom_call" | custom-call | flops 2147483648 | bytes 4194304 | tf_op jit(solution)/shard_map/beam_other/pallas_call | solution.py:323
  30.6 0.6 collective-permute-start.1
  31.2 1.0 %collective-permute-done.1 = f32[128,256]{1,0:T(8,128)S(1)} collective-permute-done((f32[128,256]{1,0:T(8,128)S(1)}, f32[128,256]{1,0:T(8,128)S(1)}, u32[]{:S(2)}, u32[]{:S(2)}) %collective-permute-start.1) | collective-permute-done | bytes 131104 | tf_op jit(solution)/shard_map/ppermute | solution.py:253
  32.2 0.4 collective-permute-start.8
  32.6 1.7 %collective-permute-start.4 = (bf16[128,256]{1,0:T(8,128)(2,1)S(1)}, bf16[128,256]{1,0:T(8,128)(2,1)S(1)}, u32[]{:S(2)}, u32[]{:S(2)}) collective-permute-start(bf16[128,256]{1,0:T(8,128)(2,1)S(1)} %convert_element_type.15), channel_id=1, source_target_pairs={{0,32},{16,48},{32,0},{48,16},{64,96},{80,112},{96,64},{112,80},{1... | collective-permute-start | bytes 196616 | tf_op jit(solution)/shard_map/ppermute | solution.py:256
  34.3 1.4 %collective-permute-start.3 = (bf16[128,256]{1,0:T(8,128)(2,1)S(1)}, bf16[128,256]{1,0:T(8,128)(2,1)S(1)}, u32[]{:S(2)}, u32[]{:S(2)}) collective-permute-start(bf16[128,256]{1,0:T(8,128)(2,1)S(1)} %convert_element_type.15), channel_id=1, source_target_pairs={{0,48},{16,32},{32,16},{48,0},{64,112},{80,96},{96,80},{112,64},{1... | collective-permute-start | bytes 196616 | tf_op jit(solution)/shard_map/ppermute | solution.py:256
  35.7 0.5 collective-permute-start.2
  36.2 2.3 %collective-permute-done.4 = bf16[128,256]{1,0:T(8,128)(2,1)S(1)} collective-permute-done((bf16[128,256]{1,0:T(8,128)(2,1)S(1)}, bf16[128,256]{1,0:T(8,128)(2,1)S(1)}, u32[]{:S(2)}, u32[]{:S(2)}) %collective-permute-start.4) | collective-permute-done | bytes 65568 | tf_op jit(solution)/shard_map/ppermute | solution.py:256
  38.5 1.4 %collective-permute-done.3 = bf16[128,256]{1,0:T(8,128)(2,1)S(1)} collective-permute-done((bf16[128,256]{1,0:T(8,128)(2,1)S(1)}, bf16[128,256]{1,0:T(8,128)(2,1)S(1)}, u32[]{:S(2)}, u32[]{:S(2)}) %collective-permute-start.3) | collective-permute-done | bytes 65568 | tf_op jit(solution)/shard_map/ppermute | solution.py:256
  39.9 0.1 collective-permute-done.2
  40.0 0.1 collective-permute-start.6
  40.1 2.0 %collective-permute-start.7 = (bf16[128,256]{1,0:T(8,128)(2,1)S(1)}, bf16[128,256]{1,0:T(8,128)(2,1)S(1)}, u32[]{:S(2)}, u32[]{:S(2)}) collective-permute-start(bf16[128,256]{1,0:T(8,128)(2,1)S(1)} %get-tuple-element.37), channel_id=1, source_target_pairs={{0,65},{1,64},{16,81},{17,80},{32,97},{33,96},{48,113},{49,112},{6... | collective-permute-start | bytes 196616 | tf_op jit(solution)/shard_map/ppermute | solution.py:341
  42.1 1.7 %collective-permute-start.5 = (bf16[128,256]{1,0:T(8,128)(2,1)S(1)}, bf16[128,256]{1,0:T(8,128)(2,1)S(1)}, u32[]{:S(2)}, u32[]{:S(2)}) collective-permute-start(bf16[128,256]{1,0:T(8,128)(2,1)S(1)} %get-tuple-element.37), channel_id=1, source_target_pairs={{0,64},{16,80},{32,96},{48,112},{64,0},{80,16},{96,32},{112,48},{1... | collective-permute-start | bytes 196616 | tf_op jit(solution)/shard_map/ppermute | solution.py:256
  43.8 1.8 %collective-permute-done.7.far_twin = bf16[128,256]{1,0:T(8,128)(2,1)S(1)} collective-permute-done((bf16[128,256]{1,0:T(8,128)(2,1)S(1)}, bf16[128,256]{1,0:T(8,128)(2,1)S(1)}, u32[]{:S(2)}, u32[]{:S(2)}) %collective-permute-start.7) | collective-permute-done | bytes 65568 | tf_op jit(solution)/shard_map/ppermute | solution.py:341
  45.6 2.3 %collective-permute-done.5.far = bf16[128,256]{1,0:T(8,128)(2,1)S(1)} collective-permute-done((bf16[128,256]{1,0:T(8,128)(2,1)S(1)}, bf16[128,256]{1,0:T(8,128)(2,1)S(1)}, u32[]{:S(2)}, u32[]{:S(2)}) %collective-permute-start.5) | collective-permute-done | bytes 65568 | tf_op jit(solution)/shard_map/ppermute | solution.py:256
  47.9 0.0 collective-permute-done.6.twin
  47.9 0.0 collective-permute-done.8.peer_ref
  47.9 1.6 %filter.1 = bf16[8,2,16,2048]{3,2,1,0:T(8,128)(2,1)S(1)} custom-call(f32[128,256]{1,0:T(8,128)S(1)} %get-tuple-element.38.mine, bf16[128,256]{1,0:T(8,128)(2,1)S(1)} %collective-permute-done.5.far, f32[128,256]{1,0:T(8,128)S(1)} %collective-permute-done.6.twin, bf16[128,256]{1,0:T(8,128)(2,1)S(1)} %collective-permute-done.7.far_twin, ...), custom_call_target="tpu_custom_call" | custom-call | tf_op jit(solution)/shard_map/filter/pallas_call | solution.py:346
  49.5 17.7 %all_to_all.10.got = bf16[8,2,16,2048]{3,2,1,0:T(8,128)(2,1)S(1)} all-to-all(bf16[8,2,16,2048]{3,2,1,0:T(8,128)(2,1)S(1)} %filter.1), channel_id=1, replica_groups=mesh['chan'=8,'bin'=8,'core'=2] {'bin'}, dimensions={0} | all-to-all | bytes 2097152 | tf_op jit(solution)/shard_map/all_to_all | solution.py:356
  67.1 1.3 %place.1 = bf16[16,2,8,2048]{3,2,1,0:T(8,128)(2,1)} custom-call(bf16[8,2,16,2048]{3,2,1,0:T(8,128)(2,1)S(1)} %all_to_all.10.got), custom_call_target="tpu_custom_call" | custom-call | tf_op jit(solution)/shard_map/place/pallas_call | solution.py:357
  (3 shorter events, 0.1 us)
Async XLA Ops:
  1.8 24.5 %all-to-all-start = ((bf16[64,2,16,128]{3,2,1,0:T(8,128)(2,1)}), bf16[64,2,16,128]{3,2,1,0:T(8,128)(2,1)S(1)}, u32[]{:S(2)}, u32[]{:S(2)}) async-start(bf16[64,2,16,128]{3,2,1,0:T(8,128)(2,1)} %get-tuple-element.21), calls=%async_computation | async-start | bytes 1048576 | tf_op jit(solution)/shard_map/all_to_all | solution.py:281
  26.3 2.4 %collective-permute-start = (bf16[64,2,16,128]{3,2,1,0:T(8,128)(2,1)S(1)}, bf16[64,2,16,128]{3,2,1,0:T(8,128)(2,1)S(1)}, u32[]{:S(2)}, u32[]{:S(2)}) collective-permute-start(bf16[64,2,16,128]{3,2,1,0:T(8,128)(2,1)S(1)} %all-to-all-done), channel_id=1, source_target_pairs={{0,1},{1,0},{2,3},{3,2},{4,5},{5,4},{6,7},{7,6},{8,9},{9,8},{10,11... | collective-permute-start | bytes 1572872 | tf_op jit(solution)/shard_map/ppermute | solution.py:253
  30.6 1.6 %collective-permute-start.1 = (f32[128,256]{1,0:T(8,128)S(1)}, f32[128,256]{1,0:T(8,128)S(1)}, u32[]{:S(2)}, u32[]{:S(2)}) collective-permute-start(f32[128,256]{1,0:T(8,128)S(1)} %get-tuple-element.33), channel_id=1, source_target_pairs={{0,1},{1,0},{2,3},{3,2},{4,5},{5,4},{6,7},{7,6},{8,9},{9,8},{10,11... | collective-permute-start | bytes 393224 | tf_op jit(solution)/shard_map/ppermute | solution.py:253
  32.2 15.7 %collective-permute-start.8 = (bf16[512,1024]{1,0:T(8,128)(2,1)S(1)}, bf16[512,1024]{1,0:T(8,128)(2,1)S(1)}, u32[]{:S(2)}, u32[]{:S(2)}) collective-permute-start(bf16[512,1024]{1,0:T(8,128)(2,1)S(1)} %get-tuple-element.36.y_ref), channel_id=1, source_target_pairs={{0,1},{1,0},{2,3},{3,2},{4,5},{5,4},{6,7},{7,6},{8,9},{9,8},{10,11... | collective-permute-start | bytes 3145736 | tf_op jit(solution)/shard_map/ppermute | solution.py:253
  32.6 5.9 %collective-permute-start.4 = (bf16[128,256]{1,0:T(8,128)(2,1)S(1)}, bf16[128,256]{1,0:T(8,128)(2,1)S(1)}, u32[]{:S(2)}, u32[]{:S(2)}) collective-permute-start(bf16[128,256]{1,0:T(8,128)(2,1)S(1)} %convert_element_type.15), channel_id=1, source_target_pairs={{0,32},{16,48},{32,0},{48,16},{64,96},{80,112},{96,64},{112,80},{1... | collective-permute-start | bytes 196616 | tf_op jit(solution)/shard_map/ppermute | solution.py:256
  34.3 5.6 %collective-permute-start.3 = (bf16[128,256]{1,0:T(8,128)(2,1)S(1)}, bf16[128,256]{1,0:T(8,128)(2,1)S(1)}, u32[]{:S(2)}, u32[]{:S(2)}) collective-permute-start(bf16[128,256]{1,0:T(8,128)(2,1)S(1)} %convert_element_type.15), channel_id=1, source_target_pairs={{0,48},{16,32},{32,16},{48,0},{64,112},{80,96},{96,80},{112,64},{1... | collective-permute-start | bytes 196616 | tf_op jit(solution)/shard_map/ppermute | solution.py:256
  35.7 4.3 %collective-permute-start.2 = (bf16[128,256]{1,0:T(8,128)(2,1)S(1)}, bf16[128,256]{1,0:T(8,128)(2,1)S(1)}, u32[]{:S(2)}, u32[]{:S(2)}) collective-permute-start(bf16[128,256]{1,0:T(8,128)(2,1)S(1)} %convert_element_type.15), channel_id=1, source_target_pairs={{0,16},{16,0},{32,48},{48,32},{64,80},{80,64},{96,112},{112,96},{1... | collective-permute-start | bytes 196616 | tf_op jit(solution)/shard_map/ppermute | solution.py:256
  40.0 7.8 %collective-permute-start.6 = (f32[128,256]{1,0:T(8,128)S(1)}, f32[128,256]{1,0:T(8,128)S(1)}, u32[]{:S(2)}, u32[]{:S(2)}) collective-permute-start(f32[128,256]{1,0:T(8,128)S(1)} %get-tuple-element.38.mine), channel_id=1, source_target_pairs={{0,1},{1,0},{2,3},{3,2},{4,5},{5,4},{6,7},{7,6},{8,9},{9,8},{10,11... | collective-permute-start | bytes 393224 | tf_op jit(solution)/shard_map/ppermute | solution.py:253
  40.1 5.4 %collective-permute-start.7 = (bf16[128,256]{1,0:T(8,128)(2,1)S(1)}, bf16[128,256]{1,0:T(8,128)(2,1)S(1)}, u32[]{:S(2)}, u32[]{:S(2)}) collective-permute-start(bf16[128,256]{1,0:T(8,128)(2,1)S(1)} %get-tuple-element.37), channel_id=1, source_target_pairs={{0,65},{1,64},{16,81},{17,80},{32,97},{33,96},{48,113},{49,112},{6... | collective-permute-start | bytes 196616 | tf_op jit(solution)/shard_map/ppermute | solution.py:341
  42.1 5.8 %collective-permute-start.5 = (bf16[128,256]{1,0:T(8,128)(2,1)S(1)}, bf16[128,256]{1,0:T(8,128)(2,1)S(1)}, u32[]{:S(2)}, u32[]{:S(2)}) collective-permute-start(bf16[128,256]{1,0:T(8,128)(2,1)S(1)} %get-tuple-element.37), channel_id=1, source_target_pairs={{0,64},{16,80},{32,96},{48,112},{64,0},{80,16},{96,32},{112,48},{1... | collective-permute-start | bytes 196616 | tf_op jit(solution)/shard_map/ppermute | solution.py:256

commit v18 on v16

--- a/solution.py
+++ b/solution.py
@@ -167,7 +167,7 @@
         products[:frames, frames:] - products[frames:, :frames]
     )
     keep_ref[...] = gram[pl.ds(here, half), :]
-    send_ref[...] = gram[pl.ds(there, half), :]
+    send_ref[...] = gram[pl.ds(there, half), :].astype(BF16)
 
 
 def halves(x):
@@ -323,7 +323,7 @@
     y, keep, send = pl.pallas_call(
         other_kernel,
         name="beam_other",
-        out_shape=(shape(2 * frames, voxels), shape(half, frames, dtype=F32), shape(half, frames, dtype=F32)),
+        out_shape=(shape(2 * frames, voxels), shape(half, frames, dtype=F32), shape(half, frames)),
         in_specs=[VMEM, VMEM, VMEM, VMEM],
         out_specs=(VMEM, VMEM, VMEM),
         scratch_shapes=[pltpu.VMEM((frames, channels), BF16), pltpu.VMEM((frames, frames), F32)],
@@ -331,7 +331,7 @@
         cost_estimate=beam_cost,
     )(upper, lower, other, mine)
 
-    total = keep + swap(send)
+    total = keep + swap(send).astype(F32)
     total, y = lax.optimization_barrier((total, y))
     peer = swap(y)
     narrow = total.astype(BF16)

time: 68.7 us -> 68.6 us (level)
  no operation moved by 1% of the time
where the time goes in v18:
time: 68.6 us; the launch traced here: 68.3 us
  starting transfers between devices  19.8 us (29%)
  blocking collectives  17.7 us (26%)
  waiting for transfers between devices  16.7 us (24%)
  Pallas kernels  14 us (20%)
    all_to_all x1, blocking collectives, shards(): lax.all_to_all(applied, 'bin', split_axis=0, concat_axis=0, tiled=True)  17.7 us
    all_to_all x1, starting transfers between devices, shards(): lax.all_to_all(by_bin, ('chan', 'bin'), split_axis=0, concat_axis=0, tile...  11.5 us
    all_to_all x1, waiting for transfers between devices, shards(): lax.all_to_all(by_bin, ('chan', 'bin'), split_axis=0, concat_axis=0, tile...  7.88 us
    ppermute x4, waiting for transfers between devices, across(): return lax.ppermute(x, 'chan', [(a, a ^ bits) for a in range(chans)])  6.12 us
    ppermute x4, starting transfers between devices, across(): return lax.ppermute(x, 'chan', [(a, a ^ bits) for a in range(chans)])  5.24 us
    pallas_call x1, Pallas kernels, shards(): pl.pallas_call(operator_kernel, name='operator', out_shape=(shape(2, chan...  5.05 us
    pallas_call x1, Pallas kernels, shards(): pl.pallas_call(own_kernel, name='beam_own', out_shape=(shape(frames, voxe...  2.41 us
    ppermute x1, starting transfers between devices, shards(): lax.ppermute(narrow, ('chan', 'core'), [(2 * a + c, 2 * (a ^ 4) + 1 - c)...  1.97 us
  transfers between devices with their start and end apart: 10, of which 7 were waited for; matrix products, arithmetic and copies ran while one was open for 0% of the time, Pallas kernels for 11%

profile of v18, /device:TPU:0, one launch (start us, length us, event | category | flops | bytes accessed | tf_op | source)
XLA Modules:
  0.0 68.3 jit_solution(17454586655903462592)
XLA Ops:
  0.0 1.8 %spread.1 = (bf16[64,2,16,128]{3,2,1,0:T(8,128)(2,1)}, bf16[1024,8]{1,0:T(8,128)(2,1)S(1)}, bf16[2,8,1024]{2,1,0:T(8,128)(2,1)S(1)}, f32[2,1024]{1,0:T(2,128)S(1)}) custom-call(bf16[2,8,16,128]{3,2,1,0:T(8,128)(2,1)} %rf_ref.1, s32[3,1024]{1,0:T(4,128)} %elem_ref.1, s32[3,2048]{1,0:T(4,128)} %vox_ref.1, s32[8]{0:T(128)} %bins_ref.1), custom_call_target="tpu_custom_call" | custom-call | tf_op jit(solution)/shard_map/spread/pallas_call | solution.py:261
  1.8 11.5 %all-to-all-start = ((bf16[64,2,16,128]{3,2,1,0:T(8,128)(2,1)}), bf16[64,2,16,128]{3,2,1,0:T(8,128)(2,1)S(1)}, u32[]{:S(2)}, u32[]{:S(2)}) async-start(bf16[64,2,16,128]{3,2,1,0:T(8,128)(2,1)} %get-tuple-element.21), calls=%async_computation | async-start | bytes 1048576 | tf_op jit(solution)/shard_map/all_to_all | solution.py:281
  13.3 5.1 %operator.1 = (bf16[2,1024,512]{2,1,0:T(8,128)(2,1)S(1)}, bf16[2,1024,512]{2,1,0:T(8,128)(2,1)}) custom-call(bf16[1024,8]{1,0:T(8,128)(2,1)S(1)} %get-tuple-element.22.lhs_ref, bf16[2,8,1024]{2,1,0:T(8,128)(2,1)S(1)} %get-tuple-element.23.rhs_ref, f32[2,1024]{1,0:T(2,128)S(1)} %get-tuple-element.24.wave_ref), custom_call_target="tpu_custom_call" | custom-call | flops 62914560 | bytes 4194304 | tf_op jit(solution)/shard_map/operator/pallas_call | solution.py:284
  18.4 7.9 %all-to-all-done = bf16[64,2,16,128]{3,2,1,0:T(8,128)(2,1)S(1)} async-done(((bf16[64,2,16,128]{3,2,1,0:T(8,128)(2,1)}), bf16[64,2,16,128]{3,2,1,0:T(8,128)(2,1)S(1)}, u32[]{:S(2)}, u32[]{:S(2)}) %all-to-all-start) | async-done | bytes 524320 | tf_op jit(solution)/shard_map/all_to_all | solution.py:281
  26.3 0.0 collective-permute-start
  26.3 2.4 %beam_own.1 = (bf16[256,1024]{1,0:T(8,128)(2,1)S(1)}, bf16[2,1024,512]{2,1,0:T(8,128)(2,1)S(1)}) custom-call(bf16[2,1024,512]{2,1,0:T(8,128)(2,1)S(1)} %get-tuple-element.27.upper, bf16[2,1024,512]{2,1,0:T(8,128)(2,1)} %get-tuple-element.28.lower_ref, bf16[8,8,2,16,128]{4,3,2,1,0:T(8,128)(2,1)S(1)} %bitcast.2), custom_call_target="tpu_custom_call" | custom-call | flops 2147483648 | bytes 4194304 | tf_op jit(solution)/shard_map/beam_own/pallas_call | solution.py:310
  28.7 0.0 collective-permute-done
  28.7 1.9 %beam_other.1 = (bf16[512,1024]{1,0:T(8,128)(2,1)S(1)}, f32[128,256]{1,0:T(8,128)S(1)}, bf16[128,256]{1,0:T(8,128)(2,1)S(1)}) custom-call(bf16[2,1024,512]{2,1,0:T(8,128)(2,1)S(1)} %get-tuple-element.27.upper, bf16[2,1024,512]{2,1,0:T(8,128)(2,1)S(1)} %get-tuple-element.30.lower, bf16[8,8,2,16,128]{4,3,2,1,0:T(8,128)(2,1)S(1)} %bitcast.3, ...), custom_call_target="tpu_custom_call" | custom-call | flops 2147483648 | bytes 4194304 | tf_op jit(solution)/shard_map/beam_other/pallas_call | solution.py:323
  30.6 0.6 collective-permute-start.1
  31.2 0.9 %collective-permute-done.1 = bf16[128,256]{1,0:T(8,128)(2,1)S(1)} collective-permute-done((bf16[128,256]{1,0:T(8,128)(2,1)S(1)}, bf16[128,256]{1,0:T(8,128)(2,1)S(1)}, u32[]{:S(2)}, u32[]{:S(2)}) %collective-permute-start.1) | collective-permute-done | bytes 65568 | tf_op jit(solution)/shard_map/ppermute | solution.py:253
  32.1 0.4 collective-permute-start.8
  32.5 1.7 %collective-permute-start.4 = (bf16[128,256]{1,0:T(8,128)(2,1)S(1)}, bf16[128,256]{1,0:T(8,128)(2,1)S(1)}, u32[]{:S(2)}, u32[]{:S(2)}) collective-permute-start(bf16[128,256]{1,0:T(8,128)(2,1)S(1)} %convert_element_type.19), channel_id=1, source_target_pairs={{0,32},{16,48},{32,0},{48,16},{64,96},{80,112},{96,64},{112,80},{1... | collective-permute-start | bytes 196616 | tf_op jit(solution)/shard_map/ppermute | solution.py:256
  34.2 1.4 %collective-permute-start.3 = (bf16[128,256]{1,0:T(8,128)(2,1)S(1)}, bf16[128,256]{1,0:T(8,128)(2,1)S(1)}, u32[]{:S(2)}, u32[]{:S(2)}) collective-permute-start(bf16[128,256]{1,0:T(8,128)(2,1)S(1)} %convert_element_type.19), channel_id=1, source_target_pairs={{0,48},{16,32},{32,16},{48,0},{64,112},{80,96},{96,80},{112,64},{1... | collective-permute-start | bytes 196616 | tf_op jit(solution)/shard_map/ppermute | solution.py:256
  35.6 0.5 collective-permute-start.2
  36.1 2.3 %collective-permute-done.4 = bf16[128,256]{1,0:T(8,128)(2,1)S(1)} collective-permute-done((bf16[128,256]{1,0:T(8,128)(2,1)S(1)}, bf16[128,256]{1,0:T(8,128)(2,1)S(1)}, u32[]{:S(2)}, u32[]{:S(2)}) %collective-permute-start.4) | collective-permute-done | bytes 65568 | tf_op jit(solution)/shard_map/ppermute | solution.py:256
  38.4 1.4 %collective-permute-done.3 = bf16[128,256]{1,0:T(8,128)(2,1)S(1)} collective-permute-done((bf16[128,256]{1,0:T(8,128)(2,1)S(1)}, bf16[128,256]{1,0:T(8,128)(2,1)S(1)}, u32[]{:S(2)}, u32[]{:S(2)}) %collective-permute-start.3) | collective-permute-done | bytes 65568 | tf_op jit(solution)/shard_map/ppermute | solution.py:256
  39.8 0.1 collective-permute-done.2
  39.9 0.1 collective-permute-start.6
  40.0 2.0 %collective-permute-start.7 = (bf16[128,256]{1,0:T(8,128)(2,1)S(1)}, bf16[128,256]{1,0:T(8,128)(2,1)S(1)}, u32[]{:S(2)}, u32[]{:S(2)}) collective-permute-start(bf16[128,256]{1,0:T(8,128)(2,1)S(1)} %get-tuple-element.37), channel_id=1, source_target_pairs={{0,65},{1,64},{16,81},{17,80},{32,97},{33,96},{48,113},{49,112},{6... | collective-permute-start | bytes 196616 | tf_op jit(solution)/shard_map/ppermute | solution.py:341
  42.0 1.7 %collective-permute-start.5 = (bf16[128,256]{1,0:T(8,128)(2,1)S(1)}, bf16[128,256]{1,0:T(8,128)(2,1)S(1)}, u32[]{:S(2)}, u32[]{:S(2)}) collective-permute-start(bf16[128,256]{1,0:T(8,128)(2,1)S(1)} %get-tuple-element.37), channel_id=1, source_target_pairs={{0,64},{16,80},{32,96},{48,112},{64,0},{80,16},{96,32},{112,48},{1... | collective-permute-start | bytes 196616 | tf_op jit(solution)/shard_map/ppermute | solution.py:256
  43.7 1.8 %collective-permute-done.7.far_twin = bf16[128,256]{1,0:T(8,128)(2,1)S(1)} collective-permute-done((bf16[128,256]{1,0:T(8,128)(2,1)S(1)}, bf16[128,256]{1,0:T(8,128)(2,1)S(1)}, u32[]{:S(2)}, u32[]{:S(2)}) %collective-permute-start.7) | collective-permute-done | bytes 65568 | tf_op jit(solution)/shard_map/ppermute | solution.py:341
  45.5 2.3 %collective-permute-done.5.far = bf16[128,256]{1,0:T(8,128)(2,1)S(1)} collective-permute-done((bf16[128,256]{1,0:T(8,128)(2,1)S(1)}, bf16[128,256]{1,0:T(8,128)(2,1)S(1)}, u32[]{:S(2)}, u32[]{:S(2)}) %collective-permute-start.5) | collective-permute-done | bytes 65568 | tf_op jit(solution)/shard_map/ppermute | solution.py:256
  47.8 0.0 collective-permute-done.6.twin
  47.8 0.0 collective-permute-done.8.peer_ref
  47.8 1.6 %filter.1 = bf16[8,2,16,2048]{3,2,1,0:T(8,128)(2,1)S(1)} custom-call(f32[128,256]{1,0:T(8,128)S(1)} %get-tuple-element.38.mine, bf16[128,256]{1,0:T(8,128)(2,1)S(1)} %collective-permute-done.5.far, f32[128,256]{1,0:T(8,128)S(1)} %collective-permute-done.6.twin, bf16[128,256]{1,0:T(8,128)(2,1)S(1)} %collective-permute-done.7.far_twin, ...), custom_call_target="tpu_custom_call" | custom-call | tf_op jit(solution)/shard_map/filter/pallas_call | solution.py:346
  49.4 17.7 %all_to_all.10.got = bf16[8,2,16,2048]{3,2,1,0:T(8,128)(2,1)S(1)} all-to-all(bf16[8,2,16,2048]{3,2,1,0:T(8,128)(2,1)S(1)} %filter.1), channel_id=1, replica_groups=mesh['chan'=8,'bin'=8,'core'=2] {'bin'}, dimensions={0} | all-to-all | bytes 2097152 | tf_op jit(solution)/shard_map/all_to_all | solution.py:356
  67.0 1.3 %place.1 = bf16[16,2,8,2048]{3,2,1,0:T(8,128)(2,1)} custom-call(bf16[8,2,16,2048]{3,2,1,0:T(8,128)(2,1)S(1)} %all_to_all.10.got), custom_call_target="tpu_custom_call" | custom-call | tf_op jit(solution)/shard_map/place/pallas_call | solution.py:357
  (3 shorter events, 0.1 us)
Async XLA Ops:
  1.8 24.5 %all-to-all-start = ((bf16[64,2,16,128]{3,2,1,0:T(8,128)(2,1)}), bf16[64,2,16,128]{3,2,1,0:T(8,128)(2,1)S(1)}, u32[]{:S(2)}, u32[]{:S(2)}) async-start(bf16[64,2,16,128]{3,2,1,0:T(8,128)(2,1)} %get-tuple-element.21), calls=%async_computation | async-start | bytes 1048576 | tf_op jit(solution)/shard_map/all_to_all | solution.py:281
  26.3 2.4 %collective-permute-start = (bf16[64,2,16,128]{3,2,1,0:T(8,128)(2,1)S(1)}, bf16[64,2,16,128]{3,2,1,0:T(8,128)(2,1)S(1)}, u32[]{:S(2)}, u32[]{:S(2)}) collective-permute-start(bf16[64,2,16,128]{3,2,1,0:T(8,128)(2,1)S(1)} %all-to-all-done), channel_id=1, source_target_pairs={{0,1},{1,0},{2,3},{3,2},{4,5},{5,4},{6,7},{7,6},{8,9},{9,8},{10,11... | collective-permute-start | bytes 1572872 | tf_op jit(solution)/shard_map/ppermute | solution.py:253
  30.6 1.5 %collective-permute-start.1 = (bf16[128,256]{1,0:T(8,128)(2,1)S(1)}, bf16[128,256]{1,0:T(8,128)(2,1)S(1)}, u32[]{:S(2)}, u32[]{:S(2)}) collective-permute-start(bf16[128,256]{1,0:T(8,128)(2,1)S(1)} %get-tuple-element.33), channel_id=1, source_target_pairs={{0,1},{1,0},{2,3},{3,2},{4,5},{5,4},{6,7},{7,6},{8,9},{9,8},{10,11... | collective-permute-start | bytes 196616 | tf_op jit(solution)/shard_map/ppermute | solution.py:253
  32.1 15.7 %collective-permute-start.8 = (bf16[512,1024]{1,0:T(8,128)(2,1)S(1)}, bf16[512,1024]{1,0:T(8,128)(2,1)S(1)}, u32[]{:S(2)}, u32[]{:S(2)}) collective-permute-start(bf16[512,1024]{1,0:T(8,128)(2,1)S(1)} %get-tuple-element.36.y_ref), channel_id=1, source_target_pairs={{0,1},{1,0},{2,3},{3,2},{4,5},{5,4},{6,7},{7,6},{8,9},{9,8},{10,11... | collective-permute-start | bytes 3145736 | tf_op jit(solution)/shard_map/ppermute | solution.py:253
  32.5 5.9 %collective-permute-start.4 = (bf16[128,256]{1,0:T(8,128)(2,1)S(1)}, bf16[128,256]{1,0:T(8,128)(2,1)S(1)}, u32[]{:S(2)}, u32[]{:S(2)}) collective-permute-start(bf16[128,256]{1,0:T(8,128)(2,1)S(1)} %convert_element_type.19), channel_id=1, source_target_pairs={{0,32},{16,48},{32,0},{48,16},{64,96},{80,112},{96,64},{112,80},{1... | collective-permute-start | bytes 196616 | tf_op jit(solution)/shard_map/ppermute | solution.py:256
  34.2 5.6 %collective-permute-start.3 = (bf16[128,256]{1,0:T(8,128)(2,1)S(1)}, bf16[128,256]{1,0:T(8,128)(2,1)S(1)}, u32[]{:S(2)}, u32[]{:S(2)}) collective-permute-start(bf16[128,256]{1,0:T(8,128)(2,1)S(1)} %convert_element_type.19), channel_id=1, source_target_pairs={{0,48},{16,32},{32,16},{48,0},{64,112},{80,96},{96,80},{112,64},{1... | collective-permute-start | bytes 196616 | tf_op jit(solution)/shard_map/ppermute | solution.py:256
  35.6 4.3 %collective-permute-start.2 = (bf16[128,256]{1,0:T(8,128)(2,1)S(1)}, bf16[128,256]{1,0:T(8,128)(2,1)S(1)}, u32[]{:S(2)}, u32[]{:S(2)}) collective-permute-start(bf16[128,256]{1,0:T(8,128)(2,1)S(1)} %convert_element_type.19), channel_id=1, source_target_pairs={{0,16},{16,0},{32,48},{48,32},{64,80},{80,64},{96,112},{112,96},{1... | collective-permute-start | bytes 196616 | tf_op jit(solution)/shard_map/ppermute | solution.py:256
  39.9 7.8 %collective-permute-start.6 = (f32[128,256]{1,0:T(8,128)S(1)}, f32[128,256]{1,0:T(8,128)S(1)}, u32[]{:S(2)}, u32[]{:S(2)}) collective-permute-start(f32[128,256]{1,0:T(8,128)S(1)} %get-tuple-element.38.mine), channel_id=1, source_target_pairs={{0,1},{1,0},{2,3},{3,2},{4,5},{5,4},{6,7},{7,6},{8,9},{9,8},{10,11... | collective-permute-start | bytes 393224 | tf_op jit(solution)/shard_map/ppermute | solution.py:253
  40.0 5.4 %collective-permute-start.7 = (bf16[128,256]{1,0:T(8,128)(2,1)S(1)}, bf16[128,256]{1,0:T(8,128)(2,1)S(1)}, u32[]{:S(2)}, u32[]{:S(2)}) collective-permute-start(bf16[128,256]{1,0:T(8,128)(2,1)S(1)} %get-tuple-element.37), channel_id=1, source_target_pairs={{0,65},{1,64},{16,81},{17,80},{32,97},{33,96},{48,113},{49,112},{6... | collective-permute-start | bytes 196616 | tf_op jit(solution)/shard_map/ppermute | solution.py:341
  42.0 5.8 %collective-permute-start.5 = (bf16[128,256]{1,0:T(8,128)(2,1)S(1)}, bf16[128,256]{1,0:T(8,128)(2,1)S(1)}, u32[]{:S(2)}, u32[]{:S(2)}) collective-permute-start(bf16[128,256]{1,0:T(8,128)(2,1)S(1)} %get-tuple-element.37), channel_id=1, source_target_pairs={{0,64},{16,80},{32,96},{48,112},{64,0},{80,16},{96,32},{112,48},{1... | collective-permute-start | bytes 196616 | tf_op jit(solution)/shard_map/ppermute | solution.py:256

commit v19 on v16

--- a/solution.py
+++ b/solution.py
@@ -43,7 +43,7 @@
 
 
 def spread_kernel(
-    rf_ref, elem_ref, vox_ref, bins_ref, out_ref, lhs_ref, rhs_ref, wave_ref, held, elem, vox, numbers, sems
+    rf_ref, elem_ref, vox_ref, bins_ref, out_ref, lhs_ref, rhs_ref, wave_ref, held, block, elem, vox, numbers, sems
 ):
     parts, bins = held.shape[:2]
     chans = out_ref.shape[0] // bins
@@ -56,12 +56,10 @@
     for copy in reads:
         copy.start()
     reads[0].wait()
+    for part in range(parts):
+        block[:, part] = held[part]
     copies = [
-        pltpu.make_async_copy(
-            held.at[part], out_ref.at[k * bins : (k + 1) * bins, part], sems.at[4 + k * parts + part]
-        )
-        for k in range(chans)
-        for part in range(parts)
+        pltpu.make_async_copy(block, out_ref.at[k * bins : (k + 1) * bins], sems.at[4 + k]) for k in range(chans)
     ]
     for copy in copies:
         copy.start()
@@ -271,10 +269,11 @@
         out_specs=(HBM, VMEM, VMEM, VMEM),
         scratch_shapes=[
             pltpu.VMEM(rf_data.shape, BF16),
+            pltpu.VMEM((bins, parts, group, width), BF16),
             pltpu.VMEM(elem_pos.shape, jnp.int32),
             pltpu.VMEM(vox_pos.shape, jnp.int32),
             pltpu.SMEM(subbands.shape, jnp.int32),
-            pltpu.SemaphoreType.DMA((chans * parts + 4,)),
+            pltpu.SemaphoreType.DMA((chans + 4,)),
         ],
         compiler_params=WIDE,
     )(in_hbm(rf_data), in_hbm(elem_pos), in_hbm(vox_pos), in_hbm(subbands))

time: 68.7 us -> 68.6 us (level)
  no operation moved by 1% of the time
where the time goes in v19:
time: 68.6 us; the launch traced here: 68.3 us
  starting transfers between devices  19.8 us (29%)
  blocking collectives  17.7 us (26%)
  waiting for transfers between devices  16.8 us (24%)
  Pallas kernels  13.9 us (20%)
    all_to_all x1, blocking collectives, shards(): lax.all_to_all(applied, 'bin', split_axis=0, concat_axis=0, tiled=True)  17.7 us
    all_to_all x1, starting transfers between devices, shards(): lax.all_to_all(by_bin, ('chan', 'bin'), split_axis=0, concat_axis=0, tile...  11.5 us
    all_to_all x1, waiting for transfers between devices, shards(): lax.all_to_all(by_bin, ('chan', 'bin'), split_axis=0, concat_axis=0, tile...  7.88 us
    ppermute x4, waiting for transfers between devices, across(): return lax.ppermute(x, 'chan', [(a, a ^ bits) for a in range(chans)])  6.13 us
    ppermute x4, starting transfers between devices, across(): return lax.ppermute(x, 'chan', [(a, a ^ bits) for a in range(chans)])  5.24 us
    pallas_call x1, Pallas kernels, shards(): pl.pallas_call(operator_kernel, name='operator', out_shape=(shape(2, chan...  5.05 us
    pallas_call x1, Pallas kernels, shards(): pl.pallas_call(own_kernel, name='beam_own', out_shape=(shape(frames, voxe...  2.41 us
    ppermute x1, starting transfers between devices, shards(): lax.ppermute(narrow, ('chan', 'core'), [(2 * a + c, 2 * (a ^ 4) + 1 - c)...  1.98 us
  transfers between devices with their start and end apart: 10, of which 7 were waited for; matrix products, arithmetic and copies ran while one was open for 0% of the time, Pallas kernels for 11%

profile of v19, /device:TPU:0, one launch (start us, length us, event | category | flops | bytes accessed | tf_op | source)
XLA Modules:
  0.0 68.3 jit_solution(12353154124541353135)
XLA Ops:
  0.0 1.7 %spread.1 = (bf16[64,2,16,128]{3,2,1,0:T(8,128)(2,1)}, bf16[1024,8]{1,0:T(8,128)(2,1)S(1)}, bf16[2,8,1024]{2,1,0:T(8,128)(2,1)S(1)}, f32[2,1024]{1,0:T(2,128)S(1)}) custom-call(bf16[2,8,16,128]{3,2,1,0:T(8,128)(2,1)} %rf_ref.1, s32[3,1024]{1,0:T(4,128)} %elem_ref.1, s32[3,2048]{1,0:T(4,128)} %vox_ref.1, s32[8]{0:T(128)} %bins_ref.1), custom_call_target="tpu_custom_call" | custom-call | tf_op jit(solution)/shard_map/spread/pallas_call | solution.py:259
  1.7 11.5 %all-to-all-start = ((bf16[64,2,16,128]{3,2,1,0:T(8,128)(2,1)}), bf16[64,2,16,128]{3,2,1,0:T(8,128)(2,1)S(1)}, u32[]{:S(2)}, u32[]{:S(2)}) async-start(bf16[64,2,16,128]{3,2,1,0:T(8,128)(2,1)} %get-tuple-element.21), calls=%async_computation | async-start | bytes 1048576 | tf_op jit(solution)/shard_map/all_to_all | solution.py:280
  13.3 5.0 %operator.1 = (bf16[2,1024,512]{2,1,0:T(8,128)(2,1)S(1)}, bf16[2,1024,512]{2,1,0:T(8,128)(2,1)}) custom-call(bf16[1024,8]{1,0:T(8,128)(2,1)S(1)} %get-tuple-element.22.lhs_ref, bf16[2,8,1024]{2,1,0:T(8,128)(2,1)S(1)} %get-tuple-element.23.rhs_ref, f32[2,1024]{1,0:T(2,128)S(1)} %get-tuple-element.24.wave_ref), custom_call_target="tpu_custom_call" | custom-call | flops 62914560 | bytes 4194304 | tf_op jit(solution)/shard_map/operator/pallas_call | solution.py:283
  18.3 7.9 %all-to-all-done = bf16[64,2,16,128]{3,2,1,0:T(8,128)(2,1)S(1)} async-done(((bf16[64,2,16,128]{3,2,1,0:T(8,128)(2,1)}), bf16[64,2,16,128]{3,2,1,0:T(8,128)(2,1)S(1)}, u32[]{:S(2)}, u32[]{:S(2)}) %all-to-all-start) | async-done | bytes 524320 | tf_op jit(solution)/shard_map/all_to_all | solution.py:280
  26.2 0.0 collective-permute-start
  26.2 2.4 %beam_own.1 = (bf16[256,1024]{1,0:T(8,128)(2,1)S(1)}, bf16[2,1024,512]{2,1,0:T(8,128)(2,1)S(1)}) custom-call(bf16[2,1024,512]{2,1,0:T(8,128)(2,1)S(1)} %get-tuple-element.27.upper, bf16[2,1024,512]{2,1,0:T(8,128)(2,1)} %get-tuple-element.28.lower_ref, bf16[8,8,2,16,128]{4,3,2,1,0:T(8,128)(2,1)S(1)} %bitcast.2), custom_call_target="tpu_custom_call" | custom-call | flops 2147483648 | bytes 4194304 | tf_op jit(solution)/shard_map/beam_own/pallas_call | solution.py:309
  28.6 0.0 collective-permute-done
  28.6 1.9 %beam_other.1 = (bf16[512,1024]{1,0:T(8,128)(2,1)S(1)}, f32[128,256]{1,0:T(8,128)S(1)}, f32[128,256]{1,0:T(8,128)S(1)}) custom-call(bf16[2,1024,512]{2,1,0:T(8,128)(2,1)S(1)} %get-tuple-element.27.upper, bf16[2,1024,512]{2,1,0:T(8,128)(2,1)S(1)} %get-tuple-element.30.lower, bf16[8,8,2,16,128]{4,3,2,1,0:T(8,128)(2,1)S(1)} %bitcast.3, ...), custom_call_target="tpu_custom_call" | custom-call | flops 2147483648 | bytes 4194304 | tf_op jit(solution)/shard_map/beam_other/pallas_call | solution.py:322
  30.5 0.6 collective-permute-start.1
  31.1 1.0 %collective-permute-done.1 = f32[128,256]{1,0:T(8,128)S(1)} collective-permute-done((f32[128,256]{1,0:T(8,128)S(1)}, f32[128,256]{1,0:T(8,128)S(1)}, u32[]{:S(2)}, u32[]{:S(2)}) %collective-permute-start.1) | collective-permute-done | bytes 131104 | tf_op jit(solution)/shard_map/ppermute | solution.py:251
  32.1 0.4 collective-permute-start.8
  32.6 1.7 %collective-permute-start.4 = (bf16[128,256]{1,0:T(8,128)(2,1)S(1)}, bf16[128,256]{1,0:T(8,128)(2,1)S(1)}, u32[]{:S(2)}, u32[]{:S(2)}) collective-permute-start(bf16[128,256]{1,0:T(8,128)(2,1)S(1)} %convert_element_type.15), channel_id=1, source_target_pairs={{0,32},{16,48},{32,0},{48,16},{64,96},{80,112},{96,64},{112,80},{1... | collective-permute-start | bytes 196616 | tf_op jit(solution)/shard_map/ppermute | solution.py:254
  34.3 1.4 %collective-permute-start.3 = (bf16[128,256]{1,0:T(8,128)(2,1)S(1)}, bf16[128,256]{1,0:T(8,128)(2,1)S(1)}, u32[]{:S(2)}, u32[]{:S(2)}) collective-permute-start(bf16[128,256]{1,0:T(8,128)(2,1)S(1)} %convert_element_type.15), channel_id=1, source_target_pairs={{0,48},{16,32},{32,16},{48,0},{64,112},{80,96},{96,80},{112,64},{1... | collective-permute-start | bytes 196616 | tf_op jit(solution)/shard_map/ppermute | solution.py:254
  35.7 0.5 collective-permute-start.2
  36.1 2.3 %collective-permute-done.4 = bf16[128,256]{1,0:T(8,128)(2,1)S(1)} collective-permute-done((bf16[128,256]{1,0:T(8,128)(2,1)S(1)}, bf16[128,256]{1,0:T(8,128)(2,1)S(1)}, u32[]{:S(2)}, u32[]{:S(2)}) %collective-permute-start.4) | collective-permute-done | bytes 65568 | tf_op jit(solution)/shard_map/ppermute | solution.py:254
  38.5 1.4 %collective-permute-done.3 = bf16[128,256]{1,0:T(8,128)(2,1)S(1)} collective-permute-done((bf16[128,256]{1,0:T(8,128)(2,1)S(1)}, bf16[128,256]{1,0:T(8,128)(2,1)S(1)}, u32[]{:S(2)}, u32[]{:S(2)}) %collective-permute-start.3) | collective-permute-done | bytes 65568 | tf_op jit(solution)/shard_map/ppermute | solution.py:254
  39.8 0.1 collective-permute-done.2
  40.0 0.1 collective-permute-start.6
  40.1 2.0 %collective-permute-start.7 = (bf16[128,256]{1,0:T(8,128)(2,1)S(1)}, bf16[128,256]{1,0:T(8,128)(2,1)S(1)}, u32[]{:S(2)}, u32[]{:S(2)}) collective-permute-start(bf16[128,256]{1,0:T(8,128)(2,1)S(1)} %get-tuple-element.37), channel_id=1, source_target_pairs={{0,65},{1,64},{16,81},{17,80},{32,97},{33,96},{48,113},{49,112},{6... | collective-permute-start | bytes 196616 | tf_op jit(solution)/shard_map/ppermute | solution.py:340
  42.0 1.7 %collective-permute-start.5 = (bf16[128,256]{1,0:T(8,128)(2,1)S(1)}, bf16[128,256]{1,0:T(8,128)(2,1)S(1)}, u32[]{:S(2)}, u32[]{:S(2)}) collective-permute-start(bf16[128,256]{1,0:T(8,128)(2,1)S(1)} %get-tuple-element.37), channel_id=1, source_target_pairs={{0,64},{16,80},{32,96},{48,112},{64,0},{80,16},{96,32},{112,48},{1... | collective-permute-start | bytes 196616 | tf_op jit(solution)/shard_map/ppermute | solution.py:254
  43.7 1.8 %collective-permute-done.7.far_twin = bf16[128,256]{1,0:T(8,128)(2,1)S(1)} collective-permute-done((bf16[128,256]{1,0:T(8,128)(2,1)S(1)}, bf16[128,256]{1,0:T(8,128)(2,1)S(1)}, u32[]{:S(2)}, u32[]{:S(2)}) %collective-permute-start.7) | collective-permute-done | bytes 65568 | tf_op jit(solution)/shard_map/ppermute | solution.py:340
  45.5 2.3 %collective-permute-done.5.far = bf16[128,256]{1,0:T(8,128)(2,1)S(1)} collective-permute-done((bf16[128,256]{1,0:T(8,128)(2,1)S(1)}, bf16[128,256]{1,0:T(8,128)(2,1)S(1)}, u32[]{:S(2)}, u32[]{:S(2)}) %collective-permute-start.5) | collective-permute-done | bytes 65568 | tf_op jit(solution)/shard_map/ppermute | solution.py:254
  47.8 0.0 collective-permute-done.6.twin
  47.8 0.0 collective-permute-done.8.peer_ref
  47.8 1.6 %filter.1 = bf16[8,2,16,2048]{3,2,1,0:T(8,128)(2,1)S(1)} custom-call(f32[128,256]{1,0:T(8,128)S(1)} %get-tuple-element.38.mine, bf16[128,256]{1,0:T(8,128)(2,1)S(1)} %collective-permute-done.5.far, f32[128,256]{1,0:T(8,128)S(1)} %collective-permute-done.6.twin, bf16[128,256]{1,0:T(8,128)(2,1)S(1)} %collective-permute-done.7.far_twin, ...), custom_call_target="tpu_custom_call" | custom-call | tf_op jit(solution)/shard_map/filter/pallas_call | solution.py:345
  49.4 17.7 %all_to_all.10.got = bf16[8,2,16,2048]{3,2,1,0:T(8,128)(2,1)S(1)} all-to-all(bf16[8,2,16,2048]{3,2,1,0:T(8,128)(2,1)S(1)} %filter.1), channel_id=1, replica_groups=mesh['chan'=8,'bin'=8,'core'=2] {'bin'}, dimensions={0} | all-to-all | bytes 2097152 | tf_op jit(solution)/shard_map/all_to_all | solution.py:355
  67.1 1.3 %place.1 = bf16[16,2,8,2048]{3,2,1,0:T(8,128)(2,1)} custom-call(bf16[8,2,16,2048]{3,2,1,0:T(8,128)(2,1)S(1)} %all_to_all.10.got), custom_call_target="tpu_custom_call" | custom-call | tf_op jit(solution)/shard_map/place/pallas_call | solution.py:356
  (3 shorter events, 0.1 us)
Async XLA Ops:
  1.7 24.5 %all-to-all-start = ((bf16[64,2,16,128]{3,2,1,0:T(8,128)(2,1)}), bf16[64,2,16,128]{3,2,1,0:T(8,128)(2,1)S(1)}, u32[]{:S(2)}, u32[]{:S(2)}) async-start(bf16[64,2,16,128]{3,2,1,0:T(8,128)(2,1)} %get-tuple-element.21), calls=%async_computation | async-start | bytes 1048576 | tf_op jit(solution)/shard_map/all_to_all | solution.py:280
  26.2 2.4 %collective-permute-start = (bf16[64,2,16,128]{3,2,1,0:T(8,128)(2,1)S(1)}, bf16[64,2,16,128]{3,2,1,0:T(8,128)(2,1)S(1)}, u32[]{:S(2)}, u32[]{:S(2)}) collective-permute-start(bf16[64,2,16,128]{3,2,1,0:T(8,128)(2,1)S(1)} %all-to-all-done), channel_id=1, source_target_pairs={{0,1},{1,0},{2,3},{3,2},{4,5},{5,4},{6,7},{7,6},{8,9},{9,8},{10,11... | collective-permute-start | bytes 1572872 | tf_op jit(solution)/shard_map/ppermute | solution.py:251
  30.5 1.6 %collective-permute-start.1 = (f32[128,256]{1,0:T(8,128)S(1)}, f32[128,256]{1,0:T(8,128)S(1)}, u32[]{:S(2)}, u32[]{:S(2)}) collective-permute-start(f32[128,256]{1,0:T(8,128)S(1)} %get-tuple-element.33), channel_id=1, source_target_pairs={{0,1},{1,0},{2,3},{3,2},{4,5},{5,4},{6,7},{7,6},{8,9},{9,8},{10,11... | collective-permute-start | bytes 393224 | tf_op jit(solution)/shard_map/ppermute | solution.py:251
  32.1 15.7 %collective-permute-start.8 = (bf16[512,1024]{1,0:T(8,128)(2,1)S(1)}, bf16[512,1024]{1,0:T(8,128)(2,1)S(1)}, u32[]{:S(2)}, u32[]{:S(2)}) collective-permute-start(bf16[512,1024]{1,0:T(8,128)(2,1)S(1)} %get-tuple-element.36.y_ref), channel_id=1, source_target_pairs={{0,1},{1,0},{2,3},{3,2},{4,5},{5,4},{6,7},{7,6},{8,9},{9,8},{10,11... | collective-permute-start | bytes 3145736 | tf_op jit(solution)/shard_map/ppermute | solution.py:251
  32.6 5.9 %collective-permute-start.4 = (bf16[128,256]{1,0:T(8,128)(2,1)S(1)}, bf16[128,256]{1,0:T(8,128)(2,1)S(1)}, u32[]{:S(2)}, u32[]{:S(2)}) collective-permute-start(bf16[128,256]{1,0:T(8,128)(2,1)S(1)} %convert_element_type.15), channel_id=1, source_target_pairs={{0,32},{16,48},{32,0},{48,16},{64,96},{80,112},{96,64},{112,80},{1... | collective-permute-start | bytes 196616 | tf_op jit(solution)/shard_map/ppermute | solution.py:254
  34.3 5.6 %collective-permute-start.3 = (bf16[128,256]{1,0:T(8,128)(2,1)S(1)}, bf16[128,256]{1,0:T(8,128)(2,1)S(1)}, u32[]{:S(2)}, u32[]{:S(2)}) collective-permute-start(bf16[128,256]{1,0:T(8,128)(2,1)S(1)} %convert_element_type.15), channel_id=1, source_target_pairs={{0,48},{16,32},{32,16},{48,0},{64,112},{80,96},{96,80},{112,64},{1... | collective-permute-start | bytes 196616 | tf_op jit(solution)/shard_map/ppermute | solution.py:254
  35.7 4.3 %collective-permute-start.2 = (bf16[128,256]{1,0:T(8,128)(2,1)S(1)}, bf16[128,256]{1,0:T(8,128)(2,1)S(1)}, u32[]{:S(2)}, u32[]{:S(2)}) collective-permute-start(bf16[128,256]{1,0:T(8,128)(2,1)S(1)} %convert_element_type.15), channel_id=1, source_target_pairs={{0,16},{16,0},{32,48},{48,32},{64,80},{80,64},{96,112},{112,96},{1... | collective-permute-start | bytes 196616 | tf_op jit(solution)/shard_map/ppermute | solution.py:254
  40.0 7.8 %collective-permute-start.6 = (f32[128,256]{1,0:T(8,128)S(1)}, f32[128,256]{1,0:T(8,128)S(1)}, u32[]{:S(2)}, u32[]{:S(2)}) collective-permute-start(f32[128,256]{1,0:T(8,128)S(1)} %get-tuple-element.38.mine), channel_id=1, source_target_pairs={{0,1},{1,0},{2,3},{3,2},{4,5},{5,4},{6,7},{7,6},{8,9},{9,8},{10,11... | collective-permute-start | bytes 393224 | tf_op jit(solution)/shard_map/ppermute | solution.py:251
  40.1 5.4 %collective-permute-start.7 = (bf16[128,256]{1,0:T(8,128)(2,1)S(1)}, bf16[128,256]{1,0:T(8,128)(2,1)S(1)}, u32[]{:S(2)}, u32[]{:S(2)}) collective-permute-start(bf16[128,256]{1,0:T(8,128)(2,1)S(1)} %get-tuple-element.37), channel_id=1, source_target_pairs={{0,65},{1,64},{16,81},{17,80},{32,97},{33,96},{48,113},{49,112},{6... | collective-permute-start | bytes 196616 | tf_op jit(solution)/shard_map/ppermute | solution.py:340
  42.0 5.8 %collective-permute-start.5 = (bf16[128,256]{1,0:T(8,128)(2,1)S(1)}, bf16[128,256]{1,0:T(8,128)(2,1)S(1)}, u32[]{:S(2)}, u32[]{:S(2)}) collective-permute-start(bf16[128,256]{1,0:T(8,128)(2,1)S(1)} %get-tuple-element.37), channel_id=1, source_target_pairs={{0,64},{16,80},{32,96},{48,112},{64,0},{80,16},{96,32},{112,48},{1... | collective-permute-start | bytes 196616 | tf_op jit(solution)/shard_map/ppermute | solution.py:254
